TPU v7x, 128 devices: a whole 4x4x4 slice. The times are simulated.
128 devices in a mesh: ep: 128 (over z, x, y, core).
Axes of the slice: x: 4, y: 4, z: 4, core: 2. Of those that a mesh axis runs over, the one named last changes fastest.
Arguments:
- tokens: bfloat16 [2, 2048, 3584], P(None, 'ep'), may hold values from -6 to 6
- expert_ids: int32 [2, 2048, 8], P(None, 'ep'), may hold values from 0 to 127, all different within a row; in each aligned block of 16 rows (0 to 15, 16 to 31, ..., all dimensions but the last counted through in order) at most 2 rows name the same one
- combine_weights: float32 [2, 2048, 8], P(None, 'ep'), may hold values from 0.05 to 0.5
- w_gate: bfloat16 [128, 3584, 1024], P('ep'), may hold values from -0.09375 to 0.09375
- w_up: bfloat16 [128, 3584, 1024], P('ep'), may hold values from -0.09375 to 0.09375
- w_down: bfloat16 [128, 1024, 3584], P('ep'), may hold values from -0.1875 to 0.1875
- shared_weights: bfloat16 [3, 3584, 16384], P(None, None, 'ep'), as said below
Outputs:
- moe_out: bfloat16 [2, 2048, 3584], P(None, 'ep')
Inputs may be any that keep to these rules, and one draw needn't show every extreme that they name: `expert_ids`: in each step the 16 rows of one device name any one expert at most 2 times; the 8 experts of a token differ. `shared_weights`: the array is 16 equal copies of one block of 1024 columns, laid end to end along the last dimension.
All inputs are finite; a program needn't handle non-finite values.
Results may differ from a plain program's by a relative error of at most 0.0055.
Values may be sent and summed in bfloat16 or wider, within the bound.
A program may use at most 128 MiB of HBM per device.

v0:
```python
import jax
import jax.numpy as jnp
from jax import lax
from jax.sharding import PartitionSpec as P


def partner_2(block, axis, apart):
    count = lax.axis_size(axis)
    route = []
    for low in range(count):
        high = low | 1 << apart
        if high != low and high < count:
            route += [(low, high), (high, low)]
    return lax.ppermute(block, axis, route)


def expert_rows(token_rows, gate_mat, up_mat, down_mat):
    gate_val = jnp.dot(token_rows, gate_mat, preferred_element_type=jnp.float32)
    up_val = jnp.dot(token_rows, up_mat, preferred_element_type=jnp.float32)
    hidden = (jax.nn.silu(gate_val) * up_val).astype(jnp.bfloat16)
    return jnp.dot(hidden, down_mat, preferred_element_type=jnp.float32).astype(jnp.bfloat16)


def route_tables(step_ids, step_weights, experts, capacity):
    row_count, top_count = step_ids.shape
    pair_count = row_count * top_count
    flat_ids = step_ids.reshape(pair_count)
    onehot = (flat_ids[:, None] == jnp.arange(experts, dtype=jnp.int32)[None, :]).astype(
        jnp.float32
    )
    earlier = (jnp.arange(pair_count)[:, None] > jnp.arange(pair_count)[None, :]).astype(
        jnp.float32
    )
    counts = jnp.dot(earlier, onehot, precision=lax.Precision.HIGHEST)
    slot_index = jnp.sum(counts * onehot, axis=1).astype(jnp.int32)
    position = flat_ids * capacity + slot_index
    placing = (
        position[:, None] == jnp.arange(experts * capacity, dtype=jnp.int32)[None, :]
    ).astype(jnp.float32)
    owner = (
        (jnp.arange(pair_count) // top_count)[:, None] == jnp.arange(row_count)[None, :]
    ).astype(jnp.float32)
    dispatch = jnp.dot(placing.T, owner, precision=lax.Precision.HIGHEST).astype(jnp.bfloat16)
    combine = jnp.dot(
        (owner * step_weights.reshape(pair_count)[:, None]).T,
        placing,
        precision=lax.Precision.HIGHEST,
    )
    return (dispatch, combine)


def join_halves(mine, partner, upper_side, axis_no):
    return jnp.where(
        upper_side,
        jnp.concatenate([partner, mine], axis=axis_no),
        jnp.concatenate([mine, partner], axis=axis_no),
    )


def shared_expert(tokens, shared_weights):
    my_index = lax.axis_index("ep")
    step_count, row_count, model_width = tokens.shape
    gathered = tokens
    for level in range(3):
        partner = partner_2(gathered, "ep", level)
        gathered = join_halves(gathered, partner, my_index >> level & 1 == 1, 1)
    flat_rows = gathered.reshape(-1, model_width)
    gate_val = jnp.dot(flat_rows, shared_weights[0], preferred_element_type=jnp.float32)
    up_val = jnp.dot(flat_rows, shared_weights[1], preferred_element_type=jnp.float32)
    hidden = (jax.nn.silu(gate_val) * up_val).astype(jnp.bfloat16)
    partial_value = lax.dot_general(
        hidden, shared_weights[2], (((1,), (1,)), ((), ())), preferred_element_type=jnp.float32
    )
    partial_value = partial_value.reshape(step_count, 8 * row_count, model_width)
    for level in range(3):
        partial_value = partial_value + partner_2(partial_value, "ep", level)
    group_rank = my_index & 7
    return lax.dynamic_slice_in_dim(partial_value, group_rank * row_count, row_count, 1)


def shards(tokens, expert_ids, combine_weights, w_gate, w_up, w_down, shared_weights):
    step_count, row_count, model_width = tokens.shape
    top_count = expert_ids.shape[2]
    device_count = lax.axis_size("ep")
    experts = w_gate.shape[0] * device_count
    capacity = max(2, row_count * top_count * 2 // experts)
    tables = [
        route_tables(expert_ids[s], combine_weights[s], experts, capacity)
        for s in range(step_count)
    ]
    outgoing = jnp.stack(
        [
            jnp.dot(tables[s][0], tokens[s], preferred_element_type=jnp.float32)
            .astype(jnp.bfloat16)
            .reshape(experts, capacity, model_width)
            for s in range(step_count)
        ]
    )
    received = lax.all_to_all(outgoing, "ep", split_axis=1, concat_axis=1, tiled=True)
    returned = lax.all_to_all(
        expert_rows(received.reshape(-1, model_width), w_gate[0], w_up[0], w_down[0]).reshape(
            received.shape
        ),
        "ep",
        split_axis=1,
        concat_axis=1,
        tiled=True,
    )
    shared = shared_expert(tokens, shared_weights)
    routed = jnp.stack(
        [
            jnp.dot(
                tables[s][1],
                returned[s].reshape(experts * capacity, model_width).astype(jnp.float32),
                precision=lax.Precision.HIGHEST,
            )
            for s in range(step_count)
        ]
    )
    return (shared + routed).astype(jnp.bfloat16)


def solution(mesh):
    placed = (
        P(None, "ep", None),
        P(None, "ep", None),
        P(None, "ep", None),
        P("ep", None, None),
        P("ep", None, None),
        P("ep", None, None),
        P(None, None, "ep"),
    )
    return jax.shard_map(
        shards, mesh=mesh, in_specs=placed, out_specs=P(None, "ep", None), check_vma=False
    )
```

profile of v0, /device:TPU:1, one launch (start us, length us, event | category | flops | bytes accessed | tf_op | source)
XLA Modules:
  0.0 318.1 jit_solution(10798912873108825325)
XLA Ops:
  5.7 2.8 convolution_convert_fusion.1
  8.5 3.9 %stack_reshape.6 = bf16[1,128,2,3584]{3,2,1,0:T(2,128)(2,1)S(1)} reshape(bf16[256,3584]{1,0:T(8,128)(2,1)} %convolution_convert_fusion.1) | data formatting | bytes 3670016 | tf_op jit(solution)/shard_map/stack;reshape | solution.py:91
  12.7 3.9 %collective-permute-done.1 = bf16[2,32,3584]{2,1,0:T(8,128)(2,1)} collective-permute-done((bf16[2,32,3584]{2,1,0:T(8,128)(2,1)S(1)}, bf16[2,32,3584]{2,1,0:T(8,128)(2,1)}, u32[]{:S(2)}, u32[]{:S(2)}) %collective-permute-start.1) | collective-permute-done | bytes 458784 | tf_op jit(solution)/shard_map/ppermute | solution.py:14
  17.9 3.1 collective-permute-start.2
  22.9 4.8 %stack_reshape.7 = bf16[1,128,2,3584]{3,2,1,0:T(2,128)(2,1)} reshape(bf16[256,3584]{1,0:T(8,128)(2,1)} %convolution_convert_fusion) | data formatting | bytes 3670016 | tf_op jit(solution)/shard_map/stack;reshape | solution.py:91
  27.7 8.2 %pad_maximum_fusion = bf16[2,128,2,3584]{3,2,0,1:T(2,128)(2,1)} fusion(bf16[1,128,2,3584]{3,2,0,1:T(2,128)(2,1)} %bitcast.57, bf16[1,128,2,3584]{3,2,0,1:T(2,128)(2,1)S(1)} %bitcast.56), kind=kLoop, calls=%fused_computation.11 | loop fusion | flops 1835008 | bytes 7340032 | tf_op jit(solution)/shard_map/stack | solution.py:91
  36.0 9.3 %all-to-all-start = ((bf16[2,128,2,3584]{3,2,0,1:T(2,128)(2,1)}), bf16[2,128,2,3584]{3,2,0,1:T(2,128)(2,1)}, u32[]{:S(2)}, u32[]{:S(2)}) async-start(bf16[2,128,2,3584]{3,2,0,1:T(2,128)(2,1)} %pad_maximum_fusion), calls=%async_computation | async-start | bytes 7340032 | tf_op jit(solution)/shard_map/all_to_all | solution.py:99
  48.9 2.6 fusion.13
  52.8 39.8 %all-to-all-done = bf16[2,128,2,3584]{3,2,0,1:T(2,128)(2,1)} async-done(((bf16[2,128,2,3584]{3,2,0,1:T(2,128)(2,1)}), bf16[2,128,2,3584]{3,2,0,1:T(2,128)(2,1)}, u32[]{:S(2)}, u32[]{:S(2)}) %all-to-all-start) | async-done | bytes 3670048 | tf_op jit(solution)/shard_map/all_to_all | solution.py:99
  92.5 6.4 %copy.28 = bf16[2,128,2,3584]{3,2,1,0:T(2,128)(2,1)} copy(bf16[2,128,2,3584]{3,2,0,1:T(2,128)(2,1)} %all-to-all-done) | data formatting | bytes 7340032 | tf_op jit(solution)/shard_map/all_to_all | solution.py:99
  99.0 8.4 %reshape.60 = bf16[512,3584]{1,0:T(8,128)(2,1)} reshape(bf16[2,128,2,3584]{3,2,1,0:T(2,128)(2,1)} %copy.28) | data formatting | bytes 7340032 | tf_op jit(solution)/shard_map/reshape | solution.py:101
  107.4 7.3 %fusion.2 = f32[512,1024]{1,0:T(8,128)S(1)} fusion(bf16[512,3584]{1,0:T(8,128)(2,1)} %reshape.60, bf16[1,3584,1024]{2,1,0:T(8,128)(2,1)} %param.11), kind=kOutput, calls=%fused_computation.2 | convolution fusion | flops 3758096384 | bytes 13107200 | tf_op jit(solution)/shard_map/dot_general | solution.py:19
  114.7 5.5 %add.43 = f32[2,128,3584]{2,1,0:T(8,128)} add(f32[2,128,3584]{2,1,0:T(8,128)} %fusion.13, f32[2,128,3584]{2,1,0:T(8,128)} %collective-permute-done.3) | non-fusion elementwise | flops 917504 | bytes 11010048 | tf_op jit(solution)/shard_map/add | solution.py:76
  120.2 16.1 %fusion.6 = bf16[512,3584]{1,0:T(8,128)(2,1)} fusion(bf16[1,1024,3584]{2,1,0:T(8,128)(2,1)} %param.12, f32[512,1024]{1,0:T(8,128)S(1)} %fusion.2, bf16[512,3584]{1,0:T(8,128)(2,1)} %reshape.60, bf16[1,3584,1024]{2,1,0:T(8,128)(2,1)} %param.10), kind=kOutput, calls=%fused_computation.6 | convolution fusion | flops 7521173504 | bytes 24117248 | tf_op jit(solution)/shard_map/dot_general | solution.py:21
  136.3 8.1 %reshape.61 = bf16[2,128,2,3584]{3,2,1,0:T(2,128)(2,1)} reshape(bf16[512,3584]{1,0:T(8,128)(2,1)} %fusion.6) | data formatting | bytes 7340032 | tf_op jit(solution)/shard_map/reshape | solution.py:101
  144.4 6.4 %copy.29 = bf16[2,128,2,3584]{3,2,0,1:T(2,128)(2,1)} copy(bf16[2,128,2,3584]{3,2,1,0:T(2,128)(2,1)} %reshape.61) | data formatting | bytes 7340032 | tf_op jit(solution)/shard_map/reshape | solution.py:101
  150.8 5.8 %all-to-all-start.1 = ((bf16[2,128,2,3584]{3,2,0,1:T(2,128)(2,1)}), bf16[2,128,2,3584]{3,2,0,1:T(2,128)(2,1)}, u32[]{:S(2)}, u32[]{:S(2)}) async-start(bf16[2,128,2,3584]{3,2,0,1:T(2,128)(2,1)} %copy.29), calls=%async_computation.1 | async-start | bytes 7340032 | tf_op jit(solution)/shard_map/all_to_all | solution.py:100
  156.7 73.4 %collective-permute-done.4 = f32[2,128,3584]{2,1,0:T(8,128)} collective-permute-done((f32[2,128,3584]{2,1,0:T(8,128)}, f32[2,128,3584]{2,1,0:T(8,128)}, u32[]{:S(2)}, u32[]{:S(2)}) %collective-permute-start.4) | collective-permute-done | bytes 3670048 | tf_op jit(solution)/shard_map/ppermute | solution.py:14
  230.0 5.5 %add.44 = f32[2,128,3584]{2,1,0:T(8,128)} add(f32[2,128,3584]{2,1,0:T(8,128)} %add.43, f32[2,128,3584]{2,1,0:T(8,128)} %collective-permute-done.4) | non-fusion elementwise | flops 917504 | bytes 11010048 | tf_op jit(solution)/shard_map/add | solution.py:76
  236.4 5.2 %all-to-all-done.1 = bf16[2,128,2,3584]{3,2,0,1:T(2,128)(2,1)} async-done(((bf16[2,128,2,3584]{3,2,0,1:T(2,128)(2,1)}), bf16[2,128,2,3584]{3,2,0,1:T(2,128)(2,1)}, u32[]{:S(2)}, u32[]{:S(2)}) %all-to-all-start.1) | async-done | bytes 3670048 | tf_op jit(solution)/shard_map/all_to_all | solution.py:100
  241.6 5.8 %fusion.51 = (bf16[1,128,2,3584]{3,2,0,1:T(2,128)(2,1)}, bf16[1,128,2,3584]{3,2,0,1:T(2,128)(2,1)S(1)}) fusion(bf16[2,128,2,3584]{3,2,0,1:T(2,128)(2,1)} %all-to-all-done.1), kind=kLoop, calls=%fused_computation.72 | loop fusion | bytes 7340032 | tf_op jit(solution)/shard_map/slice | solution.py:114
  247.4 4.9 %reshape_squeeze.14 = bf16[256,3584]{1,0:T(8,128)(2,1)} reshape(bf16[1,128,2,3584]{3,2,0,1:T(2,128)(2,1)} %get-tuple-element.5) | data formatting | bytes 3670016 | tf_op jit(solution)/shard_map/reshape;squeeze | solution.py:114
  256.3 2.3 convolution_bitcast_fusion
  258.7 57.6 %collective-permute-done.5 = f32[2,128,3584]{2,1,0:T(8,128)} collective-permute-done((f32[2,128,3584]{2,1,0:T(8,128)}, f32[2,128,3584]{2,1,0:T(8,128)}, u32[]{:S(2)}, u32[]{:S(2)}) %collective-permute-start.5) | collective-permute-done | bytes 3670048 | tf_op jit(solution)/shard_map/ppermute | solution.py:14
  (41 shorter events, 20.8 us)
Async XLA Ops:
  0.0 3.1 collective-permute-start
  4.3 12.3 %collective-permute-start.1 = (bf16[2,32,3584]{2,1,0:T(8,128)(2,1)S(1)}, bf16[2,32,3584]{2,1,0:T(8,128)(2,1)}, u32[]{:S(2)}, u32[]{:S(2)}) collective-permute-start(bf16[2,32,3584]{2,1,0:T(8,128)(2,1)S(1)} %maximum_select_fusion.2), channel_id=1, source_target_pairs={{0,2},{2,0},{1,3},{3,1},{4,6},{6,4},{5,7},{7,5},{8,10},{10,8},{9,1... | collective-permute-start | bytes 1376264 | tf_op jit(solution)/shard_map/ppermute | solution.py:14
  8.5 12.5 %copy-start = (bf16[2,16,3584]{2,1,0:T(8,128)(2,1)S(1)}, bf16[2,16,3584]{2,1,0:T(8,128)(2,1)}, u32[]{:S(2)}) copy-start(bf16[2,16,3584]{2,1,0:T(8,128)(2,1)} %param.7) | copy-start | bytes 688132
  17.9 27.4 %collective-permute-start.2 = (bf16[2,64,3584]{2,1,0:T(8,128)(2,1)S(1)}, bf16[2,64,3584]{2,1,0:T(8,128)(2,1)}, u32[]{:S(2)}, u32[]{:S(2)}) collective-permute-start(bf16[2,64,3584]{2,1,0:T(8,128)(2,1)S(1)} %maximum_select_fusion.1), channel_id=1, source_target_pairs={{0,4},{4,0},{1,5},{5,1},{2,6},{6,2},{3,7},{7,3},{8,12},{12,8},{9,1... | collective-permute-start | bytes 2752520 | tf_op jit(solution)/shard_map/ppermute | solution.py:14
  36.0 56.6 %all-to-all-start = ((bf16[2,128,2,3584]{3,2,0,1:T(2,128)(2,1)}), bf16[2,128,2,3584]{3,2,0,1:T(2,128)(2,1)}, u32[]{:S(2)}, u32[]{:S(2)}) async-start(bf16[2,128,2,3584]{3,2,0,1:T(2,128)(2,1)} %pad_maximum_fusion), calls=%async_computation | async-start | bytes 7340032 | tf_op jit(solution)/shard_map/all_to_all | solution.py:99
  45.3 2.3 copy-start.1
  51.5 63.2 %collective-permute-start.3 = (f32[2,128,3584]{2,1,0:T(8,128)}, f32[2,128,3584]{2,1,0:T(8,128)}, u32[]{:S(2)}, u32[]{:S(2)}) collective-permute-start(f32[2,128,3584]{2,1,0:T(8,128)} %fusion.13), channel_id=1, source_target_pairs={{0,1},{1,0},{2,3},{3,2},{4,5},{5,4},{6,7},{7,6},{8,9},{9,8},{10,11... | collective-permute-start | bytes 11010056 | tf_op jit(solution)/shard_map/ppermute | solution.py:14
  120.2 109.8 %collective-permute-start.4 = (f32[2,128,3584]{2,1,0:T(8,128)}, f32[2,128,3584]{2,1,0:T(8,128)}, u32[]{:S(2)}, u32[]{:S(2)}) collective-permute-start(f32[2,128,3584]{2,1,0:T(8,128)} %add.43), channel_id=1, source_target_pairs={{0,2},{2,0},{1,3},{3,1},{4,6},{6,4},{5,7},{7,5},{8,10},{10,8},{9,1... | collective-permute-start | bytes 11010056 | tf_op jit(solution)/shard_map/ppermute | solution.py:14
  150.8 90.8 %all-to-all-start.1 = ((bf16[2,128,2,3584]{3,2,0,1:T(2,128)(2,1)}), bf16[2,128,2,3584]{3,2,0,1:T(2,128)(2,1)}, u32[]{:S(2)}, u32[]{:S(2)}) async-start(bf16[2,128,2,3584]{3,2,0,1:T(2,128)(2,1)} %copy.29), calls=%async_computation.1 | async-start | bytes 7340032 | tf_op jit(solution)/shard_map/all_to_all | solution.py:100
  156.7 78.9 %copy-start.2 = (f32[2,16,8]{1,2,0:T(8,128)S(1)}, f32[2,16,8]{1,2,0:T(8,128)}, u32[]{:S(2)}) copy-start(f32[2,16,8]{1,2,0:T(8,128)} %param.9) | copy-start | bytes 3076
  235.5 80.7 %collective-permute-start.5 = (f32[2,128,3584]{2,1,0:T(8,128)}, f32[2,128,3584]{2,1,0:T(8,128)}, u32[]{:S(2)}, u32[]{:S(2)}) collective-permute-start(f32[2,128,3584]{2,1,0:T(8,128)} %add.44), channel_id=1, source_target_pairs={{0,4},{4,0},{1,5},{5,1},{2,6},{6,2},{3,7},{7,3},{8,12},{12,8},{9,1... | collective-permute-start | bytes 11010056 | tf_op jit(solution)/shard_map/ppermute | solution.py:14
where the time goes:
time: 321 us; the launch traced here: 318 us
  waiting for transfers between devices  180 us (56%)
  local copies, waits for them, and re-layouts  52.2 us (16%)
  matrix products  38 us (12%)
  other arithmetic  25.7 us (8%)
  starting transfers between devices  22.4 us (7%)
    ppermute x6, waiting for transfers between devices, partner_2(): return lax.ppermute(block, axis, route)  135 us
    all_to_all x1, waiting for transfers between devices, shards(): lax.all_to_all(outgoing, 'ep', split_axis=1, concat_axis=1, tiled=True)  39.8 us
    dot_general x1, matrix products, expert_rows(): jnp.dot(hidden, down_mat, preferred_element_type=jnp.float32)  16.1 us
    reshape x2, local copies, waits for them, and re-layouts, shards(): expert_rows(received.reshape(-1, model_width), w_gate[0], w_up[0], w_down...  14.6 us
    add x2, other arithmetic, shared_expert(): partial_value = partial_value + partner_2(partial_value, 'ep', level)  11 us
    all_to_all x1, starting transfers between devices, shards(): lax.all_to_all(outgoing, 'ep', split_axis=1, concat_axis=1, tiled=True)  9.33 us
    another operation x2, local copies, waits for them, and re-layouts, shards(): jnp.stack([jnp.dot(tables[s][0], tokens[s], preferred_element_type=jnp.fl...  8.71 us
    reshape x1, local copies, waits for them, and re-layouts, shards(): received.reshape(-1, model_width)  8.4 us
  transfers between devices with their start and end apart: 8, of which 5 were waited for; matrix products, arithmetic and copies ran while one was open for 33% of the time, Pallas kernels for 0%

commit v1 on v0

--- a/solution.py
+++ b/solution.py
@@ -61,7 +61,7 @@
     my_index = lax.axis_index("ep")
     step_count, row_count, model_width = tokens.shape
     gathered = tokens
-    for level in range(3):
+    for level in (2, 1, 0):
         partner = partner_2(gathered, "ep", level)
         gathered = join_halves(gathered, partner, my_index >> level & 1 == 1, 1)
     flat_rows = gathered.reshape(-1, model_width)
@@ -72,10 +72,13 @@
         hidden, shared_weights[2], (((1,), (1,)), ((), ())), preferred_element_type=jnp.float32
     )
     partial_value = partial_value.reshape(step_count, 8 * row_count, model_width)
-    for level in range(3):
-        partial_value = partial_value + partner_2(partial_value, "ep", level)
-    group_rank = my_index & 7
-    return lax.dynamic_slice_in_dim(partial_value, group_rank * row_count, row_count, 1)
+    for level in (0, 1, 2):
+        half = partial_value.shape[1] // 2
+        bit = my_index >> level & 1
+        keep = lax.dynamic_slice_in_dim(partial_value, bit * half, half, 1)
+        send = lax.dynamic_slice_in_dim(partial_value, (1 - bit) * half, half, 1)
+        partial_value = keep + partner_2(send, "ep", level)
+    return partial_value
 
 
 def shards(tokens, expert_ids, combine_weights, w_gate, w_up, w_down, shared_weights):

time: 321 us -> 229 us (0.71)
  waiting for transfers between devices: 180 us -> 96.5 us
  other arithmetic: 25.7 us -> 14.2 us
  starting transfers between devices: 22.4 us -> 25.8 us
    ppermute x6, waiting for transfers between devices: 135 us -> 57.5 us  [partner_2(): return lax.ppermute(block, axis, route)]
    add x2, other arithmetic: 11 us -> 3.53 us  [shared_expert(): partial_value = keep + partner_2(send, 'ep', level)]
    all_to_all x1, waiting for transfers between devices: 5.18 us -> 0.01 us  [shards(): lax.all_to_all(expert_rows(received.reshape(-1, model_width), w_gate[0],...]
    select_n x3, other arithmetic: 4.53 us -> 0.59 us  [join_halves(): jnp.where(upper_side, jnp.concatenate([partner, mine], axis=axis_no), jnp...]
  transfers between devices with their start and end apart: 8 -> 8, of which waited for: 5 -> 3; matrix products, arithmetic and copies ran while one was open for 33% -> 45% of each run, Pallas kernels for 0% -> 0%
where the time goes in v1:
time: 229 us; the launch traced here: 228 us
  waiting for transfers between devices  96.5 us (42%)
  local copies, waits for them, and re-layouts  54 us (24%)
  matrix products  37.6 us (16%)
  starting transfers between devices  25.8 us (11%)
  other arithmetic  14.2 us (6%)
    ppermute x6, waiting for transfers between devices, partner_2(): return lax.ppermute(block, axis, route)  57.5 us
    all_to_all x1, waiting for transfers between devices, shards(): lax.all_to_all(outgoing, 'ep', split_axis=1, concat_axis=1, tiled=True)  38.9 us
    dot_general x1, matrix products, expert_rows(): jnp.dot(hidden, down_mat, preferred_element_type=jnp.float32)  16.7 us
    reshape x2, local copies, waits for them, and re-layouts, shards(): expert_rows(received.reshape(-1, model_width), w_gate[0], w_up[0], w_down...  14.6 us
    all_to_all x1, starting transfers between devices, shards(): lax.all_to_all(outgoing, 'ep', split_axis=1, concat_axis=1, tiled=True)  10.3 us
    ppermute x6, starting transfers between devices, partner_2(): return lax.ppermute(block, axis, route)  10.2 us
    dot_general x1, matrix products, expert_rows(): up_val = jnp.dot(token_rows, up_mat, preferred_element_type=jnp.float32)  9.54 us
    another operation x2, local copies, waits for them, and re-layouts, shards(): jnp.stack([jnp.dot(tables[s][0], tokens[s], preferred_element_type=jnp.fl...  8.71 us
  transfers between devices with their start and end apart: 8, of which 3 were waited for; matrix products, arithmetic and copies ran while one was open for 45% of the time, Pallas kernels for 0%

profile of v1, /device:TPU:1, one launch (start us, length us, event | category | flops | bytes accessed | tf_op | source)
XLA Modules:
  0.0 228.2 jit_solution(1217827684432112928)
XLA Ops:
  0.0 3.7 %collective-permute-start = (bf16[2,16,3584]{2,1,0:T(8,128)(2,1)}, bf16[2,16,3584]{2,1,0:T(8,128)(2,1)S(1)}, u32[]{:S(2)}, u32[]{:S(2)}) collective-permute-start(bf16[2,16,3584]{2,1,0:T(8,128)(2,1)} %param.7), channel_id=1, source_target_pairs={{0,4},{4,0},{1,5},{5,1},{2,6},{6,2},{3,7},{7,3},{8,12},{12,8},{9,1... | collective-permute-start | bytes 688136 | tf_op jit(solution)/shard_map/ppermute | solution.py:14
  5.1 2.8 %convolution_convert_fusion = bf16[256,3584]{1,0:T(8,128)(2,1)} fusion(bf16[256,16]{0,1:T(8,128)(2,1)S(1)} %convolution_convert_fusion.2, bf16[2,16,3584]{2,1,0:T(8,128)(2,1)} %param.7), kind=kOutput, calls=%fused_computation.7 | convolution fusion | flops 30277632 | bytes 1957888 | tf_op jit(solution)/shard_map/dot_general | solution.py:96
  7.9 3.9 %stack_reshape.7 = bf16[1,128,2,3584]{3,2,1,0:T(2,128)(2,1)S(1)} reshape(bf16[256,3584]{1,0:T(8,128)(2,1)} %convolution_convert_fusion) | data formatting | bytes 3670016 | tf_op jit(solution)/shard_map/stack;reshape | solution.py:94
  12.4 1.9 convolution_convert_fusion.1
  14.4 4.8 %stack_reshape.6 = bf16[1,128,2,3584]{3,2,1,0:T(2,128)(2,1)} reshape(bf16[256,3584]{1,0:T(8,128)(2,1)} %convolution_convert_fusion.1) | data formatting | bytes 3670016 | tf_op jit(solution)/shard_map/stack;reshape | solution.py:94
  19.7 8.3 %pad_maximum_fusion = bf16[2,128,2,3584]{3,2,0,1:T(2,128)(2,1)} fusion(bf16[1,128,2,3584]{3,2,0,1:T(2,128)(2,1)S(1)} %bitcast.56, bf16[1,128,2,3584]{3,2,0,1:T(2,128)(2,1)} %bitcast.57), kind=kLoop, calls=%fused_computation.11 | loop fusion | flops 1835008 | bytes 7340032 | tf_op jit(solution)/shard_map/stack | solution.py:94
  28.0 10.3 %all-to-all-start = ((bf16[2,128,2,3584]{3,2,0,1:T(2,128)(2,1)}), bf16[2,128,2,3584]{3,2,0,1:T(2,128)(2,1)}, u32[]{:S(2)}, u32[]{:S(2)}) async-start(bf16[2,128,2,3584]{3,2,0,1:T(2,128)(2,1)} %pad_maximum_fusion), calls=%async_computation | async-start | bytes 7340032 | tf_op jit(solution)/shard_map/all_to_all | solution.py:102
  39.8 2.1 collective-permute-done.2
  44.2 1.8 copy-done
  46.6 38.9 %all-to-all-done = bf16[2,128,2,3584]{3,2,0,1:T(2,128)(2,1)} async-done(((bf16[2,128,2,3584]{3,2,0,1:T(2,128)(2,1)}), bf16[2,128,2,3584]{3,2,0,1:T(2,128)(2,1)}, u32[]{:S(2)}, u32[]{:S(2)}) %all-to-all-start) | async-done | bytes 3670048 | tf_op jit(solution)/shard_map/all_to_all | solution.py:102
  85.5 6.5 %copy.28 = bf16[2,128,2,3584]{3,2,1,0:T(2,128)(2,1)} copy(bf16[2,128,2,3584]{3,2,0,1:T(2,128)(2,1)} %all-to-all-done) | data formatting | bytes 7340032 | tf_op jit(solution)/shard_map/all_to_all | solution.py:102
  92.0 8.4 %reshape.60 = bf16[512,3584]{1,0:T(8,128)(2,1)} reshape(bf16[2,128,2,3584]{3,2,1,0:T(2,128)(2,1)} %copy.28) | data formatting | bytes 7340032 | tf_op jit(solution)/shard_map/reshape | solution.py:104
  100.4 9.5 %fusion.2 = f32[512,1024]{1,0:T(8,128)} fusion(bf16[512,3584]{1,0:T(8,128)(2,1)} %reshape.60, bf16[1,3584,1024]{2,1,0:T(8,128)(2,1)} %param.11), kind=kOutput, calls=%fused_computation.2 | convolution fusion | flops 3758096384 | bytes 13107200 | tf_op jit(solution)/shard_map/dot_general | solution.py:19
  109.9 16.7 %fusion.6 = bf16[512,3584]{1,0:T(8,128)(2,1)} fusion(bf16[1,1024,3584]{2,1,0:T(8,128)(2,1)} %param.12, f32[512,1024]{1,0:T(8,128)} %fusion.2, bf16[512,3584]{1,0:T(8,128)(2,1)} %reshape.60, bf16[1,3584,1024]{2,1,0:T(8,128)(2,1)} %param.10), kind=kOutput, calls=%fused_computation.6 | convolution fusion | flops 7521173504 | bytes 24117248 | tf_op jit(solution)/shard_map/dot_general | solution.py:21
  126.6 8.1 %reshape.61 = bf16[2,128,2,3584]{3,2,1,0:T(2,128)(2,1)} reshape(bf16[512,3584]{1,0:T(8,128)(2,1)} %fusion.6) | data formatting | bytes 7340032 | tf_op jit(solution)/shard_map/reshape | solution.py:104
  134.7 6.5 %copy.29 = bf16[2,128,2,3584]{3,2,0,1:T(2,128)(2,1)} copy(bf16[2,128,2,3584]{3,2,1,0:T(2,128)(2,1)} %reshape.61) | data formatting | bytes 7340032 | tf_op jit(solution)/shard_map/reshape | solution.py:104
  141.1 5.3 %all-to-all-start.1 = ((bf16[2,128,2,3584]{3,2,0,1:T(2,128)(2,1)}), bf16[2,128,2,3584]{3,2,0,1:T(2,128)(2,1)}, u32[]{:S(2)}, u32[]{:S(2)}) async-start(bf16[2,128,2,3584]{3,2,0,1:T(2,128)(2,1)} %copy.29), calls=%async_computation.1 | async-start | bytes 7340032 | tf_op jit(solution)/shard_map/all_to_all | solution.py:103
  146.5 2.3 dynamic-slice_add_fusion
  151.3 55.4 %collective-permute-done.4 = f32[2,32,3584]{2,1,0:T(8,128)} collective-permute-done((f32[2,32,3584]{2,1,0:T(8,128)S(1)}, f32[2,32,3584]{2,1,0:T(8,128)}, u32[]{:S(2)}, u32[]{:S(2)}) %collective-permute-start.4) | collective-permute-done | bytes 917536 | tf_op jit(solution)/shard_map/ppermute | solution.py:14
  208.0 2.6 %collective-permute-start.5 = (f32[2,16,3584]{2,1,0:T(8,128)S(1)}, f32[2,16,3584]{2,1,0:T(8,128)}, u32[]{:S(2)}, u32[]{:S(2)}) collective-permute-start(f32[2,16,3584]{2,1,0:T(8,128)S(1)} %constant_dynamic-slice_fusion), channel_id=1, source_target_pairs={{0,4},{4,0},{1,5},{5,1},{2,6},{6,2},{3,7},{7,3},{8,12},{12,8},{9,1... | collective-permute-start | bytes 1376264 | tf_op jit(solution)/shard_map/ppermute | solution.py:14
  210.6 5.8 %fusion.50 = (bf16[1,128,2,3584]{3,2,0,1:T(2,128)(2,1)S(1)}, bf16[1,128,2,3584]{3,2,0,1:T(2,128)(2,1)}) fusion(bf16[2,128,2,3584]{3,2,0,1:T(2,128)(2,1)} %all-to-all-done.1), kind=kLoop, calls=%fused_computation.76 | loop fusion | bytes 7340032 | tf_op jit(solution)/shard_map/slice | solution.py:117
  216.5 4.9 %reshape_squeeze.15 = bf16[256,3584]{1,0:T(8,128)(2,1)} reshape(bf16[1,128,2,3584]{3,2,0,1:T(2,128)(2,1)} %get-tuple-element.6) | data formatting | bytes 3670016 | tf_op jit(solution)/shard_map/reshape;squeeze | solution.py:117
  223.1 2.5 %convolution_bitcast_fusion = f32[1,16,3584]{2,1,0:T(8,128)S(1)} fusion(f32[16,256]{1,0:T(8,128)S(1)} %fusion.25, bf16[256,3584]{1,0:T(8,128)(2,1)} %reshape_squeeze.15), kind=kOutput, calls=%fused_computation.9 | convolution fusion | flops 176160768 | bytes 2080768 | tf_op jit(solution)/shard_map/dot_general | solution.py:115
  226.4 1.8 fusion.24
  (48 shorter events, 13.2 us)
Async XLA Ops:
  0.0 19.2 %collective-permute-start = (bf16[2,16,3584]{2,1,0:T(8,128)(2,1)}, bf16[2,16,3584]{2,1,0:T(8,128)(2,1)S(1)}, u32[]{:S(2)}, u32[]{:S(2)}) collective-permute-start(bf16[2,16,3584]{2,1,0:T(8,128)(2,1)} %param.7), channel_id=1, source_target_pairs={{0,4},{4,0},{1,5},{5,1},{2,6},{6,2},{3,7},{7,3},{8,12},{12,8},{9,1... | collective-permute-start | bytes 688136 | tf_op jit(solution)/shard_map/ppermute | solution.py:14
  7.9 4.5 %copy-start.2 = (bf16[2,16,3584]{2,1,0:T(8,128)(2,1)S(1)}, bf16[2,16,3584]{2,1,0:T(8,128)(2,1)}, u32[]{:S(2)}) copy-start(bf16[2,16,3584]{2,1,0:T(8,128)(2,1)} %param.7) | copy-start | bytes 688132
  19.2 19.0 %collective-permute-start.1 = (bf16[2,32,3584]{2,1,0:T(8,128)(2,1)S(1)}, bf16[2,32,3584]{2,1,0:T(8,128)(2,1)S(1)}, u32[]{:S(2)}, u32[]{:S(2)}) collective-permute-start(bf16[2,32,3584]{2,1,0:T(8,128)(2,1)S(1)} %maximum_select_fusion.2), channel_id=1, source_target_pairs={{0,2},{2,0},{1,3},{3,1},{4,6},{6,4},{5,7},{7,5},{8,10},{10,8},{9,1... | collective-permute-start | bytes 1376264 | tf_op jit(solution)/shard_map/ppermute | solution.py:14
  28.0 57.5 %all-to-all-start = ((bf16[2,128,2,3584]{3,2,0,1:T(2,128)(2,1)}), bf16[2,128,2,3584]{3,2,0,1:T(2,128)(2,1)}, u32[]{:S(2)}, u32[]{:S(2)}) async-start(bf16[2,128,2,3584]{3,2,0,1:T(2,128)(2,1)} %pad_maximum_fusion), calls=%async_computation | async-start | bytes 7340032 | tf_op jit(solution)/shard_map/all_to_all | solution.py:102
  38.4 3.5 %collective-permute-start.2 = (bf16[2,64,3584]{2,1,0:T(8,128)(2,1)S(1)}, bf16[2,64,3584]{2,1,0:T(8,128)(2,1)S(1)}, u32[]{:S(2)}, u32[]{:S(2)}) collective-permute-start(bf16[2,64,3584]{2,1,0:T(8,128)(2,1)S(1)} %maximum_select_fusion.1), channel_id=1, source_target_pairs={{0,1},{1,0},{2,3},{3,2},{4,5},{5,4},{6,7},{7,6},{8,9},{9,8},{10,11... | collective-permute-start | bytes 2752520 | tf_op jit(solution)/shard_map/ppermute | solution.py:14
  39.8 2.5 %copy-start.3 = (bf16[3,3584,128]{2,1,0:T(8,128)(2,1)S(1)}, bf16[3,3584,128]{2,1,0:T(8,128)(2,1)}, u32[]{:S(2)}) copy-start(bf16[3,3584,128]{2,1,0:T(8,128)(2,1)} %param.13) | copy-start | bytes 8257540
  44.2 1.8 copy-start
  46.2 100.3 %collective-permute-start.3 = (f32[2,64,3584]{2,1,0:T(8,128)S(1)}, f32[2,64,3584]{2,1,0:T(8,128)}, u32[]{:S(2)}, u32[]{:S(2)}) collective-permute-start(f32[2,64,3584]{2,1,0:T(8,128)S(1)} %constant_dynamic-slice_fusion.2), channel_id=1, source_target_pairs={{0,1},{1,0},{2,3},{3,2},{4,5},{5,4},{6,7},{7,6},{8,9},{9,8},{10,11... | collective-permute-start | bytes 5505032 | tf_op jit(solution)/shard_map/ppermute | solution.py:14
  141.1 69.5 %all-to-all-start.1 = ((bf16[2,128,2,3584]{3,2,0,1:T(2,128)(2,1)}), bf16[2,128,2,3584]{3,2,0,1:T(2,128)(2,1)}, u32[]{:S(2)}, u32[]{:S(2)}) async-start(bf16[2,128,2,3584]{3,2,0,1:T(2,128)(2,1)} %copy.29), calls=%async_computation.1 | async-start | bytes 7340032 | tf_op jit(solution)/shard_map/all_to_all | solution.py:103
  146.5 3.9 %copy-start.4 = (f32[2,16,8]{1,2,0:T(8,128)S(1)}, f32[2,16,8]{1,2,0:T(8,128)}, u32[]{:S(2)}) copy-start(f32[2,16,8]{1,2,0:T(8,128)} %param.9) | copy-start | bytes 3076
  148.8 57.9 %collective-permute-start.4 = (f32[2,32,3584]{2,1,0:T(8,128)S(1)}, f32[2,32,3584]{2,1,0:T(8,128)}, u32[]{:S(2)}, u32[]{:S(2)}) collective-permute-start(f32[2,32,3584]{2,1,0:T(8,128)S(1)} %constant_dynamic-slice_fusion.1), channel_id=1, source_target_pairs={{0,2},{2,0},{1,3},{3,1},{4,6},{6,4},{5,7},{7,5},{8,10},{10,8},{9,1... | collective-permute-start | bytes 2752520 | tf_op jit(solution)/shard_map/ppermute | solution.py:14
  208.0 18.3 %collective-permute-start.5 = (f32[2,16,3584]{2,1,0:T(8,128)S(1)}, f32[2,16,3584]{2,1,0:T(8,128)}, u32[]{:S(2)}, u32[]{:S(2)}) collective-permute-start(f32[2,16,3584]{2,1,0:T(8,128)S(1)} %constant_dynamic-slice_fusion), channel_id=1, source_target_pairs={{0,4},{4,0},{1,5},{5,1},{2,6},{6,2},{3,7},{7,3},{8,12},{12,8},{9,1... | collective-permute-start | bytes 1376264 | tf_op jit(solution)/shard_map/ppermute | solution.py:14
  223.1 2.5 %copy-start.1 = (bf16[256,3584]{1,0:T(8,128)(2,1)S(1)}, bf16[256,3584]{1,0:T(8,128)(2,1)}, u32[]{:S(2)}) copy-start(bf16[256,3584]{1,0:T(8,128)(2,1)} %reshape_squeeze.14) | copy-start | bytes 5505028

commit v2 on v1

--- a/solution.py
+++ b/solution.py
@@ -2,6 +2,8 @@
 import jax.numpy as jnp
 from jax import lax
 from jax.sharding import PartitionSpec as P
+from jax.experimental import pallas as pl
+from jax.experimental.pallas import tpu as pltpu
 
 
 def partner_2(block, axis, apart):
@@ -14,11 +16,51 @@
     return lax.ppermute(block, axis, route)
 
 
-def expert_rows(token_rows, gate_mat, up_mat, down_mat):
-    gate_val = jnp.dot(token_rows, gate_mat, preferred_element_type=jnp.float32)
-    up_val = jnp.dot(token_rows, up_mat, preferred_element_type=jnp.float32)
-    hidden = (jax.nn.silu(gate_val) * up_val).astype(jnp.bfloat16)
-    return jnp.dot(hidden, down_mat, preferred_element_type=jnp.float32).astype(jnp.bfloat16)
+def ffn_kernel(x_ref, gate_ref, up_ref, down_ref, out_ref, total):
+    step = pl.program_id(0)
+
+    @pl.when(step == 0)
+    def _():
+        total[...] = jnp.zeros_like(total)
+
+    rows = x_ref[...]
+    gate_val = jnp.dot(rows, gate_ref[...], preferred_element_type=jnp.float32)
+    up_val = jnp.dot(rows, up_ref[...], preferred_element_type=jnp.float32)
+    hidden = (gate_val / (1.0 + jnp.exp(-gate_val)) * up_val).astype(jnp.bfloat16)
+    total[...] += jnp.dot(hidden, down_ref[...], preferred_element_type=jnp.float32)
+
+    @pl.when(step == pl.num_programs(0) - 1)
+    def _():
+        out_ref[...] = total[...].astype(out_ref.dtype)
+
+
+def expert_rows(token_rows, w_gate, w_up, w_down, tile=256):
+    row_count, model_width = token_rows.shape
+    hidden_width = w_gate.shape[2]
+    steps = hidden_width // tile
+    flops = 6 * row_count * model_width * hidden_width
+    weight_bytes = 3 * model_width * hidden_width * 2
+    return pl.pallas_call(
+        ffn_kernel,
+        out_shape=jax.ShapeDtypeStruct((row_count, model_width), jnp.bfloat16),
+        grid=(steps,),
+        in_specs=[
+            pl.BlockSpec((row_count, model_width), lambda f: (0, 0)),
+            pl.BlockSpec((None, model_width, tile), lambda f: (0, 0, f)),
+            pl.BlockSpec((None, model_width, tile), lambda f: (0, 0, f)),
+            pl.BlockSpec((None, tile, model_width), lambda f: (0, f, 0)),
+        ],
+        out_specs=pl.BlockSpec((row_count, model_width), lambda f: (0, 0)),
+        scratch_shapes=[pltpu.VMEM((row_count, model_width), jnp.float32)],
+        compiler_params=pltpu.CompilerParams(
+            dimension_semantics=("arbitrary",), vmem_limit_bytes=60 * 1024 * 1024
+        ),
+        cost_estimate=pl.CostEstimate(
+            flops=flops,
+            transcendentals=row_count * hidden_width,
+            bytes_accessed=weight_bytes + 4 * row_count * model_width,
+        ),
+    )(token_rows, w_gate, w_up, w_down)
 
 
 def route_tables(step_ids, step_weights, experts, capacity):
@@ -101,7 +143,7 @@
     )
     received = lax.all_to_all(outgoing, "ep", split_axis=1, concat_axis=1, tiled=True)
     returned = lax.all_to_all(
-        expert_rows(received.reshape(-1, model_width), w_gate[0], w_up[0], w_down[0]).reshape(
+        expert_rows(received.reshape(-1, model_width), w_gate, w_up, w_down).reshape(
             received.shape
         ),
         "ep",

time: 229 us -> 222 us (0.969)
  matrix products: 37.6 us -> 11.4 us
  Pallas kernels: 0 us -> 19.2 us
    dot_general x2 -> x0, matrix products: 26.2 us -> none  [the longest x1 16.7 us: expert_rows(): jnp.dot(hidden, down_mat, preferred_element_type=jnp.float32)]
    pallas_call x0 -> x1, Pallas kernels: none -> 19.2 us  [expert_rows(): pl.pallas_call(ffn_kernel, out_shape=jax.ShapeDtypeStruct((row_count, mod...]
  transfers between devices with their start and end apart: 8 -> 8, of which waited for: 3 -> 3; matrix products, arithmetic and copies ran while one was open for 45% -> 34% of each run, Pallas kernels for 0% -> 9%
where the time goes in v2:
time: 222 us; the launch traced here: 221 us
  waiting for transfers between devices  96.4 us (43%)
  local copies, waits for them, and re-layouts  53.8 us (24%)
  starting transfers between devices  25.9 us (12%)
  Pallas kernels  19.2 us (9%)
  other arithmetic  14.2 us (6%)
  matrix products  11.4 us (5%)
    ppermute x6, waiting for transfers between devices, partner_2(): return lax.ppermute(block, axis, route)  57.3 us
    all_to_all x1, waiting for transfers between devices, shards(): lax.all_to_all(outgoing, 'ep', split_axis=1, concat_axis=1, tiled=True)  39.1 us
    pallas_call x1, Pallas kernels, expert_rows(): pl.pallas_call(ffn_kernel, out_shape=jax.ShapeDtypeStruct((row_count, mod...  19.2 us
    reshape x2, local copies, waits for them, and re-layouts, shards(): expert_rows(received.reshape(-1, model_width), w_gate, w_up, w_down)  14.6 us
    ppermute x6, starting transfers between devices, partner_2(): return lax.ppermute(block, axis, route)  10.4 us
    all_to_all x1, starting transfers between devices, shards(): lax.all_to_all(outgoing, 'ep', split_axis=1, concat_axis=1, tiled=True)  10.3 us
    another operation x2, local copies, waits for them, and re-layouts, shards(): jnp.stack([jnp.dot(tables[s][0], tokens[s], preferred_element_type=jnp.fl...  8.71 us
    reshape x1, local copies, waits for them, and re-layouts, shards(): received.reshape(-1, model_width)  8.38 us
  transfers between devices with their start and end apart: 8, of which 3 were waited for; matrix products, arithmetic and copies ran while one was open for 34% of the time, Pallas kernels for 9%

profile of v2, /device:TPU:1, one launch (start us, length us, event | category | flops | bytes accessed | tf_op | source)
XLA Modules:
  0.0 221.1 jit_solution(5060356962042705269)
XLA Ops:
  0.0 3.7 %collective-permute-start = (bf16[2,16,3584]{2,1,0:T(8,128)(2,1)}, bf16[2,16,3584]{2,1,0:T(8,128)(2,1)S(1)}, u32[]{:S(2)}, u32[]{:S(2)}) collective-permute-start(bf16[2,16,3584]{2,1,0:T(8,128)(2,1)} %param.7), channel_id=1, source_target_pairs={{0,4},{4,0},{1,5},{5,1},{2,6},{6,2},{3,7},{7,3},{8,12},{12,8},{9,1... | collective-permute-start | bytes 688136 | tf_op jit(solution)/shard_map/ppermute | solution.py:16
  5.1 2.8 %convolution_convert_fusion = bf16[256,3584]{1,0:T(8,128)(2,1)} fusion(bf16[256,16]{0,1:T(8,128)(2,1)S(1)} %convolution_convert_fusion.2, bf16[2,16,3584]{2,1,0:T(8,128)(2,1)} %param.7), kind=kOutput, calls=%fused_computation | convolution fusion | flops 30277632 | bytes 1957888 | tf_op jit(solution)/shard_map/dot_general | solution.py:138
  7.9 3.9 %stack_reshape.7 = bf16[1,128,2,3584]{3,2,1,0:T(2,128)(2,1)S(1)} reshape(bf16[256,3584]{1,0:T(8,128)(2,1)} %convolution_convert_fusion) | data formatting | bytes 3670016 | tf_op jit(solution)/shard_map/stack;reshape | solution.py:136
  12.4 1.9 convolution_convert_fusion.1
  14.4 4.8 %stack_reshape.6 = bf16[1,128,2,3584]{3,2,1,0:T(2,128)(2,1)} reshape(bf16[256,3584]{1,0:T(8,128)(2,1)} %convolution_convert_fusion.1) | data formatting | bytes 3670016 | tf_op jit(solution)/shard_map/stack;reshape | solution.py:136
  19.7 8.3 %pad_maximum_fusion = bf16[2,128,2,3584]{3,2,0,1:T(2,128)(2,1)} fusion(bf16[1,128,2,3584]{3,2,0,1:T(2,128)(2,1)S(1)} %bitcast.39, bf16[1,128,2,3584]{3,2,0,1:T(2,128)(2,1)} %bitcast.40), kind=kLoop, calls=%fused_computation.4 | loop fusion | flops 1835008 | bytes 7340032 | tf_op jit(solution)/shard_map/stack | solution.py:136
  28.0 10.3 %all-to-all-start = ((bf16[2,128,2,3584]{3,2,0,1:T(2,128)(2,1)}), bf16[2,128,2,3584]{3,2,0,1:T(2,128)(2,1)}, u32[]{:S(2)}, u32[]{:S(2)}) async-start(bf16[2,128,2,3584]{3,2,0,1:T(2,128)(2,1)} %pad_maximum_fusion), calls=%async_computation | async-start | bytes 7340032 | tf_op jit(solution)/shard_map/all_to_all | solution.py:144
  39.8 2.1 collective-permute-done.2
  46.4 39.1 %all-to-all-done = bf16[2,128,2,3584]{3,2,0,1:T(2,128)(2,1)} async-done(((bf16[2,128,2,3584]{3,2,0,1:T(2,128)(2,1)}), bf16[2,128,2,3584]{3,2,0,1:T(2,128)(2,1)}, u32[]{:S(2)}, u32[]{:S(2)}) %all-to-all-start) | async-done | bytes 3670048 | tf_op jit(solution)/shard_map/all_to_all | solution.py:144
  85.5 6.5 %copy.21 = bf16[2,128,2,3584]{3,2,1,0:T(2,128)(2,1)} copy(bf16[2,128,2,3584]{3,2,0,1:T(2,128)(2,1)} %all-to-all-done) | data formatting | bytes 7340032 | tf_op jit(solution)/shard_map/all_to_all | solution.py:144
  92.0 8.4 %reshape.60.x_ref = bf16[512,3584]{1,0:T(8,128)(2,1)} reshape(bf16[2,128,2,3584]{3,2,1,0:T(2,128)(2,1)} %copy.21) | data formatting | bytes 7340032 | tf_op jit(solution)/shard_map/reshape | solution.py:146
  100.4 19.2 %shard_map.73 = bf16[512,3584]{1,0:T(8,128)(2,1)} custom-call(bf16[512,3584]{1,0:T(8,128)(2,1)} %reshape.60.x_ref, bf16[1,3584,1024]{2,1,0:T(8,128)(2,1)} %gate_ref.1, bf16[1,3584,1024]{2,1,0:T(8,128)(2,1)} %up_ref.1, bf16[1,1024,3584]{2,1,0:T(8,128)(2,1)} %down_ref.1), custom_call_target="tpu_custom_call" | custom-call | flops 11274289152 | bytes 29360128 | tf_op jit(solution)/shard_map/pallas_call | solution.py:43
  119.5 8.1 %reshape.61 = bf16[2,128,2,3584]{3,2,1,0:T(2,128)(2,1)} reshape(bf16[512,3584]{1,0:T(8,128)(2,1)} %shard_map.73) | data formatting | bytes 7340032 | tf_op jit(solution)/shard_map/reshape | solution.py:146
  127.6 6.5 %copy.22 = bf16[2,128,2,3584]{3,2,0,1:T(2,128)(2,1)} copy(bf16[2,128,2,3584]{3,2,1,0:T(2,128)(2,1)} %reshape.61) | data formatting | bytes 7340032 | tf_op jit(solution)/shard_map/reshape | solution.py:146
  134.1 5.3 %all-to-all-start.1 = ((bf16[2,128,2,3584]{3,2,0,1:T(2,128)(2,1)}), bf16[2,128,2,3584]{3,2,0,1:T(2,128)(2,1)}, u32[]{:S(2)}, u32[]{:S(2)}) async-start(bf16[2,128,2,3584]{3,2,0,1:T(2,128)(2,1)} %copy.22), calls=%async_computation.1 | async-start | bytes 7340032 | tf_op jit(solution)/shard_map/all_to_all | solution.py:145
  139.4 2.3 %dynamic-slice_add_fusion = f32[2,64,3584]{2,1,0:T(8,128)S(1)} fusion(f32[2,64,3584]{2,1,0:T(8,128)} %collective-permute-done.3, f32[2,128,3584]{2,1,0:T(8,128)} %copy-done, s32[]{:T(128)S(6)} %select_n.79), kind=kLoop, calls=%fused_computation.6 | loop fusion | flops 458752 | bytes 5505028 | tf_op jit(solution)/shard_map/add | solution.py:122
  141.8 1.7 collective-permute-start.4
  144.4 55.2 %collective-permute-done.4 = f32[2,32,3584]{2,1,0:T(8,128)} collective-permute-done((f32[2,32,3584]{2,1,0:T(8,128)S(1)}, f32[2,32,3584]{2,1,0:T(8,128)}, u32[]{:S(2)}, u32[]{:S(2)}) %collective-permute-start.4) | collective-permute-done | bytes 917536 | tf_op jit(solution)/shard_map/ppermute | solution.py:16
  201.0 2.6 %collective-permute-start.5 = (f32[2,16,3584]{2,1,0:T(8,128)S(1)}, f32[2,16,3584]{2,1,0:T(8,128)}, u32[]{:S(2)}, u32[]{:S(2)}) collective-permute-start(f32[2,16,3584]{2,1,0:T(8,128)S(1)} %constant_dynamic-slice_fusion), channel_id=1, source_target_pairs={{0,4},{4,0},{1,5},{5,1},{2,6},{6,2},{3,7},{7,3},{8,12},{12,8},{9,1... | collective-permute-start | bytes 1376264 | tf_op jit(solution)/shard_map/ppermute | solution.py:16
  203.6 5.8 %fusion.36 = (bf16[1,128,2,3584]{3,2,0,1:T(2,128)(2,1)S(1)}, bf16[1,128,2,3584]{3,2,0,1:T(2,128)(2,1)}) fusion(bf16[2,128,2,3584]{3,2,0,1:T(2,128)(2,1)} %all-to-all-done.1), kind=kLoop, calls=%fused_computation.67 | loop fusion | bytes 7340032 | tf_op jit(solution)/shard_map/slice | solution.py:159
  209.4 4.9 %reshape_squeeze.15 = bf16[256,3584]{1,0:T(8,128)(2,1)} reshape(bf16[1,128,2,3584]{3,2,0,1:T(2,128)(2,1)} %get-tuple-element.6) | data formatting | bytes 3670016 | tf_op jit(solution)/shard_map/reshape;squeeze | solution.py:159
  214.3 1.7 reshape_squeeze.14
  216.0 2.5 %convolution_bitcast_fusion = f32[1,16,3584]{2,1,0:T(8,128)S(1)} fusion(f32[16,256]{1,0:T(8,128)S(1)} %fusion.12, bf16[256,3584]{1,0:T(8,128)(2,1)} %reshape_squeeze.15), kind=kOutput, calls=%fused_computation.2 | convolution fusion | flops 176160768 | bytes 2080768 | tf_op jit(solution)/shard_map/dot_general | solution.py:157
  219.3 1.8 fusion.11
  (47 shorter events, 11.6 us)
Async XLA Ops:
  0.0 19.2 %collective-permute-start = (bf16[2,16,3584]{2,1,0:T(8,128)(2,1)}, bf16[2,16,3584]{2,1,0:T(8,128)(2,1)S(1)}, u32[]{:S(2)}, u32[]{:S(2)}) collective-permute-start(bf16[2,16,3584]{2,1,0:T(8,128)(2,1)} %param.7), channel_id=1, source_target_pairs={{0,4},{4,0},{1,5},{5,1},{2,6},{6,2},{3,7},{7,3},{8,12},{12,8},{9,1... | collective-permute-start | bytes 688136 | tf_op jit(solution)/shard_map/ppermute | solution.py:16
  7.9 4.5 %copy-start.2 = (bf16[2,16,3584]{2,1,0:T(8,128)(2,1)S(1)}, bf16[2,16,3584]{2,1,0:T(8,128)(2,1)}, u32[]{:S(2)}) copy-start(bf16[2,16,3584]{2,1,0:T(8,128)(2,1)} %param.7) | copy-start | bytes 688132
  19.2 19.0 %collective-permute-start.1 = (bf16[2,32,3584]{2,1,0:T(8,128)(2,1)S(1)}, bf16[2,32,3584]{2,1,0:T(8,128)(2,1)S(1)}, u32[]{:S(2)}, u32[]{:S(2)}) collective-permute-start(bf16[2,32,3584]{2,1,0:T(8,128)(2,1)S(1)} %maximum_select_fusion.2), channel_id=1, source_target_pairs={{0,2},{2,0},{1,3},{3,1},{4,6},{6,4},{5,7},{7,5},{8,10},{10,8},{9,1... | collective-permute-start | bytes 1376264 | tf_op jit(solution)/shard_map/ppermute | solution.py:16
  28.0 57.5 %all-to-all-start = ((bf16[2,128,2,3584]{3,2,0,1:T(2,128)(2,1)}), bf16[2,128,2,3584]{3,2,0,1:T(2,128)(2,1)}, u32[]{:S(2)}, u32[]{:S(2)}) async-start(bf16[2,128,2,3584]{3,2,0,1:T(2,128)(2,1)} %pad_maximum_fusion), calls=%async_computation | async-start | bytes 7340032 | tf_op jit(solution)/shard_map/all_to_all | solution.py:144
  38.4 3.5 %collective-permute-start.2 = (bf16[2,64,3584]{2,1,0:T(8,128)(2,1)S(1)}, bf16[2,64,3584]{2,1,0:T(8,128)(2,1)S(1)}, u32[]{:S(2)}, u32[]{:S(2)}) collective-permute-start(bf16[2,64,3584]{2,1,0:T(8,128)(2,1)S(1)} %maximum_select_fusion.1), channel_id=1, source_target_pairs={{0,1},{1,0},{2,3},{3,2},{4,5},{5,4},{6,7},{7,6},{8,9},{9,8},{10,11... | collective-permute-start | bytes 2752520 | tf_op jit(solution)/shard_map/ppermute | solution.py:16
  39.8 2.5 %copy-start.3 = (bf16[3,3584,128]{2,1,0:T(8,128)(2,1)S(1)}, bf16[3,3584,128]{2,1,0:T(8,128)(2,1)}, u32[]{:S(2)}) copy-start(bf16[3,3584,128]{2,1,0:T(8,128)(2,1)} %param.13) | copy-start | bytes 8257540
  44.2 1.8 copy-start
  46.0 93.4 %collective-permute-start.3 = (f32[2,64,3584]{2,1,0:T(8,128)S(1)}, f32[2,64,3584]{2,1,0:T(8,128)}, u32[]{:S(2)}, u32[]{:S(2)}) collective-permute-start(f32[2,64,3584]{2,1,0:T(8,128)S(1)} %constant_dynamic-slice_fusion.2), channel_id=1, source_target_pairs={{0,1},{1,0},{2,3},{3,2},{4,5},{5,4},{6,7},{7,6},{8,9},{9,8},{10,11... | collective-permute-start | bytes 5505032 | tf_op jit(solution)/shard_map/ppermute | solution.py:16
  134.1 69.5 %all-to-all-start.1 = ((bf16[2,128,2,3584]{3,2,0,1:T(2,128)(2,1)}), bf16[2,128,2,3584]{3,2,0,1:T(2,128)(2,1)}, u32[]{:S(2)}, u32[]{:S(2)}) async-start(bf16[2,128,2,3584]{3,2,0,1:T(2,128)(2,1)} %copy.22), calls=%async_computation.1 | async-start | bytes 7340032 | tf_op jit(solution)/shard_map/all_to_all | solution.py:145
  141.7 1.8 copy-start.4
  141.8 57.9 %collective-permute-start.4 = (f32[2,32,3584]{2,1,0:T(8,128)S(1)}, f32[2,32,3584]{2,1,0:T(8,128)}, u32[]{:S(2)}, u32[]{:S(2)}) collective-permute-start(f32[2,32,3584]{2,1,0:T(8,128)S(1)} %constant_dynamic-slice_fusion.1), channel_id=1, source_target_pairs={{0,2},{2,0},{1,3},{3,1},{4,6},{6,4},{5,7},{7,5},{8,10},{10,8},{9,1... | collective-permute-start | bytes 2752520 | tf_op jit(solution)/shard_map/ppermute | solution.py:16
  201.0 18.3 %collective-permute-start.5 = (f32[2,16,3584]{2,1,0:T(8,128)S(1)}, f32[2,16,3584]{2,1,0:T(8,128)}, u32[]{:S(2)}, u32[]{:S(2)}) collective-permute-start(f32[2,16,3584]{2,1,0:T(8,128)S(1)} %constant_dynamic-slice_fusion), channel_id=1, source_target_pairs={{0,4},{4,0},{1,5},{5,1},{2,6},{6,2},{3,7},{7,3},{8,12},{12,8},{9,1... | collective-permute-start | bytes 1376264 | tf_op jit(solution)/shard_map/ppermute | solution.py:16
  216.0 2.5 %copy-start.1 = (bf16[256,3584]{1,0:T(8,128)(2,1)S(1)}, bf16[256,3584]{1,0:T(8,128)(2,1)}, u32[]{:S(2)}) copy-start(bf16[256,3584]{1,0:T(8,128)(2,1)} %reshape_squeeze.14) | copy-start | bytes 5505028

commit v3 on v2

--- a/solution.py
+++ b/solution.py
@@ -129,39 +129,28 @@
     device_count = lax.axis_size("ep")
     experts = w_gate.shape[0] * device_count
     capacity = max(2, row_count * top_count * 2 // experts)
-    tables = [
-        route_tables(expert_ids[s], combine_weights[s], experts, capacity)
-        for s in range(step_count)
-    ]
-    outgoing = jnp.stack(
-        [
-            jnp.dot(tables[s][0], tokens[s], preferred_element_type=jnp.float32)
+    routed_steps = []
+    for s in range(step_count):
+        dispatch, combine = route_tables(expert_ids[s], combine_weights[s], experts, capacity)
+        outgoing = (
+            jnp.dot(dispatch, tokens[s], preferred_element_type=jnp.float32)
             .astype(jnp.bfloat16)
             .reshape(experts, capacity, model_width)
-            for s in range(step_count)
-        ]
-    )
-    received = lax.all_to_all(outgoing, "ep", split_axis=1, concat_axis=1, tiled=True)
-    returned = lax.all_to_all(
-        expert_rows(received.reshape(-1, model_width), w_gate, w_up, w_down).reshape(
-            received.shape
-        ),
-        "ep",
-        split_axis=1,
-        concat_axis=1,
-        tiled=True,
-    )
-    shared = shared_expert(tokens, shared_weights)
-    routed = jnp.stack(
-        [
+        )
+        received = lax.all_to_all(outgoing, "ep", split_axis=0, concat_axis=0, tiled=True)
+        expert_out = expert_rows(
+            received.reshape(-1, model_width), w_gate, w_up, w_down
+        ).reshape(received.shape)
+        returned = lax.all_to_all(expert_out, "ep", split_axis=0, concat_axis=0, tiled=True)
+        routed_steps.append(
             jnp.dot(
-                tables[s][1],
-                returned[s].reshape(experts * capacity, model_width).astype(jnp.float32),
+                combine,
+                returned.reshape(experts * capacity, model_width).astype(jnp.float32),
                 precision=lax.Precision.HIGHEST,
             )
-            for s in range(step_count)
-        ]
-    )
+        )
+    shared = shared_expert(tokens, shared_weights)
+    routed = jnp.stack(routed_steps)
     return (shared + routed).astype(jnp.bfloat16)
 
 

time: 222 us -> 177 us (0.80)
  waiting for transfers between devices: 96.4 us -> 55.2 us
  local copies, waits for them, and re-layouts: 53.8 us -> 35.3 us
  starting transfers between devices: 25.9 us -> 42.4 us
  Pallas kernels: 19.2 us -> 26.6 us
  other arithmetic: 14.2 us -> 8.94 us
  matrix products: 11.4 us -> 7.55 us
    ppermute x6, waiting for transfers between devices: 57.3 us -> 15.9 us  [partner_2(): return lax.ppermute(block, axis, route)]
    another operation x4 -> x0, local copies, waits for them, and re-layouts: 15.3 us -> none  [the longest x2 8.71 us: shards(): jnp.stack([jnp.dot(tables[s][0], tokens[s], preferred_element_type=jnp.fl...]
    all_to_all x2 -> x4, starting transfers between devices: 15.6 us -> 29.8 us  [the longest x2 15.3 us: shards(): lax.all_to_all(outgoing, 'ep', split_axis=0, concat_axis=0, tiled=True)]
    another operation x1 -> x0, other arithmetic: 8.26 us -> none  [shards(): jnp.stack([jnp.dot(tables[s][0], tokens[s], preferred_element_type=jnp.fl...]
    reshape x2 -> x6, local copies, waits for them, and re-layouts: 14.6 us -> 22.7 us  [the longest x2 9.53 us: shards(): expert_out = expert_rows(received.reshape(-1, model_width), w_gate, w_up,...]
    pallas_call x1 -> x2, Pallas kernels: 19.2 us -> 26.6 us  [expert_rows(): pl.pallas_call(ffn_kernel, out_shape=jax.ShapeDtypeStruct((row_count, mod...]
    all_to_all x1 -> x0, local copies, waits for them, and re-layouts: 6.46 us -> none  [shards(): lax.all_to_all(outgoing, 'ep', split_axis=1, concat_axis=1, tiled=True)]
    slice x1 -> x0, local copies, waits for them, and re-layouts: 5.83 us -> none  [shards(): returned[s].reshape(experts * capacity, model_width).astype(jnp.float32)]
  transfers between devices with their start and end apart: 8 -> 10, of which waited for: 3 -> 6; matrix products, arithmetic and copies ran while one was open for 34% -> 26% of each run, Pallas kernels for 9% -> 15%
where the time goes in v3:
time: 177 us; the launch traced here: 176 us
  waiting for transfers between devices  55.2 us (31%)
  starting transfers between devices  42.4 us (24%)
  local copies, waits for them, and re-layouts  35.3 us (20%)
  Pallas kernels  26.6 us (15%)
  other arithmetic  8.94 us (5%)
  matrix products  7.55 us (4%)
    pallas_call x2, Pallas kernels, expert_rows(): pl.pallas_call(ffn_kernel, out_shape=jax.ShapeDtypeStruct((row_count, mod...  26.6 us
    all_to_all x2, waiting for transfers between devices, shards(): lax.all_to_all(outgoing, 'ep', split_axis=0, concat_axis=0, tiled=True)  20.5 us
    all_to_all x2, waiting for transfers between devices, shards(): lax.all_to_all(expert_out, 'ep', split_axis=0, concat_axis=0, tiled=True)  18.8 us
    ppermute x6, waiting for transfers between devices, partner_2(): return lax.ppermute(block, axis, route)  15.9 us
    all_to_all x2, starting transfers between devices, shards(): lax.all_to_all(outgoing, 'ep', split_axis=0, concat_axis=0, tiled=True)  15.3 us
    all_to_all x2, starting transfers between devices, shards(): lax.all_to_all(expert_out, 'ep', split_axis=0, concat_axis=0, tiled=True)  14.4 us
    ppermute x6, starting transfers between devices, partner_2(): return lax.ppermute(block, axis, route)  12.6 us
    reshape x2, local copies, waits for them, and re-layouts, shards(): expert_out = expert_rows(received.reshape(-1, model_width), w_gate, w_up,...  9.53 us
  transfers between devices with their start and end apart: 10, of which 6 were waited for; matrix products, arithmetic and copies ran while one was open for 26% of the time, Pallas kernels for 15%

profile of v3, /device:TPU:1, one launch (start us, length us, event | category | flops | bytes accessed | tf_op | source)
XLA Modules:
  0.0 176.1 jit_solution(8156991914871504612)
XLA Ops:
  0.0 3.7 %collective-permute-start = (bf16[2,16,3584]{2,1,0:T(8,128)(2,1)}, bf16[2,16,3584]{2,1,0:T(8,128)(2,1)S(1)}, u32[]{:S(2)}, u32[]{:S(2)}) collective-permute-start(bf16[2,16,3584]{2,1,0:T(8,128)(2,1)} %param.7), channel_id=1, source_target_pairs={{0,4},{4,0},{1,5},{5,1},{2,6},{6,2},{3,7},{7,3},{8,12},{12,8},{9,1... | collective-permute-start | bytes 688136 | tf_op jit(solution)/shard_map/ppermute | solution.py:16
  3.7 5.4 %collective-permute-done = bf16[2,16,3584]{2,1,0:T(8,128)(2,1)S(1)} collective-permute-done((bf16[2,16,3584]{2,1,0:T(8,128)(2,1)}, bf16[2,16,3584]{2,1,0:T(8,128)(2,1)S(1)}, u32[]{:S(2)}, u32[]{:S(2)}) %collective-permute-start) | collective-permute-done | bytes 229408 | tf_op jit(solution)/shard_map/ppermute | solution.py:16
  12.6 8.4 %collective-permute-done.1 = bf16[2,32,3584]{2,1,0:T(8,128)(2,1)S(1)} collective-permute-done((bf16[2,32,3584]{2,1,0:T(8,128)(2,1)S(1)}, bf16[2,32,3584]{2,1,0:T(8,128)(2,1)S(1)}, u32[]{:S(2)}, u32[]{:S(2)}) %collective-permute-start.1) | collective-permute-done | bytes 458784 | tf_op jit(solution)/shard_map/ppermute | solution.py:16
  21.1 2.4 %collective-permute-start.2 = (bf16[2,64,3584]{2,1,0:T(8,128)(2,1)S(1)}, bf16[2,64,3584]{2,1,0:T(8,128)(2,1)}, u32[]{:S(2)}, u32[]{:S(2)}) collective-permute-start(bf16[2,64,3584]{2,1,0:T(8,128)(2,1)S(1)} %maximum_select_fusion.1), channel_id=1, source_target_pairs={{0,1},{1,0},{2,3},{3,2},{4,5},{5,4},{6,7},{7,6},{8,9},{9,8},{10,11... | collective-permute-start | bytes 2752520 | tf_op jit(solution)/shard_map/ppermute | solution.py:16
  26.2 10.0 %all-to-all-start.2 = ((bf16[128,2,3584]{2,1,0:T(2,128)(2,1)}), bf16[128,2,3584]{2,1,0:T(2,128)(2,1)S(1)}, u32[]{:S(2)}, u32[]{:S(2)}) async-start(bf16[128,2,3584]{2,1,0:T(2,128)(2,1)} %reshape.82), calls=%async_computation.2 | async-start | bytes 3670016 | tf_op jit(solution)/shard_map/all_to_all | solution.py:140
  36.8 2.0 %maximum_select_fusion = bf16[2,128,3584]{2,1,0:T(8,128)(2,1)S(1)} fusion(bf16[2,64,3584]{2,1,0:T(8,128)(2,1)S(1)} %maximum_select_fusion.1, bf16[2,64,3584]{2,1,0:T(8,128)(2,1)} %collective-permute-done.2, pred[]{:T(512)S(6)} %eq.95), kind=kLoop, calls=%fused_computation.4 | loop fusion | flops 8257536 | bytes 3670017 | tf_op jit(solution)/shard_map/jit(_where)/select_n | solution.py:95
  44.4 1.9 %convolution_convert_fusion.1 = bf16[256,3584]{1,0:T(8,128)(2,1)} fusion(bf16[256,16]{1,0:T(8,128)(2,1)S(1)} %convolution_convert_fusion.3, bf16[2,16,3584]{2,1,0:T(8,128)(2,1)S(1)} %copy-done.4), kind=kOutput, calls=%fused_computation.1 | convolution fusion | flops 30277632 | bytes 2015232 | tf_op jit(solution)/shard_map/dot_general | solution.py:136
  46.4 4.8 %reshape.78 = bf16[128,2,3584]{2,1,0:T(2,128)(2,1)} reshape(bf16[256,3584]{1,0:T(8,128)(2,1)} %convolution_convert_fusion.1) | data formatting | bytes 3670016 | tf_op jit(solution)/shard_map/reshape | solution.py:138
  51.1 12.7 %all-to-all-done.2 = bf16[128,2,3584]{2,1,0:T(2,128)(2,1)S(1)} async-done(((bf16[128,2,3584]{2,1,0:T(2,128)(2,1)}), bf16[128,2,3584]{2,1,0:T(2,128)(2,1)S(1)}, u32[]{:S(2)}, u32[]{:S(2)}) %all-to-all-start.2) | async-done | bytes 1835040 | tf_op jit(solution)/shard_map/all_to_all | solution.py:140
  63.9 5.3 %all-to-all-start = ((bf16[128,2,3584]{2,1,0:T(2,128)(2,1)}), bf16[128,2,3584]{2,1,0:T(2,128)(2,1)}, u32[]{:S(2)}, u32[]{:S(2)}) async-start(bf16[128,2,3584]{2,1,0:T(2,128)(2,1)} %reshape.78), calls=%async_computation | async-start | bytes 3670016 | tf_op jit(solution)/shard_map/all_to_all | solution.py:140
  70.9 13.3 %shard_map.74 = bf16[256,3584]{1,0:T(8,128)(2,1)} custom-call(bf16[256,3584]{1,0:T(8,128)(2,1)} %reshape.83.x_ref, bf16[1,3584,1024]{2,1,0:T(8,128)(2,1)} %gate_ref.3, bf16[1,3584,1024]{2,1,0:T(8,128)(2,1)} %up_ref.3, bf16[1,1024,3584]{2,1,0:T(8,128)(2,1)} %down_ref.3), custom_call_target="tpu_custom_call" | custom-call | flops 5637144576 | bytes 25690112 | tf_op jit(solution)/shard_map/pallas_call | solution.py:43
  84.2 4.8 %reshape.84 = bf16[128,2,3584]{2,1,0:T(2,128)(2,1)} reshape(bf16[256,3584]{1,0:T(8,128)(2,1)} %shard_map.74) | data formatting | bytes 3670016 | tf_op jit(solution)/shard_map/reshape | solution.py:143
  89.0 7.8 %all-to-all-done = bf16[128,2,3584]{2,1,0:T(2,128)(2,1)} async-done(((bf16[128,2,3584]{2,1,0:T(2,128)(2,1)}), bf16[128,2,3584]{2,1,0:T(2,128)(2,1)}, u32[]{:S(2)}, u32[]{:S(2)}) %all-to-all-start) | async-done | bytes 1835040 | tf_op jit(solution)/shard_map/all_to_all | solution.py:140
  96.8 4.3 %all-to-all-start.3 = ((bf16[128,2,3584]{2,1,0:T(2,128)(2,1)}), bf16[128,2,3584]{2,1,0:T(2,128)(2,1)S(1)}, u32[]{:S(2)}, u32[]{:S(2)}) async-start(bf16[128,2,3584]{2,1,0:T(2,128)(2,1)} %reshape.84), calls=%async_computation.3 | async-start | bytes 3670016 | tf_op jit(solution)/shard_map/all_to_all | solution.py:144
  101.1 2.3 %dynamic-slice_add_fusion = f32[2,64,3584]{2,1,0:T(8,128)S(1)} fusion(f32[2,64,3584]{2,1,0:T(8,128)} %collective-permute-done.3, f32[2,128,3584]{2,1,0:T(8,128)} %copy-done, s32[]{:T(128)S(6)} %select_n.79), kind=kLoop, calls=%fused_computation.5 | loop fusion | flops 458752 | bytes 5505028 | tf_op jit(solution)/shard_map/add | solution.py:122
  106.6 4.9 %reshape.79.x_ref = bf16[256,3584]{1,0:T(8,128)(2,1)} reshape(bf16[128,2,3584]{2,1,0:T(2,128)(2,1)} %all-to-all-done) | data formatting | bytes 3670016 | tf_op jit(solution)/shard_map/reshape | solution.py:142
  111.5 13.3 %shard_map.73 = bf16[256,3584]{1,0:T(8,128)(2,1)} custom-call(bf16[256,3584]{1,0:T(8,128)(2,1)} %reshape.79.x_ref, bf16[1,3584,1024]{2,1,0:T(8,128)(2,1)} %gate_ref.3, bf16[1,3584,1024]{2,1,0:T(8,128)(2,1)} %up_ref.3, bf16[1,1024,3584]{2,1,0:T(8,128)(2,1)} %down_ref.3), custom_call_target="tpu_custom_call" | custom-call | flops 5637144576 | bytes 25690112 | tf_op jit(solution)/shard_map/pallas_call | solution.py:43
  124.8 4.8 %reshape.80 = bf16[128,2,3584]{2,1,0:T(2,128)(2,1)} reshape(bf16[256,3584]{1,0:T(8,128)(2,1)} %shard_map.73) | data formatting | bytes 3670016 | tf_op jit(solution)/shard_map/reshape | solution.py:143
  129.6 10.1 %all-to-all-start.1 = ((bf16[128,2,3584]{2,1,0:T(2,128)(2,1)}), bf16[128,2,3584]{2,1,0:T(2,128)(2,1)}, u32[]{:S(2)}, u32[]{:S(2)}) async-start(bf16[128,2,3584]{2,1,0:T(2,128)(2,1)} %reshape.80), calls=%async_computation.1 | async-start | bytes 3670016 | tf_op jit(solution)/shard_map/all_to_all | solution.py:144
  139.9 2.1 %collective-permute-done.4 = f32[2,32,3584]{2,1,0:T(8,128)} collective-permute-done((f32[2,32,3584]{2,1,0:T(8,128)S(1)}, f32[2,32,3584]{2,1,0:T(8,128)}, u32[]{:S(2)}, u32[]{:S(2)}) %collective-permute-start.4) | collective-permute-done | bytes 917536 | tf_op jit(solution)/shard_map/ppermute | solution.py:16
  143.7 2.6 %collective-permute-start.5 = (f32[2,16,3584]{2,1,0:T(8,128)S(1)}, f32[2,16,3584]{2,1,0:T(8,128)}, u32[]{:S(2)}, u32[]{:S(2)}) collective-permute-start(f32[2,16,3584]{2,1,0:T(8,128)S(1)} %constant_dynamic-slice_fusion), channel_id=1, source_target_pairs={{0,4},{4,0},{1,5},{5,1},{2,6},{6,2},{3,7},{7,3},{8,12},{12,8},{9,1... | collective-permute-start | bytes 1376264 | tf_op jit(solution)/shard_map/ppermute | solution.py:16
  148.3 18.8 %all-to-all-done.1 = bf16[128,2,3584]{2,1,0:T(2,128)(2,1)} async-done(((bf16[128,2,3584]{2,1,0:T(2,128)(2,1)}), bf16[128,2,3584]{2,1,0:T(2,128)(2,1)}, u32[]{:S(2)}, u32[]{:S(2)}) %all-to-all-start.1) | async-done | bytes 1835040 | tf_op jit(solution)/shard_map/all_to_all | solution.py:144
  167.1 4.9 %reshape.81 = bf16[256,3584]{1,0:T(8,128)(2,1)} reshape(bf16[128,2,3584]{2,1,0:T(2,128)(2,1)} %all-to-all-done.1) | data formatting | bytes 3670016 | tf_op jit(solution)/shard_map/reshape | solution.py:148
  174.3 1.8 %fusion.11 = bf16[2,16,3584]{2,1,0:T(8,128)(2,1)} fusion(f32[1,16,3584]{2,1,0:T(8,128)S(1)} %convolution_bitcast_fusion, f32[1,16,3584]{2,1,0:T(8,128)S(1)} %convolution_bitcast_fusion.1, f32[2,16,3584]{2,1,0:T(8,128)} %collective-permute-done.5, f32[2,32,3584]{2,1,0:T(8,128)S(1)} %dynamic-slice_add_fusion.1, s32[]{:T(128)S(6)} %select_n.83), kind=kLoop, calls=%fused_computation.25 | loop fusion | flops 458752 | bytes 1605636 | tf_op jit(solution)/shard_map/convert_element_type | solution.py:154
  (54 shorter events, 23.5 us)
Async XLA Ops:
  0.0 23.8 %copy-start.4 = (bf16[2,16,3584]{2,1,0:T(8,128)(2,1)S(1)}, bf16[2,16,3584]{2,1,0:T(8,128)(2,1)}, u32[]{:S(2)}) copy-start(bf16[2,16,3584]{2,1,0:T(8,128)(2,1)} %param.7) | copy-start | bytes 688132
  0.0 9.1 %collective-permute-start = (bf16[2,16,3584]{2,1,0:T(8,128)(2,1)}, bf16[2,16,3584]{2,1,0:T(8,128)(2,1)S(1)}, u32[]{:S(2)}, u32[]{:S(2)}) collective-permute-start(bf16[2,16,3584]{2,1,0:T(8,128)(2,1)} %param.7), channel_id=1, source_target_pairs={{0,4},{4,0},{1,5},{5,1},{2,6},{6,2},{3,7},{7,3},{8,12},{12,8},{9,1... | collective-permute-start | bytes 688136 | tf_op jit(solution)/shard_map/ppermute | solution.py:16
  10.3 10.7 %collective-permute-start.1 = (bf16[2,32,3584]{2,1,0:T(8,128)(2,1)S(1)}, bf16[2,32,3584]{2,1,0:T(8,128)(2,1)S(1)}, u32[]{:S(2)}, u32[]{:S(2)}) collective-permute-start(bf16[2,32,3584]{2,1,0:T(8,128)(2,1)S(1)} %maximum_select_fusion.2), channel_id=1, source_target_pairs={{0,2},{2,0},{1,3},{3,1},{4,6},{6,4},{5,7},{7,5},{8,10},{10,8},{9,1... | collective-permute-start | bytes 1376264 | tf_op jit(solution)/shard_map/ppermute | solution.py:16
  21.1 15.7 %collective-permute-start.2 = (bf16[2,64,3584]{2,1,0:T(8,128)(2,1)S(1)}, bf16[2,64,3584]{2,1,0:T(8,128)(2,1)}, u32[]{:S(2)}, u32[]{:S(2)}) collective-permute-start(bf16[2,64,3584]{2,1,0:T(8,128)(2,1)S(1)} %maximum_select_fusion.1), channel_id=1, source_target_pairs={{0,1},{1,0},{2,3},{3,2},{4,5},{5,4},{6,7},{7,6},{8,9},{9,8},{10,11... | collective-permute-start | bytes 2752520 | tf_op jit(solution)/shard_map/ppermute | solution.py:16
  26.2 37.7 %all-to-all-start.2 = ((bf16[128,2,3584]{2,1,0:T(2,128)(2,1)}), bf16[128,2,3584]{2,1,0:T(2,128)(2,1)S(1)}, u32[]{:S(2)}, u32[]{:S(2)}) async-start(bf16[128,2,3584]{2,1,0:T(2,128)(2,1)} %reshape.82), calls=%async_computation.2 | async-start | bytes 3670016 | tf_op jit(solution)/shard_map/all_to_all | solution.py:140
  36.8 2.3 %copy-start.5 = (bf16[3,3584,128]{2,1,0:T(8,128)(2,1)S(1)}, bf16[3,3584,128]{2,1,0:T(8,128)(2,1)}, u32[]{:S(2)}) copy-start(bf16[3,3584,128]{2,1,0:T(8,128)(2,1)} %param.13) | copy-start | bytes 8257540
  41.0 2.3 %copy-start = (f32[2,128,3584]{2,1,0:T(8,128)}, f32[2,128,3584]{2,1,0:T(8,128)S(1)}, u32[]{:S(2)}) copy-start(f32[2,128,3584]{2,1,0:T(8,128)S(1)} %fusion.2) | copy-start | bytes 11010052
  43.4 57.7 %collective-permute-start.3 = (f32[2,64,3584]{2,1,0:T(8,128)}, f32[2,64,3584]{2,1,0:T(8,128)}, u32[]{:S(2)}, u32[]{:S(2)}) collective-permute-start(f32[2,64,3584]{2,1,0:T(8,128)} %constant_dynamic-slice_fusion.2), channel_id=1, source_target_pairs={{0,1},{1,0},{2,3},{3,2},{4,5},{5,4},{6,7},{7,6},{8,9},{9,8},{10,11... | collective-permute-start | bytes 5505032 | tf_op jit(solution)/shard_map/ppermute | solution.py:16
  63.9 32.9 %all-to-all-start = ((bf16[128,2,3584]{2,1,0:T(2,128)(2,1)}), bf16[128,2,3584]{2,1,0:T(2,128)(2,1)}, u32[]{:S(2)}, u32[]{:S(2)}) async-start(bf16[128,2,3584]{2,1,0:T(2,128)(2,1)} %reshape.78), calls=%async_computation | async-start | bytes 3670016 | tf_op jit(solution)/shard_map/all_to_all | solution.py:140
  96.8 32.8 %all-to-all-start.3 = ((bf16[128,2,3584]{2,1,0:T(2,128)(2,1)}), bf16[128,2,3584]{2,1,0:T(2,128)(2,1)S(1)}, u32[]{:S(2)}, u32[]{:S(2)}) async-start(bf16[128,2,3584]{2,1,0:T(2,128)(2,1)} %reshape.84), calls=%async_computation.3 | async-start | bytes 3670016 | tf_op jit(solution)/shard_map/all_to_all | solution.py:144
  103.4 1.3 copy-start.3
  104.6 1.6 copy-start.6
  104.7 37.4 %collective-permute-start.4 = (f32[2,32,3584]{2,1,0:T(8,128)S(1)}, f32[2,32,3584]{2,1,0:T(8,128)}, u32[]{:S(2)}, u32[]{:S(2)}) collective-permute-start(f32[2,32,3584]{2,1,0:T(8,128)S(1)} %constant_dynamic-slice_fusion.1), channel_id=1, source_target_pairs={{0,2},{2,0},{1,3},{3,1},{4,6},{6,4},{5,7},{7,5},{8,10},{10,8},{9,1... | collective-permute-start | bytes 2752520 | tf_op jit(solution)/shard_map/ppermute | solution.py:16
  129.6 37.5 %all-to-all-start.1 = ((bf16[128,2,3584]{2,1,0:T(2,128)(2,1)}), bf16[128,2,3584]{2,1,0:T(2,128)(2,1)}, u32[]{:S(2)}, u32[]{:S(2)}) async-start(bf16[128,2,3584]{2,1,0:T(2,128)(2,1)} %reshape.80), calls=%async_computation.1 | async-start | bytes 3670016 | tf_op jit(solution)/shard_map/all_to_all | solution.py:144
  143.7 30.6 %collective-permute-start.5 = (f32[2,16,3584]{2,1,0:T(8,128)S(1)}, f32[2,16,3584]{2,1,0:T(8,128)}, u32[]{:S(2)}, u32[]{:S(2)}) collective-permute-start(f32[2,16,3584]{2,1,0:T(8,128)S(1)} %constant_dynamic-slice_fusion), channel_id=1, source_target_pairs={{0,4},{4,0},{1,5},{5,1},{2,6},{6,2},{3,7},{7,3},{8,12},{12,8},{9,1... | collective-permute-start | bytes 1376264 | tf_op jit(solution)/shard_map/ppermute | solution.py:16
  148.3 23.7 %copy-start.1 = (bf16[256,3584]{1,0:T(8,128)(2,1)S(1)}, bf16[256,3584]{1,0:T(8,128)(2,1)}, u32[]{:S(2)}) copy-start(bf16[256,3584]{1,0:T(8,128)(2,1)} %reshape.85) | copy-start | bytes 5505028
  172.0 1.5 copy-start.2

commit v4 on v3

--- a/solution.py
+++ b/solution.py
@@ -23,7 +23,7 @@
     def _():
         total[...] = jnp.zeros_like(total)
 
-    rows = x_ref[...]
+    rows = x_ref[...].reshape(-1, x_ref.shape[-1])
     gate_val = jnp.dot(rows, gate_ref[...], preferred_element_type=jnp.float32)
     up_val = jnp.dot(rows, up_ref[...], preferred_element_type=jnp.float32)
     hidden = (gate_val / (1.0 + jnp.exp(-gate_val)) * up_val).astype(jnp.bfloat16)
@@ -31,26 +31,28 @@
 
     @pl.when(step == pl.num_programs(0) - 1)
     def _():
-        out_ref[...] = total[...].astype(out_ref.dtype)
+        out_ref[...] = total[...].astype(out_ref.dtype).reshape(out_ref.shape)
 
 
-def expert_rows(token_rows, w_gate, w_up, w_down, tile=256):
-    row_count, model_width = token_rows.shape
+def expert_rows(token_block, w_gate, w_up, w_down, tile=256):
+    model_width = token_block.shape[-1]
+    row_count = token_block.size // model_width
     hidden_width = w_gate.shape[2]
     steps = hidden_width // tile
     flops = 6 * row_count * model_width * hidden_width
     weight_bytes = 3 * model_width * hidden_width * 2
+    whole = (0,) * token_block.ndim
     return pl.pallas_call(
         ffn_kernel,
-        out_shape=jax.ShapeDtypeStruct((row_count, model_width), jnp.bfloat16),
+        out_shape=jax.ShapeDtypeStruct(token_block.shape, jnp.bfloat16),
         grid=(steps,),
         in_specs=[
-            pl.BlockSpec((row_count, model_width), lambda f: (0, 0)),
+            pl.BlockSpec(token_block.shape, lambda f: whole),
             pl.BlockSpec((None, model_width, tile), lambda f: (0, 0, f)),
             pl.BlockSpec((None, model_width, tile), lambda f: (0, 0, f)),
             pl.BlockSpec((None, tile, model_width), lambda f: (0, f, 0)),
         ],
-        out_specs=pl.BlockSpec((row_count, model_width), lambda f: (0, 0)),
+        out_specs=pl.BlockSpec(token_block.shape, lambda f: whole),
         scratch_shapes=[pltpu.VMEM((row_count, model_width), jnp.float32)],
         compiler_params=pltpu.CompilerParams(
             dimension_semantics=("arbitrary",), vmem_limit_bytes=60 * 1024 * 1024
@@ -60,7 +62,7 @@
             transcendentals=row_count * hidden_width,
             bytes_accessed=weight_bytes + 4 * row_count * model_width,
         ),
-    )(token_rows, w_gate, w_up, w_down)
+    )(token_block, w_gate, w_up, w_down)
 
 
 def route_tables(step_ids, step_weights, experts, capacity):
@@ -132,20 +134,20 @@
     routed_steps = []
     for s in range(step_count):
         dispatch, combine = route_tables(expert_ids[s], combine_weights[s], experts, capacity)
-        outgoing = (
-            jnp.dot(dispatch, tokens[s], preferred_element_type=jnp.float32)
-            .astype(jnp.bfloat16)
-            .reshape(experts, capacity, model_width)
-        )
+        outgoing = jnp.einsum(
+            "ect,td->ecd",
+            dispatch.reshape(experts, capacity, row_count),
+            tokens[s],
+            preferred_element_type=jnp.float32,
+        ).astype(jnp.bfloat16)
         received = lax.all_to_all(outgoing, "ep", split_axis=0, concat_axis=0, tiled=True)
-        expert_out = expert_rows(
-            received.reshape(-1, model_width), w_gate, w_up, w_down
-        ).reshape(received.shape)
+        expert_out = expert_rows(received, w_gate, w_up, w_down)
         returned = lax.all_to_all(expert_out, "ep", split_axis=0, concat_axis=0, tiled=True)
         routed_steps.append(
-            jnp.dot(
-                combine,
-                returned.reshape(experts * capacity, model_width).astype(jnp.float32),
+            jnp.einsum(
+                "tec,ecd->td",
+                combine.reshape(row_count, experts, capacity),
+                returned.astype(jnp.float32),
                 precision=lax.Precision.HIGHEST,
             )
         )

time: 177 us -> 178 us (level)
  local copies, waits for them, and re-layouts: 35.3 us -> 13.1 us
  waiting for transfers between devices: 55.2 us -> 76.3 us
  matrix products: 7.55 us -> 9.33 us
    reshape x8 -> x0, local copies, waits for them, and re-layouts: 29.3 us -> none  [the longest x2 9.53 us: shards(): expert_out = expert_rows(received.reshape(-1, model_width), w_gate, w_up,...]
    ppermute x6, waiting for transfers between devices: 15.9 us -> 33.6 us  [partner_2(): return lax.ppermute(block, axis, route)]
    all_to_all x2, waiting for transfers between devices: 20.5 us -> 29.3 us  [shards(): lax.all_to_all(outgoing, 'ep', split_axis=0, concat_axis=0, tiled=True)]
    dot_general x0 -> x2, local copies, waits for them, and re-layouts: none -> 6.32 us  [shards(): jnp.einsum('ect,td->ecd', dispatch.reshape(experts, capacity, row_count),...]
    all_to_all x2, waiting for transfers between devices: 18.8 us -> 13.5 us  [shards(): lax.all_to_all(expert_out, 'ep', split_axis=0, concat_axis=0, tiled=True)]
    ppermute x6, starting transfers between devices: 12.6 us -> 17.7 us  [partner_2(): return lax.ppermute(block, axis, route)]
    all_to_all x2, starting transfers between devices: 14.4 us -> 9.69 us  [shards(): lax.all_to_all(expert_out, 'ep', split_axis=0, concat_axis=0, tiled=True)]
  transfers between devices with their start and end apart: 10 -> 10, of which waited for: 6 -> 8; matrix products, arithmetic and copies ran while one was open for 26% -> 14% of each run, Pallas kernels for 15% -> 15%
where the time goes in v4:
time: 178 us
  waiting for transfers between devices  76.3 us (43%)
  starting transfers between devices  42.7 us (24%)
  Pallas kernels  27 us (15%)
  local copies, waits for them, and re-layouts  13.1 us (7%)
  matrix products  9.33 us (5%)
  other arithmetic  8.93 us (5%)
    ppermute x6, waiting for transfers between devices, partner_2(): return lax.ppermute(block, axis, route)  33.6 us
    all_to_all x2, waiting for transfers between devices, shards(): lax.all_to_all(outgoing, 'ep', split_axis=0, concat_axis=0, tiled=True)  29.3 us
    pallas_call x2, Pallas kernels, expert_rows(): pl.pallas_call(ffn_kernel, out_shape=jax.ShapeDtypeStruct(token_block.sha...  27 us
    ppermute x6, starting transfers between devices, partner_2(): return lax.ppermute(block, axis, route)  17.7 us
    all_to_all x2, starting transfers between devices, shards(): lax.all_to_all(outgoing, 'ep', split_axis=0, concat_axis=0, tiled=True)  15.3 us
    all_to_all x2, waiting for transfers between devices, shards(): lax.all_to_all(expert_out, 'ep', split_axis=0, concat_axis=0, tiled=True)  13.5 us
    all_to_all x2, starting transfers between devices, shards(): lax.all_to_all(expert_out, 'ep', split_axis=0, concat_axis=0, tiled=True)  9.69 us
    dot_general x2, local copies, waits for them, and re-layouts, shards(): jnp.einsum('ect,td->ecd', dispatch.reshape(experts, capacity, row_count),...  6.32 us
  transfers between devices with their start and end apart: 10, of which 8 were waited for; matrix products, arithmetic and copies ran while one was open for 14% of the time, Pallas kernels for 15%

profile of v4, /device:TPU:1, one launch (start us, length us, event | category | flops | bytes accessed | tf_op | source)
XLA Modules:
  0.0 177.5 jit_solution(13383208685982015869)
XLA Ops:
  0.0 3.7 %collective-permute-start = (bf16[2,16,3584]{2,1,0:T(8,128)(2,1)}, bf16[2,16,3584]{2,1,0:T(8,128)(2,1)S(1)}, u32[]{:S(2)}, u32[]{:S(2)}) collective-permute-start(bf16[2,16,3584]{2,1,0:T(8,128)(2,1)} %param.7), channel_id=1, source_target_pairs={{0,4},{4,0},{1,5},{5,1},{2,6},{6,2},{3,7},{7,3},{8,12},{12,8},{9,1... | collective-permute-start | bytes 688136 | tf_op jit(solution)/shard_map/ppermute | solution.py:16
  3.7 5.4 %collective-permute-done = bf16[2,16,3584]{2,1,0:T(8,128)(2,1)S(1)} collective-permute-done((bf16[2,16,3584]{2,1,0:T(8,128)(2,1)}, bf16[2,16,3584]{2,1,0:T(8,128)(2,1)S(1)}, u32[]{:S(2)}, u32[]{:S(2)}) %collective-permute-start) | collective-permute-done | bytes 229408 | tf_op jit(solution)/shard_map/ppermute | solution.py:16
  12.6 8.4 %collective-permute-done.1 = bf16[2,32,3584]{2,1,0:T(8,128)(2,1)S(1)} collective-permute-done((bf16[2,32,3584]{2,1,0:T(8,128)(2,1)S(1)}, bf16[2,32,3584]{2,1,0:T(8,128)(2,1)S(1)}, u32[]{:S(2)}, u32[]{:S(2)}) %collective-permute-start.1) | collective-permute-done | bytes 458784 | tf_op jit(solution)/shard_map/ppermute | solution.py:16
  21.1 2.4 %collective-permute-start.2 = (bf16[2,64,3584]{2,1,0:T(8,128)(2,1)S(1)}, bf16[2,64,3584]{2,1,0:T(8,128)(2,1)}, u32[]{:S(2)}, u32[]{:S(2)}) collective-permute-start(bf16[2,64,3584]{2,1,0:T(8,128)(2,1)S(1)} %maximum_select_fusion.1), channel_id=1, source_target_pairs={{0,1},{1,0},{2,3},{3,2},{4,5},{5,4},{6,7},{7,6},{8,9},{9,8},{10,11... | collective-permute-start | bytes 2752520 | tf_op jit(solution)/shard_map/ppermute | solution.py:16
  24.5 3.2 %copy.48 = bf16[128,2,3584]{2,1,0:T(2,128)(2,1)} copy(bf16[128,2,3584]{2,0,1:T(8,128)(2,1)S(1)} %fusion.18) | data formatting | bytes 3670016 | tf_op jit(solution)/shard_map/ect,td->ecd/dot_general | solution.py:137
  27.7 10.0 %all-to-all-start.2 = ((bf16[128,2,3584]{2,1,0:T(2,128)(2,1)}), bf16[128,2,3584]{2,1,0:T(2,128)(2,1)S(1)}, u32[]{:S(2)}, u32[]{:S(2)}) async-start(bf16[128,2,3584]{2,1,0:T(2,128)(2,1)} %copy.48), calls=%async_computation.2 | async-start | bytes 3670016 | tf_op jit(solution)/shard_map/all_to_all | solution.py:143
  38.5 2.0 %maximum_select_fusion = bf16[2,128,3584]{2,1,0:T(8,128)(2,1)S(1)} fusion(bf16[2,64,3584]{2,1,0:T(8,128)(2,1)S(1)} %maximum_select_fusion.1, bf16[2,64,3584]{2,1,0:T(8,128)(2,1)} %collective-permute-done.2, pred[]{:T(512)S(6)} %eq.95), kind=kLoop, calls=%fused_computation.4 | loop fusion | flops 8257536 | bytes 3670017 | tf_op jit(solution)/shard_map/jit(_where)/select_n | solution.py:97
  46.7 3.2 %copy.49 = bf16[128,2,3584]{2,1,0:T(2,128)(2,1)} copy(bf16[128,2,3584]{2,0,1:T(8,128)(2,1)S(1)} %fusion.20) | data formatting | bytes 3670016 | tf_op jit(solution)/shard_map/ect,td->ecd/dot_general | solution.py:137
  49.9 15.6 %all-to-all-done.2.x_ref = bf16[128,2,3584]{2,1,0:T(2,128)(2,1)S(1)} async-done(((bf16[128,2,3584]{2,1,0:T(2,128)(2,1)}), bf16[128,2,3584]{2,1,0:T(2,128)(2,1)S(1)}, u32[]{:S(2)}, u32[]{:S(2)}) %all-to-all-start.2) | async-done | bytes 1835040 | tf_op jit(solution)/shard_map/all_to_all | solution.py:143
  66.6 5.3 %all-to-all-start = ((bf16[128,2,3584]{2,1,0:T(2,128)(2,1)}), bf16[128,2,3584]{2,1,0:T(2,128)(2,1)}, u32[]{:S(2)}, u32[]{:S(2)}) async-start(bf16[128,2,3584]{2,1,0:T(2,128)(2,1)} %copy.49), calls=%async_computation | async-start | bytes 3670016 | tf_op jit(solution)/shard_map/all_to_all | solution.py:143
  72.3 13.5 %shard_map.74 = bf16[128,2,3584]{2,1,0:T(2,128)(2,1)} custom-call(bf16[128,2,3584]{2,1,0:T(2,128)(2,1)} %copy-done.1, bf16[1,3584,1024]{2,1,0:T(8,128)(2,1)} %gate_ref.3, bf16[1,3584,1024]{2,1,0:T(8,128)(2,1)} %up_ref.3, bf16[1,1024,3584]{2,1,0:T(8,128)(2,1)} %down_ref.3), custom_call_target="tpu_custom_call" | custom-call | flops 5637144576 | bytes 25690112 | tf_op jit(solution)/shard_map/pallas_call | solution.py:45
  85.8 13.7 %all-to-all-done.x_ref = bf16[128,2,3584]{2,1,0:T(2,128)(2,1)} async-done(((bf16[128,2,3584]{2,1,0:T(2,128)(2,1)}), bf16[128,2,3584]{2,1,0:T(2,128)(2,1)}, u32[]{:S(2)}, u32[]{:S(2)}) %all-to-all-start) | async-done | bytes 1835040 | tf_op jit(solution)/shard_map/all_to_all | solution.py:143
  99.5 4.3 %all-to-all-start.3 = ((bf16[128,2,3584]{2,1,0:T(2,128)(2,1)}), bf16[128,2,3584]{2,1,0:T(2,128)(2,1)S(1)}, u32[]{:S(2)}, u32[]{:S(2)}) async-start(bf16[128,2,3584]{2,1,0:T(2,128)(2,1)} %shard_map.74), calls=%async_computation.3 | async-start | bytes 3670016 | tf_op jit(solution)/shard_map/all_to_all | solution.py:145
  103.9 2.3 %dynamic-slice_add_fusion = f32[2,64,3584]{2,1,0:T(8,128)S(1)} fusion(f32[2,64,3584]{2,1,0:T(8,128)} %collective-permute-done.3, f32[2,128,3584]{2,1,0:T(8,128)} %copy-done, s32[]{:T(128)S(6)} %select_n.79), kind=kLoop, calls=%fused_computation.7 | loop fusion | flops 458752 | bytes 5505028 | tf_op jit(solution)/shard_map/add | solution.py:124
  110.0 13.5 %shard_map.73 = bf16[128,2,3584]{2,1,0:T(2,128)(2,1)} custom-call(bf16[128,2,3584]{2,1,0:T(2,128)(2,1)} %all-to-all-done.x_ref, bf16[1,3584,1024]{2,1,0:T(8,128)(2,1)} %gate_ref.3, bf16[1,3584,1024]{2,1,0:T(8,128)(2,1)} %up_ref.3, bf16[1,1024,3584]{2,1,0:T(8,128)(2,1)} %down_ref.3), custom_call_target="tpu_custom_call" | custom-call | flops 5637144576 | bytes 25690112 | tf_op jit(solution)/shard_map/pallas_call | solution.py:45
  123.4 8.3 %all-to-all-done.3 = bf16[128,2,3584]{2,1,0:T(2,128)(2,1)S(1)} async-done(((bf16[128,2,3584]{2,1,0:T(2,128)(2,1)}), bf16[128,2,3584]{2,1,0:T(2,128)(2,1)S(1)}, u32[]{:S(2)}, u32[]{:S(2)}) %all-to-all-start.3) | async-done | bytes 1835040 | tf_op jit(solution)/shard_map/all_to_all | solution.py:145
  131.7 5.4 %all-to-all-start.1 = ((bf16[128,2,3584]{2,1,0:T(2,128)(2,1)}), bf16[128,2,3584]{2,1,0:T(2,128)(2,1)}, u32[]{:S(2)}, u32[]{:S(2)}) async-start(bf16[128,2,3584]{2,1,0:T(2,128)(2,1)} %shard_map.73), calls=%async_computation.1 | async-start | bytes 3670016 | tf_op jit(solution)/shard_map/all_to_all | solution.py:145
  138.1 16.1 %collective-permute-done.4 = f32[2,32,3584]{2,1,0:T(8,128)} collective-permute-done((f32[2,32,3584]{2,1,0:T(8,128)S(1)}, f32[2,32,3584]{2,1,0:T(8,128)}, u32[]{:S(2)}, u32[]{:S(2)}) %collective-permute-start.4) | collective-permute-done | bytes 917536 | tf_op jit(solution)/shard_map/ppermute | solution.py:16
  154.2 1.6 dynamic-slice_add_fusion.1
  155.8 7.7 %collective-permute-start.5 = (f32[2,16,3584]{2,1,0:T(8,128)S(1)}, f32[2,16,3584]{2,1,0:T(8,128)}, u32[]{:S(2)}, u32[]{:S(2)}) collective-permute-start(f32[2,16,3584]{2,1,0:T(8,128)S(1)} %constant_dynamic-slice_fusion), channel_id=1, source_target_pairs={{0,4},{4,0},{1,5},{5,1},{2,6},{6,2},{3,7},{7,3},{8,12},{12,8},{9,1... | collective-permute-start | bytes 1376264 | tf_op jit(solution)/shard_map/ppermute | solution.py:16
  164.4 5.2 %all-to-all-done.1 = bf16[128,2,3584]{2,1,0:T(2,128)(2,1)} async-done(((bf16[128,2,3584]{2,1,0:T(2,128)(2,1)}), bf16[128,2,3584]{2,1,0:T(2,128)(2,1)}, u32[]{:S(2)}, u32[]{:S(2)}) %all-to-all-start.1) | async-done | bytes 1835040 | tf_op jit(solution)/shard_map/all_to_all | solution.py:145
  169.6 2.5 %convolution_bitcast_fusion.1 = f32[1,16,3584]{2,1,0:T(8,128)S(1)} fusion(bf16[128,2,3584]{2,1,0:T(2,128)(2,1)} %all-to-all-done.1, f32[16,128,2]{0,2,1:T(2,128)} %bitcast.40), kind=kOutput, calls=%fused_computation.1 | convolution fusion | flops 176160768 | bytes 2080768 | tf_op jit(solution)/shard_map/tec,ecd->td/dot_general | solution.py:147
  172.0 3.7 %collective-permute-done.5 = f32[2,16,3584]{2,1,0:T(8,128)} collective-permute-done((f32[2,16,3584]{2,1,0:T(8,128)S(1)}, f32[2,16,3584]{2,1,0:T(8,128)}, u32[]{:S(2)}, u32[]{:S(2)}) %collective-permute-start.5) | collective-permute-done | bytes 458784 | tf_op jit(solution)/shard_map/ppermute | solution.py:16
  175.8 1.8 fusion.13
  (50 shorter events, 18.8 us)
Async XLA Ops:
  0.0 23.9 %copy-start.3 = (bf16[2,16,3584]{2,1,0:T(8,128)(2,1)S(1)}, bf16[2,16,3584]{2,1,0:T(8,128)(2,1)}, u32[]{:S(2)}) copy-start(bf16[2,16,3584]{2,1,0:T(8,128)(2,1)} %param.7) | copy-start | bytes 688132
  0.0 9.1 %collective-permute-start = (bf16[2,16,3584]{2,1,0:T(8,128)(2,1)}, bf16[2,16,3584]{2,1,0:T(8,128)(2,1)S(1)}, u32[]{:S(2)}, u32[]{:S(2)}) collective-permute-start(bf16[2,16,3584]{2,1,0:T(8,128)(2,1)} %param.7), channel_id=1, source_target_pairs={{0,4},{4,0},{1,5},{5,1},{2,6},{6,2},{3,7},{7,3},{8,12},{12,8},{9,1... | collective-permute-start | bytes 688136 | tf_op jit(solution)/shard_map/ppermute | solution.py:16
  10.3 10.7 %collective-permute-start.1 = (bf16[2,32,3584]{2,1,0:T(8,128)(2,1)S(1)}, bf16[2,32,3584]{2,1,0:T(8,128)(2,1)S(1)}, u32[]{:S(2)}, u32[]{:S(2)}) collective-permute-start(bf16[2,32,3584]{2,1,0:T(8,128)(2,1)S(1)} %maximum_select_fusion.2), channel_id=1, source_target_pairs={{0,2},{2,0},{1,3},{3,1},{4,6},{6,4},{5,7},{7,5},{8,10},{10,8},{9,1... | collective-permute-start | bytes 1376264 | tf_op jit(solution)/shard_map/ppermute | solution.py:16
  21.1 17.3 %collective-permute-start.2 = (bf16[2,64,3584]{2,1,0:T(8,128)(2,1)S(1)}, bf16[2,64,3584]{2,1,0:T(8,128)(2,1)}, u32[]{:S(2)}, u32[]{:S(2)}) collective-permute-start(bf16[2,64,3584]{2,1,0:T(8,128)(2,1)S(1)} %maximum_select_fusion.1), channel_id=1, source_target_pairs={{0,1},{1,0},{2,3},{3,2},{4,5},{5,4},{6,7},{7,6},{8,9},{9,8},{10,11... | collective-permute-start | bytes 2752520 | tf_op jit(solution)/shard_map/ppermute | solution.py:16
  27.7 37.7 %all-to-all-start.2 = ((bf16[128,2,3584]{2,1,0:T(2,128)(2,1)}), bf16[128,2,3584]{2,1,0:T(2,128)(2,1)S(1)}, u32[]{:S(2)}, u32[]{:S(2)}) async-start(bf16[128,2,3584]{2,1,0:T(2,128)(2,1)} %copy.48), calls=%async_computation.2 | async-start | bytes 3670016 | tf_op jit(solution)/shard_map/all_to_all | solution.py:143
  38.4 2.3 %copy-start.4 = (bf16[3,3584,128]{2,1,0:T(8,128)(2,1)S(1)}, bf16[3,3584,128]{2,1,0:T(8,128)(2,1)}, u32[]{:S(2)}) copy-start(bf16[3,3584,128]{2,1,0:T(8,128)(2,1)} %param.13) | copy-start | bytes 8257540
  42.7 2.3 %copy-start = (f32[2,128,3584]{2,1,0:T(8,128)}, f32[2,128,3584]{2,1,0:T(8,128)S(1)}, u32[]{:S(2)}) copy-start(f32[2,128,3584]{2,1,0:T(8,128)S(1)} %fusion.4) | copy-start | bytes 11010052
  45.0 58.9 %collective-permute-start.3 = (f32[2,64,3584]{2,1,0:T(8,128)}, f32[2,64,3584]{2,1,0:T(8,128)}, u32[]{:S(2)}, u32[]{:S(2)}) collective-permute-start(f32[2,64,3584]{2,1,0:T(8,128)} %constant_dynamic-slice_fusion.2), channel_id=1, source_target_pairs={{0,1},{1,0},{2,3},{3,2},{4,5},{5,4},{6,7},{7,6},{8,9},{9,8},{10,11... | collective-permute-start | bytes 5505032 | tf_op jit(solution)/shard_map/ppermute | solution.py:16
  49.8 22.1 %copy-start.6 = (f32[2,16,8]{1,2,0:T(8,128)S(1)}, f32[2,16,8]{1,2,0:T(8,128)}, u32[]{:S(2)}) copy-start(f32[2,16,8]{1,2,0:T(8,128)} %param.9) | copy-start | bytes 3076
  65.4 1.2 copy-start.1
  66.6 32.9 %all-to-all-start = ((bf16[128,2,3584]{2,1,0:T(2,128)(2,1)}), bf16[128,2,3584]{2,1,0:T(2,128)(2,1)}, u32[]{:S(2)}, u32[]{:S(2)}) async-start(bf16[128,2,3584]{2,1,0:T(2,128)(2,1)} %copy.49), calls=%async_computation | async-start | bytes 3670016 | tf_op jit(solution)/shard_map/all_to_all | solution.py:143
  99.5 32.2 %all-to-all-start.3 = ((bf16[128,2,3584]{2,1,0:T(2,128)(2,1)}), bf16[128,2,3584]{2,1,0:T(2,128)(2,1)S(1)}, u32[]{:S(2)}, u32[]{:S(2)}) async-start(bf16[128,2,3584]{2,1,0:T(2,128)(2,1)} %shard_map.74), calls=%async_computation.3 | async-start | bytes 3670016 | tf_op jit(solution)/shard_map/all_to_all | solution.py:145
  106.1 1.2 copy-start.2
  107.4 46.8 %collective-permute-start.4 = (f32[2,32,3584]{2,1,0:T(8,128)S(1)}, f32[2,32,3584]{2,1,0:T(8,128)}, u32[]{:S(2)}, u32[]{:S(2)}) collective-permute-start(f32[2,32,3584]{2,1,0:T(8,128)S(1)} %constant_dynamic-slice_fusion.1), channel_id=1, source_target_pairs={{0,2},{2,0},{1,3},{3,1},{4,6},{6,4},{5,7},{7,5},{8,10},{10,8},{9,1... | collective-permute-start | bytes 2752520 | tf_op jit(solution)/shard_map/ppermute | solution.py:16
  131.7 37.9 %all-to-all-start.1 = ((bf16[128,2,3584]{2,1,0:T(2,128)(2,1)}), bf16[128,2,3584]{2,1,0:T(2,128)(2,1)}, u32[]{:S(2)}, u32[]{:S(2)}) async-start(bf16[128,2,3584]{2,1,0:T(2,128)(2,1)} %shard_map.73), calls=%async_computation.1 | async-start | bytes 3670016 | tf_op jit(solution)/shard_map/all_to_all | solution.py:145
  138.1 25.4 %copy-start.5 = (f32[16,256]{0,1:T(8,128)S(1)}, f32[16,256]{0,1:T(8,128)}, u32[]{:S(2)}) copy-start(f32[16,256]{0,1:T(8,128)} %fusion.16) | copy-start | bytes 49156
  155.8 19.9 %collective-permute-start.5 = (f32[2,16,3584]{2,1,0:T(8,128)S(1)}, f32[2,16,3584]{2,1,0:T(8,128)}, u32[]{:S(2)}, u32[]{:S(2)}) collective-permute-start(f32[2,16,3584]{2,1,0:T(8,128)S(1)} %constant_dynamic-slice_fusion), channel_id=1, source_target_pairs={{0,4},{4,0},{1,5},{5,1},{2,6},{6,2},{3,7},{7,3},{8,12},{12,8},{9,1... | collective-permute-start | bytes 1376264 | tf_op jit(solution)/shard_map/ppermute | solution.py:16

commit v5 on v4

--- a/solution.py
+++ b/solution.py
@@ -121,7 +121,9 @@
         bit = my_index >> level & 1
         keep = lax.dynamic_slice_in_dim(partial_value, bit * half, half, 1)
         send = lax.dynamic_slice_in_dim(partial_value, (1 - bit) * half, half, 1)
-        partial_value = keep + partner_2(send, "ep", level)
+        partial_value = keep + partner_2(send.astype(jnp.bfloat16), "ep", level).astype(
+            jnp.float32
+        )
     return partial_value
 
 
@@ -131,27 +133,34 @@
     device_count = lax.axis_size("ep")
     experts = w_gate.shape[0] * device_count
     capacity = max(2, row_count * top_count * 2 // experts)
+    payloads = []
+    combines = []
+    for s in range(step_count):
+        dispatch, combine = route_tables(expert_ids[s], combine_weights[s], experts, capacity)
+        payloads.append(
+            jnp.einsum(
+                "ect,td->ecd",
+                dispatch.reshape(experts, capacity, row_count),
+                tokens[s],
+                preferred_element_type=jnp.float32,
+            ).astype(jnp.bfloat16)
+        )
+        combines.append(combine)
     routed_steps = []
     for s in range(step_count):
-        dispatch, combine = route_tables(expert_ids[s], combine_weights[s], experts, capacity)
-        outgoing = jnp.einsum(
-            "ect,td->ecd",
-            dispatch.reshape(experts, capacity, row_count),
-            tokens[s],
-            preferred_element_type=jnp.float32,
-        ).astype(jnp.bfloat16)
-        received = lax.all_to_all(outgoing, "ep", split_axis=0, concat_axis=0, tiled=True)
+        received = lax.all_to_all(payloads[s], "ep", split_axis=0, concat_axis=0, tiled=True)
         expert_out = expert_rows(received, w_gate, w_up, w_down)
         returned = lax.all_to_all(expert_out, "ep", split_axis=0, concat_axis=0, tiled=True)
         routed_steps.append(
             jnp.einsum(
                 "tec,ecd->td",
-                combine.reshape(row_count, experts, capacity),
+                combines[s].reshape(row_count, experts, capacity),
                 returned.astype(jnp.float32),
                 precision=lax.Precision.HIGHEST,
             )
         )
-    shared = shared_expert(tokens, shared_weights)
+    later_tokens = lax.optimization_barrier((tokens, *payloads))[0]
+    shared = shared_expert(later_tokens, shared_weights)
     routed = jnp.stack(routed_steps)
     return (shared + routed).astype(jnp.bfloat16)
 

time: 178 us -> 162 us (0.910)
  waiting for transfers between devices: 76.3 us -> 61 us
  matrix products: 9.33 us -> 14.3 us
  starting transfers between devices: 42.7 us -> 38.7 us
  other arithmetic: 8.93 us -> 7.01 us
    ppermute x6, waiting for transfers between devices: 33.6 us -> 7.29 us  [partner_2(): return lax.ppermute(block, axis, route)]
    all_to_all x2, waiting for transfers between devices: 13.5 us -> 31.2 us  [shards(): lax.all_to_all(expert_out, 'ep', split_axis=0, concat_axis=0, tiled=True)]
    all_to_all x2, waiting for transfers between devices: 29.3 us -> 22.4 us  [shards(): lax.all_to_all(payloads[s], 'ep', split_axis=0, concat_axis=0, tiled=True)]
    ppermute x6, starting transfers between devices: 17.7 us -> 12.1 us  [partner_2(): return lax.ppermute(block, axis, route)]
  transfers between devices with their start and end apart: 10 -> 10, of which waited for: 8 -> 6; matrix products, arithmetic and copies ran while one was open for 14% -> 12% of each run, Pallas kernels for 15% -> 17%
where the time goes in v5:
time: 162 us
  waiting for transfers between devices  61 us (38%)
  starting transfers between devices  38.7 us (24%)
  Pallas kernels  27 us (17%)
  matrix products  14.3 us (9%)
  local copies, waits for them, and re-layouts  13.2 us (8%)
  other arithmetic  7.01 us (4%)
    all_to_all x2, waiting for transfers between devices, shards(): lax.all_to_all(expert_out, 'ep', split_axis=0, concat_axis=0, tiled=True)  31.2 us
    pallas_call x2, Pallas kernels, expert_rows(): pl.pallas_call(ffn_kernel, out_shape=jax.ShapeDtypeStruct(token_block.sha...  27 us
    all_to_all x2, waiting for transfers between devices, shards(): lax.all_to_all(payloads[s], 'ep', split_axis=0, concat_axis=0, tiled=True)  22.4 us
    all_to_all x2, starting transfers between devices, shards(): lax.all_to_all(payloads[s], 'ep', split_axis=0, concat_axis=0, tiled=True)  16.9 us
    ppermute x6, starting transfers between devices, partner_2(): return lax.ppermute(block, axis, route)  12.1 us
    all_to_all x2, starting transfers between devices, shards(): lax.all_to_all(expert_out, 'ep', split_axis=0, concat_axis=0, tiled=True)  9.75 us
    ppermute x6, waiting for transfers between devices, partner_2(): return lax.ppermute(block, axis, route)  7.29 us
    dot_general x2, local copies, waits for them, and re-layouts, shards(): jnp.einsum('ect,td->ecd', dispatch.reshape(experts, capacity, row_count),...  6.31 us
  transfers between devices with their start and end apart: 10, of which 6 were waited for; matrix products, arithmetic and copies ran while one was open for 12% of the time, Pallas kernels for 17%

profile of v5, /device:TPU:1, one launch (start us, length us, event | category | flops | bytes accessed | tf_op | source)
XLA Modules:
  0.0 161.5 jit_solution(17027504434190951301)
XLA Ops:
  2.2 1.5 fusion.18
  3.7 3.1 %copy.52 = bf16[128,2,3584]{2,1,0:T(2,128)(2,1)} copy(bf16[128,2,3584]{2,0,1:T(8,128)(2,1)S(1)} %fusion.18) | data formatting | bytes 3670016 | tf_op jit(solution)/shard_map/ect,td->ecd/dot_general | solution.py:141
  7.5 3.2 %copy.53 = bf16[128,2,3584]{2,1,0:T(2,128)(2,1)} copy(bf16[128,2,3584]{2,0,1:T(8,128)(2,1)S(1)} %fusion.20) | data formatting | bytes 3670016 | tf_op jit(solution)/shard_map/ect,td->ecd/dot_general | solution.py:141
  10.6 3.8 %collective-permute-start = (bf16[2,16,3584]{2,1,0:T(8,128)(2,1)S(1)}, bf16[2,16,3584]{2,1,0:T(8,128)(2,1)S(1)}, u32[]{:S(2)}, u32[]{:S(2)}) collective-permute-start(bf16[2,16,3584]{2,1,0:T(8,128)(2,1)S(1)} %copy-done.4), channel_id=1, source_target_pairs={{0,4},{4,0},{1,5},{5,1},{2,6},{6,2},{3,7},{7,3},{8,12},{12,8},{9,1... | collective-permute-start | bytes 688136 | tf_op jit(solution)/shard_map/ppermute | solution.py:16
  14.4 5.0 %collective-permute-done = bf16[2,16,3584]{2,1,0:T(8,128)(2,1)S(1)} collective-permute-done((bf16[2,16,3584]{2,1,0:T(8,128)(2,1)S(1)}, bf16[2,16,3584]{2,1,0:T(8,128)(2,1)S(1)}, u32[]{:S(2)}, u32[]{:S(2)}) %collective-permute-start) | collective-permute-done | bytes 229408 | tf_op jit(solution)/shard_map/ppermute | solution.py:16
  20.9 11.5 %all-to-all-start.2 = ((bf16[128,2,3584]{2,1,0:T(2,128)(2,1)}), bf16[128,2,3584]{2,1,0:T(2,128)(2,1)S(1)}, u32[]{:S(2)}, u32[]{:S(2)}) async-start(bf16[128,2,3584]{2,1,0:T(2,128)(2,1)} %copy.52), calls=%async_computation.2 | async-start | bytes 3670016 | tf_op jit(solution)/shard_map/all_to_all | solution.py:151
  34.9 2.2 %collective-permute-done.2 = bf16[2,64,3584]{2,1,0:T(8,128)(2,1)} collective-permute-done((bf16[2,64,3584]{2,1,0:T(8,128)(2,1)S(1)}, bf16[2,64,3584]{2,1,0:T(8,128)(2,1)}, u32[]{:S(2)}, u32[]{:S(2)}) %collective-permute-start.2) | collective-permute-done | bytes 917536 | tf_op jit(solution)/shard_map/ppermute | solution.py:16
  37.2 1.9 %maximum_select_fusion = bf16[2,128,3584]{2,1,0:T(8,128)(2,1)S(1)} fusion(bf16[2,64,3584]{2,1,0:T(8,128)(2,1)S(1)} %maximum_select_fusion.1, bf16[2,64,3584]{2,1,0:T(8,128)(2,1)} %collective-permute-done.2, pred[]{:T(512)S(6)} %eq.95), kind=kLoop, calls=%fused_computation.4 | loop fusion | flops 8257536 | bytes 3670017 | tf_op jit(solution)/shard_map/jit(_where)/select_n | solution.py:97
  40.3 1.8 %fusion.8 = f32[256,128]{1,0:T(8,128)S(1)} fusion(bf16[256,3584]{1,0:T(8,128)(2,1)S(1)} %bitcast.35, bf16[3,3584,128]{2,1,0:T(8,128)(2,1)} %param.13), kind=kOutput, calls=%fused_computation.20 | convolution fusion | flops 234881024 | bytes 2883584 | tf_op jit(solution)/shard_map/dot_general | solution.py:112
  42.1 18.1 %all-to-all-done.2.x_ref = bf16[128,2,3584]{2,1,0:T(2,128)(2,1)S(1)} async-done(((bf16[128,2,3584]{2,1,0:T(2,128)(2,1)}), bf16[128,2,3584]{2,1,0:T(2,128)(2,1)S(1)}, u32[]{:S(2)}, u32[]{:S(2)}) %all-to-all-start.2) | async-done | bytes 1835040 | tf_op jit(solution)/shard_map/all_to_all | solution.py:151
  60.1 5.3 %all-to-all-start = ((bf16[128,2,3584]{2,1,0:T(2,128)(2,1)}), bf16[128,2,3584]{2,1,0:T(2,128)(2,1)}, u32[]{:S(2)}, u32[]{:S(2)}) async-start(bf16[128,2,3584]{2,1,0:T(2,128)(2,1)} %copy.53), calls=%async_computation | async-start | bytes 3670016 | tf_op jit(solution)/shard_map/all_to_all | solution.py:151
  65.5 2.4 %multiply_convert_fusion = bf16[256,128]{1,0:T(8,128)(2,1)S(1)} fusion(f32[256,128]{1,0:T(8,128)S(1)} %fusion.8, bf16[256,3584]{1,0:T(8,128)(2,1)} %bitcast.36, bf16[3,3584,128]{2,1,0:T(8,128)(2,1)} %param.13), kind=kOutput, calls=%fused_computation.33 | convolution fusion | flops 235077632 | bytes 2949120 | tf_op jit(solution)/shard_map/dot_general | solution.py:113
  67.9 1.8 %fusion.4 = f32[2,128,3584]{2,1,0:T(8,128)S(1)} fusion(bf16[2,128,128]{2,1,0:T(8,128)(2,1)S(1)} %bitcast.41, bf16[3,3584,128]{2,1,0:T(8,128)(2,1)} %param.13), kind=kOutput, calls=%fused_computation.16 | convolution fusion | flops 234881024 | bytes 4653056 | tf_op jit(solution)/shard_map/dot_general | solution.py:115
  69.7 1.8 %copy-done = f32[2,128,3584]{2,1,0:T(8,128)} copy-done((f32[2,128,3584]{2,1,0:T(8,128)}, f32[2,128,3584]{2,1,0:T(8,128)S(1)}, u32[]{:S(2)}) %copy-start) | copy-done | bytes 3670040
  75.1 13.5 %shard_map.74 = bf16[128,2,3584]{2,1,0:T(2,128)(2,1)} custom-call(bf16[128,2,3584]{2,1,0:T(2,128)(2,1)} %copy-done.1, bf16[1,3584,1024]{2,1,0:T(8,128)(2,1)} %gate_ref.3, bf16[1,3584,1024]{2,1,0:T(8,128)(2,1)} %up_ref.3, bf16[1,1024,3584]{2,1,0:T(8,128)(2,1)} %down_ref.3), custom_call_target="tpu_custom_call" | custom-call | flops 5637144576 | bytes 25690112 | tf_op jit(solution)/shard_map/pallas_call | solution.py:45
  88.7 4.4 %all-to-all-done.x_ref = bf16[128,2,3584]{2,1,0:T(2,128)(2,1)} async-done(((bf16[128,2,3584]{2,1,0:T(2,128)(2,1)}), bf16[128,2,3584]{2,1,0:T(2,128)(2,1)}, u32[]{:S(2)}, u32[]{:S(2)}) %all-to-all-start) | async-done | bytes 1835040 | tf_op jit(solution)/shard_map/all_to_all | solution.py:151
  93.1 4.4 %all-to-all-start.3 = ((bf16[128,2,3584]{2,1,0:T(2,128)(2,1)}), bf16[128,2,3584]{2,1,0:T(2,128)(2,1)S(1)}, u32[]{:S(2)}, u32[]{:S(2)}) async-start(bf16[128,2,3584]{2,1,0:T(2,128)(2,1)} %shard_map.74), calls=%async_computation.3 | async-start | bytes 3670016 | tf_op jit(solution)/shard_map/all_to_all | solution.py:153
  97.5 1.7 %convert_add_fusion = f32[2,64,3584]{2,1,0:T(8,128)S(1)} fusion(bf16[2,64,3584]{2,1,0:T(8,128)(2,1)S(1)} %collective-permute-done.3, f32[2,128,3584]{2,1,0:T(8,128)} %copy-done, s32[]{:T(128)S(6)} %select_n.80), kind=kLoop, calls=%fused_computation.7 | loop fusion | flops 917504 | bytes 4587524 | tf_op jit(solution)/shard_map/add | solution.py:124
  101.9 13.5 %shard_map.73 = bf16[128,2,3584]{2,1,0:T(2,128)(2,1)} custom-call(bf16[128,2,3584]{2,1,0:T(2,128)(2,1)} %all-to-all-done.x_ref, bf16[1,3584,1024]{2,1,0:T(8,128)(2,1)} %gate_ref.3, bf16[1,3584,1024]{2,1,0:T(8,128)(2,1)} %up_ref.3, bf16[1,1024,3584]{2,1,0:T(8,128)(2,1)} %down_ref.3), custom_call_target="tpu_custom_call" | custom-call | flops 5637144576 | bytes 25690112 | tf_op jit(solution)/shard_map/pallas_call | solution.py:45
  115.4 9.9 %all-to-all-done.3 = bf16[128,2,3584]{2,1,0:T(2,128)(2,1)S(1)} async-done(((bf16[128,2,3584]{2,1,0:T(2,128)(2,1)}), bf16[128,2,3584]{2,1,0:T(2,128)(2,1)S(1)}, u32[]{:S(2)}, u32[]{:S(2)}) %all-to-all-start.3) | async-done | bytes 1835040 | tf_op jit(solution)/shard_map/all_to_all | solution.py:153
  125.3 5.4 %all-to-all-start.1 = ((bf16[128,2,3584]{2,1,0:T(2,128)(2,1)}), bf16[128,2,3584]{2,1,0:T(2,128)(2,1)}, u32[]{:S(2)}, u32[]{:S(2)}) async-start(bf16[128,2,3584]{2,1,0:T(2,128)(2,1)} %shard_map.73), calls=%async_computation.1 | async-start | bytes 3670016 | tf_op jit(solution)/shard_map/all_to_all | solution.py:153
  133.0 3.1 %collective-permute-start.5 = (bf16[2,16,3584]{2,1,0:T(8,128)(2,1)S(1)}, bf16[2,16,3584]{2,1,0:T(8,128)(2,1)S(1)}, u32[]{:S(2)}, u32[]{:S(2)}) collective-permute-start(bf16[2,16,3584]{2,1,0:T(8,128)(2,1)S(1)} %dynamic-slice_convert_fusion.2), channel_id=1, source_target_pairs={{0,4},{4,0},{1,5},{5,1},{2,6},{6,2},{3,7},{7,3},{8,12},{12,8},{9,1... | collective-permute-start | bytes 688136 | tf_op jit(solution)/shard_map/ppermute | solution.py:16
  136.9 21.4 %all-to-all-done.1 = bf16[128,2,3584]{2,1,0:T(2,128)(2,1)} async-done(((bf16[128,2,3584]{2,1,0:T(2,128)(2,1)}), bf16[128,2,3584]{2,1,0:T(2,128)(2,1)}, u32[]{:S(2)}, u32[]{:S(2)}) %all-to-all-start.1) | async-done | bytes 1835040 | tf_op jit(solution)/shard_map/all_to_all | solution.py:153
  158.3 2.5 %convolution_bitcast_fusion.1 = f32[1,16,3584]{2,1,0:T(8,128)S(1)} fusion(bf16[128,2,3584]{2,1,0:T(2,128)(2,1)} %all-to-all-done.1, f32[16,128,2]{0,2,1:T(2,128)} %bitcast.40), kind=kOutput, calls=%fused_computation.1 | convolution fusion | flops 176160768 | bytes 2080768 | tf_op jit(solution)/shard_map/tec,ecd->td/dot_general | solution.py:155
  (50 shorter events, 18.3 us)
Async XLA Ops:
  3.7 3.2 %copy-start.4 = (bf16[2,16,3584]{2,1,0:T(8,128)(2,1)S(1)}, bf16[2,16,3584]{2,1,0:T(8,128)(2,1)}, u32[]{:S(2)}) copy-start(bf16[2,16,3584]{2,1,0:T(8,128)(2,1)} %param.7) | copy-start | bytes 688132
  10.6 8.8 %collective-permute-start = (bf16[2,16,3584]{2,1,0:T(8,128)(2,1)S(1)}, bf16[2,16,3584]{2,1,0:T(8,128)(2,1)S(1)}, u32[]{:S(2)}, u32[]{:S(2)}) collective-permute-start(bf16[2,16,3584]{2,1,0:T(8,128)(2,1)S(1)} %copy-done.4), channel_id=1, source_target_pairs={{0,4},{4,0},{1,5},{5,1},{2,6},{6,2},{3,7},{7,3},{8,12},{12,8},{9,1... | collective-permute-start | bytes 688136 | tf_op jit(solution)/shard_map/ppermute | solution.py:16
  19.5 12.9 %collective-permute-start.1 = (bf16[2,32,3584]{2,1,0:T(8,128)(2,1)S(1)}, bf16[2,32,3584]{2,1,0:T(8,128)(2,1)}, u32[]{:S(2)}, u32[]{:S(2)}) collective-permute-start(bf16[2,32,3584]{2,1,0:T(8,128)(2,1)S(1)} %maximum_select_fusion.2), channel_id=1, source_target_pairs={{0,2},{2,0},{1,3},{3,1},{4,6},{6,4},{5,7},{7,5},{8,10},{10,8},{9,1... | collective-permute-start | bytes 1376264 | tf_op jit(solution)/shard_map/ppermute | solution.py:16
  20.9 39.2 %all-to-all-start.2 = ((bf16[128,2,3584]{2,1,0:T(2,128)(2,1)}), bf16[128,2,3584]{2,1,0:T(2,128)(2,1)S(1)}, u32[]{:S(2)}, u32[]{:S(2)}) async-start(bf16[128,2,3584]{2,1,0:T(2,128)(2,1)} %copy.52), calls=%async_computation.2 | async-start | bytes 3670016 | tf_op jit(solution)/shard_map/all_to_all | solution.py:151
  33.8 3.4 %collective-permute-start.2 = (bf16[2,64,3584]{2,1,0:T(8,128)(2,1)S(1)}, bf16[2,64,3584]{2,1,0:T(8,128)(2,1)}, u32[]{:S(2)}, u32[]{:S(2)}) collective-permute-start(bf16[2,64,3584]{2,1,0:T(8,128)(2,1)S(1)} %maximum_select_fusion.1), channel_id=1, source_target_pairs={{0,1},{1,0},{2,3},{3,2},{4,5},{5,4},{6,7},{7,6},{8,9},{9,8},{10,11... | collective-permute-start | bytes 2752520 | tf_op jit(solution)/shard_map/ppermute | solution.py:16
  39.1 1.2 copy-start.3
  60.1 7.7 %copy-start.1 = (bf16[128,2,3584]{2,1,0:T(2,128)(2,1)}, bf16[128,2,3584]{2,1,0:T(2,128)(2,1)S(1)}, u32[]{:S(2)}) copy-start(bf16[128,2,3584]{2,1,0:T(2,128)(2,1)S(1)} %all-to-all-done.2.x_ref) | copy-start | bytes 5505028
  60.1 32.9 %all-to-all-start = ((bf16[128,2,3584]{2,1,0:T(2,128)(2,1)}), bf16[128,2,3584]{2,1,0:T(2,128)(2,1)}, u32[]{:S(2)}, u32[]{:S(2)}) async-start(bf16[128,2,3584]{2,1,0:T(2,128)(2,1)} %copy.53), calls=%async_computation | async-start | bytes 3670016 | tf_op jit(solution)/shard_map/all_to_all | solution.py:151
  69.7 1.8 %copy-start = (f32[2,128,3584]{2,1,0:T(8,128)}, f32[2,128,3584]{2,1,0:T(8,128)S(1)}, u32[]{:S(2)}) copy-start(f32[2,128,3584]{2,1,0:T(8,128)S(1)} %fusion.4) | copy-start | bytes 11010052
  71.5 2.3 %copy-start.6 = (f32[2,16,8]{1,2,0:T(8,128)S(1)}, f32[2,16,8]{1,2,0:T(8,128)}, u32[]{:S(2)}) copy-start(f32[2,16,8]{1,2,0:T(8,128)} %param.9) | copy-start | bytes 3076
  72.5 25.0 %collective-permute-start.3 = (bf16[2,64,3584]{2,1,0:T(8,128)(2,1)}, bf16[2,64,3584]{2,1,0:T(8,128)(2,1)S(1)}, u32[]{:S(2)}, u32[]{:S(2)}) collective-permute-start(bf16[2,64,3584]{2,1,0:T(8,128)(2,1)} %dynamic-slice_convert_fusion), channel_id=1, source_target_pairs={{0,1},{1,0},{2,3},{3,2},{4,5},{5,4},{6,7},{7,6},{8,9},{9,8},{10,11... | collective-permute-start | bytes 2752520 | tf_op jit(solution)/shard_map/ppermute | solution.py:16
  93.1 32.2 %all-to-all-start.3 = ((bf16[128,2,3584]{2,1,0:T(2,128)(2,1)}), bf16[128,2,3584]{2,1,0:T(2,128)(2,1)S(1)}, u32[]{:S(2)}, u32[]{:S(2)}) async-start(bf16[128,2,3584]{2,1,0:T(2,128)(2,1)} %shard_map.74), calls=%async_computation.3 | async-start | bytes 3670016 | tf_op jit(solution)/shard_map/all_to_all | solution.py:153
  99.2 1.2 copy-start.2
  100.4 31.2 %collective-permute-start.4 = (bf16[2,32,3584]{2,1,0:T(8,128)(2,1)S(1)}, bf16[2,32,3584]{2,1,0:T(8,128)(2,1)S(1)}, u32[]{:S(2)}, u32[]{:S(2)}) collective-permute-start(bf16[2,32,3584]{2,1,0:T(8,128)(2,1)S(1)} %dynamic-slice_convert_fusion.1), channel_id=1, source_target_pairs={{0,2},{2,0},{1,3},{3,1},{4,6},{6,4},{5,7},{7,5},{8,10},{10,8},{9,1... | collective-permute-start | bytes 1376264 | tf_op jit(solution)/shard_map/ppermute | solution.py:16
  125.3 33.1 %all-to-all-start.1 = ((bf16[128,2,3584]{2,1,0:T(2,128)(2,1)}), bf16[128,2,3584]{2,1,0:T(2,128)(2,1)}, u32[]{:S(2)}, u32[]{:S(2)}) async-start(bf16[128,2,3584]{2,1,0:T(2,128)(2,1)} %shard_map.73), calls=%async_computation.1 | async-start | bytes 3670016 | tf_op jit(solution)/shard_map/all_to_all | solution.py:153
  130.6 5.4 %copy-start.5 = (f32[16,256]{0,1:T(8,128)S(1)}, f32[16,256]{0,1:T(8,128)}, u32[]{:S(2)}) copy-start(f32[16,256]{0,1:T(8,128)} %fusion.16) | copy-start | bytes 49156
  133.0 27.8 %collective-permute-start.5 = (bf16[2,16,3584]{2,1,0:T(8,128)(2,1)S(1)}, bf16[2,16,3584]{2,1,0:T(8,128)(2,1)S(1)}, u32[]{:S(2)}, u32[]{:S(2)}) collective-permute-start(bf16[2,16,3584]{2,1,0:T(8,128)(2,1)S(1)} %dynamic-slice_convert_fusion.2), channel_id=1, source_target_pairs={{0,4},{4,0},{1,5},{5,1},{2,6},{6,2},{3,7},{7,3},{8,12},{12,8},{9,1... | collective-permute-start | bytes 688136 | tf_op jit(solution)/shard_map/ppermute | solution.py:16

commit v6 on v5

--- a/solution.py
+++ b/solution.py
@@ -102,12 +102,10 @@
 
 
 def shared_expert(tokens, shared_weights):
-    my_index = lax.axis_index("ep")
     step_count, row_count, model_width = tokens.shape
-    gathered = tokens
-    for level in (2, 1, 0):
-        partner = partner_2(gathered, "ep", level)
-        gathered = join_halves(gathered, partner, my_index >> level & 1 == 1, 1)
+    count = lax.axis_size("ep")
+    groups = [list(range(g, g + 8)) for g in range(0, count, 8)]
+    gathered = lax.all_gather(tokens, "ep", axis=1, tiled=True, axis_index_groups=groups)
     flat_rows = gathered.reshape(-1, model_width)
     gate_val = jnp.dot(flat_rows, shared_weights[0], preferred_element_type=jnp.float32)
     up_val = jnp.dot(flat_rows, shared_weights[1], preferred_element_type=jnp.float32)
@@ -116,15 +114,9 @@
         hidden, shared_weights[2], (((1,), (1,)), ((), ())), preferred_element_type=jnp.float32
     )
     partial_value = partial_value.reshape(step_count, 8 * row_count, model_width)
-    for level in (0, 1, 2):
-        half = partial_value.shape[1] // 2
-        bit = my_index >> level & 1
-        keep = lax.dynamic_slice_in_dim(partial_value, bit * half, half, 1)
-        send = lax.dynamic_slice_in_dim(partial_value, (1 - bit) * half, half, 1)
-        partial_value = keep + partner_2(send.astype(jnp.bfloat16), "ep", level).astype(
-            jnp.float32
-        )
-    return partial_value
+    return lax.psum_scatter(
+        partial_value, "ep", scatter_dimension=1, tiled=True, axis_index_groups=groups
+    )
 
 
 def shards(tokens, expert_ids, combine_weights, w_gate, w_up, w_down, shared_weights):
@@ -159,8 +151,7 @@
                 precision=lax.Precision.HIGHEST,
             )
         )
-    later_tokens = lax.optimization_barrier((tokens, *payloads))[0]
-    shared = shared_expert(later_tokens, shared_weights)
+    shared = shared_expert(tokens, shared_weights)
     routed = jnp.stack(routed_steps)
     return (shared + routed).astype(jnp.bfloat16)
 

time: 162 us -> 182 us (1.12)
  waiting for transfers between devices: 61 us -> 84.7 us
  between operations: 0.21 us -> 13.5 us
  starting transfers between devices: 38.7 us -> 30.5 us
  other arithmetic: 7.01 us -> 1.77 us
  local copies, waits for them, and re-layouts: 13.2 us -> 9.39 us
    all_gather x0 -> x1, waiting for transfers between devices: none -> 29.8 us  [shared_expert(): lax.all_gather(tokens, 'ep', axis=1, tiled=True, axis_index_groups=groups)]
    ppermute x6 -> x0, starting transfers between devices: 12.1 us -> none  [partner_2(): return lax.ppermute(block, axis, route)]
    all_to_all x2, waiting for transfers between devices: 31.2 us -> 39.7 us  [shards(): lax.all_to_all(expert_out, 'ep', split_axis=0, concat_axis=0, tiled=True)]
    all_to_all x2, waiting for transfers between devices: 22.4 us -> 14.5 us  [shards(): lax.all_to_all(payloads[s], 'ep', split_axis=0, concat_axis=0, tiled=True)]
    ppermute x6 -> x0, waiting for transfers between devices: 7.29 us -> none  [partner_2(): return lax.ppermute(block, axis, route)]
    select_n x3 -> x0, other arithmetic: 3.3 us -> none  [join_halves(): jnp.where(upper_side, jnp.concatenate([partner, mine], axis=axis_no), jnp...]
    all_to_all x2, starting transfers between devices: 16.9 us -> 20 us  [shards(): lax.all_to_all(payloads[s], 'ep', split_axis=0, concat_axis=0, tiled=True)]
    add x2 -> x0, other arithmetic: 2.94 us -> none  [shared_expert(): keep + partner_2(send.astype(jnp.bfloat16), 'ep', level).astype(jnp.float32)]
  transfers between devices with their start and end apart: 10 -> 6, of which waited for: 6 -> 4; matrix products, arithmetic and copies ran while one was open for 12% -> 12% of each run, Pallas kernels for 17% -> 15%
where the time goes in v6:
time: 182 us; the launch traced here: 181 us
  waiting for transfers between devices  84.7 us (47%)
  starting transfers between devices  30.5 us (17%)
  Pallas kernels  27.2 us (15%)
  matrix products  14 us (8%)
  between operations  13.5 us (7%)
  local copies, waits for them, and re-layouts  9.39 us (5%)
    all_to_all x2, waiting for transfers between devices, shards(): lax.all_to_all(expert_out, 'ep', split_axis=0, concat_axis=0, tiled=True)  39.7 us
    all_gather x1, waiting for transfers between devices, shared_expert(): lax.all_gather(tokens, 'ep', axis=1, tiled=True, axis_index_groups=groups)  29.8 us
    pallas_call x2, Pallas kernels, expert_rows(): pl.pallas_call(ffn_kernel, out_shape=jax.ShapeDtypeStruct(token_block.sha...  27.2 us
    all_to_all x2, starting transfers between devices, shards(): lax.all_to_all(payloads[s], 'ep', split_axis=0, concat_axis=0, tiled=True)  20 us
    all_to_all x2, waiting for transfers between devices, shards(): lax.all_to_all(payloads[s], 'ep', split_axis=0, concat_axis=0, tiled=True)  14.5 us
    all_to_all x2, starting transfers between devices, shards(): lax.all_to_all(expert_out, 'ep', split_axis=0, concat_axis=0, tiled=True)  10.4 us
    dot_general x2, local copies, waits for them, and re-layouts, shards(): jnp.einsum('ect,td->ecd', dispatch.reshape(experts, capacity, row_count),...  6.28 us
  transfers between devices with their start and end apart: 6, of which 4 were waited for; matrix products, arithmetic and copies ran while one was open for 12% of the time, Pallas kernels for 15%

profile of v6, /device:TPU:1, one launch (start us, length us, event | category | flops | bytes accessed | tf_op | source)
XLA Modules:
  0.0 181.0 jit_solution(17245619447511721661)
XLA Ops:
  6.5 0.7 all-gather.2.cloned.1.call-update
  7.3 0.7 fusion.45
  8.7 1.5 fusion.18
  10.2 3.1 %copy.48 = bf16[128,2,3584]{2,1,0:T(2,128)(2,1)} copy(bf16[128,2,3584]{2,0,1:T(8,128)(2,1)S(1)} %fusion.18) | data formatting | bytes 3670016 | tf_op jit(solution)/shard_map/ect,td->ecd/dot_general | solution.py:133
  13.3 11.5 %all-to-all-start.2 = ((bf16[128,2,3584]{2,1,0:T(2,128)(2,1)}), bf16[128,2,3584]{2,1,0:T(2,128)(2,1)S(1)}, u32[]{:S(2)}, u32[]{:S(2)}) async-start(bf16[128,2,3584]{2,1,0:T(2,128)(2,1)} %copy.48), calls=%async_computation.3 | async-start | bytes 3670016 | tf_op jit(solution)/shard_map/all_to_all | solution.py:143
  24.9 29.8 %all-gather.2.cloned.1.call-done = bf16[2,128,3584]{2,1,0:T(8,128)(2,1)} async-done(((bf16[2,16,3584]{2,1,0:T(8,128)(2,1)}), bf16[2,128,3584]{2,1,0:T(8,128)(2,1)}) %all-gather.2.cloned.1.call-update) | async-done | bytes 1835024 | tf_op jit(solution)/shard_map/all_gather | solution.py:108
  54.7 2.5 %fusion.8 = f32[256,128]{1,0:T(8,128)S(1)} fusion(bf16[256,3584]{1,0:T(8,128)(2,1)} %bitcast.38, bf16[3,3584,128]{2,1,0:T(8,128)(2,1)} %param.13), kind=kOutput, calls=%fused_computation.17 | convolution fusion | flops 234881024 | bytes 2883584 | tf_op jit(solution)/shard_map/dot_general | solution.py:110
  57.3 2.1 %fusion.2 = bf16[256,128]{1,0:T(8,128)(2,1)S(1)} fusion(bf16[256,3584]{1,0:T(8,128)(2,1)} %bitcast.39, bf16[3,3584,128]{2,1,0:T(8,128)(2,1)S(1)} %copy-done.2, f32[256,128]{1,0:T(8,128)S(1)} %fusion.8), kind=kOutput, calls=%fused_computation.7 | convolution fusion | flops 235077632 | bytes 2949120 | tf_op jit(solution)/shard_map/dot_general | solution.py:111
  59.4 2.4 %fusion.5 = f32[2,128,3584]{2,1,0:T(8,128)} fusion(bf16[2,128,128]{2,1,0:T(8,128)(2,1)S(1)} %bitcast.37, bf16[3,3584,128]{2,1,0:T(8,128)(2,1)S(1)} %copy-done.2), kind=kOutput, calls=%fused_computation.14 | convolution fusion | flops 234881024 | bytes 4653056 | tf_op jit(solution)/shard_map/dot_general | solution.py:113
  62.8 0.6 fusion.20
  63.4 3.2 %copy.49 = bf16[128,2,3584]{2,1,0:T(2,128)(2,1)} copy(bf16[128,2,3584]{2,0,1:T(8,128)(2,1)S(1)} %fusion.20) | data formatting | bytes 3670016 | tf_op jit(solution)/shard_map/ect,td->ecd/dot_general | solution.py:133
  66.6 1.2 copy-done
  67.8 8.5 %all-to-all-start = ((bf16[128,2,3584]{2,1,0:T(2,128)(2,1)}), bf16[128,2,3584]{2,1,0:T(2,128)(2,1)}, u32[]{:S(2)}, u32[]{:S(2)}) async-start(bf16[128,2,3584]{2,1,0:T(2,128)(2,1)} %copy.49), calls=%async_computation.1 | async-start | bytes 3670016 | tf_op jit(solution)/shard_map/all_to_all | solution.py:143
  76.3 13.6 %shard_map.74 = bf16[128,2,3584]{2,1,0:T(2,128)(2,1)} custom-call(bf16[128,2,3584]{2,1,0:T(2,128)(2,1)} %copy-done, bf16[1,3584,1024]{2,1,0:T(8,128)(2,1)} %gate_ref.3, bf16[1,3584,1024]{2,1,0:T(8,128)(2,1)} %up_ref.3, bf16[1,1024,3584]{2,1,0:T(8,128)(2,1)} %down_ref.3), custom_call_target="tpu_custom_call" | custom-call | flops 5637144576 | bytes 25690112 | tf_op jit(solution)/shard_map/pallas_call | solution.py:45
  90.0 14.5 %all-to-all-done.x_ref = bf16[128,2,3584]{2,1,0:T(2,128)(2,1)} async-done(((bf16[128,2,3584]{2,1,0:T(2,128)(2,1)}), bf16[128,2,3584]{2,1,0:T(2,128)(2,1)}, u32[]{:S(2)}, u32[]{:S(2)}) %all-to-all-start) | async-done | bytes 1835040 | tf_op jit(solution)/shard_map/all_to_all | solution.py:143
  104.5 5.0 %all-to-all-start.3 = ((bf16[128,2,3584]{2,1,0:T(2,128)(2,1)}), bf16[128,2,3584]{2,1,0:T(2,128)(2,1)S(1)}, u32[]{:S(2)}, u32[]{:S(2)}) async-start(bf16[128,2,3584]{2,1,0:T(2,128)(2,1)} %shard_map.74), calls=%async_computation.4 | async-start | bytes 3670016 | tf_op jit(solution)/shard_map/all_to_all | solution.py:145
  109.4 13.6 %shard_map.73 = bf16[128,2,3584]{2,1,0:T(2,128)(2,1)} custom-call(bf16[128,2,3584]{2,1,0:T(2,128)(2,1)} %all-to-all-done.x_ref, bf16[1,3584,1024]{2,1,0:T(8,128)(2,1)} %gate_ref.3, bf16[1,3584,1024]{2,1,0:T(8,128)(2,1)} %up_ref.3, bf16[1,1024,3584]{2,1,0:T(8,128)(2,1)} %down_ref.3), custom_call_target="tpu_custom_call" | custom-call | flops 5637144576 | bytes 25690112 | tf_op jit(solution)/shard_map/pallas_call | solution.py:45
  123.0 14.1 %all-to-all-done.3 = bf16[128,2,3584]{2,1,0:T(2,128)(2,1)S(1)} async-done(((bf16[128,2,3584]{2,1,0:T(2,128)(2,1)}), bf16[128,2,3584]{2,1,0:T(2,128)(2,1)S(1)}, u32[]{:S(2)}, u32[]{:S(2)}) %all-to-all-start.3) | async-done | bytes 1835040 | tf_op jit(solution)/shard_map/all_to_all | solution.py:145
  137.1 5.4 %all-to-all-start.1 = ((bf16[128,2,3584]{2,1,0:T(2,128)(2,1)}), bf16[128,2,3584]{2,1,0:T(2,128)(2,1)}, u32[]{:S(2)}, u32[]{:S(2)}) async-start(bf16[128,2,3584]{2,1,0:T(2,128)(2,1)} %shard_map.73), calls=%async_computation.2 | async-start | bytes 3670016 | tf_op jit(solution)/shard_map/all_to_all | solution.py:145
  142.9 0.4 fusion.16
  143.6 0.9 convolution_bitcast_fusion
  144.5 25.5 %all-to-all-done.1 = bf16[128,2,3584]{2,1,0:T(2,128)(2,1)} async-done(((bf16[128,2,3584]{2,1,0:T(2,128)(2,1)}), bf16[128,2,3584]{2,1,0:T(2,128)(2,1)}, u32[]{:S(2)}, u32[]{:S(2)}) %all-to-all-start.1) | async-done | bytes 1835040 | tf_op jit(solution)/shard_map/all_to_all | solution.py:145
  170.1 2.4 %convolution_bitcast_fusion.1 = f32[1,16,3584]{2,1,0:T(8,128)S(1)} fusion(bf16[128,2,3584]{2,1,0:T(2,128)(2,1)} %all-to-all-done.1, f32[16,128,2]{0,2,1:T(2,128)S(1)} %bitcast.35), kind=kOutput, calls=%fused_computation.1 | convolution fusion | flops 176160768 | bytes 2080768 | tf_op jit(solution)/shard_map/tec,ecd->td/dot_general | solution.py:147
  172.4 1.8 fusion.13
  (30 shorter events, 2.5 us)
Async XLA Ops:
  6.5 48.1 %all-gather.2.cloned.1.call-start = ((), (), s32[]{:S(2)}) async-start(), calls=%async_computation.5 | async-start | bytes 2064384 | tf_op jit(solution)/shard_map/all_gather | solution.py:108
  13.3 53.2 %all-to-all-start.2 = ((bf16[128,2,3584]{2,1,0:T(2,128)(2,1)}), bf16[128,2,3584]{2,1,0:T(2,128)(2,1)S(1)}, u32[]{:S(2)}, u32[]{:S(2)}) async-start(bf16[128,2,3584]{2,1,0:T(2,128)(2,1)} %copy.48), calls=%async_computation.3 | async-start | bytes 3670016 | tf_op jit(solution)/shard_map/all_to_all | solution.py:143
  24.9 147.6 %reduce-scatter.2.cloned.1.call-start = ((), (), s32[]{:S(2)}) async-start(), calls=%async_computation.6 | async-start | bytes 4128768 | tf_op jit(solution)/shard_map/reduce_scatter | solution.py:117
  54.7 2.6 %copy-start.2 = (bf16[3,3584,128]{2,1,0:T(8,128)(2,1)S(1)}, bf16[3,3584,128]{2,1,0:T(8,128)(2,1)}, u32[]{:S(2)}) copy-start(bf16[3,3584,128]{2,1,0:T(8,128)(2,1)} %param.13) | copy-start | bytes 8257540
  61.9 0.9 copy-start.1
  66.5 1.2 copy-start
  67.8 36.7 %all-to-all-start = ((bf16[128,2,3584]{2,1,0:T(2,128)(2,1)}), bf16[128,2,3584]{2,1,0:T(2,128)(2,1)}, u32[]{:S(2)}, u32[]{:S(2)}) async-start(bf16[128,2,3584]{2,1,0:T(2,128)(2,1)} %copy.49), calls=%async_computation.1 | async-start | bytes 3670016 | tf_op jit(solution)/shard_map/all_to_all | solution.py:143
  104.5 32.7 %all-to-all-start.3 = ((bf16[128,2,3584]{2,1,0:T(2,128)(2,1)}), bf16[128,2,3584]{2,1,0:T(2,128)(2,1)S(1)}, u32[]{:S(2)}, u32[]{:S(2)}) async-start(bf16[128,2,3584]{2,1,0:T(2,128)(2,1)} %shard_map.74), calls=%async_computation.4 | async-start | bytes 3670016 | tf_op jit(solution)/shard_map/all_to_all | solution.py:145
  123.0 19.6 %copy-start.3 = (f32[2,16,8]{1,2,0:T(8,128)S(1)}, f32[2,16,8]{1,2,0:T(8,128)}, u32[]{:S(2)}) copy-start(f32[2,16,8]{1,2,0:T(8,128)} %param.9) | copy-start | bytes 3076
  137.1 32.9 %all-to-all-start.1 = ((bf16[128,2,3584]{2,1,0:T(2,128)(2,1)}), bf16[128,2,3584]{2,1,0:T(2,128)(2,1)}, u32[]{:S(2)}, u32[]{:S(2)}) async-start(bf16[128,2,3584]{2,1,0:T(2,128)(2,1)} %shard_map.73), calls=%async_computation.2 | async-start | bytes 3670016 | tf_op jit(solution)/shard_map/all_to_all | solution.py:145
Sparse Core Ops, SparseCore 0:
  9.0 45.5 all-gather.1
  62.0 64.9 reduce-scatter.1

commit v7 on v5

--- a/solution.py
+++ b/solution.py
@@ -65,6 +65,24 @@
     )(token_block, w_gate, w_up, w_down)
 
 
+def dispatch_kernel(select_ref, token_ref, out_ref):
+    picked = jnp.dot(select_ref[...], token_ref[...], preferred_element_type=jnp.float32)
+    out_ref[...] = picked.astype(out_ref.dtype).reshape(out_ref.shape)
+
+
+def dispatch_rows(select, step_tokens, experts, capacity):
+    model_width = step_tokens.shape[-1]
+    return pl.pallas_call(
+        dispatch_kernel,
+        out_shape=jax.ShapeDtypeStruct((experts, capacity, model_width), step_tokens.dtype),
+        in_specs=[
+            pl.BlockSpec(memory_space=pltpu.VMEM),
+            pl.BlockSpec(memory_space=pltpu.VMEM),
+        ],
+        out_specs=pl.BlockSpec(memory_space=pltpu.VMEM),
+    )(select, step_tokens)
+
+
 def route_tables(step_ids, step_weights, experts, capacity):
     row_count, top_count = step_ids.shape
     pair_count = row_count * top_count
@@ -121,9 +139,7 @@
         bit = my_index >> level & 1
         keep = lax.dynamic_slice_in_dim(partial_value, bit * half, half, 1)
         send = lax.dynamic_slice_in_dim(partial_value, (1 - bit) * half, half, 1)
-        partial_value = keep + partner_2(send.astype(jnp.bfloat16), "ep", level).astype(
-            jnp.float32
-        )
+        partial_value = keep + partner_2(send, "ep", level)
     return partial_value
 
 
@@ -137,14 +153,7 @@
     combines = []
     for s in range(step_count):
         dispatch, combine = route_tables(expert_ids[s], combine_weights[s], experts, capacity)
-        payloads.append(
-            jnp.einsum(
-                "ect,td->ecd",
-                dispatch.reshape(experts, capacity, row_count),
-                tokens[s],
-                preferred_element_type=jnp.float32,
-            ).astype(jnp.bfloat16)
-        )
+        payloads.append(dispatch_rows(dispatch, tokens[s], experts, capacity))
         combines.append(combine)
     routed_steps = []
     for s in range(step_count):

time: 162 us -> 183 us (1.13)
  waiting for transfers between devices: 61 us -> 81.1 us
  matrix products: 14.3 us -> 8.12 us
  Pallas kernels: 27 us -> 32.7 us
  starting transfers between devices: 38.7 us -> 43.2 us
  local copies, waits for them, and re-layouts: 13.2 us -> 9.71 us
    ppermute x6, waiting for transfers between devices: 7.29 us -> 34.1 us  [partner_2(): return lax.ppermute(block, axis, route)]
    all_to_all x2, waiting for transfers between devices: 31.2 us -> 13.3 us  [shards(): lax.all_to_all(expert_out, 'ep', split_axis=0, concat_axis=0, tiled=True)]
    all_to_all x2, waiting for transfers between devices: 22.4 us -> 33.7 us  [shards(): lax.all_to_all(payloads[s], 'ep', split_axis=0, concat_axis=0, tiled=True)]
    dot_general x2 -> x0, local copies, waits for them, and re-layouts: 6.31 us -> none  [shards(): jnp.einsum('ect,td->ecd', dispatch.reshape(experts, capacity, row_count),...]
    ppermute x6, starting transfers between devices: 12.1 us -> 18.1 us  [partner_2(): return lax.ppermute(block, axis, route)]
    pallas_call x0 -> x2, Pallas kernels: none -> 5.68 us  [dispatch_rows(): pl.pallas_call(dispatch_kernel, out_shape=jax.ShapeDtypeStruct((experts,...]
    dot_general x2 -> x0, matrix products: 2.1 us -> none  [shards(): jnp.einsum('ect,td->ecd', dispatch.reshape(experts, capacity, row_count),...]
  transfers between devices with their start and end apart: 10 -> 10, of which waited for: 6 -> 8; matrix products, arithmetic and copies ran while one was open for 12% -> 8% of each run, Pallas kernels for 17% -> 15%
where the time goes in v7:
time: 183 us
  waiting for transfers between devices  81.1 us (44%)
  starting transfers between devices  43.2 us (24%)
  Pallas kernels  32.7 us (18%)
  local copies, waits for them, and re-layouts  9.71 us (5%)
  matrix products  8.12 us (4%)
  other arithmetic  7.86 us (4%)
    ppermute x6, waiting for transfers between devices, partner_2(): return lax.ppermute(block, axis, route)  34.1 us
    all_to_all x2, waiting for transfers between devices, shards(): lax.all_to_all(payloads[s], 'ep', split_axis=0, concat_axis=0, tiled=True)  33.7 us
    pallas_call x2, Pallas kernels, expert_rows(): pl.pallas_call(ffn_kernel, out_shape=jax.ShapeDtypeStruct(token_block.sha...  27 us
    ppermute x6, starting transfers between devices, partner_2(): return lax.ppermute(block, axis, route)  18.1 us
    all_to_all x2, starting transfers between devices, shards(): lax.all_to_all(payloads[s], 'ep', split_axis=0, concat_axis=0, tiled=True)  15.4 us
    all_to_all x2, waiting for transfers between devices, shards(): lax.all_to_all(expert_out, 'ep', split_axis=0, concat_axis=0, tiled=True)  13.3 us
    all_to_all x2, starting transfers between devices, shards(): lax.all_to_all(expert_out, 'ep', split_axis=0, concat_axis=0, tiled=True)  9.7 us
    pallas_call x2, Pallas kernels, dispatch_rows(): pl.pallas_call(dispatch_kernel, out_shape=jax.ShapeDtypeStruct((experts,...  5.68 us
  transfers between devices with their start and end apart: 10, of which 8 were waited for; matrix products, arithmetic and copies ran while one was open for 8% of the time, Pallas kernels for 15%

profile of v7, /device:TPU:1, one launch (start us, length us, event | category | flops | bytes accessed | tf_op | source)
XLA Modules:
  0.0 182.9 jit_solution(1172949733874787396)
XLA Ops:
  5.1 2.9 %shard_map.74 = bf16[128,2,3584]{2,1,0:T(2,128)(2,1)} custom-call(bf16[256,16]{1,0:T(8,128)(2,1)} %copy.33.select_ref, bf16[16,3584]{1,0:T(8,128)(2,1)} %get-tuple-element.8.token_ref), custom_call_target="tpu_custom_call" | custom-call | tf_op jit(solution)/shard_map/pallas_call | solution.py:75
  7.9 2.8 %shard_map.73 = bf16[128,2,3584]{2,1,0:T(2,128)(2,1)} custom-call(bf16[256,16]{1,0:T(8,128)(2,1)} %copy.31.select_ref, bf16[16,3584]{1,0:T(8,128)(2,1)} %get-tuple-element.7.token_ref), custom_call_target="tpu_custom_call" | custom-call | tf_op jit(solution)/shard_map/pallas_call | solution.py:75
  10.8 3.8 %collective-permute-start = (bf16[2,16,3584]{2,1,0:T(8,128)(2,1)S(1)}, bf16[2,16,3584]{2,1,0:T(8,128)(2,1)S(1)}, u32[]{:S(2)}, u32[]{:S(2)}) collective-permute-start(bf16[2,16,3584]{2,1,0:T(8,128)(2,1)S(1)} %copy-done.3), channel_id=1, source_target_pairs={{0,4},{4,0},{1,5},{5,1},{2,6},{6,2},{3,7},{7,3},{8,12},{12,8},{9,1... | collective-permute-start | bytes 688136 | tf_op jit(solution)/shard_map/ppermute | solution.py:16
  14.5 5.1 %collective-permute-done = bf16[2,16,3584]{2,1,0:T(8,128)(2,1)S(1)} collective-permute-done((bf16[2,16,3584]{2,1,0:T(8,128)(2,1)S(1)}, bf16[2,16,3584]{2,1,0:T(8,128)(2,1)S(1)}, u32[]{:S(2)}, u32[]{:S(2)}) %collective-permute-start) | collective-permute-done | bytes 229408 | tf_op jit(solution)/shard_map/ppermute | solution.py:16
  21.0 9.2 %collective-permute-done.1 = bf16[2,32,3584]{2,1,0:T(8,128)(2,1)S(1)} collective-permute-done((bf16[2,32,3584]{2,1,0:T(8,128)(2,1)S(1)}, bf16[2,32,3584]{2,1,0:T(8,128)(2,1)S(1)}, u32[]{:S(2)}, u32[]{:S(2)}) %collective-permute-start.1) | collective-permute-done | bytes 458784 | tf_op jit(solution)/shard_map/ppermute | solution.py:16
  30.4 2.5 %collective-permute-start.2 = (bf16[2,64,3584]{2,1,0:T(8,128)(2,1)S(1)}, bf16[2,64,3584]{2,1,0:T(8,128)(2,1)}, u32[]{:S(2)}, u32[]{:S(2)}) collective-permute-start(bf16[2,64,3584]{2,1,0:T(8,128)(2,1)S(1)} %maximum_select_fusion.1), channel_id=1, source_target_pairs={{0,1},{1,0},{2,3},{3,2},{4,5},{5,4},{6,7},{7,6},{8,9},{9,8},{10,11... | collective-permute-start | bytes 2752520 | tf_op jit(solution)/shard_map/ppermute | solution.py:16
  32.9 10.1 %all-to-all-start.2 = ((bf16[128,2,3584]{2,1,0:T(2,128)(2,1)}), bf16[128,2,3584]{2,1,0:T(2,128)(2,1)S(1)}, u32[]{:S(2)}, u32[]{:S(2)}) async-start(bf16[128,2,3584]{2,1,0:T(2,128)(2,1)} %shard_map.74), calls=%async_computation.2 | async-start | bytes 3670016 | tf_op jit(solution)/shard_map/all_to_all | solution.py:160
  43.0 2.0 %maximum_select_fusion = bf16[2,128,3584]{2,1,0:T(8,128)(2,1)S(1)} fusion(bf16[2,64,3584]{2,1,0:T(8,128)(2,1)S(1)} %maximum_select_fusion.1, bf16[2,64,3584]{2,1,0:T(8,128)(2,1)} %collective-permute-done.2, pred[]{:T(512)S(6)} %eq.95), kind=kLoop, calls=%fused_computation.2 | loop fusion | flops 8257536 | bytes 3670017 | tf_op jit(solution)/shard_map/jit(_where)/select_n | solution.py:115
  50.7 20.0 %all-to-all-done.2.x_ref = bf16[128,2,3584]{2,1,0:T(2,128)(2,1)S(1)} async-done(((bf16[128,2,3584]{2,1,0:T(2,128)(2,1)}), bf16[128,2,3584]{2,1,0:T(2,128)(2,1)S(1)}, u32[]{:S(2)}, u32[]{:S(2)}) %all-to-all-start.2) | async-done | bytes 1835040 | tf_op jit(solution)/shard_map/all_to_all | solution.py:160
  72.0 5.3 %all-to-all-start = ((bf16[128,2,3584]{2,1,0:T(2,128)(2,1)}), bf16[128,2,3584]{2,1,0:T(2,128)(2,1)}, u32[]{:S(2)}, u32[]{:S(2)}) async-start(bf16[128,2,3584]{2,1,0:T(2,128)(2,1)} %shard_map.73), calls=%async_computation | async-start | bytes 3670016 | tf_op jit(solution)/shard_map/all_to_all | solution.py:160
  77.7 13.5 %shard_map.76 = bf16[128,2,3584]{2,1,0:T(2,128)(2,1)} custom-call(bf16[128,2,3584]{2,1,0:T(2,128)(2,1)} %copy-done.1, bf16[1,3584,1024]{2,1,0:T(8,128)(2,1)} %gate_ref.3, bf16[1,3584,1024]{2,1,0:T(8,128)(2,1)} %up_ref.3, bf16[1,1024,3584]{2,1,0:T(8,128)(2,1)} %down_ref.3), custom_call_target="tpu_custom_call" | custom-call | flops 5637144576 | bytes 25690112 | tf_op jit(solution)/shard_map/pallas_call | solution.py:45
  91.2 13.7 %all-to-all-done.x_ref = bf16[128,2,3584]{2,1,0:T(2,128)(2,1)} async-done(((bf16[128,2,3584]{2,1,0:T(2,128)(2,1)}), bf16[128,2,3584]{2,1,0:T(2,128)(2,1)}, u32[]{:S(2)}, u32[]{:S(2)}) %all-to-all-start) | async-done | bytes 1835040 | tf_op jit(solution)/shard_map/all_to_all | solution.py:160
  104.9 4.3 %all-to-all-start.3 = ((bf16[128,2,3584]{2,1,0:T(2,128)(2,1)}), bf16[128,2,3584]{2,1,0:T(2,128)(2,1)S(1)}, u32[]{:S(2)}, u32[]{:S(2)}) async-start(bf16[128,2,3584]{2,1,0:T(2,128)(2,1)} %shard_map.76), calls=%async_computation.3 | async-start | bytes 3670016 | tf_op jit(solution)/shard_map/all_to_all | solution.py:162
  109.2 2.3 %dynamic-slice_add_fusion = f32[2,64,3584]{2,1,0:T(8,128)S(1)} fusion(f32[2,64,3584]{2,1,0:T(8,128)} %collective-permute-done.3, f32[2,128,3584]{2,1,0:T(8,128)} %copy-done, s32[]{:T(128)S(6)} %select_n.80), kind=kLoop, calls=%fused_computation.5 | loop fusion | flops 458752 | bytes 5505028 | tf_op jit(solution)/shard_map/add | solution.py:142
  112.8 1.7 collective-permute-start.4
  115.5 13.5 %shard_map.75 = bf16[128,2,3584]{2,1,0:T(2,128)(2,1)} custom-call(bf16[128,2,3584]{2,1,0:T(2,128)(2,1)} %all-to-all-done.x_ref, bf16[1,3584,1024]{2,1,0:T(8,128)(2,1)} %gate_ref.3, bf16[1,3584,1024]{2,1,0:T(8,128)(2,1)} %up_ref.3, bf16[1,1024,3584]{2,1,0:T(8,128)(2,1)} %down_ref.3), custom_call_target="tpu_custom_call" | custom-call | flops 5637144576 | bytes 25690112 | tf_op jit(solution)/shard_map/pallas_call | solution.py:45
  128.9 8.1 %all-to-all-done.3 = bf16[128,2,3584]{2,1,0:T(2,128)(2,1)S(1)} async-done(((bf16[128,2,3584]{2,1,0:T(2,128)(2,1)}), bf16[128,2,3584]{2,1,0:T(2,128)(2,1)S(1)}, u32[]{:S(2)}, u32[]{:S(2)}) %all-to-all-start.3) | async-done | bytes 1835040 | tf_op jit(solution)/shard_map/all_to_all | solution.py:162
  137.1 5.4 %all-to-all-start.1 = ((bf16[128,2,3584]{2,1,0:T(2,128)(2,1)}), bf16[128,2,3584]{2,1,0:T(2,128)(2,1)}, u32[]{:S(2)}, u32[]{:S(2)}) async-start(bf16[128,2,3584]{2,1,0:T(2,128)(2,1)} %shard_map.75), calls=%async_computation.1 | async-start | bytes 3670016 | tf_op jit(solution)/shard_map/all_to_all | solution.py:162
  143.4 16.1 %collective-permute-done.4 = f32[2,32,3584]{2,1,0:T(8,128)} collective-permute-done((f32[2,32,3584]{2,1,0:T(8,128)S(1)}, f32[2,32,3584]{2,1,0:T(8,128)}, u32[]{:S(2)}, u32[]{:S(2)}) %collective-permute-start.4) | collective-permute-done | bytes 917536 | tf_op jit(solution)/shard_map/ppermute | solution.py:16
  161.1 7.7 %collective-permute-start.5 = (f32[2,16,3584]{2,1,0:T(8,128)S(1)}, f32[2,16,3584]{2,1,0:T(8,128)}, u32[]{:S(2)}, u32[]{:S(2)}) collective-permute-start(f32[2,16,3584]{2,1,0:T(8,128)S(1)} %constant_dynamic-slice_fusion), channel_id=1, source_target_pairs={{0,4},{4,0},{1,5},{5,1},{2,6},{6,2},{3,7},{7,3},{8,12},{12,8},{9,1... | collective-permute-start | bytes 1376264 | tf_op jit(solution)/shard_map/ppermute | solution.py:16
  169.7 5.2 %all-to-all-done.1 = bf16[128,2,3584]{2,1,0:T(2,128)(2,1)} async-done(((bf16[128,2,3584]{2,1,0:T(2,128)(2,1)}), bf16[128,2,3584]{2,1,0:T(2,128)(2,1)}, u32[]{:S(2)}, u32[]{:S(2)}) %all-to-all-start.1) | async-done | bytes 1835040 | tf_op jit(solution)/shard_map/all_to_all | solution.py:162
  174.9 2.5 %convolution_bitcast_fusion.1 = f32[1,16,3584]{2,1,0:T(8,128)S(1)} fusion(bf16[128,2,3584]{2,1,0:T(2,128)(2,1)} %all-to-all-done.1, f32[16,128,2]{0,2,1:T(2,128)} %bitcast.32), kind=kOutput, calls=%fused_computation.1 | convolution fusion | flops 176160768 | bytes 2080768 | tf_op jit(solution)/shard_map/tec,ecd->td/dot_general | solution.py:164
  177.4 3.7 %collective-permute-done.5 = f32[2,16,3584]{2,1,0:T(8,128)} collective-permute-done((f32[2,16,3584]{2,1,0:T(8,128)S(1)}, f32[2,16,3584]{2,1,0:T(8,128)}, u32[]{:S(2)}, u32[]{:S(2)}) %collective-permute-start.5) | collective-permute-done | bytes 458784 | tf_op jit(solution)/shard_map/ppermute | solution.py:16
  181.1 1.8 fusion.13
  (49 shorter events, 19.6 us)
Async XLA Ops:
  5.1 5.7 %copy-start.3 = (bf16[2,16,3584]{2,1,0:T(8,128)(2,1)S(1)}, bf16[2,16,3584]{2,1,0:T(8,128)(2,1)}, u32[]{:S(2)}) copy-start(bf16[2,16,3584]{2,1,0:T(8,128)(2,1)} %param.7) | copy-start | bytes 688132
  10.8 8.8 %collective-permute-start = (bf16[2,16,3584]{2,1,0:T(8,128)(2,1)S(1)}, bf16[2,16,3584]{2,1,0:T(8,128)(2,1)S(1)}, u32[]{:S(2)}, u32[]{:S(2)}) collective-permute-start(bf16[2,16,3584]{2,1,0:T(8,128)(2,1)S(1)} %copy-done.3), channel_id=1, source_target_pairs={{0,4},{4,0},{1,5},{5,1},{2,6},{6,2},{3,7},{7,3},{8,12},{12,8},{9,1... | collective-permute-start | bytes 688136 | tf_op jit(solution)/shard_map/ppermute | solution.py:16
  19.7 10.6 %collective-permute-start.1 = (bf16[2,32,3584]{2,1,0:T(8,128)(2,1)S(1)}, bf16[2,32,3584]{2,1,0:T(8,128)(2,1)S(1)}, u32[]{:S(2)}, u32[]{:S(2)}) collective-permute-start(bf16[2,32,3584]{2,1,0:T(8,128)(2,1)S(1)} %maximum_select_fusion.2), channel_id=1, source_target_pairs={{0,2},{2,0},{1,3},{3,1},{4,6},{6,4},{5,7},{7,5},{8,10},{10,8},{9,1... | collective-permute-start | bytes 1376264 | tf_op jit(solution)/shard_map/ppermute | solution.py:16
  30.4 12.6 %collective-permute-start.2 = (bf16[2,64,3584]{2,1,0:T(8,128)(2,1)S(1)}, bf16[2,64,3584]{2,1,0:T(8,128)(2,1)}, u32[]{:S(2)}, u32[]{:S(2)}) collective-permute-start(bf16[2,64,3584]{2,1,0:T(8,128)(2,1)S(1)} %maximum_select_fusion.1), channel_id=1, source_target_pairs={{0,1},{1,0},{2,3},{3,2},{4,5},{5,4},{6,7},{7,6},{8,9},{9,8},{10,11... | collective-permute-start | bytes 2752520 | tf_op jit(solution)/shard_map/ppermute | solution.py:16
  32.9 37.8 %all-to-all-start.2 = ((bf16[128,2,3584]{2,1,0:T(2,128)(2,1)}), bf16[128,2,3584]{2,1,0:T(2,128)(2,1)S(1)}, u32[]{:S(2)}, u32[]{:S(2)}) async-start(bf16[128,2,3584]{2,1,0:T(2,128)(2,1)} %shard_map.74), calls=%async_computation.2 | async-start | bytes 3670016 | tf_op jit(solution)/shard_map/all_to_all | solution.py:160
  43.0 2.3 %copy-start.4 = (bf16[3,3584,128]{2,1,0:T(8,128)(2,1)S(1)}, bf16[3,3584,128]{2,1,0:T(8,128)(2,1)}, u32[]{:S(2)}) copy-start(bf16[3,3584,128]{2,1,0:T(8,128)(2,1)} %param.13) | copy-start | bytes 8257540
  47.2 2.4 %copy-start = (f32[2,128,3584]{2,1,0:T(8,128)}, f32[2,128,3584]{2,1,0:T(8,128)S(1)}, u32[]{:S(2)}) copy-start(f32[2,128,3584]{2,1,0:T(8,128)S(1)} %fusion.4) | copy-start | bytes 11010052
  49.6 27.7 %copy-start.6 = (f32[2,16,8]{1,2,0:T(8,128)S(1)}, f32[2,16,8]{1,2,0:T(8,128)}, u32[]{:S(2)}) copy-start(f32[2,16,8]{1,2,0:T(8,128)} %param.9) | copy-start | bytes 3076
  49.6 59.6 %collective-permute-start.3 = (f32[2,64,3584]{2,1,0:T(8,128)}, f32[2,64,3584]{2,1,0:T(8,128)}, u32[]{:S(2)}, u32[]{:S(2)}) collective-permute-start(f32[2,64,3584]{2,1,0:T(8,128)} %constant_dynamic-slice_fusion.2), channel_id=1, source_target_pairs={{0,1},{1,0},{2,3},{3,2},{4,5},{5,4},{6,7},{7,6},{8,9},{9,8},{10,11... | collective-permute-start | bytes 5505032 | tf_op jit(solution)/shard_map/ppermute | solution.py:16
  70.7 1.2 copy-start.1
  72.0 32.9 %all-to-all-start = ((bf16[128,2,3584]{2,1,0:T(2,128)(2,1)}), bf16[128,2,3584]{2,1,0:T(2,128)(2,1)}, u32[]{:S(2)}, u32[]{:S(2)}) async-start(bf16[128,2,3584]{2,1,0:T(2,128)(2,1)} %shard_map.73), calls=%async_computation | async-start | bytes 3670016 | tf_op jit(solution)/shard_map/all_to_all | solution.py:160
  104.9 32.2 %all-to-all-start.3 = ((bf16[128,2,3584]{2,1,0:T(2,128)(2,1)}), bf16[128,2,3584]{2,1,0:T(2,128)(2,1)S(1)}, u32[]{:S(2)}, u32[]{:S(2)}) async-start(bf16[128,2,3584]{2,1,0:T(2,128)(2,1)} %shard_map.76), calls=%async_computation.3 | async-start | bytes 3670016 | tf_op jit(solution)/shard_map/all_to_all | solution.py:162
  111.5 1.2 copy-start.2
  112.8 46.8 %collective-permute-start.4 = (f32[2,32,3584]{2,1,0:T(8,128)S(1)}, f32[2,32,3584]{2,1,0:T(8,128)}, u32[]{:S(2)}, u32[]{:S(2)}) collective-permute-start(f32[2,32,3584]{2,1,0:T(8,128)S(1)} %constant_dynamic-slice_fusion.1), channel_id=1, source_target_pairs={{0,2},{2,0},{1,3},{3,1},{4,6},{6,4},{5,7},{7,5},{8,10},{10,8},{9,1... | collective-permute-start | bytes 2752520 | tf_op jit(solution)/shard_map/ppermute | solution.py:16
  137.1 37.9 %all-to-all-start.1 = ((bf16[128,2,3584]{2,1,0:T(2,128)(2,1)}), bf16[128,2,3584]{2,1,0:T(2,128)(2,1)}, u32[]{:S(2)}, u32[]{:S(2)}) async-start(bf16[128,2,3584]{2,1,0:T(2,128)(2,1)} %shard_map.75), calls=%async_computation.1 | async-start | bytes 3670016 | tf_op jit(solution)/shard_map/all_to_all | solution.py:162
  143.4 25.4 %copy-start.5 = (f32[16,256]{0,1:T(8,128)S(1)}, f32[16,256]{0,1:T(8,128)}, u32[]{:S(2)}) copy-start(f32[16,256]{0,1:T(8,128)} %fusion.16) | copy-start | bytes 49156
  161.1 20.0 %collective-permute-start.5 = (f32[2,16,3584]{2,1,0:T(8,128)S(1)}, f32[2,16,3584]{2,1,0:T(8,128)}, u32[]{:S(2)}, u32[]{:S(2)}) collective-permute-start(f32[2,16,3584]{2,1,0:T(8,128)S(1)} %constant_dynamic-slice_fusion), channel_id=1, source_target_pairs={{0,4},{4,0},{1,5},{5,1},{2,6},{6,2},{3,7},{7,3},{8,12},{12,8},{9,1... | collective-permute-start | bytes 1376264 | tf_op jit(solution)/shard_map/ppermute | solution.py:16

commit v8 on v7

--- a/solution.py
+++ b/solution.py
@@ -155,10 +155,14 @@
         dispatch, combine = route_tables(expert_ids[s], combine_weights[s], experts, capacity)
         payloads.append(dispatch_rows(dispatch, tokens[s], experts, capacity))
         combines.append(combine)
+    later_tokens = lax.optimization_barrier((tokens, *payloads))[0]
+    shared = shared_expert(later_tokens, shared_weights)
     routed_steps = []
     for s in range(step_count):
         received = lax.all_to_all(payloads[s], "ep", split_axis=0, concat_axis=0, tiled=True)
         expert_out = expert_rows(received, w_gate, w_up, w_down)
+        if s == 0:
+            expert_out, shared = lax.optimization_barrier((expert_out, shared))
         returned = lax.all_to_all(expert_out, "ep", split_axis=0, concat_axis=0, tiled=True)
         routed_steps.append(
             jnp.einsum(
@@ -168,8 +172,6 @@
                 precision=lax.Precision.HIGHEST,
             )
         )
-    later_tokens = lax.optimization_barrier((tokens, *payloads))[0]
-    shared = shared_expert(later_tokens, shared_weights)
     routed = jnp.stack(routed_steps)
     return (shared + routed).astype(jnp.bfloat16)
 

time: 183 us -> 194 us (1.060)
  waiting for transfers between devices: 81.1 us -> 97.3 us
  starting transfers between devices: 43.2 us -> 41.1 us
    all_to_all x2, waiting for transfers between devices: 13.3 us -> 25.5 us  [shards(): lax.all_to_all(expert_out, 'ep', split_axis=0, concat_axis=0, tiled=True)]
    ppermute x6, starting transfers between devices: 18.1 us -> 12.6 us  [partner_2(): return lax.ppermute(block, axis, route)]
    all_to_all x2, waiting for transfers between devices: 33.7 us -> 37.6 us  [shards(): lax.all_to_all(payloads[s], 'ep', split_axis=0, concat_axis=0, tiled=True)]
    all_to_all x2, starting transfers between devices: 9.7 us -> 13 us  [shards(): lax.all_to_all(expert_out, 'ep', split_axis=0, concat_axis=0, tiled=True)]
    add x2 -> x3, other arithmetic: 3.81 us -> 4.59 us  [shared_expert(): partial_value = keep + partner_2(send, 'ep', level)]
  transfers between devices with their start and end apart: 10 -> 10, of which waited for: 8 -> 8; matrix products, arithmetic and copies ran while one was open for 8% -> 3% of each run, Pallas kernels for 15% -> 14%
where the time goes in v8:
time: 194 us
  waiting for transfers between devices  97.3 us (50%)
  starting transfers between devices  41.1 us (21%)
  Pallas kernels  32.8 us (17%)
  local copies, waits for them, and re-layouts  9.42 us (5%)
  matrix products  6.74 us (3%)
  other arithmetic  5.93 us (3%)
    all_to_all x2, waiting for transfers between devices, shards(): lax.all_to_all(payloads[s], 'ep', split_axis=0, concat_axis=0, tiled=True)  37.6 us
    ppermute x6, waiting for transfers between devices, partner_2(): return lax.ppermute(block, axis, route)  34.2 us
    pallas_call x2, Pallas kernels, expert_rows(): pl.pallas_call(ffn_kernel, out_shape=jax.ShapeDtypeStruct(token_block.sha...  27.1 us
    all_to_all x2, waiting for transfers between devices, shards(): lax.all_to_all(expert_out, 'ep', split_axis=0, concat_axis=0, tiled=True)  25.5 us
    all_to_all x2, starting transfers between devices, shards(): lax.all_to_all(payloads[s], 'ep', split_axis=0, concat_axis=0, tiled=True)  15.6 us
    all_to_all x2, starting transfers between devices, shards(): lax.all_to_all(expert_out, 'ep', split_axis=0, concat_axis=0, tiled=True)  13 us
    ppermute x6, starting transfers between devices, partner_2(): return lax.ppermute(block, axis, route)  12.6 us
    pallas_call x2, Pallas kernels, dispatch_rows(): pl.pallas_call(dispatch_kernel, out_shape=jax.ShapeDtypeStruct((experts,...  5.68 us
  transfers between devices with their start and end apart: 10, of which 8 were waited for; matrix products, arithmetic and copies ran while one was open for 3% of the time, Pallas kernels for 14%

profile of v8, /device:TPU:1, one launch (start us, length us, event | category | flops | bytes accessed | tf_op | source)
XLA Modules:
  0.0 193.5 jit_solution(10811286211239137073)
XLA Ops:
  3.4 1.7 slice_bitcast_fusion
  5.1 2.9 %shard_map.75 = bf16[128,2,3584]{2,1,0:T(2,128)(2,1)} custom-call(bf16[256,16]{1,0:T(8,128)(2,1)} %copy.33.select_ref, bf16[16,3584]{1,0:T(8,128)(2,1)} %get-tuple-element.11.token_ref), custom_call_target="tpu_custom_call" | custom-call | tf_op jit(solution)/shard_map/pallas_call | solution.py:75
  7.9 2.8 %shard_map.73 = bf16[128,2,3584]{2,1,0:T(2,128)(2,1)} custom-call(bf16[256,16]{1,0:T(8,128)(2,1)} %copy.31.select_ref, bf16[16,3584]{1,0:T(8,128)(2,1)} %get-tuple-element.12.token_ref), custom_call_target="tpu_custom_call" | custom-call | tf_op jit(solution)/shard_map/pallas_call | solution.py:75
  10.8 3.7 %collective-permute-start = (bf16[2,16,3584]{2,1,0:T(8,128)(2,1)S(1)}, bf16[2,16,3584]{2,1,0:T(8,128)(2,1)S(1)}, u32[]{:S(2)}, u32[]{:S(2)}) collective-permute-start(bf16[2,16,3584]{2,1,0:T(8,128)(2,1)S(1)} %copy-done.4), channel_id=1, source_target_pairs={{0,4},{4,0},{1,5},{5,1},{2,6},{6,2},{3,7},{7,3},{8,12},{12,8},{9,1... | collective-permute-start | bytes 688136 | tf_op jit(solution)/shard_map/ppermute | solution.py:16
  14.5 5.0 %collective-permute-done = bf16[2,16,3584]{2,1,0:T(8,128)(2,1)S(1)} collective-permute-done((bf16[2,16,3584]{2,1,0:T(8,128)(2,1)S(1)}, bf16[2,16,3584]{2,1,0:T(8,128)(2,1)S(1)}, u32[]{:S(2)}, u32[]{:S(2)}) %collective-permute-start) | collective-permute-done | bytes 229408 | tf_op jit(solution)/shard_map/ppermute | solution.py:16
  19.6 1.4 collective-permute-start.1
  21.0 9.2 %collective-permute-done.1 = bf16[2,32,3584]{2,1,0:T(8,128)(2,1)S(1)} collective-permute-done((bf16[2,32,3584]{2,1,0:T(8,128)(2,1)S(1)}, bf16[2,32,3584]{2,1,0:T(8,128)(2,1)S(1)}, u32[]{:S(2)}, u32[]{:S(2)}) %collective-permute-start.1) | collective-permute-done | bytes 458784 | tf_op jit(solution)/shard_map/ppermute | solution.py:16
  30.3 2.5 %collective-permute-start.2 = (bf16[2,64,3584]{2,1,0:T(8,128)(2,1)S(1)}, bf16[2,64,3584]{2,1,0:T(8,128)(2,1)S(1)}, u32[]{:S(2)}, u32[]{:S(2)}) collective-permute-start(bf16[2,64,3584]{2,1,0:T(8,128)(2,1)S(1)} %maximum_select_fusion.1), channel_id=1, source_target_pairs={{0,1},{1,0},{2,3},{3,2},{4,5},{5,4},{6,7},{7,6},{8,9},{9,8},{10,11... | collective-permute-start | bytes 2752520 | tf_op jit(solution)/shard_map/ppermute | solution.py:16
  32.8 2.1 %collective-permute-done.2 = bf16[2,64,3584]{2,1,0:T(8,128)(2,1)S(1)} collective-permute-done((bf16[2,64,3584]{2,1,0:T(8,128)(2,1)S(1)}, bf16[2,64,3584]{2,1,0:T(8,128)(2,1)S(1)}, u32[]{:S(2)}, u32[]{:S(2)}) %collective-permute-start.2) | collective-permute-done | bytes 917536 | tf_op jit(solution)/shard_map/ppermute | solution.py:16
  37.2 1.5 constant_dynamic-slice_fusion.2
  39.9 10.2 %all-to-all-start.2 = ((bf16[128,2,3584]{2,1,0:T(2,128)(2,1)}), bf16[128,2,3584]{2,1,0:T(2,128)(2,1)S(1)}, u32[]{:S(2)}, u32[]{:S(2)}) async-start(bf16[128,2,3584]{2,1,0:T(2,128)(2,1)} %shard_map.75), calls=%async_computation.2 | async-start | bytes 3670016 | tf_op jit(solution)/shard_map/all_to_all | solution.py:162
  50.2 2.3 %dynamic-slice_add_fusion = f32[2,64,3584]{2,1,0:T(8,128)S(1)} fusion(f32[2,64,3584]{2,1,0:T(8,128)} %collective-permute-done.3, f32[2,128,3584]{2,1,0:T(8,128)} %copy-done, s32[]{:T(128)S(6)} %select_n.80), kind=kLoop, calls=%fused_computation.5 | loop fusion | flops 458752 | bytes 5505028 | tf_op jit(solution)/shard_map/add | solution.py:142
  53.7 1.4 collective-permute-start.4
  55.1 22.7 %all-to-all-done.2.x_ref = bf16[128,2,3584]{2,1,0:T(2,128)(2,1)S(1)} async-done(((bf16[128,2,3584]{2,1,0:T(2,128)(2,1)}), bf16[128,2,3584]{2,1,0:T(2,128)(2,1)S(1)}, u32[]{:S(2)}, u32[]{:S(2)}) %all-to-all-start.2) | async-done | bytes 1835040 | tf_op jit(solution)/shard_map/all_to_all | solution.py:162
  79.1 5.4 %all-to-all-start = ((bf16[128,2,3584]{2,1,0:T(2,128)(2,1)}), bf16[128,2,3584]{2,1,0:T(2,128)(2,1)}, u32[]{:S(2)}, u32[]{:S(2)}) async-start(bf16[128,2,3584]{2,1,0:T(2,128)(2,1)} %shard_map.73), calls=%async_computation | async-start | bytes 3670016 | tf_op jit(solution)/shard_map/all_to_all | solution.py:162
  84.5 13.6 %shard_map.76 = bf16[128,2,3584]{2,1,0:T(2,128)(2,1)} custom-call(bf16[128,2,3584]{2,1,0:T(2,128)(2,1)} %copy-done.1, bf16[1,3584,1024]{2,1,0:T(8,128)(2,1)} %gate_ref.3, bf16[1,3584,1024]{2,1,0:T(8,128)(2,1)} %up_ref.3, bf16[1,1024,3584]{2,1,0:T(8,128)(2,1)} %down_ref.3), custom_call_target="tpu_custom_call" | custom-call | flops 5637144576 | bytes 25690112 | tf_op jit(solution)/shard_map/pallas_call | solution.py:45
  100.6 14.9 %all-to-all-done.x_ref = bf16[128,2,3584]{2,1,0:T(2,128)(2,1)} async-done(((bf16[128,2,3584]{2,1,0:T(2,128)(2,1)}), bf16[128,2,3584]{2,1,0:T(2,128)(2,1)}, u32[]{:S(2)}, u32[]{:S(2)}) %all-to-all-start) | async-done | bytes 1835040 | tf_op jit(solution)/shard_map/all_to_all | solution.py:162
  115.5 5.2 %all-to-all-start.3 = ((bf16[128,2,3584]{2,1,0:T(2,128)(2,1)}), bf16[128,2,3584]{2,1,0:T(2,128)(2,1)S(1)}, u32[]{:S(2)}, u32[]{:S(2)}) async-start(bf16[128,2,3584]{2,1,0:T(2,128)(2,1)} %shard_map.76), calls=%async_computation.3 | async-start | bytes 3670016 | tf_op jit(solution)/shard_map/all_to_all | solution.py:166
  120.7 3.2 %collective-permute-start.5 = (f32[2,16,3584]{2,1,0:T(8,128)S(1)}, f32[2,16,3584]{2,1,0:T(8,128)}, u32[]{:S(2)}, u32[]{:S(2)}) collective-permute-start(f32[2,16,3584]{2,1,0:T(8,128)S(1)} %constant_dynamic-slice_fusion), channel_id=1, source_target_pairs={{0,4},{4,0},{1,5},{5,1},{2,6},{6,2},{3,7},{7,3},{8,12},{12,8},{9,1... | collective-permute-start | bytes 1376264 | tf_op jit(solution)/shard_map/ppermute | solution.py:16
  123.9 13.5 %shard_map.74 = bf16[128,2,3584]{2,1,0:T(2,128)(2,1)} custom-call(bf16[128,2,3584]{2,1,0:T(2,128)(2,1)} %all-to-all-done.x_ref, bf16[1,3584,1024]{2,1,0:T(8,128)(2,1)} %gate_ref.3, bf16[1,3584,1024]{2,1,0:T(8,128)(2,1)} %up_ref.3, bf16[1,1024,3584]{2,1,0:T(8,128)(2,1)} %down_ref.3), custom_call_target="tpu_custom_call" | custom-call | flops 5637144576 | bytes 25690112 | tf_op jit(solution)/shard_map/pallas_call | solution.py:45
  137.4 16.8 %collective-permute-done.5 = f32[2,16,3584]{2,1,0:T(8,128)} collective-permute-done((f32[2,16,3584]{2,1,0:T(8,128)S(1)}, f32[2,16,3584]{2,1,0:T(8,128)}, u32[]{:S(2)}, u32[]{:S(2)}) %collective-permute-start.5) | collective-permute-done | bytes 458784 | tf_op jit(solution)/shard_map/ppermute | solution.py:16
  155.2 7.7 %all-to-all-start.1 = ((bf16[128,2,3584]{2,1,0:T(2,128)(2,1)}), bf16[128,2,3584]{2,1,0:T(2,128)(2,1)}, u32[]{:S(2)}, u32[]{:S(2)}) async-start(bf16[128,2,3584]{2,1,0:T(2,128)(2,1)} %shard_map.74), calls=%async_computation.1 | async-start | bytes 3670016 | tf_op jit(solution)/shard_map/all_to_all | solution.py:166
  165.0 25.5 %all-to-all-done.1 = bf16[128,2,3584]{2,1,0:T(2,128)(2,1)} async-done(((bf16[128,2,3584]{2,1,0:T(2,128)(2,1)}), bf16[128,2,3584]{2,1,0:T(2,128)(2,1)}, u32[]{:S(2)}, u32[]{:S(2)}) %all-to-all-start.1) | async-done | bytes 1835040 | tf_op jit(solution)/shard_map/all_to_all | solution.py:166
  190.4 2.4 %convolution_bitcast_fusion.1 = f32[1,16,3584]{2,1,0:T(8,128)S(1)} fusion(bf16[128,2,3584]{2,1,0:T(2,128)(2,1)} %all-to-all-done.1, f32[16,128,2]{0,2,1:T(2,128)S(1)} %bitcast.31), kind=kOutput, calls=%fused_computation.1 | convolution fusion | flops 176160768 | bytes 2080768 | tf_op jit(solution)/shard_map/tec,ecd->td/dot_general | solution.py:168
  (50 shorter events, 15.9 us)
Async XLA Ops:
  5.1 5.7 %copy-start.4 = (bf16[2,16,3584]{2,1,0:T(8,128)(2,1)S(1)}, bf16[2,16,3584]{2,1,0:T(8,128)(2,1)}, u32[]{:S(2)}) copy-start(bf16[2,16,3584]{2,1,0:T(8,128)(2,1)} %param.7) | copy-start | bytes 688132
  10.8 8.8 %collective-permute-start = (bf16[2,16,3584]{2,1,0:T(8,128)(2,1)S(1)}, bf16[2,16,3584]{2,1,0:T(8,128)(2,1)S(1)}, u32[]{:S(2)}, u32[]{:S(2)}) collective-permute-start(bf16[2,16,3584]{2,1,0:T(8,128)(2,1)S(1)} %copy-done.4), channel_id=1, source_target_pairs={{0,4},{4,0},{1,5},{5,1},{2,6},{6,2},{3,7},{7,3},{8,12},{12,8},{9,1... | collective-permute-start | bytes 688136 | tf_op jit(solution)/shard_map/ppermute | solution.py:16
  19.6 10.6 %collective-permute-start.1 = (bf16[2,32,3584]{2,1,0:T(8,128)(2,1)S(1)}, bf16[2,32,3584]{2,1,0:T(8,128)(2,1)S(1)}, u32[]{:S(2)}, u32[]{:S(2)}) collective-permute-start(bf16[2,32,3584]{2,1,0:T(8,128)(2,1)S(1)} %maximum_select_fusion.2), channel_id=1, source_target_pairs={{0,2},{2,0},{1,3},{3,1},{4,6},{6,4},{5,7},{7,5},{8,10},{10,8},{9,1... | collective-permute-start | bytes 1376264 | tf_op jit(solution)/shard_map/ppermute | solution.py:16
  30.3 4.6 %collective-permute-start.2 = (bf16[2,64,3584]{2,1,0:T(8,128)(2,1)S(1)}, bf16[2,64,3584]{2,1,0:T(8,128)(2,1)S(1)}, u32[]{:S(2)}, u32[]{:S(2)}) collective-permute-start(bf16[2,64,3584]{2,1,0:T(8,128)(2,1)S(1)} %maximum_select_fusion.1), channel_id=1, source_target_pairs={{0,1},{1,0},{2,3},{3,2},{4,5},{5,4},{6,7},{7,6},{8,9},{9,8},{10,11... | collective-permute-start | bytes 2752520 | tf_op jit(solution)/shard_map/ppermute | solution.py:16
  32.8 2.5 %copy-start.5 = (bf16[3,3584,128]{2,1,0:T(8,128)(2,1)S(1)}, bf16[3,3584,128]{2,1,0:T(8,128)(2,1)}, u32[]{:S(2)}) copy-start(bf16[3,3584,128]{2,1,0:T(8,128)(2,1)} %param.13) | copy-start | bytes 8257540
  37.2 2.3 %copy-start = (f32[2,128,3584]{2,1,0:T(8,128)}, f32[2,128,3584]{2,1,0:T(8,128)S(1)}, u32[]{:S(2)}) copy-start(f32[2,128,3584]{2,1,0:T(8,128)S(1)} %fusion.4) | copy-start | bytes 11010052
  39.6 10.6 %collective-permute-start.3 = (f32[2,64,3584]{2,1,0:T(8,128)}, f32[2,64,3584]{2,1,0:T(8,128)}, u32[]{:S(2)}, u32[]{:S(2)}) collective-permute-start(f32[2,64,3584]{2,1,0:T(8,128)} %constant_dynamic-slice_fusion.2), channel_id=1, source_target_pairs={{0,1},{1,0},{2,3},{3,2},{4,5},{5,4},{6,7},{7,6},{8,9},{9,8},{10,11... | collective-permute-start | bytes 5505032 | tf_op jit(solution)/shard_map/ppermute | solution.py:16
  39.9 37.9 %all-to-all-start.2 = ((bf16[128,2,3584]{2,1,0:T(2,128)(2,1)}), bf16[128,2,3584]{2,1,0:T(2,128)(2,1)S(1)}, u32[]{:S(2)}, u32[]{:S(2)}) async-start(bf16[128,2,3584]{2,1,0:T(2,128)(2,1)} %shard_map.75), calls=%async_computation.2 | async-start | bytes 3670016 | tf_op jit(solution)/shard_map/all_to_all | solution.py:162
  52.4 1.3 copy-start.2
  53.7 45.5 %collective-permute-start.4 = (f32[2,32,3584]{2,1,0:T(8,128)S(1)}, f32[2,32,3584]{2,1,0:T(8,128)}, u32[]{:S(2)}, u32[]{:S(2)}) collective-permute-start(f32[2,32,3584]{2,1,0:T(8,128)S(1)} %constant_dynamic-slice_fusion.1), channel_id=1, source_target_pairs={{0,2},{2,0},{1,3},{3,1},{4,6},{6,4},{5,7},{7,5},{8,10},{10,8},{9,1... | collective-permute-start | bytes 2752520 | tf_op jit(solution)/shard_map/ppermute | solution.py:16
  77.9 1.3 copy-start.1
  79.1 36.3 %all-to-all-start = ((bf16[128,2,3584]{2,1,0:T(2,128)(2,1)}), bf16[128,2,3584]{2,1,0:T(2,128)(2,1)}, u32[]{:S(2)}, u32[]{:S(2)}) async-start(bf16[128,2,3584]{2,1,0:T(2,128)(2,1)} %shard_map.73), calls=%async_computation | async-start | bytes 3670016 | tf_op jit(solution)/shard_map/all_to_all | solution.py:162
  84.5 14.8 %copy-start.3 = (f32[2,64,3584]{2,1,0:T(8,128)S(1)}, f32[2,64,3584]{2,1,0:T(8,128)}, u32[]{:S(2)}) copy-start(f32[2,64,3584]{2,1,0:T(8,128)} %copy-done.2) | copy-start | bytes 5505028
  115.5 39.8 %all-to-all-start.3 = ((bf16[128,2,3584]{2,1,0:T(2,128)(2,1)}), bf16[128,2,3584]{2,1,0:T(2,128)(2,1)S(1)}, u32[]{:S(2)}, u32[]{:S(2)}) async-start(bf16[128,2,3584]{2,1,0:T(2,128)(2,1)} %shard_map.76), calls=%async_computation.3 | async-start | bytes 3670016 | tf_op jit(solution)/shard_map/all_to_all | solution.py:166
  120.7 33.4 %collective-permute-start.5 = (f32[2,16,3584]{2,1,0:T(8,128)S(1)}, f32[2,16,3584]{2,1,0:T(8,128)}, u32[]{:S(2)}, u32[]{:S(2)}) collective-permute-start(f32[2,16,3584]{2,1,0:T(8,128)S(1)} %constant_dynamic-slice_fusion), channel_id=1, source_target_pairs={{0,4},{4,0},{1,5},{5,1},{2,6},{6,2},{3,7},{7,3},{8,12},{12,8},{9,1... | collective-permute-start | bytes 1376264 | tf_op jit(solution)/shard_map/ppermute | solution.py:16
  155.2 7.8 %copy-start.6 = (f32[2,16,8]{1,2,0:T(8,128)S(1)}, f32[2,16,8]{1,2,0:T(8,128)}, u32[]{:S(2)}) copy-start(f32[2,16,8]{1,2,0:T(8,128)} %param.9) | copy-start | bytes 3076
  155.2 35.2 %all-to-all-start.1 = ((bf16[128,2,3584]{2,1,0:T(2,128)(2,1)}), bf16[128,2,3584]{2,1,0:T(2,128)(2,1)}, u32[]{:S(2)}, u32[]{:S(2)}) async-start(bf16[128,2,3584]{2,1,0:T(2,128)(2,1)} %shard_map.74), calls=%async_computation.1 | async-start | bytes 3670016 | tf_op jit(solution)/shard_map/all_to_all | solution.py:166

commit v9 on v7

--- a/solution.py
+++ b/solution.py
@@ -119,7 +119,16 @@
     )
 
 
-def shared_expert(tokens, shared_weights):
+def ring_shift(block, direction, ring):
+    count = lax.axis_size("ep")
+    route = []
+    for low in range(count):
+        place = low // 2 % ring
+        route.append((low, low + ((place + direction) % ring - place) * 2))
+    return lax.ppermute(block, "ep", route)
+
+
+def shared_expert(tokens, shared_weights, ring=4):
     my_index = lax.axis_index("ep")
     step_count, row_count, model_width = tokens.shape
     gathered = tokens
@@ -134,13 +143,26 @@
         hidden, shared_weights[2], (((1,), (1,)), ((), ())), preferred_element_type=jnp.float32
     )
     partial_value = partial_value.reshape(step_count, 8 * row_count, model_width)
-    for level in (0, 1, 2):
-        half = partial_value.shape[1] // 2
-        bit = my_index >> level & 1
-        keep = lax.dynamic_slice_in_dim(partial_value, bit * half, half, 1)
-        send = lax.dynamic_slice_in_dim(partial_value, (1 - bit) * half, half, 1)
-        partial_value = keep + partner_2(send, "ep", level)
-    return partial_value
+    half = partial_value.shape[1] // 2
+    bit = my_index & 1
+    keep = lax.dynamic_slice_in_dim(partial_value, bit * half, half, 1)
+    send = lax.dynamic_slice_in_dim(partial_value, (1 - bit) * half, half, 1)
+    partial_value = keep + partner_2(send, "ep", 0)
+    chunks = partial_value.reshape(step_count, ring, row_count, model_width)
+    place = my_index // 2 % ring
+
+    def chunk(s, target):
+        slot = target % 2 * 2 + target // 2
+        return lax.dynamic_index_in_dim(chunks[s], slot, 0, keepdims=False)
+
+    results = []
+    for s, direction in ((0, 1), (1, -1)):
+        total = chunk(s, (place - direction) % ring)
+        for k in range(ring - 1):
+            arrived = ring_shift(total, direction, ring)
+            total = arrived + chunk(s, (place - direction * (k + 2)) % ring)
+        results.append(total)
+    return jnp.stack(results)
 
 
 def shards(tokens, expert_ids, combine_weights, w_gate, w_up, w_down, shared_weights):

time: 183 us -> 180 us (0.984); the launches traced: 183 us -> 178 us
  waiting for transfers between devices: 81.1 us -> 68.9 us
  matrix products: 8.12 us -> 13.1 us
  local copies, waits for them, and re-layouts: 9.71 us -> 12.9 us
    ppermute x6 -> x4, waiting for transfers between devices: 34.1 us -> 7.27 us  [partner_2(): return lax.ppermute(block, axis, route)]
    all_to_all x2, waiting for transfers between devices: 13.3 us -> 29 us  [shards(): lax.all_to_all(expert_out, 'ep', split_axis=0, concat_axis=0, tiled=True)]
    ppermute x6 -> x4, starting transfers between devices: 18.1 us -> 7.51 us  [partner_2(): return lax.ppermute(block, axis, route)]
    all_to_all x2, waiting for transfers between devices: 33.7 us -> 24.4 us  [shards(): lax.all_to_all(payloads[s], 'ep', split_axis=0, concat_axis=0, tiled=True)]
    ppermute x0 -> x6, starting transfers between devices: none -> 8.44 us  [ring_shift(): return lax.ppermute(block, 'ep', route)]
    ppermute x0 -> x6, waiting for transfers between devices: none -> 8.3 us  [ring_shift(): return lax.ppermute(block, 'ep', route)]
    unnamed x14 -> x20, local copies, waits for them, and re-layouts: 3.55 us -> 4.42 us
    add x2 -> x5, other arithmetic: 3.81 us -> 4.02 us  [the longest x1 2.95 us: shared_expert(): partial_value = keep + partner_2(send, 'ep', 0)]
  transfers between devices with their start and end apart: 10 -> 14, of which waited for: 8 -> 8; matrix products, arithmetic and copies ran while one was open for 8% -> 13% of each run, Pallas kernels for 15% -> 15%
where the time goes in v9:
time: 180 us; the launch traced here: 178 us
  waiting for transfers between devices  68.9 us (38%)
  starting transfers between devices  41.5 us (23%)
  Pallas kernels  32.8 us (18%)
  matrix products  13.1 us (7%)
  local copies, waits for them, and re-layouts  12.9 us (7%)
  other arithmetic  8.19 us (5%)
    all_to_all x2, waiting for transfers between devices, shards(): lax.all_to_all(expert_out, 'ep', split_axis=0, concat_axis=0, tiled=True)  29 us
    pallas_call x2, Pallas kernels, expert_rows(): pl.pallas_call(ffn_kernel, out_shape=jax.ShapeDtypeStruct(token_block.sha...  27.1 us
    all_to_all x2, waiting for transfers between devices, shards(): lax.all_to_all(payloads[s], 'ep', split_axis=0, concat_axis=0, tiled=True)  24.4 us
    all_to_all x2, starting transfers between devices, shards(): lax.all_to_all(payloads[s], 'ep', split_axis=0, concat_axis=0, tiled=True)  15.9 us
    all_to_all x2, starting transfers between devices, shards(): lax.all_to_all(expert_out, 'ep', split_axis=0, concat_axis=0, tiled=True)  9.69 us
    ppermute x6, starting transfers between devices, ring_shift(): return lax.ppermute(block, 'ep', route)  8.44 us
    ppermute x6, waiting for transfers between devices, ring_shift(): return lax.ppermute(block, 'ep', route)  8.3 us
    ppermute x4, starting transfers between devices, partner_2(): return lax.ppermute(block, axis, route)  7.51 us
  transfers between devices with their start and end apart: 14, of which 8 were waited for; matrix products, arithmetic and copies ran while one was open for 13% of the time, Pallas kernels for 15%

profile of v9, /device:TPU:1, one launch (start us, length us, event | category | flops | bytes accessed | tf_op | source)
XLA Modules:
  0.0 177.6 jit_solution(15876474585349645218)
XLA Ops:
  5.1 2.8 %shard_map.74 = bf16[128,2,3584]{2,1,0:T(2,128)(2,1)} custom-call(bf16[256,16]{1,0:T(8,128)(2,1)} %copy.33.select_ref, bf16[16,3584]{1,0:T(8,128)(2,1)} %get-tuple-element.9.token_ref), custom_call_target="tpu_custom_call" | custom-call | tf_op jit(solution)/shard_map/pallas_call | solution.py:75
  7.9 2.8 %shard_map.73 = bf16[128,2,3584]{2,1,0:T(2,128)(2,1)} custom-call(bf16[256,16]{1,0:T(8,128)(2,1)} %copy.31.select_ref, bf16[16,3584]{1,0:T(8,128)(2,1)} %get-tuple-element.10.token_ref), custom_call_target="tpu_custom_call" | custom-call | tf_op jit(solution)/shard_map/pallas_call | solution.py:75
  10.7 3.7 %collective-permute-start = (bf16[2,16,3584]{2,1,0:T(8,128)(2,1)S(1)}, bf16[2,16,3584]{2,1,0:T(8,128)(2,1)S(1)}, u32[]{:S(2)}, u32[]{:S(2)}) collective-permute-start(bf16[2,16,3584]{2,1,0:T(8,128)(2,1)S(1)} %copy-done.7), channel_id=1, source_target_pairs={{0,4},{4,0},{1,5},{5,1},{2,6},{6,2},{3,7},{7,3},{8,12},{12,8},{9,1... | collective-permute-start | bytes 688136 | tf_op jit(solution)/shard_map/ppermute | solution.py:16
  14.4 5.0 %collective-permute-done = bf16[2,16,3584]{2,1,0:T(8,128)(2,1)S(1)} collective-permute-done((bf16[2,16,3584]{2,1,0:T(8,128)(2,1)S(1)}, bf16[2,16,3584]{2,1,0:T(8,128)(2,1)S(1)}, u32[]{:S(2)}, u32[]{:S(2)}) %collective-permute-start) | collective-permute-done | bytes 229408 | tf_op jit(solution)/shard_map/ppermute | solution.py:16
  21.0 11.5 %all-to-all-start.2 = ((bf16[128,2,3584]{2,1,0:T(2,128)(2,1)}), bf16[128,2,3584]{2,1,0:T(2,128)(2,1)S(1)}, u32[]{:S(2)}, u32[]{:S(2)}) async-start(bf16[128,2,3584]{2,1,0:T(2,128)(2,1)} %shard_map.74), calls=%async_computation.2 | async-start | bytes 3670016 | tf_op jit(solution)/shard_map/all_to_all | solution.py:182
  35.0 2.2 %collective-permute-done.2 = bf16[2,64,3584]{2,1,0:T(8,128)(2,1)} collective-permute-done((bf16[2,64,3584]{2,1,0:T(8,128)(2,1)S(1)}, bf16[2,64,3584]{2,1,0:T(8,128)(2,1)}, u32[]{:S(2)}, u32[]{:S(2)}) %collective-permute-start.2) | collective-permute-done | bytes 917536 | tf_op jit(solution)/shard_map/ppermute | solution.py:16
  37.2 1.9 %maximum_select_fusion = bf16[2,128,3584]{2,1,0:T(8,128)(2,1)S(1)} fusion(bf16[2,64,3584]{2,1,0:T(8,128)(2,1)S(1)} %maximum_select_fusion.1, bf16[2,64,3584]{2,1,0:T(8,128)(2,1)} %collective-permute-done.2, pred[]{:T(512)S(6)} %eq.113), kind=kLoop, calls=%fused_computation.2 | loop fusion | flops 8257536 | bytes 3670017 | tf_op jit(solution)/shard_map/jit(_where)/select_n | solution.py:115
  42.2 18.0 %all-to-all-done.2.x_ref = bf16[128,2,3584]{2,1,0:T(2,128)(2,1)S(1)} async-done(((bf16[128,2,3584]{2,1,0:T(2,128)(2,1)}), bf16[128,2,3584]{2,1,0:T(2,128)(2,1)S(1)}, u32[]{:S(2)}, u32[]{:S(2)}) %all-to-all-start.2) | async-done | bytes 1835040 | tf_op jit(solution)/shard_map/all_to_all | solution.py:182
  61.4 4.3 %all-to-all-start = ((bf16[128,2,3584]{2,1,0:T(2,128)(2,1)}), bf16[128,2,3584]{2,1,0:T(2,128)(2,1)S(1)}, u32[]{:S(2)}, u32[]{:S(2)}) async-start(bf16[128,2,3584]{2,1,0:T(2,128)(2,1)} %shard_map.73), calls=%async_computation | async-start | bytes 3670016 | tf_op jit(solution)/shard_map/all_to_all | solution.py:182
  65.8 2.4 %multiply_convert_fusion = bf16[256,128]{1,0:T(8,128)(2,1)S(1)} fusion(f32[256,128]{1,0:T(8,128)S(1)} %fusion.8, bf16[256,3584]{1,0:T(8,128)(2,1)} %bitcast.64, bf16[3,3584,128]{2,1,0:T(8,128)(2,1)} %param.13), kind=kOutput, calls=%fused_computation.37 | convolution fusion | flops 235077632 | bytes 2949120 | tf_op jit(solution)/shard_map/dot_general | solution.py:140
  73.7 13.6 %shard_map.76 = bf16[128,2,3584]{2,1,0:T(2,128)(2,1)} custom-call(bf16[128,2,3584]{2,1,0:T(2,128)(2,1)} %copy-done.3, bf16[1,3584,1024]{2,1,0:T(8,128)(2,1)} %gate_ref.3, bf16[1,3584,1024]{2,1,0:T(8,128)(2,1)} %up_ref.3, bf16[1,1024,3584]{2,1,0:T(8,128)(2,1)} %down_ref.3), custom_call_target="tpu_custom_call" | custom-call | flops 5637144576 | bytes 25690112 | tf_op jit(solution)/shard_map/pallas_call | solution.py:45
  87.3 6.3 %all-to-all-done.x_ref = bf16[128,2,3584]{2,1,0:T(2,128)(2,1)S(1)} async-done(((bf16[128,2,3584]{2,1,0:T(2,128)(2,1)}), bf16[128,2,3584]{2,1,0:T(2,128)(2,1)S(1)}, u32[]{:S(2)}, u32[]{:S(2)}) %all-to-all-start) | async-done | bytes 1835040 | tf_op jit(solution)/shard_map/all_to_all | solution.py:182
  94.8 5.4 %all-to-all-start.3 = ((bf16[128,2,3584]{2,1,0:T(2,128)(2,1)}), bf16[128,2,3584]{2,1,0:T(2,128)(2,1)}, u32[]{:S(2)}, u32[]{:S(2)}) async-start(bf16[128,2,3584]{2,1,0:T(2,128)(2,1)} %shard_map.76), calls=%async_computation.3 | async-start | bytes 3670016 | tf_op jit(solution)/shard_map/all_to_all | solution.py:184
  102.4 13.6 %shard_map.75 = bf16[128,2,3584]{2,1,0:T(2,128)(2,1)} custom-call(bf16[128,2,3584]{2,1,0:T(2,128)(2,1)} %copy-done.2, bf16[1,3584,1024]{2,1,0:T(8,128)(2,1)} %gate_ref.3, bf16[1,3584,1024]{2,1,0:T(8,128)(2,1)} %up_ref.3, bf16[1,1024,3584]{2,1,0:T(8,128)(2,1)} %down_ref.3), custom_call_target="tpu_custom_call" | custom-call | flops 5637144576 | bytes 25690112 | tf_op jit(solution)/shard_map/pallas_call | solution.py:45
  116.0 3.0 %dynamic-slice_add_fusion = f32[2,64,3584]{2,1,0:T(8,128)} fusion(f32[2,64,3584]{2,1,0:T(8,128)} %collective-permute-done.3, f32[2,128,3584]{2,1,0:T(8,128)S(1)} %copy-done.1, s32[]{:T(128)S(6)} %select_n.192), kind=kLoop, calls=%fused_computation.5 | loop fusion | flops 458752 | bytes 5505028 | tf_op jit(solution)/shard_map/add | solution.py:150
  119.0 8.8 %all-to-all-done.3 = bf16[128,2,3584]{2,1,0:T(2,128)(2,1)} async-done(((bf16[128,2,3584]{2,1,0:T(2,128)(2,1)}), bf16[128,2,3584]{2,1,0:T(2,128)(2,1)}, u32[]{:S(2)}, u32[]{:S(2)}) %all-to-all-start.3) | async-done | bytes 1835040 | tf_op jit(solution)/shard_map/all_to_all | solution.py:184
  127.8 4.3 %all-to-all-start.1 = ((bf16[128,2,3584]{2,1,0:T(2,128)(2,1)}), bf16[128,2,3584]{2,1,0:T(2,128)(2,1)S(1)}, u32[]{:S(2)}, u32[]{:S(2)}) async-start(bf16[128,2,3584]{2,1,0:T(2,128)(2,1)} %shard_map.75), calls=%async_computation.1 | async-start | bytes 3670016 | tf_op jit(solution)/shard_map/all_to_all | solution.py:184
  137.4 2.4 %convolution_bitcast_fusion = f32[1,16,3584]{2,1,0:T(8,128)S(1)} fusion(bf16[128,2,3584]{2,1,0:T(2,128)(2,1)} %all-to-all-done.3, f32[16,128,2]{0,2,1:T(2,128)S(1)} %bitcast.65), kind=kOutput, calls=%fused_computation | convolution fusion | flops 176160768 | bytes 2080768 | tf_op jit(solution)/shard_map/tec,ecd->td/dot_general | solution.py:186
  139.8 20.2 %all-to-all-done.1 = bf16[128,2,3584]{2,1,0:T(2,128)(2,1)S(1)} async-done(((bf16[128,2,3584]{2,1,0:T(2,128)(2,1)}), bf16[128,2,3584]{2,1,0:T(2,128)(2,1)S(1)}, u32[]{:S(2)}, u32[]{:S(2)}) %all-to-all-start.1) | async-done | bytes 1835040 | tf_op jit(solution)/shard_map/all_to_all | solution.py:184
  160.0 1.9 %convolution_bitcast_fusion.1 = f32[1,16,3584]{2,1,0:T(8,128)S(1)} fusion(bf16[128,2,3584]{2,1,0:T(2,128)(2,1)S(1)} %all-to-all-done.1, f32[16,128,2]{0,2,1:T(2,128)} %bitcast.66), kind=kOutput, calls=%fused_computation.1 | convolution fusion | flops 176160768 | bytes 2080768 | tf_op jit(solution)/shard_map/tec,ecd->td/dot_general | solution.py:186
  162.9 2.7 %collective-permute-start.8 = (f32[16,3584]{1,0:T(8,128)S(1)}, f32[16,3584]{1,0:T(8,128)S(1)}, u32[]{:S(2)}, u32[]{:S(2)}) collective-permute-start(f32[16,3584]{1,0:T(8,128)S(1)} %bitcast_add_fusion.2), channel_id=1, source_target_pairs={{0,6},{1,7},{2,0},{3,1},{4,2},{5,3},{6,4},{7,5},{8,14},{9,15},{10,... | collective-permute-start | bytes 688136 | tf_op jit(solution)/shard_map/ppermute | solution.py:128
  165.7 4.6 %collective-permute-done.5 = f32[16,3584]{1,0:T(8,128)S(1)} collective-permute-done((f32[16,3584]{1,0:T(8,128)S(1)}, f32[16,3584]{1,0:T(8,128)S(1)}, u32[]{:S(2)}, u32[]{:S(2)}) %collective-permute-start.5) | collective-permute-done | bytes 229408 | tf_op jit(solution)/shard_map/ppermute | solution.py:128
  170.4 2.7 %collective-permute-start.9 = (f32[16,3584]{1,0:T(8,128)S(1)}, f32[16,3584]{1,0:T(8,128)S(1)}, u32[]{:S(2)}, u32[]{:S(2)}) collective-permute-start(f32[16,3584]{1,0:T(8,128)S(1)} %bitcast_add_fusion.1), channel_id=1, source_target_pairs={{0,6},{1,7},{2,0},{3,1},{4,2},{5,3},{6,4},{7,5},{8,14},{9,15},{10,... | collective-permute-start | bytes 688136 | tf_op jit(solution)/shard_map/ppermute | solution.py:128
  173.1 3.7 %collective-permute-done.6 = f32[16,3584]{1,0:T(8,128)S(1)} collective-permute-done((f32[16,3584]{1,0:T(8,128)S(1)}, f32[16,3584]{1,0:T(8,128)S(1)}, u32[]{:S(2)}, u32[]{:S(2)}) %collective-permute-start.6) | collective-permute-done | bytes 229408 | tf_op jit(solution)/shard_map/ppermute | solution.py:128
  (69 shorter events, 29.5 us)
Async XLA Ops:
  5.0 5.6 %copy-start.7 = (bf16[2,16,3584]{2,1,0:T(8,128)(2,1)S(1)}, bf16[2,16,3584]{2,1,0:T(8,128)(2,1)}, u32[]{:S(2)}) copy-start(bf16[2,16,3584]{2,1,0:T(8,128)(2,1)} %param.7) | copy-start | bytes 688132
  10.7 8.8 %collective-permute-start = (bf16[2,16,3584]{2,1,0:T(8,128)(2,1)S(1)}, bf16[2,16,3584]{2,1,0:T(8,128)(2,1)S(1)}, u32[]{:S(2)}, u32[]{:S(2)}) collective-permute-start(bf16[2,16,3584]{2,1,0:T(8,128)(2,1)S(1)} %copy-done.7), channel_id=1, source_target_pairs={{0,4},{4,0},{1,5},{5,1},{2,6},{6,2},{3,7},{7,3},{8,12},{12,8},{9,1... | collective-permute-start | bytes 688136 | tf_op jit(solution)/shard_map/ppermute | solution.py:16
  19.6 12.9 %collective-permute-start.1 = (bf16[2,32,3584]{2,1,0:T(8,128)(2,1)S(1)}, bf16[2,32,3584]{2,1,0:T(8,128)(2,1)}, u32[]{:S(2)}, u32[]{:S(2)}) collective-permute-start(bf16[2,32,3584]{2,1,0:T(8,128)(2,1)S(1)} %maximum_select_fusion.2), channel_id=1, source_target_pairs={{0,2},{2,0},{1,3},{3,1},{4,6},{6,4},{5,7},{7,5},{8,10},{10,8},{9,1... | collective-permute-start | bytes 1376264 | tf_op jit(solution)/shard_map/ppermute | solution.py:16
  21.0 39.2 %all-to-all-start.2 = ((bf16[128,2,3584]{2,1,0:T(2,128)(2,1)}), bf16[128,2,3584]{2,1,0:T(2,128)(2,1)S(1)}, u32[]{:S(2)}, u32[]{:S(2)}) async-start(bf16[128,2,3584]{2,1,0:T(2,128)(2,1)} %shard_map.74), calls=%async_computation.2 | async-start | bytes 3670016 | tf_op jit(solution)/shard_map/all_to_all | solution.py:182
  33.9 3.4 %collective-permute-start.2 = (bf16[2,64,3584]{2,1,0:T(8,128)(2,1)S(1)}, bf16[2,64,3584]{2,1,0:T(8,128)(2,1)}, u32[]{:S(2)}, u32[]{:S(2)}) collective-permute-start(bf16[2,64,3584]{2,1,0:T(8,128)(2,1)S(1)} %maximum_select_fusion.1), channel_id=1, source_target_pairs={{0,1},{1,0},{2,3},{3,2},{4,5},{5,4},{6,7},{7,6},{8,9},{9,8},{10,11... | collective-permute-start | bytes 2752520 | tf_op jit(solution)/shard_map/ppermute | solution.py:16
  39.2 1.2 copy-start.6
  60.2 1.2 copy-start.3
  61.4 32.2 %all-to-all-start = ((bf16[128,2,3584]{2,1,0:T(2,128)(2,1)}), bf16[128,2,3584]{2,1,0:T(2,128)(2,1)S(1)}, u32[]{:S(2)}, u32[]{:S(2)}) async-start(bf16[128,2,3584]{2,1,0:T(2,128)(2,1)} %shard_map.73), calls=%async_computation | async-start | bytes 3670016 | tf_op jit(solution)/shard_map/all_to_all | solution.py:182
  70.0 2.4 %copy-start = (f32[2,128,3584]{2,1,0:T(8,128)}, f32[2,128,3584]{2,1,0:T(8,128)S(1)}, u32[]{:S(2)}) copy-start(f32[2,128,3584]{2,1,0:T(8,128)S(1)} %fusion.4) | copy-start | bytes 11010052
  70.0 3.6 %copy-start.9 = (f32[2,16,8]{1,2,0:T(8,128)S(1)}, f32[2,16,8]{1,2,0:T(8,128)}, u32[]{:S(2)}) copy-start(f32[2,16,8]{1,2,0:T(8,128)} %param.9) | copy-start | bytes 3076
  72.3 43.7 %collective-permute-start.3 = (f32[2,64,3584]{2,1,0:T(8,128)}, f32[2,64,3584]{2,1,0:T(8,128)}, u32[]{:S(2)}, u32[]{:S(2)}) collective-permute-start(f32[2,64,3584]{2,1,0:T(8,128)} %constant_dynamic-slice_fusion), channel_id=1, source_target_pairs={{0,1},{1,0},{2,3},{3,2},{4,5},{5,4},{6,7},{7,6},{8,9},{9,8},{10,11... | collective-permute-start | bytes 5505032 | tf_op jit(solution)/shard_map/ppermute | solution.py:16
  93.6 1.2 copy-start.2
  94.8 32.9 %all-to-all-start.3 = ((bf16[128,2,3584]{2,1,0:T(2,128)(2,1)}), bf16[128,2,3584]{2,1,0:T(2,128)(2,1)}, u32[]{:S(2)}, u32[]{:S(2)}) async-start(bf16[128,2,3584]{2,1,0:T(2,128)(2,1)} %shard_map.76), calls=%async_computation.3 | async-start | bytes 3670016 | tf_op jit(solution)/shard_map/all_to_all | solution.py:184
  102.4 13.6 %copy-start.1 = (f32[2,128,3584]{2,1,0:T(8,128)S(1)}, f32[2,128,3584]{2,1,0:T(8,128)}, u32[]{:S(2)}) copy-start(f32[2,128,3584]{2,1,0:T(8,128)} %copy-done) | copy-start | bytes 11010052
  127.8 32.2 %all-to-all-start.1 = ((bf16[128,2,3584]{2,1,0:T(2,128)(2,1)}), bf16[128,2,3584]{2,1,0:T(2,128)(2,1)S(1)}, u32[]{:S(2)}, u32[]{:S(2)}) async-start(bf16[128,2,3584]{2,1,0:T(2,128)(2,1)} %shard_map.75), calls=%async_computation.1 | async-start | bytes 3670016 | tf_op jit(solution)/shard_map/all_to_all | solution.py:184
  132.1 5.3 %copy-start.8 = (f32[16,256]{0,1:T(8,128)S(1)}, f32[16,256]{0,1:T(8,128)}, u32[]{:S(2)}) copy-start(f32[16,256]{0,1:T(8,128)} %fusion.18) | copy-start | bytes 49156
  133.7 3.6 %copy-start.4 = (f32[1,64,3584]{2,1,0:T(8,128)}, f32[1,64,3584]{2,1,0:T(8,128)S(1)}, u32[]{:S(2)}) copy-start(f32[1,64,3584]{2,1,0:T(8,128)S(1)} %get-tuple-element.7) | copy-start | bytes 2752516
  134.5 27.3 %collective-permute-start.4 = (f32[16,3584]{1,0:T(8,128)}, f32[16,3584]{1,0:T(8,128)}, u32[]{:S(2)}, u32[]{:S(2)}) collective-permute-start(f32[16,3584]{1,0:T(8,128)} %dynamic-slice_bitcast_fusion.1), channel_id=1, source_target_pairs={{0,2},{1,3},{2,4},{3,5},{4,6},{5,7},{6,0},{7,1},{8,10},{9,11},{10,... | collective-permute-start | bytes 688136 | tf_op jit(solution)/shard_map/ppermute | solution.py:128
  136.0 26.9 %collective-permute-start.7 = (f32[16,3584]{1,0:T(8,128)S(1)}, f32[16,3584]{1,0:T(8,128)S(1)}, u32[]{:S(2)}, u32[]{:S(2)}) collective-permute-start(f32[16,3584]{1,0:T(8,128)S(1)} %dynamic-slice_bitcast_fusion), channel_id=1, source_target_pairs={{0,6},{1,7},{2,0},{3,1},{4,2},{5,3},{6,4},{7,5},{8,14},{9,15},{10,... | collective-permute-start | bytes 688136 | tf_op jit(solution)/shard_map/ppermute | solution.py:128
  160.0 1.9 %copy-start.5 = (f32[1,64,3584]{2,1,0:T(8,128)S(1)}, f32[1,64,3584]{2,1,0:T(8,128)}, u32[]{:S(2)}) copy-start(f32[1,64,3584]{2,1,0:T(8,128)} %copy-done.4) | copy-start | bytes 2752516
  162.8 7.5 %collective-permute-start.5 = (f32[16,3584]{1,0:T(8,128)S(1)}, f32[16,3584]{1,0:T(8,128)S(1)}, u32[]{:S(2)}, u32[]{:S(2)}) collective-permute-start(f32[16,3584]{1,0:T(8,128)S(1)} %bitcast_add_fusion.5), channel_id=1, source_target_pairs={{0,2},{1,3},{2,4},{3,5},{4,6},{5,7},{6,0},{7,1},{8,10},{9,11},{10,... | collective-permute-start | bytes 688136 | tf_op jit(solution)/shard_map/ppermute | solution.py:128
  162.9 7.4 %collective-permute-start.8 = (f32[16,3584]{1,0:T(8,128)S(1)}, f32[16,3584]{1,0:T(8,128)S(1)}, u32[]{:S(2)}, u32[]{:S(2)}) collective-permute-start(f32[16,3584]{1,0:T(8,128)S(1)} %bitcast_add_fusion.2), channel_id=1, source_target_pairs={{0,6},{1,7},{2,0},{3,1},{4,2},{5,3},{6,4},{7,5},{8,14},{9,15},{10,... | collective-permute-start | bytes 688136 | tf_op jit(solution)/shard_map/ppermute | solution.py:128
  170.3 6.5 %collective-permute-start.6 = (f32[16,3584]{1,0:T(8,128)S(1)}, f32[16,3584]{1,0:T(8,128)S(1)}, u32[]{:S(2)}, u32[]{:S(2)}) collective-permute-start(f32[16,3584]{1,0:T(8,128)S(1)} %bitcast_add_fusion.4), channel_id=1, source_target_pairs={{0,2},{1,3},{2,4},{3,5},{4,6},{5,7},{6,0},{7,1},{8,10},{9,11},{10,... | collective-permute-start | bytes 688136 | tf_op jit(solution)/shard_map/ppermute | solution.py:128
  170.4 6.4 %collective-permute-start.9 = (f32[16,3584]{1,0:T(8,128)S(1)}, f32[16,3584]{1,0:T(8,128)S(1)}, u32[]{:S(2)}, u32[]{:S(2)}) collective-permute-start(f32[16,3584]{1,0:T(8,128)S(1)} %bitcast_add_fusion.1), channel_id=1, source_target_pairs={{0,6},{1,7},{2,0},{3,1},{4,2},{5,3},{6,4},{7,5},{8,14},{9,15},{10,... | collective-permute-start | bytes 688136 | tf_op jit(solution)/shard_map/ppermute | solution.py:128

commit v10 on v9

--- a/solution.py
+++ b/solution.py
@@ -177,9 +177,13 @@
         dispatch, combine = route_tables(expert_ids[s], combine_weights[s], experts, capacity)
         payloads.append(dispatch_rows(dispatch, tokens[s], experts, capacity))
         combines.append(combine)
+    later_tokens = lax.optimization_barrier((tokens, *payloads))[0]
+    shared = shared_expert(later_tokens, shared_weights)
     routed_steps = []
     for s in range(step_count):
         received = lax.all_to_all(payloads[s], "ep", split_axis=0, concat_axis=0, tiled=True)
+        if s == step_count - 1:
+            received, shared = lax.optimization_barrier((received, shared))
         expert_out = expert_rows(received, w_gate, w_up, w_down)
         returned = lax.all_to_all(expert_out, "ep", split_axis=0, concat_axis=0, tiled=True)
         routed_steps.append(
@@ -190,8 +194,6 @@
                 precision=lax.Precision.HIGHEST,
             )
         )
-    later_tokens = lax.optimization_barrier((tokens, *payloads))[0]
-    shared = shared_expert(later_tokens, shared_weights)
     routed = jnp.stack(routed_steps)
     return (shared + routed).astype(jnp.bfloat16)
 

time: 180 us -> 194 us (1.078)
  waiting for transfers between devices: 68.9 us -> 92.5 us
  matrix products: 13.1 us -> 6.74 us
  starting transfers between devices: 41.5 us -> 47.2 us
  local copies, waits for them, and re-layouts: 12.9 us -> 8.52 us
  other arithmetic: 8.19 us -> 4.95 us
    all_to_all x2, waiting for transfers between devices: 29 us -> 39.7 us  [shards(): lax.all_to_all(expert_out, 'ep', split_axis=0, concat_axis=0, tiled=True)]
    ppermute x6, waiting for transfers between devices: 8.3 us -> 18.7 us  [ring_shift(): return lax.ppermute(block, 'ep', route)]
    ppermute x4, waiting for transfers between devices: 7.27 us -> 14.2 us  [partner_2(): return lax.ppermute(block, axis, route)]
    all_to_all x2, starting transfers between devices: 9.69 us -> 14.4 us  [shards(): lax.all_to_all(expert_out, 'ep', split_axis=0, concat_axis=0, tiled=True)]
    all_to_all x2, waiting for transfers between devices: 24.4 us -> 20 us  [shards(): lax.all_to_all(payloads[s], 'ep', split_axis=0, concat_axis=0, tiled=True)]
    unnamed x20 -> x12, local copies, waits for them, and re-layouts: 4.42 us -> 2.32 us
  transfers between devices with their start and end apart: 14 -> 14, of which waited for: 8 -> 8; matrix products, arithmetic and copies ran while one was open for 13% -> 5% of each run, Pallas kernels for 15% -> 14%
where the time goes in v10:
time: 194 us; the launch traced here: 193 us
  waiting for transfers between devices  92.5 us (48%)
  starting transfers between devices  47.2 us (24%)
  Pallas kernels  32.8 us (17%)
  local copies, waits for them, and re-layouts  8.52 us (4%)
  matrix products  6.74 us (3%)
  other arithmetic  4.95 us (3%)
    all_to_all x2, waiting for transfers between devices, shards(): lax.all_to_all(expert_out, 'ep', split_axis=0, concat_axis=0, tiled=True)  39.7 us
    pallas_call x2, Pallas kernels, expert_rows(): pl.pallas_call(ffn_kernel, out_shape=jax.ShapeDtypeStruct(token_block.sha...  27.1 us
    all_to_all x2, waiting for transfers between devices, shards(): lax.all_to_all(payloads[s], 'ep', split_axis=0, concat_axis=0, tiled=True)  20 us
    ppermute x6, waiting for transfers between devices, ring_shift(): return lax.ppermute(block, 'ep', route)  18.7 us
    all_to_all x2, starting transfers between devices, shards(): lax.all_to_all(payloads[s], 'ep', split_axis=0, concat_axis=0, tiled=True)  15.5 us
    all_to_all x2, starting transfers between devices, shards(): lax.all_to_all(expert_out, 'ep', split_axis=0, concat_axis=0, tiled=True)  14.4 us
    ppermute x4, waiting for transfers between devices, partner_2(): return lax.ppermute(block, axis, route)  14.2 us
    ppermute x4, starting transfers between devices, partner_2(): return lax.ppermute(block, axis, route)  8.76 us
  transfers between devices with their start and end apart: 14, of which 8 were waited for; matrix products, arithmetic and copies ran while one was open for 5% of the time, Pallas kernels for 14%

profile of v10, /device:TPU:1, one launch (start us, length us, event | category | flops | bytes accessed | tf_op | source)
XLA Modules:
  0.0 192.9 jit_solution(2962635372708903970)
XLA Ops:
  3.4 1.7 slice_bitcast_fusion
  5.1 2.8 %shard_map.74 = bf16[128,2,3584]{2,1,0:T(2,128)(2,1)} custom-call(bf16[256,16]{1,0:T(8,128)(2,1)} %copy.33.select_ref, bf16[16,3584]{1,0:T(8,128)(2,1)} %get-tuple-element.13.token_ref), custom_call_target="tpu_custom_call" | custom-call | tf_op jit(solution)/shard_map/pallas_call | solution.py:75
  7.9 2.8 %shard_map.73 = bf16[128,2,3584]{2,1,0:T(2,128)(2,1)} custom-call(bf16[256,16]{1,0:T(8,128)(2,1)} %copy.31.select_ref, bf16[16,3584]{1,0:T(8,128)(2,1)} %get-tuple-element.14.token_ref), custom_call_target="tpu_custom_call" | custom-call | tf_op jit(solution)/shard_map/pallas_call | solution.py:75
  10.7 3.7 %collective-permute-start = (bf16[2,16,3584]{2,1,0:T(8,128)(2,1)S(1)}, bf16[2,16,3584]{2,1,0:T(8,128)(2,1)S(1)}, u32[]{:S(2)}, u32[]{:S(2)}) collective-permute-start(bf16[2,16,3584]{2,1,0:T(8,128)(2,1)S(1)} %copy-done.3), channel_id=1, source_target_pairs={{0,4},{4,0},{1,5},{5,1},{2,6},{6,2},{3,7},{7,3},{8,12},{12,8},{9,1... | collective-permute-start | bytes 688136 | tf_op jit(solution)/shard_map/ppermute | solution.py:16
  14.5 5.0 %collective-permute-done = bf16[2,16,3584]{2,1,0:T(8,128)(2,1)S(1)} collective-permute-done((bf16[2,16,3584]{2,1,0:T(8,128)(2,1)S(1)}, bf16[2,16,3584]{2,1,0:T(8,128)(2,1)S(1)}, u32[]{:S(2)}, u32[]{:S(2)}) %collective-permute-start) | collective-permute-done | bytes 229408 | tf_op jit(solution)/shard_map/ppermute | solution.py:16
  21.0 9.1 %collective-permute-done.1 = bf16[2,32,3584]{2,1,0:T(8,128)(2,1)S(1)} collective-permute-done((bf16[2,32,3584]{2,1,0:T(8,128)(2,1)S(1)}, bf16[2,32,3584]{2,1,0:T(8,128)(2,1)S(1)}, u32[]{:S(2)}, u32[]{:S(2)}) %collective-permute-start.1) | collective-permute-done | bytes 458784 | tf_op jit(solution)/shard_map/ppermute | solution.py:16
  30.3 2.5 %collective-permute-start.2 = (bf16[2,64,3584]{2,1,0:T(8,128)(2,1)S(1)}, bf16[2,64,3584]{2,1,0:T(8,128)(2,1)}, u32[]{:S(2)}, u32[]{:S(2)}) collective-permute-start(bf16[2,64,3584]{2,1,0:T(8,128)(2,1)S(1)} %maximum_select_fusion.1), channel_id=1, source_target_pairs={{0,1},{1,0},{2,3},{3,2},{4,5},{5,4},{6,7},{7,6},{8,9},{9,8},{10,11... | collective-permute-start | bytes 2752520 | tf_op jit(solution)/shard_map/ppermute | solution.py:16
  32.8 10.2 %all-to-all-start.1 = ((bf16[128,2,3584]{2,1,0:T(2,128)(2,1)}), bf16[128,2,3584]{2,1,0:T(2,128)(2,1)S(1)}, u32[]{:S(2)}, u32[]{:S(2)}) async-start(bf16[128,2,3584]{2,1,0:T(2,128)(2,1)} %shard_map.74), calls=%async_computation.1 | async-start | bytes 3670016 | tf_op jit(solution)/shard_map/all_to_all | solution.py:184
  43.0 2.0 %maximum_select_fusion = bf16[2,128,3584]{2,1,0:T(8,128)(2,1)S(1)} fusion(bf16[2,64,3584]{2,1,0:T(8,128)(2,1)S(1)} %maximum_select_fusion.1, bf16[2,64,3584]{2,1,0:T(8,128)(2,1)} %collective-permute-done.2, pred[]{:T(512)S(6)} %eq.121), kind=kLoop, calls=%fused_computation.2 | loop fusion | flops 8257536 | bytes 3670017 | tf_op jit(solution)/shard_map/jit(_where)/select_n | solution.py:115
  50.7 20.0 %all-to-all-done.1.x_ref = bf16[128,2,3584]{2,1,0:T(2,128)(2,1)S(1)} async-done(((bf16[128,2,3584]{2,1,0:T(2,128)(2,1)}), bf16[128,2,3584]{2,1,0:T(2,128)(2,1)S(1)}, u32[]{:S(2)}, u32[]{:S(2)}) %all-to-all-start.1) | async-done | bytes 1835040 | tf_op jit(solution)/shard_map/all_to_all | solution.py:184
  71.9 5.3 %all-to-all-start = ((bf16[128,2,3584]{2,1,0:T(2,128)(2,1)}), bf16[128,2,3584]{2,1,0:T(2,128)(2,1)}, u32[]{:S(2)}, u32[]{:S(2)}) async-start(bf16[128,2,3584]{2,1,0:T(2,128)(2,1)} %shard_map.73), calls=%async_computation | async-start | bytes 3670016 | tf_op jit(solution)/shard_map/all_to_all | solution.py:184
  77.3 13.6 %shard_map.75 = bf16[128,2,3584]{2,1,0:T(2,128)(2,1)} custom-call(bf16[128,2,3584]{2,1,0:T(2,128)(2,1)} %copy-done.2, bf16[1,3584,1024]{2,1,0:T(8,128)(2,1)} %gate_ref.3, bf16[1,3584,1024]{2,1,0:T(8,128)(2,1)} %up_ref.3, bf16[1,1024,3584]{2,1,0:T(8,128)(2,1)} %down_ref.3), custom_call_target="tpu_custom_call" | custom-call | flops 5637144576 | bytes 25690112 | tf_op jit(solution)/shard_map/pallas_call | solution.py:45
  90.9 1.7 dynamic-slice_add_fusion
  95.7 9.6 %collective-permute-done.4 = f32[16,3584]{1,0:T(8,128)S(1)} collective-permute-done((f32[16,3584]{1,0:T(8,128)S(1)}, f32[16,3584]{1,0:T(8,128)S(1)}, u32[]{:S(2)}, u32[]{:S(2)}) %collective-permute-start.4) | collective-permute-done | bytes 229408 | tf_op jit(solution)/shard_map/ppermute | solution.py:128
  105.5 2.7 %collective-permute-start.8 = (f32[16,3584]{1,0:T(8,128)S(1)}, f32[16,3584]{1,0:T(8,128)S(1)}, u32[]{:S(2)}, u32[]{:S(2)}) collective-permute-start(f32[16,3584]{1,0:T(8,128)S(1)} %bitcast_add_fusion.2), channel_id=1, source_target_pairs={{0,6},{1,7},{2,0},{3,1},{4,2},{5,3},{6,4},{7,5},{8,14},{9,15},{10,... | collective-permute-start | bytes 688136 | tf_op jit(solution)/shard_map/ppermute | solution.py:128
  108.2 5.0 %collective-permute-done.5 = f32[16,3584]{1,0:T(8,128)S(1)} collective-permute-done((f32[16,3584]{1,0:T(8,128)S(1)}, f32[16,3584]{1,0:T(8,128)S(1)}, u32[]{:S(2)}, u32[]{:S(2)}) %collective-permute-start.5) | collective-permute-done | bytes 229408 | tf_op jit(solution)/shard_map/ppermute | solution.py:128
  113.4 2.7 %collective-permute-start.9 = (f32[16,3584]{1,0:T(8,128)S(1)}, f32[16,3584]{1,0:T(8,128)S(1)}, u32[]{:S(2)}, u32[]{:S(2)}) collective-permute-start(f32[16,3584]{1,0:T(8,128)S(1)} %bitcast_add_fusion.1), channel_id=1, source_target_pairs={{0,6},{1,7},{2,0},{3,1},{4,2},{5,3},{6,4},{7,5},{8,14},{9,15},{10,... | collective-permute-start | bytes 688136 | tf_op jit(solution)/shard_map/ppermute | solution.py:128
  116.1 4.0 %collective-permute-done.6 = f32[16,3584]{1,0:T(8,128)S(1)} collective-permute-done((f32[16,3584]{1,0:T(8,128)S(1)}, f32[16,3584]{1,0:T(8,128)S(1)}, u32[]{:S(2)}, u32[]{:S(2)}) %collective-permute-start.6) | collective-permute-done | bytes 229408 | tf_op jit(solution)/shard_map/ppermute | solution.py:128
  120.2 9.0 %all-to-all-start.2 = ((bf16[128,2,3584]{2,1,0:T(2,128)(2,1)}), bf16[128,2,3584]{2,1,0:T(2,128)(2,1)S(1)}, u32[]{:S(2)}, u32[]{:S(2)}) async-start(bf16[128,2,3584]{2,1,0:T(2,128)(2,1)} %shard_map.75), calls=%async_computation.2 | async-start | bytes 3670016 | tf_op jit(solution)/shard_map/all_to_all | solution.py:188
  129.3 13.5 %shard_map.76 = bf16[128,2,3584]{2,1,0:T(2,128)(2,1)} custom-call(bf16[128,2,3584]{2,1,0:T(2,128)(2,1)} %all-to-all-done.x_ref, bf16[1,3584,1024]{2,1,0:T(8,128)(2,1)} %gate_ref.3, bf16[1,3584,1024]{2,1,0:T(8,128)(2,1)} %up_ref.3, bf16[1,1024,3584]{2,1,0:T(8,128)(2,1)} %down_ref.3), custom_call_target="tpu_custom_call" | custom-call | flops 5637144576 | bytes 25690112 | tf_op jit(solution)/shard_map/pallas_call | solution.py:45
  142.8 14.1 %all-to-all-done.2 = bf16[128,2,3584]{2,1,0:T(2,128)(2,1)S(1)} async-done(((bf16[128,2,3584]{2,1,0:T(2,128)(2,1)}), bf16[128,2,3584]{2,1,0:T(2,128)(2,1)S(1)}, u32[]{:S(2)}, u32[]{:S(2)}) %all-to-all-start.2) | async-done | bytes 1835040 | tf_op jit(solution)/shard_map/all_to_all | solution.py:188
  156.9 5.3 %all-to-all-start.3 = ((bf16[128,2,3584]{2,1,0:T(2,128)(2,1)}), bf16[128,2,3584]{2,1,0:T(2,128)(2,1)}, u32[]{:S(2)}, u32[]{:S(2)}) async-start(bf16[128,2,3584]{2,1,0:T(2,128)(2,1)} %shard_map.76), calls=%async_computation.3 | async-start | bytes 3670016 | tf_op jit(solution)/shard_map/all_to_all | solution.py:188
  164.2 25.6 %all-to-all-done.3 = bf16[128,2,3584]{2,1,0:T(2,128)(2,1)} async-done(((bf16[128,2,3584]{2,1,0:T(2,128)(2,1)}), bf16[128,2,3584]{2,1,0:T(2,128)(2,1)}, u32[]{:S(2)}, u32[]{:S(2)}) %all-to-all-start.3) | async-done | bytes 1835040 | tf_op jit(solution)/shard_map/all_to_all | solution.py:188
  189.8 2.4 %convolution_bitcast_fusion = f32[1,16,3584]{2,1,0:T(8,128)S(1)} fusion(bf16[128,2,3584]{2,1,0:T(2,128)(2,1)} %all-to-all-done.3, f32[16,128,2]{0,2,1:T(2,128)S(1)} %bitcast.65), kind=kOutput, calls=%fused_computation | convolution fusion | flops 176160768 | bytes 2080768 | tf_op jit(solution)/shard_map/tec,ecd->td/dot_general | solution.py:190
  (62 shorter events, 18.1 us)
Async XLA Ops:
  5.1 5.7 %copy-start.3 = (bf16[2,16,3584]{2,1,0:T(8,128)(2,1)S(1)}, bf16[2,16,3584]{2,1,0:T(8,128)(2,1)}, u32[]{:S(2)}) copy-start(bf16[2,16,3584]{2,1,0:T(8,128)(2,1)} %param.7) | copy-start | bytes 688132
  10.7 8.8 %collective-permute-start = (bf16[2,16,3584]{2,1,0:T(8,128)(2,1)S(1)}, bf16[2,16,3584]{2,1,0:T(8,128)(2,1)S(1)}, u32[]{:S(2)}, u32[]{:S(2)}) collective-permute-start(bf16[2,16,3584]{2,1,0:T(8,128)(2,1)S(1)} %copy-done.3), channel_id=1, source_target_pairs={{0,4},{4,0},{1,5},{5,1},{2,6},{6,2},{3,7},{7,3},{8,12},{12,8},{9,1... | collective-permute-start | bytes 688136 | tf_op jit(solution)/shard_map/ppermute | solution.py:16
  19.6 10.6 %collective-permute-start.1 = (bf16[2,32,3584]{2,1,0:T(8,128)(2,1)S(1)}, bf16[2,32,3584]{2,1,0:T(8,128)(2,1)S(1)}, u32[]{:S(2)}, u32[]{:S(2)}) collective-permute-start(bf16[2,32,3584]{2,1,0:T(8,128)(2,1)S(1)} %maximum_select_fusion.2), channel_id=1, source_target_pairs={{0,2},{2,0},{1,3},{3,1},{4,6},{6,4},{5,7},{7,5},{8,10},{10,8},{9,1... | collective-permute-start | bytes 1376264 | tf_op jit(solution)/shard_map/ppermute | solution.py:16
  30.3 12.7 %collective-permute-start.2 = (bf16[2,64,3584]{2,1,0:T(8,128)(2,1)S(1)}, bf16[2,64,3584]{2,1,0:T(8,128)(2,1)}, u32[]{:S(2)}, u32[]{:S(2)}) collective-permute-start(bf16[2,64,3584]{2,1,0:T(8,128)(2,1)S(1)} %maximum_select_fusion.1), channel_id=1, source_target_pairs={{0,1},{1,0},{2,3},{3,2},{4,5},{5,4},{6,7},{7,6},{8,9},{9,8},{10,11... | collective-permute-start | bytes 2752520 | tf_op jit(solution)/shard_map/ppermute | solution.py:16
  32.8 37.9 %all-to-all-start.1 = ((bf16[128,2,3584]{2,1,0:T(2,128)(2,1)}), bf16[128,2,3584]{2,1,0:T(2,128)(2,1)S(1)}, u32[]{:S(2)}, u32[]{:S(2)}) async-start(bf16[128,2,3584]{2,1,0:T(2,128)(2,1)} %shard_map.74), calls=%async_computation.1 | async-start | bytes 3670016 | tf_op jit(solution)/shard_map/all_to_all | solution.py:184
  43.0 2.3 %copy-start.4 = (bf16[3,3584,128]{2,1,0:T(8,128)(2,1)S(1)}, bf16[3,3584,128]{2,1,0:T(8,128)(2,1)}, u32[]{:S(2)}) copy-start(bf16[3,3584,128]{2,1,0:T(8,128)(2,1)} %param.13) | copy-start | bytes 8257540
  47.2 2.4 %copy-start = (f32[2,128,3584]{2,1,0:T(8,128)}, f32[2,128,3584]{2,1,0:T(8,128)S(1)}, u32[]{:S(2)}) copy-start(f32[2,128,3584]{2,1,0:T(8,128)S(1)} %fusion.4) | copy-start | bytes 11010052
  49.6 41.3 %collective-permute-start.3 = (f32[2,64,3584]{2,1,0:T(8,128)}, f32[2,64,3584]{2,1,0:T(8,128)}, u32[]{:S(2)}, u32[]{:S(2)}) collective-permute-start(f32[2,64,3584]{2,1,0:T(8,128)} %constant_dynamic-slice_fusion), channel_id=1, source_target_pairs={{0,1},{1,0},{2,3},{3,2},{4,5},{5,4},{6,7},{7,6},{8,9},{9,8},{10,11... | collective-permute-start | bytes 5505032 | tf_op jit(solution)/shard_map/ppermute | solution.py:16
  70.7 1.2 copy-start.2
  71.9 48.2 %all-to-all-start = ((bf16[128,2,3584]{2,1,0:T(2,128)(2,1)}), bf16[128,2,3584]{2,1,0:T(2,128)(2,1)}, u32[]{:S(2)}, u32[]{:S(2)}) async-start(bf16[128,2,3584]{2,1,0:T(2,128)(2,1)} %shard_map.73), calls=%async_computation | async-start | bytes 3670016 | tf_op jit(solution)/shard_map/all_to_all | solution.py:184
  77.3 13.6 %copy-start.1 = (f32[2,128,3584]{2,1,0:T(8,128)S(1)}, f32[2,128,3584]{2,1,0:T(8,128)}, u32[]{:S(2)}) copy-start(f32[2,128,3584]{2,1,0:T(8,128)} %copy-done) | copy-start | bytes 11010052
  92.7 12.6 %collective-permute-start.4 = (f32[16,3584]{1,0:T(8,128)S(1)}, f32[16,3584]{1,0:T(8,128)S(1)}, u32[]{:S(2)}, u32[]{:S(2)}) collective-permute-start(f32[16,3584]{1,0:T(8,128)S(1)} %dynamic-slice_bitcast_fusion.1), channel_id=1, source_target_pairs={{0,2},{1,3},{2,4},{3,5},{4,6},{5,7},{6,0},{7,1},{8,10},{9,11},{10,... | collective-permute-start | bytes 688136 | tf_op jit(solution)/shard_map/ppermute | solution.py:128
  94.3 11.2 %collective-permute-start.7 = (f32[16,3584]{1,0:T(8,128)S(1)}, f32[16,3584]{1,0:T(8,128)S(1)}, u32[]{:S(2)}, u32[]{:S(2)}) collective-permute-start(f32[16,3584]{1,0:T(8,128)S(1)} %dynamic-slice_bitcast_fusion), channel_id=1, source_target_pairs={{0,6},{1,7},{2,0},{3,1},{4,2},{5,3},{6,4},{7,5},{8,14},{9,15},{10,... | collective-permute-start | bytes 688136 | tf_op jit(solution)/shard_map/ppermute | solution.py:128
  105.4 7.8 %collective-permute-start.5 = (f32[16,3584]{1,0:T(8,128)S(1)}, f32[16,3584]{1,0:T(8,128)S(1)}, u32[]{:S(2)}, u32[]{:S(2)}) collective-permute-start(f32[16,3584]{1,0:T(8,128)S(1)} %bitcast_add_fusion.5), channel_id=1, source_target_pairs={{0,2},{1,3},{2,4},{3,5},{4,6},{5,7},{6,0},{7,1},{8,10},{9,11},{10,... | collective-permute-start | bytes 688136 | tf_op jit(solution)/shard_map/ppermute | solution.py:128
  105.5 7.8 %collective-permute-start.8 = (f32[16,3584]{1,0:T(8,128)S(1)}, f32[16,3584]{1,0:T(8,128)S(1)}, u32[]{:S(2)}, u32[]{:S(2)}) collective-permute-start(f32[16,3584]{1,0:T(8,128)S(1)} %bitcast_add_fusion.2), channel_id=1, source_target_pairs={{0,6},{1,7},{2,0},{3,1},{4,2},{5,3},{6,4},{7,5},{8,14},{9,15},{10,... | collective-permute-start | bytes 688136 | tf_op jit(solution)/shard_map/ppermute | solution.py:128
  113.2 6.9 %collective-permute-start.6 = (f32[16,3584]{1,0:T(8,128)S(1)}, f32[16,3584]{1,0:T(8,128)S(1)}, u32[]{:S(2)}, u32[]{:S(2)}) collective-permute-start(f32[16,3584]{1,0:T(8,128)S(1)} %bitcast_add_fusion.4), channel_id=1, source_target_pairs={{0,2},{1,3},{2,4},{3,5},{4,6},{5,7},{6,0},{7,1},{8,10},{9,11},{10,... | collective-permute-start | bytes 688136 | tf_op jit(solution)/shard_map/ppermute | solution.py:128
  113.4 15.8 %collective-permute-start.9 = (f32[16,3584]{1,0:T(8,128)S(1)}, f32[16,3584]{1,0:T(8,128)S(1)}, u32[]{:S(2)}, u32[]{:S(2)}) collective-permute-start(f32[16,3584]{1,0:T(8,128)S(1)} %bitcast_add_fusion.1), channel_id=1, source_target_pairs={{0,6},{1,7},{2,0},{3,1},{4,2},{5,3},{6,4},{7,5},{8,14},{9,15},{10,... | collective-permute-start | bytes 688136 | tf_op jit(solution)/shard_map/ppermute | solution.py:128
  120.2 36.7 %all-to-all-start.2 = ((bf16[128,2,3584]{2,1,0:T(2,128)(2,1)}), bf16[128,2,3584]{2,1,0:T(2,128)(2,1)S(1)}, u32[]{:S(2)}, u32[]{:S(2)}) async-start(bf16[128,2,3584]{2,1,0:T(2,128)(2,1)} %shard_map.75), calls=%async_computation.2 | async-start | bytes 3670016 | tf_op jit(solution)/shard_map/all_to_all | solution.py:188
  142.8 19.4 %copy-start.5 = (f32[2,16,8]{1,2,0:T(8,128)S(1)}, f32[2,16,8]{1,2,0:T(8,128)}, u32[]{:S(2)}) copy-start(f32[2,16,8]{1,2,0:T(8,128)} %param.9) | copy-start | bytes 3076
  156.9 32.9 %all-to-all-start.3 = ((bf16[128,2,3584]{2,1,0:T(2,128)(2,1)}), bf16[128,2,3584]{2,1,0:T(2,128)(2,1)}, u32[]{:S(2)}, u32[]{:S(2)}) async-start(bf16[128,2,3584]{2,1,0:T(2,128)(2,1)} %shard_map.76), calls=%async_computation.3 | async-start | bytes 3670016 | tf_op jit(solution)/shard_map/all_to_all | solution.py:188

commit v11 on v6

--- a/solution.py
+++ b/solution.py
@@ -101,11 +101,12 @@
     )
 
 
-def shared_expert(tokens, shared_weights):
+def shared_expert(tokens, shared_weights, after):
     step_count, row_count, model_width = tokens.shape
     count = lax.axis_size("ep")
     groups = [list(range(g, g + 8)) for g in range(0, count, 8)]
     gathered = lax.all_gather(tokens, "ep", axis=1, tiled=True, axis_index_groups=groups)
+    gathered = lax.optimization_barrier((gathered, after))[0]
     flat_rows = gathered.reshape(-1, model_width)
     gate_val = jnp.dot(flat_rows, shared_weights[0], preferred_element_type=jnp.float32)
     up_val = jnp.dot(flat_rows, shared_weights[1], preferred_element_type=jnp.float32)
@@ -139,8 +140,10 @@
         )
         combines.append(combine)
     routed_steps = []
+    arrived = []
     for s in range(step_count):
         received = lax.all_to_all(payloads[s], "ep", split_axis=0, concat_axis=0, tiled=True)
+        arrived.append(received)
         expert_out = expert_rows(received, w_gate, w_up, w_down)
         returned = lax.all_to_all(expert_out, "ep", split_axis=0, concat_axis=0, tiled=True)
         routed_steps.append(
@@ -151,7 +154,7 @@
                 precision=lax.Precision.HIGHEST,
             )
         )
-    shared = shared_expert(tokens, shared_weights)
+    shared = shared_expert(tokens, shared_weights, arrived[0])
     routed = jnp.stack(routed_steps)
     return (shared + routed).astype(jnp.bfloat16)
 

time: 182 us -> 178 us (0.978)
  blocking collectives: 0 us -> 42.2 us
  waiting for transfers between devices: 84.7 us -> 54.2 us
  starting transfers between devices: 30.5 us -> 18.4 us
    all_to_all x0 -> x1, blocking collectives: none -> 42.2 us  [shards(): lax.all_to_all(payloads[s], 'ep', split_axis=0, concat_axis=0, tiled=True)]
    all_gather x1, waiting for transfers between devices: 29.8 us -> 0.56 us  [shared_expert(): lax.all_gather(tokens, 'ep', axis=1, tiled=True, axis_index_groups=groups)]
    all_to_all x2 -> x1, starting transfers between devices: 20 us -> 8.44 us  [shards(): lax.all_to_all(payloads[s], 'ep', split_axis=0, concat_axis=0, tiled=True)]
    all_to_all x2 -> x1, waiting for transfers between devices: 14.5 us -> 14.8 us  [shards(): lax.all_to_all(payloads[s], 'ep', split_axis=0, concat_axis=0, tiled=True)]
  transfers between devices with their start and end apart: 6 -> 5, of which waited for: 4 -> 4; matrix products, arithmetic and copies ran while one was open for 12% -> 8% of each run, Pallas kernels for 15% -> 15%
where the time goes in v11:
time: 178 us
  waiting for transfers between devices  54.2 us (30%)
  blocking collectives  42.2 us (24%)
  Pallas kernels  27.3 us (15%)
  starting transfers between devices  18.4 us (10%)
  between operations  13.5 us (8%)
  matrix products  12.3 us (7%)
  local copies, waits for them, and re-layouts  8.08 us (5%)
    all_to_all x1, blocking collectives, shards(): lax.all_to_all(payloads[s], 'ep', split_axis=0, concat_axis=0, tiled=True)  42.2 us
    all_to_all x2, waiting for transfers between devices, shards(): lax.all_to_all(expert_out, 'ep', split_axis=0, concat_axis=0, tiled=True)  38.1 us
    pallas_call x2, Pallas kernels, expert_rows(): pl.pallas_call(ffn_kernel, out_shape=jax.ShapeDtypeStruct(token_block.sha...  27.3 us
    all_to_all x1, waiting for transfers between devices, shards(): lax.all_to_all(payloads[s], 'ep', split_axis=0, concat_axis=0, tiled=True)  14.8 us
    all_to_all x2, starting transfers between devices, shards(): lax.all_to_all(expert_out, 'ep', split_axis=0, concat_axis=0, tiled=True)  9.91 us
    all_to_all x1, starting transfers between devices, shards(): lax.all_to_all(payloads[s], 'ep', split_axis=0, concat_axis=0, tiled=True)  8.44 us
    dot_general x2, local copies, waits for them, and re-layouts, shards(): jnp.einsum('ect,td->ecd', dispatch.reshape(experts, capacity, row_count),...  5.07 us
  transfers between devices with their start and end apart: 5, of which 4 were waited for; matrix products, arithmetic and copies ran while one was open for 8% of the time, Pallas kernels for 15%

profile of v11, /device:TPU:1, one launch (start us, length us, event | category | flops | bytes accessed | tf_op | source)
XLA Modules:
  0.0 177.8 jit_solution(2650057966697001970)
XLA Ops:
  6.5 0.7 all-gather.2.cloned.1.call-update
  7.3 0.7 fusion.45
  8.8 1.5 fusion.20
  10.3 1.9 %copy.51 = bf16[128,2,3584]{2,1,0:T(2,128)(2,1)S(1)} copy(bf16[128,2,3584]{2,0,1:T(8,128)(2,1)S(1)} %fusion.20) | data formatting | bytes 3670016 | tf_op jit(solution)/shard_map/ect,td->ecd/dot_general | solution.py:134
  12.2 42.2 %all_to_all.20.x_ref = bf16[128,2,3584]{2,1,0:T(2,128)(2,1)} all-to-all(bf16[128,2,3584]{2,1,0:T(2,128)(2,1)S(1)} %copy.51), channel_id=1, replica_groups=mesh['ep'=128] {'ep'}, dimensions={0} | all-to-all | bytes 3670016 | tf_op jit(solution)/shard_map/all_to_all | solution.py:145
  54.4 0.6 all-gather.2.cloned.1.call-done
  55.0 2.3 %fusion.8 = f32[256,128]{1,0:T(8,128)S(1)} fusion(bf16[256,3584]{1,0:T(8,128)(2,1)} %bitcast.38, bf16[3,3584,128]{2,1,0:T(8,128)(2,1)S(1)} %copy-done.2), kind=kOutput, calls=%fused_computation.17 | convolution fusion | flops 234881024 | bytes 2883584 | tf_op jit(solution)/shard_map/dot_general | solution.py:111
  57.2 0.6 fusion.2
  57.9 2.4 %fusion.5 = f32[2,128,3584]{2,1,0:T(8,128)} fusion(bf16[2,128,128]{2,1,0:T(8,128)(2,1)S(1)} %bitcast.37, bf16[3,3584,128]{2,1,0:T(8,128)(2,1)S(1)} %copy-done.2), kind=kOutput, calls=%fused_computation.14 | convolution fusion | flops 234881024 | bytes 4653056 | tf_op jit(solution)/shard_map/dot_general | solution.py:114
  61.3 0.6 fusion.18
  61.9 3.2 %copy.50 = bf16[128,2,3584]{2,1,0:T(2,128)(2,1)} copy(bf16[128,2,3584]{2,0,1:T(8,128)(2,1)S(1)} %fusion.18) | data formatting | bytes 3670016 | tf_op jit(solution)/shard_map/ect,td->ecd/dot_general | solution.py:134
  65.0 8.4 %all-to-all-start.2 = ((bf16[128,2,3584]{2,1,0:T(2,128)(2,1)}), bf16[128,2,3584]{2,1,0:T(2,128)(2,1)S(1)}, u32[]{:S(2)}, u32[]{:S(2)}) async-start(bf16[128,2,3584]{2,1,0:T(2,128)(2,1)} %copy.50), calls=%async_computation.3 | async-start | bytes 3670016 | tf_op jit(solution)/shard_map/all_to_all | solution.py:145
  73.5 13.7 %shard_map.73 = bf16[128,2,3584]{2,1,0:T(2,128)(2,1)} custom-call(bf16[128,2,3584]{2,1,0:T(2,128)(2,1)} %all_to_all.20.x_ref, bf16[1,3584,1024]{2,1,0:T(8,128)(2,1)} %gate_ref.3, bf16[1,3584,1024]{2,1,0:T(8,128)(2,1)} %up_ref.3, bf16[1,1024,3584]{2,1,0:T(8,128)(2,1)} %down_ref.3), custom_call_target="tpu_custom_call" | custom-call | flops 5637144576 | bytes 25690112 | tf_op jit(solution)/shard_map/pallas_call | solution.py:45
  87.2 14.8 %all-to-all-done.2.x_ref = bf16[128,2,3584]{2,1,0:T(2,128)(2,1)S(1)} async-done(((bf16[128,2,3584]{2,1,0:T(2,128)(2,1)}), bf16[128,2,3584]{2,1,0:T(2,128)(2,1)S(1)}, u32[]{:S(2)}, u32[]{:S(2)}) %all-to-all-start.2) | async-done | bytes 1835040 | tf_op jit(solution)/shard_map/all_to_all | solution.py:145
  102.0 1.2 copy-done
  103.2 5.5 %all-to-all-start.1 = ((bf16[128,2,3584]{2,1,0:T(2,128)(2,1)}), bf16[128,2,3584]{2,1,0:T(2,128)(2,1)}, u32[]{:S(2)}, u32[]{:S(2)}) async-start(bf16[128,2,3584]{2,1,0:T(2,128)(2,1)} %shard_map.73), calls=%async_computation.2 | async-start | bytes 3670016 | tf_op jit(solution)/shard_map/all_to_all | solution.py:148
  108.7 13.6 %shard_map.74 = bf16[128,2,3584]{2,1,0:T(2,128)(2,1)} custom-call(bf16[128,2,3584]{2,1,0:T(2,128)(2,1)} %copy-done, bf16[1,3584,1024]{2,1,0:T(8,128)(2,1)} %gate_ref.3, bf16[1,3584,1024]{2,1,0:T(8,128)(2,1)} %up_ref.3, bf16[1,1024,3584]{2,1,0:T(8,128)(2,1)} %down_ref.3), custom_call_target="tpu_custom_call" | custom-call | flops 5637144576 | bytes 25690112 | tf_op jit(solution)/shard_map/pallas_call | solution.py:45
  122.3 13.8 %all-to-all-done.1 = bf16[128,2,3584]{2,1,0:T(2,128)(2,1)} async-done(((bf16[128,2,3584]{2,1,0:T(2,128)(2,1)}), bf16[128,2,3584]{2,1,0:T(2,128)(2,1)}, u32[]{:S(2)}, u32[]{:S(2)}) %all-to-all-start.1) | async-done | bytes 1835040 | tf_op jit(solution)/shard_map/all_to_all | solution.py:148
  136.1 4.5 %all-to-all-start.3 = ((bf16[128,2,3584]{2,1,0:T(2,128)(2,1)}), bf16[128,2,3584]{2,1,0:T(2,128)(2,1)S(1)}, u32[]{:S(2)}, u32[]{:S(2)}) async-start(bf16[128,2,3584]{2,1,0:T(2,128)(2,1)} %shard_map.74), calls=%async_computation.4 | async-start | bytes 3670016 | tf_op jit(solution)/shard_map/all_to_all | solution.py:148
  140.9 0.4 fusion.16
  141.7 2.4 %convolution_bitcast_fusion.1 = f32[1,16,3584]{2,1,0:T(8,128)S(1)} fusion(bf16[128,2,3584]{2,1,0:T(2,128)(2,1)} %all-to-all-done.1, f32[16,128,2]{0,2,1:T(2,128)S(1)} %bitcast.36), kind=kOutput, calls=%fused_computation.1 | convolution fusion | flops 176160768 | bytes 2080768 | tf_op jit(solution)/shard_map/tec,ecd->td/dot_general | solution.py:150
  144.0 24.3 %all-to-all-done.3 = bf16[128,2,3584]{2,1,0:T(2,128)(2,1)S(1)} async-done(((bf16[128,2,3584]{2,1,0:T(2,128)(2,1)}), bf16[128,2,3584]{2,1,0:T(2,128)(2,1)S(1)}, u32[]{:S(2)}, u32[]{:S(2)}) %all-to-all-start.3) | async-done | bytes 1835040 | tf_op jit(solution)/shard_map/all_to_all | solution.py:148
  168.3 0.9 convolution_bitcast_fusion
  169.2 1.8 fusion.13
  (31 shorter events, 2.4 us)
Async XLA Ops:
  6.5 48.4 %all-gather.2.cloned.1.call-start = ((), (), s32[]{:S(2)}) async-start(), calls=%async_computation.5 | async-start | bytes 2064384 | tf_op jit(solution)/shard_map/all_gather | solution.py:108
  7.3 161.9 %reduce-scatter.2.cloned.1.call-start = ((), (), s32[]{:S(2)}) async-start(), calls=%async_computation.6 | async-start | bytes 4128768 | tf_op jit(solution)/shard_map/reduce_scatter | solution.py:118
  12.2 42.8 %copy-start.2 = (bf16[3,3584,128]{2,1,0:T(8,128)(2,1)S(1)}, bf16[3,3584,128]{2,1,0:T(8,128)(2,1)}, u32[]{:S(2)}) copy-start(bf16[3,3584,128]{2,1,0:T(8,128)(2,1)} %param.13) | copy-start | bytes 8257540
  55.0 2.3 %copy-start.4 = (bf16[2,128,3584]{2,1,0:T(8,128)(2,1)S(1)}, bf16[2,128,3584]{2,1,0:T(8,128)(2,1)}, u32[]{:S(2)}) copy-start(bf16[2,128,3584]{2,1,0:T(8,128)(2,1)} %all-gather.2.cloned.1.call-done) | copy-start | bytes 5505028
  60.3 0.9 copy-start.1
  65.0 37.0 %all-to-all-start.2 = ((bf16[128,2,3584]{2,1,0:T(2,128)(2,1)}), bf16[128,2,3584]{2,1,0:T(2,128)(2,1)S(1)}, u32[]{:S(2)}, u32[]{:S(2)}) async-start(bf16[128,2,3584]{2,1,0:T(2,128)(2,1)} %copy.50), calls=%async_computation.3 | async-start | bytes 3670016 | tf_op jit(solution)/shard_map/all_to_all | solution.py:145
  102.0 1.2 copy-start
  103.2 32.9 %all-to-all-start.1 = ((bf16[128,2,3584]{2,1,0:T(2,128)(2,1)}), bf16[128,2,3584]{2,1,0:T(2,128)(2,1)}, u32[]{:S(2)}, u32[]{:S(2)}) async-start(bf16[128,2,3584]{2,1,0:T(2,128)(2,1)} %shard_map.73), calls=%async_computation.2 | async-start | bytes 3670016 | tf_op jit(solution)/shard_map/all_to_all | solution.py:148
  122.3 18.2 %copy-start.3 = (f32[2,16,8]{1,2,0:T(8,128)S(1)}, f32[2,16,8]{1,2,0:T(8,128)}, u32[]{:S(2)}) copy-start(f32[2,16,8]{1,2,0:T(8,128)} %param.9) | copy-start | bytes 3076
  136.1 32.2 %all-to-all-start.3 = ((bf16[128,2,3584]{2,1,0:T(2,128)(2,1)}), bf16[128,2,3584]{2,1,0:T(2,128)(2,1)S(1)}, u32[]{:S(2)}, u32[]{:S(2)}) async-start(bf16[128,2,3584]{2,1,0:T(2,128)(2,1)} %shard_map.74), calls=%async_computation.4 | async-start | bytes 3670016 | tf_op jit(solution)/shard_map/all_to_all | solution.py:148
Sparse Core Ops, SparseCore 0:
  9.0 45.8 all-gather.1
  60.5 60.2 reduce-scatter.1

commit v12 on v9

--- a/solution.py
+++ b/solution.py
@@ -155,14 +155,11 @@
         slot = target % 2 * 2 + target // 2
         return lax.dynamic_index_in_dim(chunks[s], slot, 0, keepdims=False)
 
-    results = []
-    for s, direction in ((0, 1), (1, -1)):
-        total = chunk(s, (place - direction) % ring)
-        for k in range(ring - 1):
-            arrived = ring_shift(total, direction, ring)
-            total = arrived + chunk(s, (place - direction * (k + 2)) % ring)
-        results.append(total)
-    return jnp.stack(results)
+    total = jnp.stack([chunk(s, place) for s in range(step_count)])
+    for offset in range(1, ring):
+        outgoing = jnp.stack([chunk(s, (place + offset) % ring) for s in range(step_count)])
+        total = total + ring_shift(outgoing, offset, ring)
+    return total
 
 
 def shards(tokens, expert_ids, combine_weights, w_gate, w_up, w_down, shared_weights):

time: 180 us -> 188 us (1.044)
  waiting for transfers between devices: 68.9 us -> 87 us
  matrix products: 13.1 us -> 9.22 us
  local copies, waits for them, and re-layouts: 12.9 us -> 10.2 us
  starting transfers between devices: 41.5 us -> 39.1 us
    ppermute x4, waiting for transfers between devices: 7.27 us -> 14.3 us  [partner_2(): return lax.ppermute(block, axis, route)]
    all_to_all x2, waiting for transfers between devices: 24.4 us -> 30.4 us  [shards(): lax.all_to_all(payloads[s], 'ep', split_axis=0, concat_axis=0, tiled=True)]
    ppermute x6 -> x3, waiting for transfers between devices: 8.3 us -> 14.2 us  [ring_shift(): return lax.ppermute(block, 'ep', route)]
    ppermute x6 -> x3, starting transfers between devices: 8.44 us -> 5.09 us  [ring_shift(): return lax.ppermute(block, 'ep', route)]
    another operation x2 -> x3, other arithmetic: 0.06 us -> 2.47 us  [shared_expert(): jnp.stack([chunk(s, (place + offset) % ring) for s in range(step_count)])]
  transfers between devices with their start and end apart: 14 -> 11, of which waited for: 8 -> 8; matrix products, arithmetic and copies ran while one was open for 13% -> 9% of each run, Pallas kernels for 15% -> 14%
where the time goes in v12:
time: 188 us; the launch traced here: 187 us
  waiting for transfers between devices  87 us (46%)
  starting transfers between devices  39.1 us (21%)
  Pallas kernels  32.7 us (17%)
  local copies, waits for them, and re-layouts  10.2 us (5%)
  matrix products  9.22 us (5%)
  other arithmetic  8.4 us (4%)
    all_to_all x2, waiting for transfers between devices, shards(): lax.all_to_all(payloads[s], 'ep', split_axis=0, concat_axis=0, tiled=True)  30.4 us
    all_to_all x2, waiting for transfers between devices, shards(): lax.all_to_all(expert_out, 'ep', split_axis=0, concat_axis=0, tiled=True)  28.2 us
    pallas_call x2, Pallas kernels, expert_rows(): pl.pallas_call(ffn_kernel, out_shape=jax.ShapeDtypeStruct(token_block.sha...  27 us
    all_to_all x2, starting transfers between devices, shards(): lax.all_to_all(payloads[s], 'ep', split_axis=0, concat_axis=0, tiled=True)  15.4 us
    ppermute x4, waiting for transfers between devices, partner_2(): return lax.ppermute(block, axis, route)  14.3 us
    ppermute x3, waiting for transfers between devices, ring_shift(): return lax.ppermute(block, 'ep', route)  14.2 us
    all_to_all x2, starting transfers between devices, shards(): lax.all_to_all(expert_out, 'ep', split_axis=0, concat_axis=0, tiled=True)  9.69 us
    ppermute x4, starting transfers between devices, partner_2(): return lax.ppermute(block, axis, route)  8.92 us
  transfers between devices with their start and end apart: 11, of which 8 were waited for; matrix products, arithmetic and copies ran while one was open for 9% of the time, Pallas kernels for 14%

profile of v12, /device:TPU:1, one launch (start us, length us, event | category | flops | bytes accessed | tf_op | source)
XLA Modules:
  0.0 186.9 jit_solution(1424678703515323659)
XLA Ops:
  5.1 2.8 %shard_map.74 = bf16[128,2,3584]{2,1,0:T(2,128)(2,1)} custom-call(bf16[256,16]{1,0:T(8,128)(2,1)} %copy.33.select_ref, bf16[16,3584]{1,0:T(8,128)(2,1)} %get-tuple-element.17.token_ref), custom_call_target="tpu_custom_call" | custom-call | tf_op jit(solution)/shard_map/pallas_call | solution.py:75
  7.9 2.8 %shard_map.73 = bf16[128,2,3584]{2,1,0:T(2,128)(2,1)} custom-call(bf16[256,16]{1,0:T(8,128)(2,1)} %copy.31.select_ref, bf16[16,3584]{1,0:T(8,128)(2,1)} %get-tuple-element.18.token_ref), custom_call_target="tpu_custom_call" | custom-call | tf_op jit(solution)/shard_map/pallas_call | solution.py:75
  10.7 3.7 %collective-permute-start = (bf16[2,16,3584]{2,1,0:T(8,128)(2,1)S(1)}, bf16[2,16,3584]{2,1,0:T(8,128)(2,1)S(1)}, u32[]{:S(2)}, u32[]{:S(2)}) collective-permute-start(bf16[2,16,3584]{2,1,0:T(8,128)(2,1)S(1)} %copy-done.3), channel_id=1, source_target_pairs={{0,4},{4,0},{1,5},{5,1},{2,6},{6,2},{3,7},{7,3},{8,12},{12,8},{9,1... | collective-permute-start | bytes 688136 | tf_op jit(solution)/shard_map/ppermute | solution.py:16
  14.5 5.0 %collective-permute-done = bf16[2,16,3584]{2,1,0:T(8,128)(2,1)S(1)} collective-permute-done((bf16[2,16,3584]{2,1,0:T(8,128)(2,1)S(1)}, bf16[2,16,3584]{2,1,0:T(8,128)(2,1)S(1)}, u32[]{:S(2)}, u32[]{:S(2)}) %collective-permute-start) | collective-permute-done | bytes 229408 | tf_op jit(solution)/shard_map/ppermute | solution.py:16
  21.0 9.2 %collective-permute-done.1 = bf16[2,32,3584]{2,1,0:T(8,128)(2,1)S(1)} collective-permute-done((bf16[2,32,3584]{2,1,0:T(8,128)(2,1)S(1)}, bf16[2,32,3584]{2,1,0:T(8,128)(2,1)S(1)}, u32[]{:S(2)}, u32[]{:S(2)}) %collective-permute-start.1) | collective-permute-done | bytes 458784 | tf_op jit(solution)/shard_map/ppermute | solution.py:16
  30.3 2.5 %collective-permute-start.2 = (bf16[2,64,3584]{2,1,0:T(8,128)(2,1)S(1)}, bf16[2,64,3584]{2,1,0:T(8,128)(2,1)}, u32[]{:S(2)}, u32[]{:S(2)}) collective-permute-start(bf16[2,64,3584]{2,1,0:T(8,128)(2,1)S(1)} %maximum_select_fusion.1), channel_id=1, source_target_pairs={{0,1},{1,0},{2,3},{3,2},{4,5},{5,4},{6,7},{7,6},{8,9},{9,8},{10,11... | collective-permute-start | bytes 2752520 | tf_op jit(solution)/shard_map/ppermute | solution.py:16
  32.8 10.1 %all-to-all-start.2 = ((bf16[128,2,3584]{2,1,0:T(2,128)(2,1)}), bf16[128,2,3584]{2,1,0:T(2,128)(2,1)S(1)}, u32[]{:S(2)}, u32[]{:S(2)}) async-start(bf16[128,2,3584]{2,1,0:T(2,128)(2,1)} %shard_map.74), calls=%async_computation.2 | async-start | bytes 3670016 | tf_op jit(solution)/shard_map/all_to_all | solution.py:179
  43.0 2.0 %maximum_select_fusion = bf16[2,128,3584]{2,1,0:T(8,128)(2,1)S(1)} fusion(bf16[2,64,3584]{2,1,0:T(8,128)(2,1)S(1)} %maximum_select_fusion.1, bf16[2,64,3584]{2,1,0:T(8,128)(2,1)} %collective-permute-done.2, pred[]{:T(512)S(6)} %eq.111), kind=kLoop, calls=%fused_computation.2 | loop fusion | flops 8257536 | bytes 3670017 | tf_op jit(solution)/shard_map/jit(_where)/select_n | solution.py:115
  46.5 24.1 %all-to-all-done.2.x_ref = bf16[128,2,3584]{2,1,0:T(2,128)(2,1)S(1)} async-done(((bf16[128,2,3584]{2,1,0:T(2,128)(2,1)}), bf16[128,2,3584]{2,1,0:T(2,128)(2,1)S(1)}, u32[]{:S(2)}, u32[]{:S(2)}) %all-to-all-start.2) | async-done | bytes 1835040 | tf_op jit(solution)/shard_map/all_to_all | solution.py:179
  71.9 5.3 %all-to-all-start = ((bf16[128,2,3584]{2,1,0:T(2,128)(2,1)}), bf16[128,2,3584]{2,1,0:T(2,128)(2,1)}, u32[]{:S(2)}, u32[]{:S(2)}) async-start(bf16[128,2,3584]{2,1,0:T(2,128)(2,1)} %shard_map.73), calls=%async_computation | async-start | bytes 3670016 | tf_op jit(solution)/shard_map/all_to_all | solution.py:179
  77.3 1.8 fusion.4
  85.1 13.4 %shard_map.76 = bf16[128,2,3584]{2,1,0:T(2,128)(2,1)} custom-call(bf16[128,2,3584]{2,1,0:T(2,128)(2,1)} %copy-done.2, bf16[1,3584,1024]{2,1,0:T(8,128)(2,1)} %gate_ref.3, bf16[1,3584,1024]{2,1,0:T(8,128)(2,1)} %up_ref.3, bf16[1,1024,3584]{2,1,0:T(8,128)(2,1)} %down_ref.3), custom_call_target="tpu_custom_call" | custom-call | flops 5637144576 | bytes 25690112 | tf_op jit(solution)/shard_map/pallas_call | solution.py:45
  98.5 6.3 %all-to-all-done.x_ref = bf16[128,2,3584]{2,1,0:T(2,128)(2,1)} async-done(((bf16[128,2,3584]{2,1,0:T(2,128)(2,1)}), bf16[128,2,3584]{2,1,0:T(2,128)(2,1)}, u32[]{:S(2)}, u32[]{:S(2)}) %all-to-all-start) | async-done | bytes 1835040 | tf_op jit(solution)/shard_map/all_to_all | solution.py:179
  104.8 5.4 %all-to-all-start.3 = ((bf16[128,2,3584]{2,1,0:T(2,128)(2,1)}), bf16[128,2,3584]{2,1,0:T(2,128)(2,1)}, u32[]{:S(2)}, u32[]{:S(2)}) async-start(bf16[128,2,3584]{2,1,0:T(2,128)(2,1)} %shard_map.76), calls=%async_computation.3 | async-start | bytes 3670016 | tf_op jit(solution)/shard_map/all_to_all | solution.py:181
  110.2 13.6 %shard_map.75 = bf16[128,2,3584]{2,1,0:T(2,128)(2,1)} custom-call(bf16[128,2,3584]{2,1,0:T(2,128)(2,1)} %all-to-all-done.x_ref, bf16[1,3584,1024]{2,1,0:T(8,128)(2,1)} %gate_ref.3, bf16[1,3584,1024]{2,1,0:T(8,128)(2,1)} %up_ref.3, bf16[1,1024,3584]{2,1,0:T(8,128)(2,1)} %down_ref.3), custom_call_target="tpu_custom_call" | custom-call | flops 5637144576 | bytes 25690112 | tf_op jit(solution)/shard_map/pallas_call | solution.py:45
  123.8 1.7 dynamic-slice_add_fusion
  126.5 11.2 %all-to-all-done.3 = bf16[128,2,3584]{2,1,0:T(2,128)(2,1)} async-done(((bf16[128,2,3584]{2,1,0:T(2,128)(2,1)}), bf16[128,2,3584]{2,1,0:T(2,128)(2,1)}, u32[]{:S(2)}, u32[]{:S(2)}) %all-to-all-start.3) | async-done | bytes 1835040 | tf_op jit(solution)/shard_map/all_to_all | solution.py:181
  137.7 4.3 %all-to-all-start.1 = ((bf16[128,2,3584]{2,1,0:T(2,128)(2,1)}), bf16[128,2,3584]{2,1,0:T(2,128)(2,1)S(1)}, u32[]{:S(2)}, u32[]{:S(2)}) async-start(bf16[128,2,3584]{2,1,0:T(2,128)(2,1)} %shard_map.75), calls=%async_computation.1 | async-start | bytes 3670016 | tf_op jit(solution)/shard_map/all_to_all | solution.py:181
  146.1 2.5 %collective-permute-start.5 = (f32[2,16,3584]{2,1,0:T(8,128)}, f32[2,16,3584]{2,1,0:T(8,128)}, u32[]{:S(2)}, u32[]{:S(2)}) collective-permute-start(f32[2,16,3584]{2,1,0:T(8,128)} %pad_maximum_fusion.1), channel_id=1, source_target_pairs={{0,4},{1,5},{2,6},{3,7},{4,0},{5,1},{6,2},{7,3},{8,12},{9,13},{10,... | collective-permute-start | bytes 1376264 | tf_op jit(solution)/shard_map/ppermute | solution.py:128
  150.6 2.4 %convolution_bitcast_fusion = f32[1,16,3584]{2,1,0:T(8,128)S(1)} fusion(bf16[128,2,3584]{2,1,0:T(2,128)(2,1)} %all-to-all-done.3, f32[16,128,2]{0,2,1:T(2,128)S(1)} %bitcast.36), kind=kOutput, calls=%fused_computation | convolution fusion | flops 176160768 | bytes 2080768 | tf_op jit(solution)/shard_map/tec,ecd->td/dot_general | solution.py:183
  153.0 17.0 %all-to-all-done.1 = bf16[128,2,3584]{2,1,0:T(2,128)(2,1)S(1)} async-done(((bf16[128,2,3584]{2,1,0:T(2,128)(2,1)}), bf16[128,2,3584]{2,1,0:T(2,128)(2,1)S(1)}, u32[]{:S(2)}, u32[]{:S(2)}) %all-to-all-start.1) | async-done | bytes 1835040 | tf_op jit(solution)/shard_map/all_to_all | solution.py:181
  170.8 3.6 %collective-permute-done.4 = f32[2,16,3584]{2,1,0:T(8,128)S(1)} collective-permute-done((f32[2,16,3584]{2,1,0:T(8,128)}, f32[2,16,3584]{2,1,0:T(8,128)S(1)}, u32[]{:S(2)}, u32[]{:S(2)}) %collective-permute-start.4) | collective-permute-done | bytes 458784 | tf_op jit(solution)/shard_map/ppermute | solution.py:128
  174.4 10.6 %collective-permute-done.5 = f32[2,16,3584]{2,1,0:T(8,128)} collective-permute-done((f32[2,16,3584]{2,1,0:T(8,128)}, f32[2,16,3584]{2,1,0:T(8,128)}, u32[]{:S(2)}, u32[]{:S(2)}) %collective-permute-start.5) | collective-permute-done | bytes 458784 | tf_op jit(solution)/shard_map/ppermute | solution.py:128
  185.0 2.0 %fusion.16 = bf16[2,16,3584]{2,1,0:T(8,128)(2,1)} fusion(f32[2,16,3584]{2,1,0:T(8,128)} %collective-permute-done.6, f32[2,16,3584]{2,1,0:T(8,128)} %collective-permute-done.5, f32[2,16,3584]{2,1,0:T(8,128)S(1)} %collective-permute-done.4, f32[1,16,3584]{2,1,0:T(8,128)S(1)} %get-tuple-element.13, f32[1,16,3584]{2,1,0:T(8,128)S(1)} %get-tuple-element.9, ...), kind=kLoop, calls=%fused_computation.27 | loop fusion | flops 802816 | bytes 2523136 | tf_op jit(solution)/shard_map/convert_element_type | solution.py:193
  (60 shorter events, 23.2 us)
Async XLA Ops:
  5.1 5.6 %copy-start.3 = (bf16[2,16,3584]{2,1,0:T(8,128)(2,1)S(1)}, bf16[2,16,3584]{2,1,0:T(8,128)(2,1)}, u32[]{:S(2)}) copy-start(bf16[2,16,3584]{2,1,0:T(8,128)(2,1)} %param.7) | copy-start | bytes 688132
  10.7 8.8 %collective-permute-start = (bf16[2,16,3584]{2,1,0:T(8,128)(2,1)S(1)}, bf16[2,16,3584]{2,1,0:T(8,128)(2,1)S(1)}, u32[]{:S(2)}, u32[]{:S(2)}) collective-permute-start(bf16[2,16,3584]{2,1,0:T(8,128)(2,1)S(1)} %copy-done.3), channel_id=1, source_target_pairs={{0,4},{4,0},{1,5},{5,1},{2,6},{6,2},{3,7},{7,3},{8,12},{12,8},{9,1... | collective-permute-start | bytes 688136 | tf_op jit(solution)/shard_map/ppermute | solution.py:16
  19.6 10.6 %collective-permute-start.1 = (bf16[2,32,3584]{2,1,0:T(8,128)(2,1)S(1)}, bf16[2,32,3584]{2,1,0:T(8,128)(2,1)S(1)}, u32[]{:S(2)}, u32[]{:S(2)}) collective-permute-start(bf16[2,32,3584]{2,1,0:T(8,128)(2,1)S(1)} %maximum_select_fusion.2), channel_id=1, source_target_pairs={{0,2},{2,0},{1,3},{3,1},{4,6},{6,4},{5,7},{7,5},{8,10},{10,8},{9,1... | collective-permute-start | bytes 1376264 | tf_op jit(solution)/shard_map/ppermute | solution.py:16
  30.3 12.6 %collective-permute-start.2 = (bf16[2,64,3584]{2,1,0:T(8,128)(2,1)S(1)}, bf16[2,64,3584]{2,1,0:T(8,128)(2,1)}, u32[]{:S(2)}, u32[]{:S(2)}) collective-permute-start(bf16[2,64,3584]{2,1,0:T(8,128)(2,1)S(1)} %maximum_select_fusion.1), channel_id=1, source_target_pairs={{0,1},{1,0},{2,3},{3,2},{4,5},{5,4},{6,7},{7,6},{8,9},{9,8},{10,11... | collective-permute-start | bytes 2752520 | tf_op jit(solution)/shard_map/ppermute | solution.py:16
  32.8 37.8 %all-to-all-start.2 = ((bf16[128,2,3584]{2,1,0:T(2,128)(2,1)}), bf16[128,2,3584]{2,1,0:T(2,128)(2,1)S(1)}, u32[]{:S(2)}, u32[]{:S(2)}) async-start(bf16[128,2,3584]{2,1,0:T(2,128)(2,1)} %shard_map.74), calls=%async_computation.2 | async-start | bytes 3670016 | tf_op jit(solution)/shard_map/all_to_all | solution.py:179
  42.9 2.3 %copy-start.6 = (bf16[3,3584,128]{2,1,0:T(8,128)(2,1)S(1)}, bf16[3,3584,128]{2,1,0:T(8,128)(2,1)}, u32[]{:S(2)}) copy-start(bf16[3,3584,128]{2,1,0:T(8,128)(2,1)} %param.13) | copy-start | bytes 8257540
  70.7 1.2 copy-start.2
  71.9 32.9 %all-to-all-start = ((bf16[128,2,3584]{2,1,0:T(2,128)(2,1)}), bf16[128,2,3584]{2,1,0:T(2,128)(2,1)}, u32[]{:S(2)}, u32[]{:S(2)}) async-start(bf16[128,2,3584]{2,1,0:T(2,128)(2,1)} %shard_map.73), calls=%async_computation | async-start | bytes 3670016 | tf_op jit(solution)/shard_map/all_to_all | solution.py:179
  79.1 2.4 %copy-start = (f32[2,128,3584]{2,1,0:T(8,128)}, f32[2,128,3584]{2,1,0:T(8,128)S(1)}, u32[]{:S(2)}) copy-start(f32[2,128,3584]{2,1,0:T(8,128)S(1)} %fusion.4) | copy-start | bytes 11010052
  79.1 3.6 %copy-start.9 = (f32[2,16,8]{1,2,0:T(8,128)S(1)}, f32[2,16,8]{1,2,0:T(8,128)}, u32[]{:S(2)}) copy-start(f32[2,16,8]{1,2,0:T(8,128)} %param.9) | copy-start | bytes 3076
  81.5 42.3 %collective-permute-start.3 = (f32[2,64,3584]{2,1,0:T(8,128)}, f32[2,64,3584]{2,1,0:T(8,128)}, u32[]{:S(2)}, u32[]{:S(2)}) collective-permute-start(f32[2,64,3584]{2,1,0:T(8,128)} %constant_dynamic-slice_fusion.8), channel_id=1, source_target_pairs={{0,1},{1,0},{2,3},{3,2},{4,5},{5,4},{6,7},{7,6},{8,9},{9,8},{10,11... | collective-permute-start | bytes 5505032 | tf_op jit(solution)/shard_map/ppermute | solution.py:16
  104.8 32.9 %all-to-all-start.3 = ((bf16[128,2,3584]{2,1,0:T(2,128)(2,1)}), bf16[128,2,3584]{2,1,0:T(2,128)(2,1)}, u32[]{:S(2)}, u32[]{:S(2)}) async-start(bf16[128,2,3584]{2,1,0:T(2,128)(2,1)} %shard_map.76), calls=%async_computation.3 | async-start | bytes 3670016 | tf_op jit(solution)/shard_map/all_to_all | solution.py:181
  110.2 13.6 %copy-start.1 = (f32[2,128,3584]{2,1,0:T(8,128)S(1)}, f32[2,128,3584]{2,1,0:T(8,128)}, u32[]{:S(2)}) copy-start(f32[2,128,3584]{2,1,0:T(8,128)} %copy-done) | copy-start | bytes 11010052
  137.7 32.2 %all-to-all-start.1 = ((bf16[128,2,3584]{2,1,0:T(2,128)(2,1)}), bf16[128,2,3584]{2,1,0:T(2,128)(2,1)S(1)}, u32[]{:S(2)}, u32[]{:S(2)}) async-start(bf16[128,2,3584]{2,1,0:T(2,128)(2,1)} %shard_map.75), calls=%async_computation.1 | async-start | bytes 3670016 | tf_op jit(solution)/shard_map/all_to_all | solution.py:181
  142.1 0.9 copy-start.5
  142.1 3.2 %copy-start.4 = (f32[1,16,3584]{2,1,0:T(8,128)S(1)}, f32[1,16,3584]{2,1,0:T(8,128)}, u32[]{:S(2)}) copy-start(f32[1,16,3584]{2,1,0:T(8,128)} %get-tuple-element.15) | copy-start | bytes 688132
  142.2 8.4 %copy-start.8 = (f32[16,256]{0,1:T(8,128)S(1)}, f32[16,256]{0,1:T(8,128)}, u32[]{:S(2)}) copy-start(f32[16,256]{0,1:T(8,128)} %fusion.19) | copy-start | bytes 49156
  143.8 30.6 %collective-permute-start.4 = (f32[2,16,3584]{2,1,0:T(8,128)}, f32[2,16,3584]{2,1,0:T(8,128)S(1)}, u32[]{:S(2)}, u32[]{:S(2)}) collective-permute-start(f32[2,16,3584]{2,1,0:T(8,128)} %pad_maximum_fusion), channel_id=1, source_target_pairs={{0,2},{1,3},{2,4},{3,5},{4,6},{5,7},{6,0},{7,1},{8,10},{9,11},{10,... | collective-permute-start | bytes 1376264 | tf_op jit(solution)/shard_map/ppermute | solution.py:128
  145.3 24.7 %copy-start.7 = (f32[16,256]{0,1:T(8,128)S(1)}, f32[16,256]{0,1:T(8,128)}, u32[]{:S(2)}) copy-start(f32[16,256]{0,1:T(8,128)} %fusion.20) | copy-start | bytes 49156
  146.1 38.9 %collective-permute-start.5 = (f32[2,16,3584]{2,1,0:T(8,128)}, f32[2,16,3584]{2,1,0:T(8,128)}, u32[]{:S(2)}, u32[]{:S(2)}) collective-permute-start(f32[2,16,3584]{2,1,0:T(8,128)} %pad_maximum_fusion.1), channel_id=1, source_target_pairs={{0,4},{1,5},{2,6},{3,7},{4,0},{5,1},{6,2},{7,3},{8,12},{9,13},{10,... | collective-permute-start | bytes 1376264 | tf_op jit(solution)/shard_map/ppermute | solution.py:128
  149.5 35.5 %collective-permute-start.6 = (f32[2,16,3584]{2,1,0:T(8,128)}, f32[2,16,3584]{2,1,0:T(8,128)}, u32[]{:S(2)}, u32[]{:S(2)}) collective-permute-start(f32[2,16,3584]{2,1,0:T(8,128)} %pad_maximum_fusion.2), channel_id=1, source_target_pairs={{0,6},{1,7},{2,0},{3,1},{4,2},{5,3},{6,4},{7,5},{8,14},{9,15},{10,... | collective-permute-start | bytes 1376264 | tf_op jit(solution)/shard_map/ppermute | solution.py:128

commit v13 on v10

--- a/solution.py
+++ b/solution.py
@@ -182,9 +182,9 @@
     routed_steps = []
     for s in range(step_count):
         received = lax.all_to_all(payloads[s], "ep", split_axis=0, concat_axis=0, tiled=True)
+        expert_out = expert_rows(received, w_gate, w_up, w_down)
         if s == step_count - 1:
-            received, shared = lax.optimization_barrier((received, shared))
-        expert_out = expert_rows(received, w_gate, w_up, w_down)
+            expert_out, shared = lax.optimization_barrier((expert_out, shared))
         returned = lax.all_to_all(expert_out, "ep", split_axis=0, concat_axis=0, tiled=True)
         routed_steps.append(
             jnp.einsum(

time: 194 us -> 195 us (level)
  waiting for transfers between devices: 92.5 us -> 89.9 us
  starting transfers between devices: 47.2 us -> 49.7 us
    all_to_all x2, waiting for transfers between devices: 39.7 us -> 24.3 us  [shards(): lax.all_to_all(expert_out, 'ep', split_axis=0, concat_axis=0, tiled=True)]
    all_to_all x2, waiting for transfers between devices: 20 us -> 32.8 us  [shards(): lax.all_to_all(payloads[s], 'ep', split_axis=0, concat_axis=0, tiled=True)]
    all_to_all x2, starting transfers between devices: 14.4 us -> 16.9 us  [shards(): lax.all_to_all(expert_out, 'ep', split_axis=0, concat_axis=0, tiled=True)]
  transfers between devices with their start and end apart: 14 -> 14, of which waited for: 8 -> 8; matrix products, arithmetic and copies ran while one was open for 5% -> 6% of each run, Pallas kernels for 14% -> 14%
where the time goes in v13:
time: 195 us; the launch traced here: 194 us
  waiting for transfers between devices  89.9 us (46%)
  starting transfers between devices  49.7 us (25%)
  Pallas kernels  32.7 us (17%)
  local copies, waits for them, and re-layouts  8.52 us (4%)
  matrix products  7.92 us (4%)
  other arithmetic  4.94 us (3%)
    all_to_all x2, waiting for transfers between devices, shards(): lax.all_to_all(payloads[s], 'ep', split_axis=0, concat_axis=0, tiled=True)  32.8 us
    pallas_call x2, Pallas kernels, expert_rows(): pl.pallas_call(ffn_kernel, out_shape=jax.ShapeDtypeStruct(token_block.sha...  27 us
    all_to_all x2, waiting for transfers between devices, shards(): lax.all_to_all(expert_out, 'ep', split_axis=0, concat_axis=0, tiled=True)  24.3 us
    ppermute x6, waiting for transfers between devices, ring_shift(): return lax.ppermute(block, 'ep', route)  18.6 us
    all_to_all x2, starting transfers between devices, shards(): lax.all_to_all(expert_out, 'ep', split_axis=0, concat_axis=0, tiled=True)  16.9 us
    all_to_all x2, starting transfers between devices, shards(): lax.all_to_all(payloads[s], 'ep', split_axis=0, concat_axis=0, tiled=True)  15.4 us
    ppermute x4, waiting for transfers between devices, partner_2(): return lax.ppermute(block, axis, route)  14.3 us
    ppermute x4, starting transfers between devices, partner_2(): return lax.ppermute(block, axis, route)  8.89 us
  transfers between devices with their start and end apart: 14, of which 8 were waited for; matrix products, arithmetic and copies ran while one was open for 6% of the time, Pallas kernels for 14%

profile of v13, /device:TPU:1, one launch (start us, length us, event | category | flops | bytes accessed | tf_op | source)
XLA Modules:
  0.0 194.0 jit_solution(4350021559652013290)
XLA Ops:
  5.1 2.9 %shard_map.75 = bf16[128,2,3584]{2,1,0:T(2,128)(2,1)} custom-call(bf16[256,16]{1,0:T(8,128)(2,1)} %copy.33.select_ref, bf16[16,3584]{1,0:T(8,128)(2,1)} %get-tuple-element.13.token_ref), custom_call_target="tpu_custom_call" | custom-call | tf_op jit(solution)/shard_map/pallas_call | solution.py:75
  7.9 2.8 %shard_map.73 = bf16[128,2,3584]{2,1,0:T(2,128)(2,1)} custom-call(bf16[256,16]{1,0:T(8,128)(2,1)} %copy.31.select_ref, bf16[16,3584]{1,0:T(8,128)(2,1)} %get-tuple-element.14.token_ref), custom_call_target="tpu_custom_call" | custom-call | tf_op jit(solution)/shard_map/pallas_call | solution.py:75
  10.7 3.8 %collective-permute-start = (bf16[2,16,3584]{2,1,0:T(8,128)(2,1)S(1)}, bf16[2,16,3584]{2,1,0:T(8,128)(2,1)S(1)}, u32[]{:S(2)}, u32[]{:S(2)}) collective-permute-start(bf16[2,16,3584]{2,1,0:T(8,128)(2,1)S(1)} %copy-done.3), channel_id=1, source_target_pairs={{0,4},{4,0},{1,5},{5,1},{2,6},{6,2},{3,7},{7,3},{8,12},{12,8},{9,1... | collective-permute-start | bytes 688136 | tf_op jit(solution)/shard_map/ppermute | solution.py:16
  14.5 5.1 %collective-permute-done = bf16[2,16,3584]{2,1,0:T(8,128)(2,1)S(1)} collective-permute-done((bf16[2,16,3584]{2,1,0:T(8,128)(2,1)S(1)}, bf16[2,16,3584]{2,1,0:T(8,128)(2,1)S(1)}, u32[]{:S(2)}, u32[]{:S(2)}) %collective-permute-start) | collective-permute-done | bytes 229408 | tf_op jit(solution)/shard_map/ppermute | solution.py:16
  21.0 9.2 %collective-permute-done.1 = bf16[2,32,3584]{2,1,0:T(8,128)(2,1)S(1)} collective-permute-done((bf16[2,32,3584]{2,1,0:T(8,128)(2,1)S(1)}, bf16[2,32,3584]{2,1,0:T(8,128)(2,1)S(1)}, u32[]{:S(2)}, u32[]{:S(2)}) %collective-permute-start.1) | collective-permute-done | bytes 458784 | tf_op jit(solution)/shard_map/ppermute | solution.py:16
  30.4 2.5 %collective-permute-start.2 = (bf16[2,64,3584]{2,1,0:T(8,128)(2,1)S(1)}, bf16[2,64,3584]{2,1,0:T(8,128)(2,1)}, u32[]{:S(2)}, u32[]{:S(2)}) collective-permute-start(bf16[2,64,3584]{2,1,0:T(8,128)(2,1)S(1)} %maximum_select_fusion.1), channel_id=1, source_target_pairs={{0,1},{1,0},{2,3},{3,2},{4,5},{5,4},{6,7},{7,6},{8,9},{9,8},{10,11... | collective-permute-start | bytes 2752520 | tf_op jit(solution)/shard_map/ppermute | solution.py:16
  32.9 10.1 %all-to-all-start.1 = ((bf16[128,2,3584]{2,1,0:T(2,128)(2,1)}), bf16[128,2,3584]{2,1,0:T(2,128)(2,1)S(1)}, u32[]{:S(2)}, u32[]{:S(2)}) async-start(bf16[128,2,3584]{2,1,0:T(2,128)(2,1)} %shard_map.75), calls=%async_computation.1 | async-start | bytes 3670016 | tf_op jit(solution)/shard_map/all_to_all | solution.py:184
  43.0 2.0 %maximum_select_fusion = bf16[2,128,3584]{2,1,0:T(8,128)(2,1)S(1)} fusion(bf16[2,64,3584]{2,1,0:T(8,128)(2,1)S(1)} %maximum_select_fusion.1, bf16[2,64,3584]{2,1,0:T(8,128)(2,1)} %collective-permute-done.2, pred[]{:T(512)S(6)} %eq.121), kind=kLoop, calls=%fused_computation.2 | loop fusion | flops 8257536 | bytes 3670017 | tf_op jit(solution)/shard_map/jit(_where)/select_n | solution.py:115
  46.6 24.1 %all-to-all-done.1.x_ref = bf16[128,2,3584]{2,1,0:T(2,128)(2,1)S(1)} async-done(((bf16[128,2,3584]{2,1,0:T(2,128)(2,1)}), bf16[128,2,3584]{2,1,0:T(2,128)(2,1)S(1)}, u32[]{:S(2)}, u32[]{:S(2)}) %all-to-all-start.1) | async-done | bytes 1835040 | tf_op jit(solution)/shard_map/all_to_all | solution.py:184
  71.9 5.3 %all-to-all-start = ((bf16[128,2,3584]{2,1,0:T(2,128)(2,1)}), bf16[128,2,3584]{2,1,0:T(2,128)(2,1)}, u32[]{:S(2)}, u32[]{:S(2)}) async-start(bf16[128,2,3584]{2,1,0:T(2,128)(2,1)} %shard_map.73), calls=%async_computation | async-start | bytes 3670016 | tf_op jit(solution)/shard_map/all_to_all | solution.py:184
  77.3 1.8 fusion.4
  82.7 13.4 %shard_map.76 = bf16[128,2,3584]{2,1,0:T(2,128)(2,1)} custom-call(bf16[128,2,3584]{2,1,0:T(2,128)(2,1)} %copy-done.2, bf16[1,3584,1024]{2,1,0:T(8,128)(2,1)} %gate_ref.3, bf16[1,3584,1024]{2,1,0:T(8,128)(2,1)} %up_ref.3, bf16[1,1024,3584]{2,1,0:T(8,128)(2,1)} %down_ref.3), custom_call_target="tpu_custom_call" | custom-call | flops 5637144576 | bytes 25690112 | tf_op jit(solution)/shard_map/pallas_call | solution.py:45
  96.2 8.6 %all-to-all-done.x_ref = bf16[128,2,3584]{2,1,0:T(2,128)(2,1)} async-done(((bf16[128,2,3584]{2,1,0:T(2,128)(2,1)}), bf16[128,2,3584]{2,1,0:T(2,128)(2,1)}, u32[]{:S(2)}, u32[]{:S(2)}) %all-to-all-start) | async-done | bytes 1835040 | tf_op jit(solution)/shard_map/all_to_all | solution.py:184
  104.8 5.3 %all-to-all-start.2 = ((bf16[128,2,3584]{2,1,0:T(2,128)(2,1)}), bf16[128,2,3584]{2,1,0:T(2,128)(2,1)}, u32[]{:S(2)}, u32[]{:S(2)}) async-start(bf16[128,2,3584]{2,1,0:T(2,128)(2,1)} %shard_map.76), calls=%async_computation.2 | async-start | bytes 3670016 | tf_op jit(solution)/shard_map/all_to_all | solution.py:188
  110.2 13.6 %shard_map.74 = bf16[128,2,3584]{2,1,0:T(2,128)(2,1)} custom-call(bf16[128,2,3584]{2,1,0:T(2,128)(2,1)} %all-to-all-done.x_ref, bf16[1,3584,1024]{2,1,0:T(8,128)(2,1)} %gate_ref.3, bf16[1,3584,1024]{2,1,0:T(8,128)(2,1)} %up_ref.3, bf16[1,1024,3584]{2,1,0:T(8,128)(2,1)} %down_ref.3), custom_call_target="tpu_custom_call" | custom-call | flops 5637144576 | bytes 25690112 | tf_op jit(solution)/shard_map/pallas_call | solution.py:45
  123.8 1.7 dynamic-slice_add_fusion
  128.6 9.6 %collective-permute-done.4 = f32[16,3584]{1,0:T(8,128)S(1)} collective-permute-done((f32[16,3584]{1,0:T(8,128)S(1)}, f32[16,3584]{1,0:T(8,128)S(1)}, u32[]{:S(2)}, u32[]{:S(2)}) %collective-permute-start.4) | collective-permute-done | bytes 229408 | tf_op jit(solution)/shard_map/ppermute | solution.py:128
  138.4 2.7 %collective-permute-start.8 = (f32[16,3584]{1,0:T(8,128)S(1)}, f32[16,3584]{1,0:T(8,128)S(1)}, u32[]{:S(2)}, u32[]{:S(2)}) collective-permute-start(f32[16,3584]{1,0:T(8,128)S(1)} %bitcast_add_fusion.2), channel_id=1, source_target_pairs={{0,6},{1,7},{2,0},{3,1},{4,2},{5,3},{6,4},{7,5},{8,14},{9,15},{10,... | collective-permute-start | bytes 688136 | tf_op jit(solution)/shard_map/ppermute | solution.py:128
  141.1 4.9 %collective-permute-done.5 = f32[16,3584]{1,0:T(8,128)S(1)} collective-permute-done((f32[16,3584]{1,0:T(8,128)S(1)}, f32[16,3584]{1,0:T(8,128)S(1)}, u32[]{:S(2)}, u32[]{:S(2)}) %collective-permute-start.5) | collective-permute-done | bytes 229408 | tf_op jit(solution)/shard_map/ppermute | solution.py:128
  146.2 2.7 %collective-permute-start.9 = (f32[16,3584]{1,0:T(8,128)S(1)}, f32[16,3584]{1,0:T(8,128)S(1)}, u32[]{:S(2)}, u32[]{:S(2)}) collective-permute-start(f32[16,3584]{1,0:T(8,128)S(1)} %bitcast_add_fusion.1), channel_id=1, source_target_pairs={{0,6},{1,7},{2,0},{3,1},{4,2},{5,3},{6,4},{7,5},{8,14},{9,15},{10,... | collective-permute-start | bytes 688136 | tf_op jit(solution)/shard_map/ppermute | solution.py:128
  149.0 4.0 %collective-permute-done.6 = f32[16,3584]{1,0:T(8,128)S(1)} collective-permute-done((f32[16,3584]{1,0:T(8,128)S(1)}, f32[16,3584]{1,0:T(8,128)S(1)}, u32[]{:S(2)}, u32[]{:S(2)}) %collective-permute-start.6) | collective-permute-done | bytes 229408 | tf_op jit(solution)/shard_map/ppermute | solution.py:128
  153.1 11.5 %all-to-all-start.3 = ((bf16[128,2,3584]{2,1,0:T(2,128)(2,1)}), bf16[128,2,3584]{2,1,0:T(2,128)(2,1)S(1)}, u32[]{:S(2)}, u32[]{:S(2)}) async-start(bf16[128,2,3584]{2,1,0:T(2,128)(2,1)} %shard_map.74), calls=%async_computation.3 | async-start | bytes 3670016 | tf_op jit(solution)/shard_map/all_to_all | solution.py:188
  165.7 2.4 %convolution_bitcast_fusion.1 = f32[1,16,3584]{2,1,0:T(8,128)S(1)} fusion(bf16[128,2,3584]{2,1,0:T(2,128)(2,1)} %all-to-all-done.2, f32[16,128,2]{0,2,1:T(2,128)S(1)} %bitcast.66), kind=kOutput, calls=%fused_computation.1 | convolution fusion | flops 176160768 | bytes 2080768 | tf_op jit(solution)/shard_map/tec,ecd->td/dot_general | solution.py:190
  168.1 24.3 %all-to-all-done.3 = bf16[128,2,3584]{2,1,0:T(2,128)(2,1)S(1)} async-done(((bf16[128,2,3584]{2,1,0:T(2,128)(2,1)}), bf16[128,2,3584]{2,1,0:T(2,128)(2,1)S(1)}, u32[]{:S(2)}, u32[]{:S(2)}) %all-to-all-start.3) | async-done | bytes 1835040 | tf_op jit(solution)/shard_map/all_to_all | solution.py:188
  (62 shorter events, 19.2 us)
Async XLA Ops:
  5.1 5.7 %copy-start.3 = (bf16[2,16,3584]{2,1,0:T(8,128)(2,1)S(1)}, bf16[2,16,3584]{2,1,0:T(8,128)(2,1)}, u32[]{:S(2)}) copy-start(bf16[2,16,3584]{2,1,0:T(8,128)(2,1)} %param.7) | copy-start | bytes 688132
  10.7 8.8 %collective-permute-start = (bf16[2,16,3584]{2,1,0:T(8,128)(2,1)S(1)}, bf16[2,16,3584]{2,1,0:T(8,128)(2,1)S(1)}, u32[]{:S(2)}, u32[]{:S(2)}) collective-permute-start(bf16[2,16,3584]{2,1,0:T(8,128)(2,1)S(1)} %copy-done.3), channel_id=1, source_target_pairs={{0,4},{4,0},{1,5},{5,1},{2,6},{6,2},{3,7},{7,3},{8,12},{12,8},{9,1... | collective-permute-start | bytes 688136 | tf_op jit(solution)/shard_map/ppermute | solution.py:16
  19.6 10.6 %collective-permute-start.1 = (bf16[2,32,3584]{2,1,0:T(8,128)(2,1)S(1)}, bf16[2,32,3584]{2,1,0:T(8,128)(2,1)S(1)}, u32[]{:S(2)}, u32[]{:S(2)}) collective-permute-start(bf16[2,32,3584]{2,1,0:T(8,128)(2,1)S(1)} %maximum_select_fusion.2), channel_id=1, source_target_pairs={{0,2},{2,0},{1,3},{3,1},{4,6},{6,4},{5,7},{7,5},{8,10},{10,8},{9,1... | collective-permute-start | bytes 1376264 | tf_op jit(solution)/shard_map/ppermute | solution.py:16
  30.4 12.6 %collective-permute-start.2 = (bf16[2,64,3584]{2,1,0:T(8,128)(2,1)S(1)}, bf16[2,64,3584]{2,1,0:T(8,128)(2,1)}, u32[]{:S(2)}, u32[]{:S(2)}) collective-permute-start(bf16[2,64,3584]{2,1,0:T(8,128)(2,1)S(1)} %maximum_select_fusion.1), channel_id=1, source_target_pairs={{0,1},{1,0},{2,3},{3,2},{4,5},{5,4},{6,7},{7,6},{8,9},{9,8},{10,11... | collective-permute-start | bytes 2752520 | tf_op jit(solution)/shard_map/ppermute | solution.py:16
  32.9 37.8 %all-to-all-start.1 = ((bf16[128,2,3584]{2,1,0:T(2,128)(2,1)}), bf16[128,2,3584]{2,1,0:T(2,128)(2,1)S(1)}, u32[]{:S(2)}, u32[]{:S(2)}) async-start(bf16[128,2,3584]{2,1,0:T(2,128)(2,1)} %shard_map.75), calls=%async_computation.1 | async-start | bytes 3670016 | tf_op jit(solution)/shard_map/all_to_all | solution.py:184
  43.0 2.3 %copy-start.4 = (bf16[3,3584,128]{2,1,0:T(8,128)(2,1)S(1)}, bf16[3,3584,128]{2,1,0:T(8,128)(2,1)}, u32[]{:S(2)}) copy-start(bf16[3,3584,128]{2,1,0:T(8,128)(2,1)} %param.13) | copy-start | bytes 8257540
  70.7 1.2 copy-start.2
  71.9 32.9 %all-to-all-start = ((bf16[128,2,3584]{2,1,0:T(2,128)(2,1)}), bf16[128,2,3584]{2,1,0:T(2,128)(2,1)}, u32[]{:S(2)}, u32[]{:S(2)}) async-start(bf16[128,2,3584]{2,1,0:T(2,128)(2,1)} %shard_map.73), calls=%async_computation | async-start | bytes 3670016 | tf_op jit(solution)/shard_map/all_to_all | solution.py:184
  79.1 2.4 %copy-start = (f32[2,128,3584]{2,1,0:T(8,128)}, f32[2,128,3584]{2,1,0:T(8,128)S(1)}, u32[]{:S(2)}) copy-start(f32[2,128,3584]{2,1,0:T(8,128)S(1)} %fusion.4) | copy-start | bytes 11010052
  81.5 42.3 %collective-permute-start.3 = (f32[2,64,3584]{2,1,0:T(8,128)}, f32[2,64,3584]{2,1,0:T(8,128)}, u32[]{:S(2)}, u32[]{:S(2)}) collective-permute-start(f32[2,64,3584]{2,1,0:T(8,128)} %constant_dynamic-slice_fusion), channel_id=1, source_target_pairs={{0,1},{1,0},{2,3},{3,2},{4,5},{5,4},{6,7},{7,6},{8,9},{9,8},{10,11... | collective-permute-start | bytes 5505032 | tf_op jit(solution)/shard_map/ppermute | solution.py:16
  104.8 48.3 %all-to-all-start.2 = ((bf16[128,2,3584]{2,1,0:T(2,128)(2,1)}), bf16[128,2,3584]{2,1,0:T(2,128)(2,1)}, u32[]{:S(2)}, u32[]{:S(2)}) async-start(bf16[128,2,3584]{2,1,0:T(2,128)(2,1)} %shard_map.76), calls=%async_computation.2 | async-start | bytes 3670016 | tf_op jit(solution)/shard_map/all_to_all | solution.py:188
  110.2 13.6 %copy-start.1 = (f32[2,128,3584]{2,1,0:T(8,128)S(1)}, f32[2,128,3584]{2,1,0:T(8,128)}, u32[]{:S(2)}) copy-start(f32[2,128,3584]{2,1,0:T(8,128)} %copy-done) | copy-start | bytes 11010052
  125.7 12.6 %collective-permute-start.4 = (f32[16,3584]{1,0:T(8,128)S(1)}, f32[16,3584]{1,0:T(8,128)S(1)}, u32[]{:S(2)}, u32[]{:S(2)}) collective-permute-start(f32[16,3584]{1,0:T(8,128)S(1)} %dynamic-slice_bitcast_fusion.1), channel_id=1, source_target_pairs={{0,2},{1,3},{2,4},{3,5},{4,6},{5,7},{6,0},{7,1},{8,10},{9,11},{10,... | collective-permute-start | bytes 688136 | tf_op jit(solution)/shard_map/ppermute | solution.py:128
  127.2 11.2 %collective-permute-start.7 = (f32[16,3584]{1,0:T(8,128)S(1)}, f32[16,3584]{1,0:T(8,128)S(1)}, u32[]{:S(2)}, u32[]{:S(2)}) collective-permute-start(f32[16,3584]{1,0:T(8,128)S(1)} %dynamic-slice_bitcast_fusion), channel_id=1, source_target_pairs={{0,6},{1,7},{2,0},{3,1},{4,2},{5,3},{6,4},{7,5},{8,14},{9,15},{10,... | collective-permute-start | bytes 688136 | tf_op jit(solution)/shard_map/ppermute | solution.py:128
  138.3 7.8 %collective-permute-start.5 = (f32[16,3584]{1,0:T(8,128)S(1)}, f32[16,3584]{1,0:T(8,128)S(1)}, u32[]{:S(2)}, u32[]{:S(2)}) collective-permute-start(f32[16,3584]{1,0:T(8,128)S(1)} %bitcast_add_fusion.5), channel_id=1, source_target_pairs={{0,2},{1,3},{2,4},{3,5},{4,6},{5,7},{6,0},{7,1},{8,10},{9,11},{10,... | collective-permute-start | bytes 688136 | tf_op jit(solution)/shard_map/ppermute | solution.py:128
  138.4 7.8 %collective-permute-start.8 = (f32[16,3584]{1,0:T(8,128)S(1)}, f32[16,3584]{1,0:T(8,128)S(1)}, u32[]{:S(2)}, u32[]{:S(2)}) collective-permute-start(f32[16,3584]{1,0:T(8,128)S(1)} %bitcast_add_fusion.2), channel_id=1, source_target_pairs={{0,6},{1,7},{2,0},{3,1},{4,2},{5,3},{6,4},{7,5},{8,14},{9,15},{10,... | collective-permute-start | bytes 688136 | tf_op jit(solution)/shard_map/ppermute | solution.py:128
  146.1 6.9 %collective-permute-start.6 = (f32[16,3584]{1,0:T(8,128)S(1)}, f32[16,3584]{1,0:T(8,128)S(1)}, u32[]{:S(2)}, u32[]{:S(2)}) collective-permute-start(f32[16,3584]{1,0:T(8,128)S(1)} %bitcast_add_fusion.4), channel_id=1, source_target_pairs={{0,2},{1,3},{2,4},{3,5},{4,6},{5,7},{6,0},{7,1},{8,10},{9,11},{10,... | collective-permute-start | bytes 688136 | tf_op jit(solution)/shard_map/ppermute | solution.py:128
  146.2 6.8 %collective-permute-start.9 = (f32[16,3584]{1,0:T(8,128)S(1)}, f32[16,3584]{1,0:T(8,128)S(1)}, u32[]{:S(2)}, u32[]{:S(2)}) collective-permute-start(f32[16,3584]{1,0:T(8,128)S(1)} %bitcast_add_fusion.1), channel_id=1, source_target_pairs={{0,6},{1,7},{2,0},{3,1},{4,2},{5,3},{6,4},{7,5},{8,14},{9,15},{10,... | collective-permute-start | bytes 688136 | tf_op jit(solution)/shard_map/ppermute | solution.py:128
  153.1 11.6 %copy-start.5 = (f32[2,16,8]{1,2,0:T(8,128)S(1)}, f32[2,16,8]{1,2,0:T(8,128)}, u32[]{:S(2)}) copy-start(f32[2,16,8]{1,2,0:T(8,128)} %param.9) | copy-start | bytes 3076
  153.1 39.3 %all-to-all-start.3 = ((bf16[128,2,3584]{2,1,0:T(2,128)(2,1)}), bf16[128,2,3584]{2,1,0:T(2,128)(2,1)S(1)}, u32[]{:S(2)}, u32[]{:S(2)}) async-start(bf16[128,2,3584]{2,1,0:T(2,128)(2,1)} %shard_map.74), calls=%async_computation.3 | async-start | bytes 3670016 | tf_op jit(solution)/shard_map/all_to_all | solution.py:188

commit v14 on v7

--- a/solution.py
+++ b/solution.py
@@ -149,27 +149,22 @@
     device_count = lax.axis_size("ep")
     experts = w_gate.shape[0] * device_count
     capacity = max(2, row_count * top_count * 2 // experts)
-    payloads = []
-    combines = []
+    routed_steps = []
     for s in range(step_count):
         dispatch, combine = route_tables(expert_ids[s], combine_weights[s], experts, capacity)
-        payloads.append(dispatch_rows(dispatch, tokens[s], experts, capacity))
-        combines.append(combine)
-    routed_steps = []
-    for s in range(step_count):
-        received = lax.all_to_all(payloads[s], "ep", split_axis=0, concat_axis=0, tiled=True)
+        outgoing = dispatch_rows(dispatch, tokens[s], experts, capacity)
+        received = lax.all_to_all(outgoing, "ep", split_axis=0, concat_axis=0, tiled=True)
         expert_out = expert_rows(received, w_gate, w_up, w_down)
         returned = lax.all_to_all(expert_out, "ep", split_axis=0, concat_axis=0, tiled=True)
         routed_steps.append(
             jnp.einsum(
                 "tec,ecd->td",
-                combines[s].reshape(row_count, experts, capacity),
+                combine.reshape(row_count, experts, capacity),
                 returned.astype(jnp.float32),
                 precision=lax.Precision.HIGHEST,
             )
         )
-    later_tokens = lax.optimization_barrier((tokens, *payloads))[0]
-    shared = shared_expert(later_tokens, shared_weights)
+    shared = shared_expert(tokens, shared_weights)
     routed = jnp.stack(routed_steps)
     return (shared + routed).astype(jnp.bfloat16)
 

time: 183 us -> 178 us (0.973)
  waiting for transfers between devices: 81.1 us -> 75.7 us
  local copies, waits for them, and re-layouts: 9.71 us -> 7.21 us
    all_to_all x2, waiting for transfers between devices: 33.7 us -> 29.7 us  [shards(): lax.all_to_all(outgoing, 'ep', split_axis=0, concat_axis=0, tiled=True)]
  transfers between devices with their start and end apart: 10 -> 10, of which waited for: 8 -> 8; matrix products, arithmetic and copies ran while one was open for 8% -> 11% of each run, Pallas kernels for 15% -> 18%
where the time goes in v14:
time: 178 us; the launch traced here: 177 us
  waiting for transfers between devices  75.7 us (43%)
  starting transfers between devices  42.9 us (24%)
  Pallas kernels  32.6 us (18%)
  matrix products  9.42 us (5%)
  other arithmetic  8.92 us (5%)
  local copies, waits for them, and re-layouts  7.21 us (4%)
    ppermute x6, waiting for transfers between devices, partner_2(): return lax.ppermute(block, axis, route)  32.7 us
    all_to_all x2, waiting for transfers between devices, shards(): lax.all_to_all(outgoing, 'ep', split_axis=0, concat_axis=0, tiled=True)  29.7 us
    pallas_call x2, Pallas kernels, expert_rows(): pl.pallas_call(ffn_kernel, out_shape=jax.ShapeDtypeStruct(token_block.sha...  26.9 us
    ppermute x6, starting transfers between devices, partner_2(): return lax.ppermute(block, axis, route)  17.9 us
    all_to_all x2, starting transfers between devices, shards(): lax.all_to_all(outgoing, 'ep', split_axis=0, concat_axis=0, tiled=True)  15.3 us
    all_to_all x2, waiting for transfers between devices, shards(): lax.all_to_all(expert_out, 'ep', split_axis=0, concat_axis=0, tiled=True)  13.3 us
    all_to_all x2, starting transfers between devices, shards(): lax.all_to_all(expert_out, 'ep', split_axis=0, concat_axis=0, tiled=True)  9.7 us
    pallas_call x2, Pallas kernels, dispatch_rows(): pl.pallas_call(dispatch_kernel, out_shape=jax.ShapeDtypeStruct((experts,...  5.68 us
  transfers between devices with their start and end apart: 10, of which 8 were waited for; matrix products, arithmetic and copies ran while one was open for 11% of the time, Pallas kernels for 18%

profile of v14, /device:TPU:1, one launch (start us, length us, event | category | flops | bytes accessed | tf_op | source)
XLA Modules:
  0.0 177.0 jit_solution(17010942236398145927)
XLA Ops:
  0.0 3.7 %collective-permute-start = (bf16[2,16,3584]{2,1,0:T(8,128)(2,1)}, bf16[2,16,3584]{2,1,0:T(8,128)(2,1)S(1)}, u32[]{:S(2)}, u32[]{:S(2)}) collective-permute-start(bf16[2,16,3584]{2,1,0:T(8,128)(2,1)} %param.7), channel_id=1, source_target_pairs={{0,4},{4,0},{1,5},{5,1},{2,6},{6,2},{3,7},{7,3},{8,12},{12,8},{9,1... | collective-permute-start | bytes 688136 | tf_op jit(solution)/shard_map/ppermute | solution.py:16
  4.6 4.5 %collective-permute-done = bf16[2,16,3584]{2,1,0:T(8,128)(2,1)S(1)} collective-permute-done((bf16[2,16,3584]{2,1,0:T(8,128)(2,1)}, bf16[2,16,3584]{2,1,0:T(8,128)(2,1)S(1)}, u32[]{:S(2)}, u32[]{:S(2)}) %collective-permute-start) | collective-permute-done | bytes 229408 | tf_op jit(solution)/shard_map/ppermute | solution.py:16
  12.7 8.3 %collective-permute-done.1 = bf16[2,32,3584]{2,1,0:T(8,128)(2,1)S(1)} collective-permute-done((bf16[2,32,3584]{2,1,0:T(8,128)(2,1)S(1)}, bf16[2,32,3584]{2,1,0:T(8,128)(2,1)S(1)}, u32[]{:S(2)}, u32[]{:S(2)}) %collective-permute-start.1) | collective-permute-done | bytes 458784 | tf_op jit(solution)/shard_map/ppermute | solution.py:16
  21.1 2.4 %collective-permute-start.2 = (bf16[2,64,3584]{2,1,0:T(8,128)(2,1)S(1)}, bf16[2,64,3584]{2,1,0:T(8,128)(2,1)}, u32[]{:S(2)}, u32[]{:S(2)}) collective-permute-start(bf16[2,64,3584]{2,1,0:T(8,128)(2,1)S(1)} %maximum_select_fusion.1), channel_id=1, source_target_pairs={{0,1},{1,0},{2,3},{3,2},{4,5},{5,4},{6,7},{7,6},{8,9},{9,8},{10,11... | collective-permute-start | bytes 2752520 | tf_op jit(solution)/shard_map/ppermute | solution.py:16
  24.2 2.9 %shard_map.75 = bf16[128,2,3584]{2,1,0:T(2,128)(2,1)} custom-call(bf16[256,16]{1,0:T(8,128)(2,1)} %convolution_convert_fusion.select_ref, bf16[16,3584]{1,0:T(8,128)(2,1)} %get-tuple-element.6.token_ref), custom_call_target="tpu_custom_call" | custom-call | tf_op jit(solution)/shard_map/pallas_call | solution.py:75
  27.1 10.0 %all-to-all-start.2 = ((bf16[128,2,3584]{2,1,0:T(2,128)(2,1)}), bf16[128,2,3584]{2,1,0:T(2,128)(2,1)S(1)}, u32[]{:S(2)}, u32[]{:S(2)}) async-start(bf16[128,2,3584]{2,1,0:T(2,128)(2,1)} %shard_map.75), calls=%async_computation.2 | async-start | bytes 3670016 | tf_op jit(solution)/shard_map/all_to_all | solution.py:156
  37.5 2.0 %maximum_select_fusion = bf16[2,128,3584]{2,1,0:T(8,128)(2,1)S(1)} fusion(bf16[2,64,3584]{2,1,0:T(8,128)(2,1)S(1)} %maximum_select_fusion.1, bf16[2,64,3584]{2,1,0:T(8,128)(2,1)} %collective-permute-done.2, pred[]{:T(512)S(6)} %eq.95), kind=kLoop, calls=%fused_computation.2 | loop fusion | flops 8257536 | bytes 3670017 | tf_op jit(solution)/shard_map/jit(_where)/select_n | solution.py:115
  46.0 2.8 %shard_map.73 = bf16[128,2,3584]{2,1,0:T(2,128)(2,1)} custom-call(bf16[256,16]{1,0:T(8,128)(2,1)} %convolution_convert_fusion.1.select_ref, bf16[16,3584]{1,0:T(8,128)(2,1)} %get-tuple-element.5.token_ref), custom_call_target="tpu_custom_call" | custom-call | tf_op jit(solution)/shard_map/pallas_call | solution.py:75
  48.8 16.0 %all-to-all-done.2.x_ref = bf16[128,2,3584]{2,1,0:T(2,128)(2,1)S(1)} async-done(((bf16[128,2,3584]{2,1,0:T(2,128)(2,1)}), bf16[128,2,3584]{2,1,0:T(2,128)(2,1)S(1)}, u32[]{:S(2)}, u32[]{:S(2)}) %all-to-all-start.2) | async-done | bytes 1835040 | tf_op jit(solution)/shard_map/all_to_all | solution.py:156
  66.0 5.3 %all-to-all-start = ((bf16[128,2,3584]{2,1,0:T(2,128)(2,1)}), bf16[128,2,3584]{2,1,0:T(2,128)(2,1)}, u32[]{:S(2)}, u32[]{:S(2)}) async-start(bf16[128,2,3584]{2,1,0:T(2,128)(2,1)} %shard_map.73), calls=%async_computation | async-start | bytes 3670016 | tf_op jit(solution)/shard_map/all_to_all | solution.py:156
  71.7 13.5 %shard_map.76 = bf16[128,2,3584]{2,1,0:T(2,128)(2,1)} custom-call(bf16[128,2,3584]{2,1,0:T(2,128)(2,1)} %copy-done.1, bf16[1,3584,1024]{2,1,0:T(8,128)(2,1)} %gate_ref.3, bf16[1,3584,1024]{2,1,0:T(8,128)(2,1)} %up_ref.3, bf16[1,1024,3584]{2,1,0:T(8,128)(2,1)} %down_ref.3), custom_call_target="tpu_custom_call" | custom-call | flops 5637144576 | bytes 25690112 | tf_op jit(solution)/shard_map/pallas_call | solution.py:45
  85.2 13.7 %all-to-all-done.x_ref = bf16[128,2,3584]{2,1,0:T(2,128)(2,1)} async-done(((bf16[128,2,3584]{2,1,0:T(2,128)(2,1)}), bf16[128,2,3584]{2,1,0:T(2,128)(2,1)}, u32[]{:S(2)}, u32[]{:S(2)}) %all-to-all-start) | async-done | bytes 1835040 | tf_op jit(solution)/shard_map/all_to_all | solution.py:156
  98.9 4.3 %all-to-all-start.3 = ((bf16[128,2,3584]{2,1,0:T(2,128)(2,1)}), bf16[128,2,3584]{2,1,0:T(2,128)(2,1)S(1)}, u32[]{:S(2)}, u32[]{:S(2)}) async-start(bf16[128,2,3584]{2,1,0:T(2,128)(2,1)} %shard_map.76), calls=%async_computation.3 | async-start | bytes 3670016 | tf_op jit(solution)/shard_map/all_to_all | solution.py:158
  103.3 2.3 %dynamic-slice_add_fusion = f32[2,64,3584]{2,1,0:T(8,128)S(1)} fusion(f32[2,64,3584]{2,1,0:T(8,128)} %collective-permute-done.3, f32[2,128,3584]{2,1,0:T(8,128)} %copy-done, s32[]{:T(128)S(6)} %select_n.79), kind=kLoop, calls=%fused_computation.5 | loop fusion | flops 458752 | bytes 5505028 | tf_op jit(solution)/shard_map/add | solution.py:142
  106.8 1.7 collective-permute-start.4
  109.6 13.5 %shard_map.74 = bf16[128,2,3584]{2,1,0:T(2,128)(2,1)} custom-call(bf16[128,2,3584]{2,1,0:T(2,128)(2,1)} %all-to-all-done.x_ref, bf16[1,3584,1024]{2,1,0:T(8,128)(2,1)} %gate_ref.3, bf16[1,3584,1024]{2,1,0:T(8,128)(2,1)} %up_ref.3, bf16[1,1024,3584]{2,1,0:T(8,128)(2,1)} %down_ref.3), custom_call_target="tpu_custom_call" | custom-call | flops 5637144576 | bytes 25690112 | tf_op jit(solution)/shard_map/pallas_call | solution.py:45
  123.0 8.1 %all-to-all-done.3 = bf16[128,2,3584]{2,1,0:T(2,128)(2,1)S(1)} async-done(((bf16[128,2,3584]{2,1,0:T(2,128)(2,1)}), bf16[128,2,3584]{2,1,0:T(2,128)(2,1)S(1)}, u32[]{:S(2)}, u32[]{:S(2)}) %all-to-all-start.3) | async-done | bytes 1835040 | tf_op jit(solution)/shard_map/all_to_all | solution.py:158
  131.1 5.4 %all-to-all-start.1 = ((bf16[128,2,3584]{2,1,0:T(2,128)(2,1)}), bf16[128,2,3584]{2,1,0:T(2,128)(2,1)}, u32[]{:S(2)}, u32[]{:S(2)}) async-start(bf16[128,2,3584]{2,1,0:T(2,128)(2,1)} %shard_map.74), calls=%async_computation.1 | async-start | bytes 3670016 | tf_op jit(solution)/shard_map/all_to_all | solution.py:158
  137.5 16.1 %collective-permute-done.4 = f32[2,32,3584]{2,1,0:T(8,128)} collective-permute-done((f32[2,32,3584]{2,1,0:T(8,128)S(1)}, f32[2,32,3584]{2,1,0:T(8,128)}, u32[]{:S(2)}, u32[]{:S(2)}) %collective-permute-start.4) | collective-permute-done | bytes 917536 | tf_op jit(solution)/shard_map/ppermute | solution.py:16
  155.2 7.7 %collective-permute-start.5 = (f32[2,16,3584]{2,1,0:T(8,128)S(1)}, f32[2,16,3584]{2,1,0:T(8,128)}, u32[]{:S(2)}, u32[]{:S(2)}) collective-permute-start(f32[2,16,3584]{2,1,0:T(8,128)S(1)} %constant_dynamic-slice_fusion), channel_id=1, source_target_pairs={{0,4},{4,0},{1,5},{5,1},{2,6},{6,2},{3,7},{7,3},{8,12},{12,8},{9,1... | collective-permute-start | bytes 1376264 | tf_op jit(solution)/shard_map/ppermute | solution.py:16
  163.8 5.2 %all-to-all-done.1 = bf16[128,2,3584]{2,1,0:T(2,128)(2,1)} async-done(((bf16[128,2,3584]{2,1,0:T(2,128)(2,1)}), bf16[128,2,3584]{2,1,0:T(2,128)(2,1)}, u32[]{:S(2)}, u32[]{:S(2)}) %all-to-all-start.1) | async-done | bytes 1835040 | tf_op jit(solution)/shard_map/all_to_all | solution.py:158
  169.0 2.5 %convolution_bitcast_fusion.1 = f32[1,16,3584]{2,1,0:T(8,128)S(1)} fusion(bf16[128,2,3584]{2,1,0:T(2,128)(2,1)} %all-to-all-done.1, f32[16,128,2]{0,2,1:T(2,128)} %bitcast.32), kind=kOutput, calls=%fused_computation.1 | convolution fusion | flops 176160768 | bytes 2080768 | tf_op jit(solution)/shard_map/tec,ecd->td/dot_general | solution.py:160
  171.5 3.7 %collective-permute-done.5 = f32[2,16,3584]{2,1,0:T(8,128)} collective-permute-done((f32[2,16,3584]{2,1,0:T(8,128)S(1)}, f32[2,16,3584]{2,1,0:T(8,128)}, u32[]{:S(2)}, u32[]{:S(2)}) %collective-permute-start.5) | collective-permute-done | bytes 458784 | tf_op jit(solution)/shard_map/ppermute | solution.py:16
  175.2 1.8 %fusion.13 = bf16[2,16,3584]{2,1,0:T(8,128)(2,1)} fusion(f32[1,16,3584]{2,1,0:T(8,128)S(1)} %convolution_bitcast_fusion, f32[1,16,3584]{2,1,0:T(8,128)S(1)} %convolution_bitcast_fusion.1, f32[2,16,3584]{2,1,0:T(8,128)} %collective-permute-done.5, f32[2,32,3584]{2,1,0:T(8,128)S(1)} %dynamic-slice_add_fusion.1, s32[]{:T(128)S(6)} %select_n.83), kind=kLoop, calls=%fused_computation.25 | loop fusion | flops 458752 | bytes 1605636 | tf_op jit(solution)/shard_map/convert_element_type | solution.py:169
  (47 shorter events, 19.4 us)
Async XLA Ops:
  0.0 23.5 %copy-start.3 = (bf16[2,16,3584]{2,1,0:T(8,128)(2,1)S(1)}, bf16[2,16,3584]{2,1,0:T(8,128)(2,1)}, u32[]{:S(2)}) copy-start(bf16[2,16,3584]{2,1,0:T(8,128)(2,1)} %param.7) | copy-start | bytes 688132
  0.0 9.1 %collective-permute-start = (bf16[2,16,3584]{2,1,0:T(8,128)(2,1)}, bf16[2,16,3584]{2,1,0:T(8,128)(2,1)S(1)}, u32[]{:S(2)}, u32[]{:S(2)}) collective-permute-start(bf16[2,16,3584]{2,1,0:T(8,128)(2,1)} %param.7), channel_id=1, source_target_pairs={{0,4},{4,0},{1,5},{5,1},{2,6},{6,2},{3,7},{7,3},{8,12},{12,8},{9,1... | collective-permute-start | bytes 688136 | tf_op jit(solution)/shard_map/ppermute | solution.py:16
  10.3 10.7 %collective-permute-start.1 = (bf16[2,32,3584]{2,1,0:T(8,128)(2,1)S(1)}, bf16[2,32,3584]{2,1,0:T(8,128)(2,1)S(1)}, u32[]{:S(2)}, u32[]{:S(2)}) collective-permute-start(bf16[2,32,3584]{2,1,0:T(8,128)(2,1)S(1)} %maximum_select_fusion.2), channel_id=1, source_target_pairs={{0,2},{2,0},{1,3},{3,1},{4,6},{6,4},{5,7},{7,5},{8,10},{10,8},{9,1... | collective-permute-start | bytes 1376264 | tf_op jit(solution)/shard_map/ppermute | solution.py:16
  21.1 16.3 %collective-permute-start.2 = (bf16[2,64,3584]{2,1,0:T(8,128)(2,1)S(1)}, bf16[2,64,3584]{2,1,0:T(8,128)(2,1)}, u32[]{:S(2)}, u32[]{:S(2)}) collective-permute-start(bf16[2,64,3584]{2,1,0:T(8,128)(2,1)S(1)} %maximum_select_fusion.1), channel_id=1, source_target_pairs={{0,1},{1,0},{2,3},{3,2},{4,5},{5,4},{6,7},{7,6},{8,9},{9,8},{10,11... | collective-permute-start | bytes 2752520 | tf_op jit(solution)/shard_map/ppermute | solution.py:16
  27.1 37.7 %all-to-all-start.2 = ((bf16[128,2,3584]{2,1,0:T(2,128)(2,1)}), bf16[128,2,3584]{2,1,0:T(2,128)(2,1)S(1)}, u32[]{:S(2)}, u32[]{:S(2)}) async-start(bf16[128,2,3584]{2,1,0:T(2,128)(2,1)} %shard_map.75), calls=%async_computation.2 | async-start | bytes 3670016 | tf_op jit(solution)/shard_map/all_to_all | solution.py:156
  37.4 2.3 %copy-start.4 = (bf16[3,3584,128]{2,1,0:T(8,128)(2,1)S(1)}, bf16[3,3584,128]{2,1,0:T(8,128)(2,1)}, u32[]{:S(2)}) copy-start(bf16[3,3584,128]{2,1,0:T(8,128)(2,1)} %param.13) | copy-start | bytes 8257540
  41.7 2.4 %copy-start = (f32[2,128,3584]{2,1,0:T(8,128)}, f32[2,128,3584]{2,1,0:T(8,128)S(1)}, u32[]{:S(2)}) copy-start(f32[2,128,3584]{2,1,0:T(8,128)S(1)} %fusion.4) | copy-start | bytes 11010052
  44.0 59.2 %collective-permute-start.3 = (f32[2,64,3584]{2,1,0:T(8,128)}, f32[2,64,3584]{2,1,0:T(8,128)}, u32[]{:S(2)}, u32[]{:S(2)}) collective-permute-start(f32[2,64,3584]{2,1,0:T(8,128)} %constant_dynamic-slice_fusion.2), channel_id=1, source_target_pairs={{0,1},{1,0},{2,3},{3,2},{4,5},{5,4},{6,7},{7,6},{8,9},{9,8},{10,11... | collective-permute-start | bytes 5505032 | tf_op jit(solution)/shard_map/ppermute | solution.py:16
  48.8 22.5 %copy-start.6 = (f32[2,16,8]{1,2,0:T(8,128)S(1)}, f32[2,16,8]{1,2,0:T(8,128)}, u32[]{:S(2)}) copy-start(f32[2,16,8]{1,2,0:T(8,128)} %param.9) | copy-start | bytes 3076
  64.8 1.2 copy-start.1
  66.0 32.9 %all-to-all-start = ((bf16[128,2,3584]{2,1,0:T(2,128)(2,1)}), bf16[128,2,3584]{2,1,0:T(2,128)(2,1)}, u32[]{:S(2)}, u32[]{:S(2)}) async-start(bf16[128,2,3584]{2,1,0:T(2,128)(2,1)} %shard_map.73), calls=%async_computation | async-start | bytes 3670016 | tf_op jit(solution)/shard_map/all_to_all | solution.py:156
  98.9 32.2 %all-to-all-start.3 = ((bf16[128,2,3584]{2,1,0:T(2,128)(2,1)}), bf16[128,2,3584]{2,1,0:T(2,128)(2,1)S(1)}, u32[]{:S(2)}, u32[]{:S(2)}) async-start(bf16[128,2,3584]{2,1,0:T(2,128)(2,1)} %shard_map.76), calls=%async_computation.3 | async-start | bytes 3670016 | tf_op jit(solution)/shard_map/all_to_all | solution.py:158
  105.6 1.2 copy-start.2
  106.8 46.8 %collective-permute-start.4 = (f32[2,32,3584]{2,1,0:T(8,128)S(1)}, f32[2,32,3584]{2,1,0:T(8,128)}, u32[]{:S(2)}, u32[]{:S(2)}) collective-permute-start(f32[2,32,3584]{2,1,0:T(8,128)S(1)} %constant_dynamic-slice_fusion.1), channel_id=1, source_target_pairs={{0,2},{2,0},{1,3},{3,1},{4,6},{6,4},{5,7},{7,5},{8,10},{10,8},{9,1... | collective-permute-start | bytes 2752520 | tf_op jit(solution)/shard_map/ppermute | solution.py:16
  131.1 37.9 %all-to-all-start.1 = ((bf16[128,2,3584]{2,1,0:T(2,128)(2,1)}), bf16[128,2,3584]{2,1,0:T(2,128)(2,1)}, u32[]{:S(2)}, u32[]{:S(2)}) async-start(bf16[128,2,3584]{2,1,0:T(2,128)(2,1)} %shard_map.74), calls=%async_computation.1 | async-start | bytes 3670016 | tf_op jit(solution)/shard_map/all_to_all | solution.py:158
  137.5 25.4 %copy-start.5 = (f32[16,256]{0,1:T(8,128)S(1)}, f32[16,256]{0,1:T(8,128)}, u32[]{:S(2)}) copy-start(f32[16,256]{0,1:T(8,128)} %fusion.16) | copy-start | bytes 49156
  155.2 20.0 %collective-permute-start.5 = (f32[2,16,3584]{2,1,0:T(8,128)S(1)}, f32[2,16,3584]{2,1,0:T(8,128)}, u32[]{:S(2)}, u32[]{:S(2)}) collective-permute-start(f32[2,16,3584]{2,1,0:T(8,128)S(1)} %constant_dynamic-slice_fusion), channel_id=1, source_target_pairs={{0,4},{4,0},{1,5},{5,1},{2,6},{6,2},{3,7},{7,3},{8,12},{12,8},{9,1... | collective-permute-start | bytes 1376264 | tf_op jit(solution)/shard_map/ppermute | solution.py:16

commit v15 on v14

--- a/solution.py
+++ b/solution.py
@@ -119,13 +119,15 @@
     )
 
 
-def shared_expert(tokens, shared_weights):
-    my_index = lax.axis_index("ep")
+def xor_partner(block, mask):
+    count = lax.axis_size("ep")
+    return lax.ppermute(block, "ep", [(low, low ^ mask) for low in range(count)])
+
+
+def shared_expert(tokens, shared_weights, group=8):
     step_count, row_count, model_width = tokens.shape
-    gathered = tokens
-    for level in (2, 1, 0):
-        partner = partner_2(gathered, "ep", level)
-        gathered = join_halves(gathered, partner, my_index >> level & 1 == 1, 1)
+    pieces = [tokens] + [xor_partner(tokens, mask) for mask in range(1, group)]
+    gathered = jnp.concatenate(pieces, axis=1)
     flat_rows = gathered.reshape(-1, model_width)
     gate_val = jnp.dot(flat_rows, shared_weights[0], preferred_element_type=jnp.float32)
     up_val = jnp.dot(flat_rows, shared_weights[1], preferred_element_type=jnp.float32)
@@ -133,14 +135,14 @@
     partial_value = lax.dot_general(
         hidden, shared_weights[2], (((1,), (1,)), ((), ())), preferred_element_type=jnp.float32
     )
-    partial_value = partial_value.reshape(step_count, 8 * row_count, model_width)
-    for level in (0, 1, 2):
-        half = partial_value.shape[1] // 2
-        bit = my_index >> level & 1
-        keep = lax.dynamic_slice_in_dim(partial_value, bit * half, half, 1)
-        send = lax.dynamic_slice_in_dim(partial_value, (1 - bit) * half, half, 1)
-        partial_value = keep + partner_2(send, "ep", level)
-    return partial_value
+    partial_value = partial_value.reshape(step_count, group, row_count, model_width)
+    level = 0
+    while partial_value.shape[1] > 1:
+        keep = partial_value[:, 0::2]
+        send = partial_value[:, 1::2]
+        partial_value = keep + xor_partner(send, 1 << level)
+        level += 1
+    return partial_value[:, 0]
 
 
 def shards(tokens, expert_ids, combine_weights, w_gate, w_up, w_down, shared_weights):

time: 178 us -> 173 us (0.972)
  waiting for transfers between devices: 75.7 us -> 66.2 us
  starting transfers between devices: 42.9 us -> 49.4 us
  other arithmetic: 8.92 us -> 5.59 us
    all_to_all x2, waiting for transfers between devices: 29.7 us -> 8.61 us  [shards(): lax.all_to_all(outgoing, 'ep', split_axis=0, concat_axis=0, tiled=True)]
    ppermute x6 -> x10, waiting for transfers between devices: 32.7 us -> 43.3 us  [xor_partner(): lax.ppermute(block, 'ep', [(low, low ^ mask) for low in range(count)])]
    all_to_all x2, starting transfers between devices: 15.3 us -> 18.7 us  [shards(): lax.all_to_all(outgoing, 'ep', split_axis=0, concat_axis=0, tiled=True)]
    select_n x3 -> x0, other arithmetic: 3.33 us -> none  [join_halves(): jnp.where(upper_side, jnp.concatenate([partner, mine], axis=axis_no), jnp...]
    ppermute x6 -> x10, starting transfers between devices: 17.9 us -> 21.1 us  [xor_partner(): lax.ppermute(block, 'ep', [(low, low ^ mask) for low in range(count)])]
  transfers between devices with their start and end apart: 10 -> 14, of which waited for: 8 -> 7; matrix products, arithmetic and copies ran while one was open for 11% -> 11% of each run, Pallas kernels for 18% -> 19%
where the time goes in v15:
time: 173 us; the launch traced here: 172 us
  waiting for transfers between devices  66.2 us (38%)
  starting transfers between devices  49.4 us (29%)
  Pallas kernels  32.7 us (19%)
  matrix products  9.98 us (6%)
  local copies, waits for them, and re-layouts  8.09 us (5%)
  other arithmetic  5.59 us (3%)
    ppermute x10, waiting for transfers between devices, xor_partner(): lax.ppermute(block, 'ep', [(low, low ^ mask) for low in range(count)])  43.3 us
    pallas_call x2, Pallas kernels, expert_rows(): pl.pallas_call(ffn_kernel, out_shape=jax.ShapeDtypeStruct(token_block.sha...  27 us
    ppermute x10, starting transfers between devices, xor_partner(): lax.ppermute(block, 'ep', [(low, low ^ mask) for low in range(count)])  21.1 us
    all_to_all x2, starting transfers between devices, shards(): lax.all_to_all(outgoing, 'ep', split_axis=0, concat_axis=0, tiled=True)  18.7 us
    all_to_all x2, waiting for transfers between devices, shards(): lax.all_to_all(expert_out, 'ep', split_axis=0, concat_axis=0, tiled=True)  14.3 us
    all_to_all x2, starting transfers between devices, shards(): lax.all_to_all(expert_out, 'ep', split_axis=0, concat_axis=0, tiled=True)  9.7 us
    all_to_all x2, waiting for transfers between devices, shards(): lax.all_to_all(outgoing, 'ep', split_axis=0, concat_axis=0, tiled=True)  8.61 us
    pallas_call x2, Pallas kernels, dispatch_rows(): pl.pallas_call(dispatch_kernel, out_shape=jax.ShapeDtypeStruct((experts,...  5.69 us
  transfers between devices with their start and end apart: 14, of which 7 were waited for; matrix products, arithmetic and copies ran while one was open for 11% of the time, Pallas kernels for 19%

profile of v15, /device:TPU:1, one launch (start us, length us, event | category | flops | bytes accessed | tf_op | source)
XLA Modules:
  0.0 172.2 jit_solution(1736492938259427778)
XLA Ops:
  3.1 3.0 %collective-permute-start.3 = (bf16[2,16,3584]{2,1,0:T(8,128)(2,1)}, bf16[2,16,3584]{2,1,0:T(8,128)(2,1)S(1)}, u32[]{:S(2)}, u32[]{:S(2)}) collective-permute-start(bf16[2,16,3584]{2,1,0:T(8,128)(2,1)} %param.7), channel_id=1, source_target_pairs={{0,4},{1,5},{2,6},{3,7},{4,0},{5,1},{6,2},{7,3},{8,12},{9,13},{10,... | collective-permute-start | bytes 688136 | tf_op jit(solution)/shard_map/ppermute | solution.py:124
  6.4 1.7 slice_bitcast_fusion.1
  10.1 2.8 %shard_map.75 = bf16[128,2,3584]{2,1,0:T(2,128)(2,1)} custom-call(bf16[256,16]{1,0:T(8,128)(2,1)} %convolution_convert_fusion.select_ref, bf16[16,3584]{1,0:T(8,128)(2,1)} %get-tuple-element.6.token_ref), custom_call_target="tpu_custom_call" | custom-call | tf_op jit(solution)/shard_map/pallas_call | solution.py:75
  12.9 10.2 %all-to-all-start.2 = ((bf16[128,2,3584]{2,1,0:T(2,128)(2,1)}), bf16[128,2,3584]{2,1,0:T(2,128)(2,1)S(1)}, u32[]{:S(2)}, u32[]{:S(2)}) async-start(bf16[128,2,3584]{2,1,0:T(2,128)(2,1)} %shard_map.75), calls=%async_computation.2 | async-start | bytes 3670016 | tf_op jit(solution)/shard_map/all_to_all | solution.py:158
  24.4 2.9 %shard_map.73 = bf16[128,2,3584]{2,1,0:T(2,128)(2,1)} custom-call(bf16[256,16]{1,0:T(8,128)(2,1)} %convolution_convert_fusion.1.select_ref, bf16[16,3584]{1,0:T(8,128)(2,1)} %get-tuple-element.5.token_ref), custom_call_target="tpu_custom_call" | custom-call | tf_op jit(solution)/shard_map/pallas_call | solution.py:75
  27.3 2.7 %collective-permute-start.5 = (bf16[2,16,3584]{2,1,0:T(8,128)(2,1)S(1)}, bf16[2,16,3584]{2,1,0:T(8,128)(2,1)S(1)}, u32[]{:S(2)}, u32[]{:S(2)}) collective-permute-start(bf16[2,16,3584]{2,1,0:T(8,128)(2,1)S(1)} %copy-done.3), channel_id=1, source_target_pairs={{0,6},{1,7},{2,4},{3,5},{4,2},{5,3},{6,0},{7,1},{8,14},{9,15},{10,... | collective-permute-start | bytes 688136 | tf_op jit(solution)/shard_map/ppermute | solution.py:124
  31.5 19.2 %collective-permute-done.5 = bf16[2,16,3584]{2,1,0:T(8,128)(2,1)S(1)} collective-permute-done((bf16[2,16,3584]{2,1,0:T(8,128)(2,1)S(1)}, bf16[2,16,3584]{2,1,0:T(8,128)(2,1)S(1)}, u32[]{:S(2)}, u32[]{:S(2)}) %collective-permute-start.5) | collective-permute-done | bytes 229408 | tf_op jit(solution)/shard_map/ppermute | solution.py:124
  50.7 5.0 %collective-permute-done.6 = bf16[2,16,3584]{2,1,0:T(8,128)(2,1)S(1)} collective-permute-done((bf16[2,16,3584]{2,1,0:T(8,128)(2,1)S(1)}, bf16[2,16,3584]{2,1,0:T(8,128)(2,1)S(1)}, u32[]{:S(2)}, u32[]{:S(2)}) %collective-permute-start.6) | collective-permute-done | bytes 229408 | tf_op jit(solution)/shard_map/ppermute | solution.py:124
  58.3 8.5 %all-to-all-start = ((bf16[128,2,3584]{2,1,0:T(2,128)(2,1)}), bf16[128,2,3584]{2,1,0:T(2,128)(2,1)}, u32[]{:S(2)}, u32[]{:S(2)}) async-start(bf16[128,2,3584]{2,1,0:T(2,128)(2,1)} %shard_map.73), calls=%async_computation | async-start | bytes 3670016 | tf_op jit(solution)/shard_map/all_to_all | solution.py:158
  66.8 1.8 %fusion.4 = f32[2,8,16,3584]{3,2,1,0:T(8,128)S(1)} fusion(bf16[2,8,16,128]{3,2,1,0:T(8,128)(2,1)S(1)} %bitcast.40, bf16[3,3584,128]{2,1,0:T(8,128)(2,1)} %param.13), kind=kOutput, calls=%fused_computation.11 | convolution fusion | flops 234881024 | bytes 4653056 | tf_op jit(solution)/shard_map/dot_general | solution.py:135
  72.1 13.5 %shard_map.76 = bf16[128,2,3584]{2,1,0:T(2,128)(2,1)} custom-call(bf16[128,2,3584]{2,1,0:T(2,128)(2,1)} %copy-done.1, bf16[1,3584,1024]{2,1,0:T(8,128)(2,1)} %gate_ref.3, bf16[1,3584,1024]{2,1,0:T(8,128)(2,1)} %up_ref.3, bf16[1,1024,3584]{2,1,0:T(8,128)(2,1)} %down_ref.3), custom_call_target="tpu_custom_call" | custom-call | flops 5637144576 | bytes 25690112 | tf_op jit(solution)/shard_map/pallas_call | solution.py:45
  85.6 8.6 %all-to-all-done.x_ref = bf16[128,2,3584]{2,1,0:T(2,128)(2,1)} async-done(((bf16[128,2,3584]{2,1,0:T(2,128)(2,1)}), bf16[128,2,3584]{2,1,0:T(2,128)(2,1)}, u32[]{:S(2)}, u32[]{:S(2)}) %all-to-all-start) | async-done | bytes 1835040 | tf_op jit(solution)/shard_map/all_to_all | solution.py:158
  94.2 4.3 %all-to-all-start.3 = ((bf16[128,2,3584]{2,1,0:T(2,128)(2,1)}), bf16[128,2,3584]{2,1,0:T(2,128)(2,1)S(1)}, u32[]{:S(2)}, u32[]{:S(2)}) async-start(bf16[128,2,3584]{2,1,0:T(2,128)(2,1)} %shard_map.76), calls=%async_computation.3 | async-start | bytes 3670016 | tf_op jit(solution)/shard_map/all_to_all | solution.py:160
  98.6 2.3 %slice_add_fusion = f32[2,4,16,3584]{3,2,1,0:T(8,128)S(1)} fusion(f32[2,4,16,3584]{3,2,1,0:T(8,128)} %collective-permute-done.7, f32[2,8,16,3584]{3,2,1,0:T(8,128)} %copy-done), kind=kLoop, calls=%fused_computation.4 | loop fusion | flops 458752 | bytes 5505024 | tf_op jit(solution)/shard_map/add | solution.py:143
  102.1 1.7 collective-permute-start.8
  103.8 13.5 %shard_map.74 = bf16[128,2,3584]{2,1,0:T(2,128)(2,1)} custom-call(bf16[128,2,3584]{2,1,0:T(2,128)(2,1)} %all-to-all-done.x_ref, bf16[1,3584,1024]{2,1,0:T(8,128)(2,1)} %gate_ref.3, bf16[1,3584,1024]{2,1,0:T(8,128)(2,1)} %up_ref.3, bf16[1,1024,3584]{2,1,0:T(8,128)(2,1)} %down_ref.3), custom_call_target="tpu_custom_call" | custom-call | flops 5637144576 | bytes 25690112 | tf_op jit(solution)/shard_map/pallas_call | solution.py:45
  117.3 9.1 %all-to-all-done.3 = bf16[128,2,3584]{2,1,0:T(2,128)(2,1)S(1)} async-done(((bf16[128,2,3584]{2,1,0:T(2,128)(2,1)}), bf16[128,2,3584]{2,1,0:T(2,128)(2,1)S(1)}, u32[]{:S(2)}, u32[]{:S(2)}) %all-to-all-start.3) | async-done | bytes 1835040 | tf_op jit(solution)/shard_map/all_to_all | solution.py:160
  126.4 5.4 %all-to-all-start.1 = ((bf16[128,2,3584]{2,1,0:T(2,128)(2,1)}), bf16[128,2,3584]{2,1,0:T(2,128)(2,1)}, u32[]{:S(2)}, u32[]{:S(2)}) async-start(bf16[128,2,3584]{2,1,0:T(2,128)(2,1)} %shard_map.74), calls=%async_computation.1 | async-start | bytes 3670016 | tf_op jit(solution)/shard_map/all_to_all | solution.py:160
  133.5 15.4 %collective-permute-done.8 = f32[2,2,16,3584]{3,2,1,0:T(8,128)} collective-permute-done((f32[2,2,16,3584]{3,2,1,0:T(8,128)S(1)}, f32[2,2,16,3584]{3,2,1,0:T(8,128)}, u32[]{:S(2)}, u32[]{:S(2)}) %collective-permute-start.8) | collective-permute-done | bytes 917536 | tf_op jit(solution)/shard_map/ppermute | solution.py:124
  150.5 7.7 %collective-permute-start.9 = (f32[2,1,16,3584]{3,2,1,0:T(8,128)S(1)}, f32[2,1,16,3584]{3,2,1,0:T(8,128)}, u32[]{:S(2)}, u32[]{:S(2)}) collective-permute-start(f32[2,1,16,3584]{3,2,1,0:T(8,128)S(1)} %slice.63), channel_id=1, source_target_pairs={{0,4},{1,5},{2,6},{3,7},{4,0},{5,1},{6,2},{7,3},{8,12},{9,13},{10,... | collective-permute-start | bytes 1376264 | tf_op jit(solution)/shard_map/ppermute | solution.py:124
  159.1 5.2 %all-to-all-done.1 = bf16[128,2,3584]{2,1,0:T(2,128)(2,1)} async-done(((bf16[128,2,3584]{2,1,0:T(2,128)(2,1)}), bf16[128,2,3584]{2,1,0:T(2,128)(2,1)}, u32[]{:S(2)}, u32[]{:S(2)}) %all-to-all-start.1) | async-done | bytes 1835040 | tf_op jit(solution)/shard_map/all_to_all | solution.py:160
  164.3 2.5 %convolution_bitcast_fusion.1 = f32[1,16,3584]{2,1,0:T(8,128)S(1)} fusion(bf16[128,2,3584]{2,1,0:T(2,128)(2,1)} %all-to-all-done.1, f32[16,128,2]{0,2,1:T(2,128)} %bitcast.38), kind=kOutput, calls=%fused_computation.1 | convolution fusion | flops 176160768 | bytes 2080768 | tf_op jit(solution)/shard_map/tec,ecd->td/dot_general | solution.py:162
  166.7 3.7 %collective-permute-done.9 = f32[2,1,16,3584]{3,2,1,0:T(8,128)} collective-permute-done((f32[2,1,16,3584]{3,2,1,0:T(8,128)S(1)}, f32[2,1,16,3584]{3,2,1,0:T(8,128)}, u32[]{:S(2)}, u32[]{:S(2)}) %collective-permute-start.9) | collective-permute-done | bytes 458784 | tf_op jit(solution)/shard_map/ppermute | solution.py:124
  170.5 1.8 %fusion.15 = bf16[2,16,3584]{2,1,0:T(8,128)(2,1)} fusion(f32[2,1,16,3584]{3,2,1,0:T(8,128)} %collective-permute-done.9, f32[2,2,16,3584]{3,2,1,0:T(8,128)S(1)} %slice_add_fusion.1, f32[1,16,3584]{2,1,0:T(8,128)S(1)} %convolution_bitcast_fusion, f32[1,16,3584]{2,1,0:T(8,128)S(1)} %convolution_bitcast_fusion.1), kind=kLoop, calls=%fused_computation.24 | loop fusion | flops 458752 | bytes 1605632 | tf_op jit(solution)/shard_map/convert_element_type | solution.py:171
  (58 shorter events, 19.6 us)
Async XLA Ops:
  0.0 27.3 %collective-permute-start = (bf16[2,16,3584]{2,1,0:T(8,128)(2,1)}, bf16[2,16,3584]{2,1,0:T(8,128)(2,1)S(1)}, u32[]{:S(2)}, u32[]{:S(2)}) collective-permute-start(bf16[2,16,3584]{2,1,0:T(8,128)(2,1)} %param.7), channel_id=1, source_target_pairs={{0,1},{1,0},{2,3},{3,2},{4,5},{5,4},{6,7},{7,6},{8,9},{9,8},{10,11... | collective-permute-start | bytes 688136 | tf_op jit(solution)/shard_map/ppermute | solution.py:124
  1.4 28.6 %collective-permute-start.1 = (bf16[2,16,3584]{2,1,0:T(8,128)(2,1)}, bf16[2,16,3584]{2,1,0:T(8,128)(2,1)S(1)}, u32[]{:S(2)}, u32[]{:S(2)}) collective-permute-start(bf16[2,16,3584]{2,1,0:T(8,128)(2,1)} %param.7), channel_id=1, source_target_pairs={{0,2},{1,3},{2,0},{3,1},{4,6},{5,7},{6,4},{7,5},{8,10},{9,11},{10,... | collective-permute-start | bytes 688136 | tf_op jit(solution)/shard_map/ppermute | solution.py:124
  2.8 28.6 %collective-permute-start.2 = (bf16[2,16,3584]{2,1,0:T(8,128)(2,1)}, bf16[2,16,3584]{2,1,0:T(8,128)(2,1)S(1)}, u32[]{:S(2)}, u32[]{:S(2)}) collective-permute-start(bf16[2,16,3584]{2,1,0:T(8,128)(2,1)} %param.7), channel_id=1, source_target_pairs={{0,3},{1,2},{2,1},{3,0},{4,7},{5,6},{6,5},{7,4},{8,11},{9,10},{10,... | collective-permute-start | bytes 688136 | tf_op jit(solution)/shard_map/ppermute | solution.py:124
  3.1 28.4 %collective-permute-start.3 = (bf16[2,16,3584]{2,1,0:T(8,128)(2,1)}, bf16[2,16,3584]{2,1,0:T(8,128)(2,1)S(1)}, u32[]{:S(2)}, u32[]{:S(2)}) collective-permute-start(bf16[2,16,3584]{2,1,0:T(8,128)(2,1)} %param.7), channel_id=1, source_target_pairs={{0,4},{1,5},{2,6},{3,7},{4,0},{5,1},{6,2},{7,3},{8,12},{9,13},{10,... | collective-permute-start | bytes 688136 | tf_op jit(solution)/shard_map/ppermute | solution.py:124
  6.1 25.4 %collective-permute-start.4 = (bf16[2,16,3584]{2,1,0:T(8,128)(2,1)}, bf16[2,16,3584]{2,1,0:T(8,128)(2,1)S(1)}, u32[]{:S(2)}, u32[]{:S(2)}) collective-permute-start(bf16[2,16,3584]{2,1,0:T(8,128)(2,1)} %param.7), channel_id=1, source_target_pairs={{0,5},{1,4},{2,7},{3,6},{4,1},{5,0},{6,3},{7,2},{8,13},{9,12},{10,... | collective-permute-start | bytes 688136 | tf_op jit(solution)/shard_map/ppermute | solution.py:124
  12.9 44.1 %all-to-all-start.2 = ((bf16[128,2,3584]{2,1,0:T(2,128)(2,1)}), bf16[128,2,3584]{2,1,0:T(2,128)(2,1)S(1)}, u32[]{:S(2)}, u32[]{:S(2)}) async-start(bf16[128,2,3584]{2,1,0:T(2,128)(2,1)} %shard_map.75), calls=%async_computation.2 | async-start | bytes 3670016 | tf_op jit(solution)/shard_map/all_to_all | solution.py:158
  23.1 4.2 %copy-start.3 = (bf16[2,16,3584]{2,1,0:T(8,128)(2,1)S(1)}, bf16[2,16,3584]{2,1,0:T(8,128)(2,1)}, u32[]{:S(2)}) copy-start(bf16[2,16,3584]{2,1,0:T(8,128)(2,1)} %param.7) | copy-start | bytes 688132
  27.3 28.5 %copy-start.4 = (bf16[3,3584,128]{2,1,0:T(8,128)(2,1)S(1)}, bf16[3,3584,128]{2,1,0:T(8,128)(2,1)}, u32[]{:S(2)}) copy-start(bf16[3,3584,128]{2,1,0:T(8,128)(2,1)} %param.13) | copy-start | bytes 8257540
  27.3 23.4 %collective-permute-start.5 = (bf16[2,16,3584]{2,1,0:T(8,128)(2,1)S(1)}, bf16[2,16,3584]{2,1,0:T(8,128)(2,1)S(1)}, u32[]{:S(2)}, u32[]{:S(2)}) collective-permute-start(bf16[2,16,3584]{2,1,0:T(8,128)(2,1)S(1)} %copy-done.3), channel_id=1, source_target_pairs={{0,6},{1,7},{2,4},{3,5},{4,2},{5,3},{6,0},{7,1},{8,14},{9,15},{10,... | collective-permute-start | bytes 688136 | tf_op jit(solution)/shard_map/ppermute | solution.py:124
  30.0 25.7 %collective-permute-start.6 = (bf16[2,16,3584]{2,1,0:T(8,128)(2,1)S(1)}, bf16[2,16,3584]{2,1,0:T(8,128)(2,1)S(1)}, u32[]{:S(2)}, u32[]{:S(2)}) collective-permute-start(bf16[2,16,3584]{2,1,0:T(8,128)(2,1)S(1)} %copy-done.3), channel_id=1, source_target_pairs={{0,7},{1,6},{2,5},{3,4},{4,3},{5,2},{6,1},{7,0},{8,15},{9,14},{10,... | collective-permute-start | bytes 688136 | tf_op jit(solution)/shard_map/ppermute | solution.py:124
  57.0 1.3 copy-start.1
  58.3 35.9 %all-to-all-start = ((bf16[128,2,3584]{2,1,0:T(2,128)(2,1)}), bf16[128,2,3584]{2,1,0:T(2,128)(2,1)}, u32[]{:S(2)}, u32[]{:S(2)}) async-start(bf16[128,2,3584]{2,1,0:T(2,128)(2,1)} %shard_map.73), calls=%async_computation | async-start | bytes 3670016 | tf_op jit(solution)/shard_map/all_to_all | solution.py:158
  68.6 2.4 %copy-start = (f32[2,8,16,3584]{3,2,1,0:T(8,128)}, f32[2,8,16,3584]{3,2,1,0:T(8,128)S(1)}, u32[]{:S(2)}) copy-start(f32[2,8,16,3584]{3,2,1,0:T(8,128)S(1)} %fusion.4) | copy-start | bytes 11010052
  71.0 27.6 %collective-permute-start.7 = (f32[2,4,16,3584]{3,2,1,0:T(8,128)}, f32[2,4,16,3584]{3,2,1,0:T(8,128)}, u32[]{:S(2)}, u32[]{:S(2)}) collective-permute-start(f32[2,4,16,3584]{3,2,1,0:T(8,128)} %slice.51), channel_id=1, source_target_pairs={{0,1},{1,0},{2,3},{3,2},{4,5},{5,4},{6,7},{7,6},{8,9},{9,8},{10,11... | collective-permute-start | bytes 5505032 | tf_op jit(solution)/shard_map/ppermute | solution.py:124
  94.2 32.2 %all-to-all-start.3 = ((bf16[128,2,3584]{2,1,0:T(2,128)(2,1)}), bf16[128,2,3584]{2,1,0:T(2,128)(2,1)S(1)}, u32[]{:S(2)}, u32[]{:S(2)}) async-start(bf16[128,2,3584]{2,1,0:T(2,128)(2,1)} %shard_map.76), calls=%async_computation.3 | async-start | bytes 3670016 | tf_op jit(solution)/shard_map/all_to_all | solution.py:160
  100.8 1.2 copy-start.2
  102.1 46.8 %collective-permute-start.8 = (f32[2,2,16,3584]{3,2,1,0:T(8,128)S(1)}, f32[2,2,16,3584]{3,2,1,0:T(8,128)}, u32[]{:S(2)}, u32[]{:S(2)}) collective-permute-start(f32[2,2,16,3584]{3,2,1,0:T(8,128)S(1)} %slice.53), channel_id=1, source_target_pairs={{0,2},{1,3},{2,0},{3,1},{4,6},{5,7},{6,4},{7,5},{8,10},{9,11},{10,... | collective-permute-start | bytes 2752520 | tf_op jit(solution)/shard_map/ppermute | solution.py:124
  117.3 14.5 %copy-start.5 = (f32[2,16,8]{1,2,0:T(8,128)S(1)}, f32[2,16,8]{1,2,0:T(8,128)}, u32[]{:S(2)}) copy-start(f32[2,16,8]{1,2,0:T(8,128)} %param.9) | copy-start | bytes 3076
  126.4 37.9 %all-to-all-start.1 = ((bf16[128,2,3584]{2,1,0:T(2,128)(2,1)}), bf16[128,2,3584]{2,1,0:T(2,128)(2,1)}, u32[]{:S(2)}, u32[]{:S(2)}) async-start(bf16[128,2,3584]{2,1,0:T(2,128)(2,1)} %shard_map.74), calls=%async_computation.1 | async-start | bytes 3670016 | tf_op jit(solution)/shard_map/all_to_all | solution.py:160
  150.5 20.0 %collective-permute-start.9 = (f32[2,1,16,3584]{3,2,1,0:T(8,128)S(1)}, f32[2,1,16,3584]{3,2,1,0:T(8,128)}, u32[]{:S(2)}, u32[]{:S(2)}) collective-permute-start(f32[2,1,16,3584]{3,2,1,0:T(8,128)S(1)} %slice.63), channel_id=1, source_target_pairs={{0,4},{1,5},{2,6},{3,7},{4,0},{5,1},{6,2},{7,3},{8,12},{9,13},{10,... | collective-permute-start | bytes 1376264 | tf_op jit(solution)/shard_map/ppermute | solution.py:124

commit v16 on v15

--- a/solution.py
+++ b/solution.py
@@ -119,9 +119,18 @@
     )
 
 
+def gray_partner(low, mask):
+    base, rank = low - low % 8, low % 8
+    place = rank >> 1
+    label = (place ^ place >> 1) << 1 | rank & 1
+    label ^= mask
+    code = label >> 1
+    return base + (code ^ code >> 1) * 2 + (label & 1)
+
+
 def xor_partner(block, mask):
     count = lax.axis_size("ep")
-    return lax.ppermute(block, "ep", [(low, low ^ mask) for low in range(count)])
+    return lax.ppermute(block, "ep", [(low, gray_partner(low, mask)) for low in range(count)])
 
 
 def shared_expert(tokens, shared_weights, group=8):

time: 173 us -> 171 us (0.988)
  starting transfers between devices: 49.4 us -> 47.5 us
where the time goes in v16:
time: 171 us; the launch traced here: 169 us
  waiting for transfers between devices  65.4 us (38%)
  starting transfers between devices  47.5 us (28%)
  Pallas kernels  32.7 us (19%)
  matrix products  9.98 us (6%)
  local copies, waits for them, and re-layouts  8.09 us (5%)
  other arithmetic  5.59 us (3%)
    ppermute x10, waiting for transfers between devices, xor_partner(): lax.ppermute(block, 'ep', [(low, gray_partner(low, mask)) for low in rang...  42.2 us
    pallas_call x2, Pallas kernels, expert_rows(): pl.pallas_call(ffn_kernel, out_shape=jax.ShapeDtypeStruct(token_block.sha...  27 us
    ppermute x10, starting transfers between devices, xor_partner(): lax.ppermute(block, 'ep', [(low, gray_partner(low, mask)) for low in rang...  20.5 us
    all_to_all x2, starting transfers between devices, shards(): lax.all_to_all(outgoing, 'ep', split_axis=0, concat_axis=0, tiled=True)  17.3 us
    all_to_all x2, waiting for transfers between devices, shards(): lax.all_to_all(expert_out, 'ep', split_axis=0, concat_axis=0, tiled=True)  14.6 us
    all_to_all x2, starting transfers between devices, shards(): lax.all_to_all(expert_out, 'ep', split_axis=0, concat_axis=0, tiled=True)  9.7 us
    all_to_all x2, waiting for transfers between devices, shards(): lax.all_to_all(outgoing, 'ep', split_axis=0, concat_axis=0, tiled=True)  8.61 us
    pallas_call x2, Pallas kernels, dispatch_rows(): pl.pallas_call(dispatch_kernel, out_shape=jax.ShapeDtypeStruct((experts,...  5.69 us
  transfers between devices with their start and end apart: 14, of which 7 were waited for; matrix products, arithmetic and copies ran while one was open for 11% of the time, Pallas kernels for 19%

profile of v16, /device:TPU:1, one launch (start us, length us, event | category | flops | bytes accessed | tf_op | source)
XLA Modules:
  0.0 169.5 jit_solution(14395641032314172937)
XLA Ops:
  3.1 2.8 %collective-permute-start.3 = (bf16[2,16,3584]{2,1,0:T(8,128)(2,1)}, bf16[2,16,3584]{2,1,0:T(8,128)(2,1)S(1)}, u32[]{:S(2)}, u32[]{:S(2)}) collective-permute-start(bf16[2,16,3584]{2,1,0:T(8,128)(2,1)} %param.7), channel_id=1, source_target_pairs={{0,6},{1,7},{2,4},{3,5},{4,2},{5,3},{6,0},{7,1},{8,14},{9,15},{10,... | collective-permute-start | bytes 688136 | tf_op jit(solution)/shard_map/ppermute | solution.py:133
  6.1 1.7 slice_bitcast_fusion.1
  9.8 2.8 %shard_map.75 = bf16[128,2,3584]{2,1,0:T(2,128)(2,1)} custom-call(bf16[256,16]{1,0:T(8,128)(2,1)} %convolution_convert_fusion.select_ref, bf16[16,3584]{1,0:T(8,128)(2,1)} %get-tuple-element.6.token_ref), custom_call_target="tpu_custom_call" | custom-call | tf_op jit(solution)/shard_map/pallas_call | solution.py:75
  12.6 10.0 %all-to-all-start.2 = ((bf16[128,2,3584]{2,1,0:T(2,128)(2,1)}), bf16[128,2,3584]{2,1,0:T(2,128)(2,1)S(1)}, u32[]{:S(2)}, u32[]{:S(2)}) async-start(bf16[128,2,3584]{2,1,0:T(2,128)(2,1)} %shard_map.75), calls=%async_computation.2 | async-start | bytes 3670016 | tf_op jit(solution)/shard_map/all_to_all | solution.py:167
  23.9 2.9 %shard_map.73 = bf16[128,2,3584]{2,1,0:T(2,128)(2,1)} custom-call(bf16[256,16]{1,0:T(8,128)(2,1)} %convolution_convert_fusion.1.select_ref, bf16[16,3584]{1,0:T(8,128)(2,1)} %get-tuple-element.5.token_ref), custom_call_target="tpu_custom_call" | custom-call | tf_op jit(solution)/shard_map/pallas_call | solution.py:75
  26.8 3.0 %collective-permute-start.5 = (bf16[2,16,3584]{2,1,0:T(8,128)(2,1)S(1)}, bf16[2,16,3584]{2,1,0:T(8,128)(2,1)S(1)}, u32[]{:S(2)}, u32[]{:S(2)}) collective-permute-start(bf16[2,16,3584]{2,1,0:T(8,128)(2,1)S(1)} %copy-done.3), channel_id=1, source_target_pairs={{0,4},{1,5},{2,6},{3,7},{4,0},{5,1},{6,2},{7,3},{8,12},{9,13},{10,... | collective-permute-start | bytes 688136 | tf_op jit(solution)/shard_map/ppermute | solution.py:133
  31.3 19.7 %collective-permute-done.5 = bf16[2,16,3584]{2,1,0:T(8,128)(2,1)S(1)} collective-permute-done((bf16[2,16,3584]{2,1,0:T(8,128)(2,1)S(1)}, bf16[2,16,3584]{2,1,0:T(8,128)(2,1)S(1)}, u32[]{:S(2)}, u32[]{:S(2)}) %collective-permute-start.5) | collective-permute-done | bytes 229408 | tf_op jit(solution)/shard_map/ppermute | solution.py:133
  51.1 4.9 %collective-permute-done.6 = bf16[2,16,3584]{2,1,0:T(8,128)(2,1)S(1)} collective-permute-done((bf16[2,16,3584]{2,1,0:T(8,128)(2,1)S(1)}, bf16[2,16,3584]{2,1,0:T(8,128)(2,1)S(1)}, u32[]{:S(2)}, u32[]{:S(2)}) %collective-permute-start.6) | collective-permute-done | bytes 229408 | tf_op jit(solution)/shard_map/ppermute | solution.py:133
  58.6 7.3 %all-to-all-start = ((bf16[128,2,3584]{2,1,0:T(2,128)(2,1)}), bf16[128,2,3584]{2,1,0:T(2,128)(2,1)}, u32[]{:S(2)}, u32[]{:S(2)}) async-start(bf16[128,2,3584]{2,1,0:T(2,128)(2,1)} %shard_map.73), calls=%async_computation | async-start | bytes 3670016 | tf_op jit(solution)/shard_map/all_to_all | solution.py:167
  65.8 1.8 %fusion.4 = f32[2,8,16,3584]{3,2,1,0:T(8,128)S(1)} fusion(bf16[2,8,16,128]{3,2,1,0:T(8,128)(2,1)S(1)} %bitcast.40, bf16[3,3584,128]{2,1,0:T(8,128)(2,1)} %param.13), kind=kOutput, calls=%fused_computation.11 | convolution fusion | flops 234881024 | bytes 4653056 | tf_op jit(solution)/shard_map/dot_general | solution.py:144
  71.2 13.5 %shard_map.76 = bf16[128,2,3584]{2,1,0:T(2,128)(2,1)} custom-call(bf16[128,2,3584]{2,1,0:T(2,128)(2,1)} %copy-done.1, bf16[1,3584,1024]{2,1,0:T(8,128)(2,1)} %gate_ref.3, bf16[1,3584,1024]{2,1,0:T(8,128)(2,1)} %up_ref.3, bf16[1,1024,3584]{2,1,0:T(8,128)(2,1)} %down_ref.3), custom_call_target="tpu_custom_call" | custom-call | flops 5637144576 | bytes 25690112 | tf_op jit(solution)/shard_map/pallas_call | solution.py:45
  84.6 8.6 %all-to-all-done.x_ref = bf16[128,2,3584]{2,1,0:T(2,128)(2,1)} async-done(((bf16[128,2,3584]{2,1,0:T(2,128)(2,1)}), bf16[128,2,3584]{2,1,0:T(2,128)(2,1)}, u32[]{:S(2)}, u32[]{:S(2)}) %all-to-all-start) | async-done | bytes 1835040 | tf_op jit(solution)/shard_map/all_to_all | solution.py:167
  93.3 4.3 %all-to-all-start.3 = ((bf16[128,2,3584]{2,1,0:T(2,128)(2,1)}), bf16[128,2,3584]{2,1,0:T(2,128)(2,1)S(1)}, u32[]{:S(2)}, u32[]{:S(2)}) async-start(bf16[128,2,3584]{2,1,0:T(2,128)(2,1)} %shard_map.76), calls=%async_computation.3 | async-start | bytes 3670016 | tf_op jit(solution)/shard_map/all_to_all | solution.py:169
  97.6 2.3 %slice_add_fusion = f32[2,4,16,3584]{3,2,1,0:T(8,128)S(1)} fusion(f32[2,4,16,3584]{3,2,1,0:T(8,128)} %collective-permute-done.7, f32[2,8,16,3584]{3,2,1,0:T(8,128)} %copy-done), kind=kLoop, calls=%fused_computation.4 | loop fusion | flops 458752 | bytes 5505024 | tf_op jit(solution)/shard_map/add | solution.py:152
  101.2 1.7 %collective-permute-start.8 = (f32[2,2,16,3584]{3,2,1,0:T(8,128)S(1)}, f32[2,2,16,3584]{3,2,1,0:T(8,128)}, u32[]{:S(2)}, u32[]{:S(2)}) collective-permute-start(f32[2,2,16,3584]{3,2,1,0:T(8,128)S(1)} %slice.53), channel_id=1, source_target_pairs={{0,2},{1,3},{2,0},{3,1},{4,6},{5,7},{6,4},{7,5},{8,10},{9,11},{10,... | collective-permute-start | bytes 2752520 | tf_op jit(solution)/shard_map/ppermute | solution.py:133
  102.9 13.5 %shard_map.74 = bf16[128,2,3584]{2,1,0:T(2,128)(2,1)} custom-call(bf16[128,2,3584]{2,1,0:T(2,128)(2,1)} %all-to-all-done.x_ref, bf16[1,3584,1024]{2,1,0:T(8,128)(2,1)} %gate_ref.3, bf16[1,3584,1024]{2,1,0:T(8,128)(2,1)} %up_ref.3, bf16[1,1024,3584]{2,1,0:T(8,128)(2,1)} %down_ref.3), custom_call_target="tpu_custom_call" | custom-call | flops 5637144576 | bytes 25690112 | tf_op jit(solution)/shard_map/pallas_call | solution.py:45
  116.4 9.1 %all-to-all-done.3 = bf16[128,2,3584]{2,1,0:T(2,128)(2,1)S(1)} async-done(((bf16[128,2,3584]{2,1,0:T(2,128)(2,1)}), bf16[128,2,3584]{2,1,0:T(2,128)(2,1)S(1)}, u32[]{:S(2)}, u32[]{:S(2)}) %all-to-all-start.3) | async-done | bytes 1835040 | tf_op jit(solution)/shard_map/all_to_all | solution.py:169
  125.5 5.4 %all-to-all-start.1 = ((bf16[128,2,3584]{2,1,0:T(2,128)(2,1)}), bf16[128,2,3584]{2,1,0:T(2,128)(2,1)}, u32[]{:S(2)}, u32[]{:S(2)}) async-start(bf16[128,2,3584]{2,1,0:T(2,128)(2,1)} %shard_map.74), calls=%async_computation.1 | async-start | bytes 3670016 | tf_op jit(solution)/shard_map/all_to_all | solution.py:169
  132.5 15.4 %collective-permute-done.8 = f32[2,2,16,3584]{3,2,1,0:T(8,128)} collective-permute-done((f32[2,2,16,3584]{3,2,1,0:T(8,128)S(1)}, f32[2,2,16,3584]{3,2,1,0:T(8,128)}, u32[]{:S(2)}, u32[]{:S(2)}) %collective-permute-start.8) | collective-permute-done | bytes 917536 | tf_op jit(solution)/shard_map/ppermute | solution.py:133
  149.5 7.2 %collective-permute-start.9 = (f32[2,1,16,3584]{3,2,1,0:T(8,128)S(1)}, f32[2,1,16,3584]{3,2,1,0:T(8,128)}, u32[]{:S(2)}, u32[]{:S(2)}) collective-permute-start(f32[2,1,16,3584]{3,2,1,0:T(8,128)S(1)} %slice.63), channel_id=1, source_target_pairs={{0,6},{1,7},{2,4},{3,5},{4,2},{5,3},{6,0},{7,1},{8,14},{9,15},{10,... | collective-permute-start | bytes 1376264 | tf_op jit(solution)/shard_map/ppermute | solution.py:133
  157.6 5.5 %all-to-all-done.1 = bf16[128,2,3584]{2,1,0:T(2,128)(2,1)} async-done(((bf16[128,2,3584]{2,1,0:T(2,128)(2,1)}), bf16[128,2,3584]{2,1,0:T(2,128)(2,1)}, u32[]{:S(2)}, u32[]{:S(2)}) %all-to-all-start.1) | async-done | bytes 1835040 | tf_op jit(solution)/shard_map/all_to_all | solution.py:169
  163.1 2.5 %convolution_bitcast_fusion.1 = f32[1,16,3584]{2,1,0:T(8,128)S(1)} fusion(bf16[128,2,3584]{2,1,0:T(2,128)(2,1)} %all-to-all-done.1, f32[16,128,2]{0,2,1:T(2,128)} %bitcast.38), kind=kOutput, calls=%fused_computation.1 | convolution fusion | flops 176160768 | bytes 2080768 | tf_op jit(solution)/shard_map/tec,ecd->td/dot_general | solution.py:171
  165.5 2.2 %collective-permute-done.9 = f32[2,1,16,3584]{3,2,1,0:T(8,128)} collective-permute-done((f32[2,1,16,3584]{3,2,1,0:T(8,128)S(1)}, f32[2,1,16,3584]{3,2,1,0:T(8,128)}, u32[]{:S(2)}, u32[]{:S(2)}) %collective-permute-start.9) | collective-permute-done | bytes 458784 | tf_op jit(solution)/shard_map/ppermute | solution.py:133
  167.7 1.8 %fusion.15 = bf16[2,16,3584]{2,1,0:T(8,128)(2,1)} fusion(f32[2,1,16,3584]{3,2,1,0:T(8,128)} %collective-permute-done.9, f32[2,2,16,3584]{3,2,1,0:T(8,128)S(1)} %slice_add_fusion.1, f32[1,16,3584]{2,1,0:T(8,128)S(1)} %convolution_bitcast_fusion, f32[1,16,3584]{2,1,0:T(8,128)S(1)} %convolution_bitcast_fusion.1), kind=kLoop, calls=%fused_computation.24 | loop fusion | flops 458752 | bytes 1605632 | tf_op jit(solution)/shard_map/convert_element_type | solution.py:180
  (58 shorter events, 19.6 us)
Async XLA Ops:
  0.0 26.8 %collective-permute-start = (bf16[2,16,3584]{2,1,0:T(8,128)(2,1)}, bf16[2,16,3584]{2,1,0:T(8,128)(2,1)S(1)}, u32[]{:S(2)}, u32[]{:S(2)}) collective-permute-start(bf16[2,16,3584]{2,1,0:T(8,128)(2,1)} %param.7), channel_id=1, source_target_pairs={{0,1},{1,0},{2,3},{3,2},{4,5},{5,4},{6,7},{7,6},{8,9},{9,8},{10,11... | collective-permute-start | bytes 688136 | tf_op jit(solution)/shard_map/ppermute | solution.py:133
  1.4 28.4 %collective-permute-start.1 = (bf16[2,16,3584]{2,1,0:T(8,128)(2,1)}, bf16[2,16,3584]{2,1,0:T(8,128)(2,1)S(1)}, u32[]{:S(2)}, u32[]{:S(2)}) collective-permute-start(bf16[2,16,3584]{2,1,0:T(8,128)(2,1)} %param.7), channel_id=1, source_target_pairs={{0,2},{1,3},{2,0},{3,1},{4,6},{5,7},{6,4},{7,5},{8,10},{9,11},{10,... | collective-permute-start | bytes 688136 | tf_op jit(solution)/shard_map/ppermute | solution.py:133
  2.8 28.4 %collective-permute-start.2 = (bf16[2,16,3584]{2,1,0:T(8,128)(2,1)}, bf16[2,16,3584]{2,1,0:T(8,128)(2,1)S(1)}, u32[]{:S(2)}, u32[]{:S(2)}) collective-permute-start(bf16[2,16,3584]{2,1,0:T(8,128)(2,1)} %param.7), channel_id=1, source_target_pairs={{0,3},{1,2},{2,1},{3,0},{4,7},{5,6},{6,5},{7,4},{8,11},{9,10},{10,... | collective-permute-start | bytes 688136 | tf_op jit(solution)/shard_map/ppermute | solution.py:133
  3.1 28.2 %collective-permute-start.3 = (bf16[2,16,3584]{2,1,0:T(8,128)(2,1)}, bf16[2,16,3584]{2,1,0:T(8,128)(2,1)S(1)}, u32[]{:S(2)}, u32[]{:S(2)}) collective-permute-start(bf16[2,16,3584]{2,1,0:T(8,128)(2,1)} %param.7), channel_id=1, source_target_pairs={{0,6},{1,7},{2,4},{3,5},{4,2},{5,3},{6,0},{7,1},{8,14},{9,15},{10,... | collective-permute-start | bytes 688136 | tf_op jit(solution)/shard_map/ppermute | solution.py:133
  5.9 25.4 %collective-permute-start.4 = (bf16[2,16,3584]{2,1,0:T(8,128)(2,1)}, bf16[2,16,3584]{2,1,0:T(8,128)(2,1)S(1)}, u32[]{:S(2)}, u32[]{:S(2)}) collective-permute-start(bf16[2,16,3584]{2,1,0:T(8,128)(2,1)} %param.7), channel_id=1, source_target_pairs={{0,7},{1,6},{2,5},{3,4},{4,3},{5,2},{6,1},{7,0},{8,15},{9,14},{10,... | collective-permute-start | bytes 688136 | tf_op jit(solution)/shard_map/ppermute | solution.py:133
  12.6 44.7 %all-to-all-start.2 = ((bf16[128,2,3584]{2,1,0:T(2,128)(2,1)}), bf16[128,2,3584]{2,1,0:T(2,128)(2,1)S(1)}, u32[]{:S(2)}, u32[]{:S(2)}) async-start(bf16[128,2,3584]{2,1,0:T(2,128)(2,1)} %shard_map.75), calls=%async_computation.2 | async-start | bytes 3670016 | tf_op jit(solution)/shard_map/all_to_all | solution.py:167
  22.6 4.2 %copy-start.3 = (bf16[2,16,3584]{2,1,0:T(8,128)(2,1)S(1)}, bf16[2,16,3584]{2,1,0:T(8,128)(2,1)}, u32[]{:S(2)}) copy-start(bf16[2,16,3584]{2,1,0:T(8,128)(2,1)} %param.7) | copy-start | bytes 688132
  26.8 29.2 %copy-start.4 = (bf16[3,3584,128]{2,1,0:T(8,128)(2,1)S(1)}, bf16[3,3584,128]{2,1,0:T(8,128)(2,1)}, u32[]{:S(2)}) copy-start(bf16[3,3584,128]{2,1,0:T(8,128)(2,1)} %param.13) | copy-start | bytes 8257540
  26.8 24.2 %collective-permute-start.5 = (bf16[2,16,3584]{2,1,0:T(8,128)(2,1)S(1)}, bf16[2,16,3584]{2,1,0:T(8,128)(2,1)S(1)}, u32[]{:S(2)}, u32[]{:S(2)}) collective-permute-start(bf16[2,16,3584]{2,1,0:T(8,128)(2,1)S(1)} %copy-done.3), channel_id=1, source_target_pairs={{0,4},{1,5},{2,6},{3,7},{4,0},{5,1},{6,2},{7,3},{8,12},{9,13},{10,... | collective-permute-start | bytes 688136 | tf_op jit(solution)/shard_map/ppermute | solution.py:133
  29.8 26.2 %collective-permute-start.6 = (bf16[2,16,3584]{2,1,0:T(8,128)(2,1)S(1)}, bf16[2,16,3584]{2,1,0:T(8,128)(2,1)S(1)}, u32[]{:S(2)}, u32[]{:S(2)}) collective-permute-start(bf16[2,16,3584]{2,1,0:T(8,128)(2,1)S(1)} %copy-done.3), channel_id=1, source_target_pairs={{0,5},{1,4},{2,7},{3,6},{4,1},{5,0},{6,3},{7,2},{8,13},{9,12},{10,... | collective-permute-start | bytes 688136 | tf_op jit(solution)/shard_map/ppermute | solution.py:133
  57.3 1.3 copy-start.1
  58.6 34.7 %all-to-all-start = ((bf16[128,2,3584]{2,1,0:T(2,128)(2,1)}), bf16[128,2,3584]{2,1,0:T(2,128)(2,1)}, u32[]{:S(2)}, u32[]{:S(2)}) async-start(bf16[128,2,3584]{2,1,0:T(2,128)(2,1)} %shard_map.73), calls=%async_computation | async-start | bytes 3670016 | tf_op jit(solution)/shard_map/all_to_all | solution.py:167
  67.7 2.4 %copy-start = (f32[2,8,16,3584]{3,2,1,0:T(8,128)}, f32[2,8,16,3584]{3,2,1,0:T(8,128)S(1)}, u32[]{:S(2)}) copy-start(f32[2,8,16,3584]{3,2,1,0:T(8,128)S(1)} %fusion.4) | copy-start | bytes 11010052
  70.0 27.6 %collective-permute-start.7 = (f32[2,4,16,3584]{3,2,1,0:T(8,128)}, f32[2,4,16,3584]{3,2,1,0:T(8,128)}, u32[]{:S(2)}, u32[]{:S(2)}) collective-permute-start(f32[2,4,16,3584]{3,2,1,0:T(8,128)} %slice.51), channel_id=1, source_target_pairs={{0,1},{1,0},{2,3},{3,2},{4,5},{5,4},{6,7},{7,6},{8,9},{9,8},{10,11... | collective-permute-start | bytes 5505032 | tf_op jit(solution)/shard_map/ppermute | solution.py:133
  93.3 32.2 %all-to-all-start.3 = ((bf16[128,2,3584]{2,1,0:T(2,128)(2,1)}), bf16[128,2,3584]{2,1,0:T(2,128)(2,1)S(1)}, u32[]{:S(2)}, u32[]{:S(2)}) async-start(bf16[128,2,3584]{2,1,0:T(2,128)(2,1)} %shard_map.76), calls=%async_computation.3 | async-start | bytes 3670016 | tf_op jit(solution)/shard_map/all_to_all | solution.py:169
  99.9 1.2 copy-start.2
  101.2 46.8 %collective-permute-start.8 = (f32[2,2,16,3584]{3,2,1,0:T(8,128)S(1)}, f32[2,2,16,3584]{3,2,1,0:T(8,128)}, u32[]{:S(2)}, u32[]{:S(2)}) collective-permute-start(f32[2,2,16,3584]{3,2,1,0:T(8,128)S(1)} %slice.53), channel_id=1, source_target_pairs={{0,2},{1,3},{2,0},{3,1},{4,6},{5,7},{6,4},{7,5},{8,10},{9,11},{10,... | collective-permute-start | bytes 2752520 | tf_op jit(solution)/shard_map/ppermute | solution.py:133
  116.4 14.5 %copy-start.5 = (f32[2,16,8]{1,2,0:T(8,128)S(1)}, f32[2,16,8]{1,2,0:T(8,128)}, u32[]{:S(2)}) copy-start(f32[2,16,8]{1,2,0:T(8,128)} %param.9) | copy-start | bytes 3076
  125.5 37.6 %all-to-all-start.1 = ((bf16[128,2,3584]{2,1,0:T(2,128)(2,1)}), bf16[128,2,3584]{2,1,0:T(2,128)(2,1)}, u32[]{:S(2)}, u32[]{:S(2)}) async-start(bf16[128,2,3584]{2,1,0:T(2,128)(2,1)} %shard_map.74), calls=%async_computation.1 | async-start | bytes 3670016 | tf_op jit(solution)/shard_map/all_to_all | solution.py:169
  149.5 18.2 %collective-permute-start.9 = (f32[2,1,16,3584]{3,2,1,0:T(8,128)S(1)}, f32[2,1,16,3584]{3,2,1,0:T(8,128)}, u32[]{:S(2)}, u32[]{:S(2)}) collective-permute-start(f32[2,1,16,3584]{3,2,1,0:T(8,128)S(1)} %slice.63), channel_id=1, source_target_pairs={{0,6},{1,7},{2,4},{3,5},{4,2},{5,3},{6,0},{7,1},{8,14},{9,15},{10,... | collective-permute-start | bytes 1376264 | tf_op jit(solution)/shard_map/ppermute | solution.py:133

commit v17 on v16

--- a/solution.py
+++ b/solution.py
@@ -145,13 +145,11 @@
         hidden, shared_weights[2], (((1,), (1,)), ((), ())), preferred_element_type=jnp.float32
     )
     partial_value = partial_value.reshape(step_count, group, row_count, model_width)
-    level = 0
-    while partial_value.shape[1] > 1:
-        keep = partial_value[:, 0::2]
-        send = partial_value[:, 1::2]
-        partial_value = keep + xor_partner(send, 1 << level)
-        level += 1
-    return partial_value[:, 0]
+    partial_value = partial_value[:, 0::2] + xor_partner(partial_value[:, 1::2], 1)
+    total = partial_value[:, 0]
+    for slot in range(1, group // 2):
+        total = total + xor_partner(partial_value[:, slot], slot * 2)
+    return total
 
 
 def shards(tokens, expert_ids, combine_weights, w_gate, w_up, w_down, shared_weights):

time: 171 us -> 171 us (level)
  local copies, waits for them, and re-layouts: 8.09 us -> 14.7 us
  starting transfers between devices: 47.5 us -> 43.2 us
  matrix products: 9.98 us -> 12.9 us
  waiting for transfers between devices: 65.4 us -> 62.8 us
    all_to_all x2, waiting for transfers between devices: 14.6 us -> 30.3 us  [shards(): lax.all_to_all(expert_out, 'ep', split_axis=0, concat_axis=0, tiled=True)]
    ppermute x10 -> x11, waiting for transfers between devices: 42.2 us -> 28.1 us  [xor_partner(): lax.ppermute(block, 'ep', [(low, gray_partner(low, mask)) for low in rang...]
    ppermute x10 -> x11, starting transfers between devices: 20.5 us -> 15.3 us  [xor_partner(): lax.ppermute(block, 'ep', [(low, gray_partner(low, mask)) for low in rang...]
    unnamed x19 -> x21, local copies, waits for them, and re-layouts: 3.46 us -> 8.39 us
    all_to_all x2, waiting for transfers between devices: 8.61 us -> 4.43 us  [shards(): lax.all_to_all(outgoing, 'ep', split_axis=0, concat_axis=0, tiled=True)]
    dot_general x1, matrix products: 0.62 us -> 2.54 us  [shared_expert(): jnp.dot(flat_rows, shared_weights[0], preferred_element_type=jnp.float32)]
    add x2 -> x1, other arithmetic: 3.8 us -> 2.25 us  [shared_expert(): partial_value[:, 0::2] + xor_partner(partial_value[:, 1::2], 1)]
  transfers between devices with their start and end apart: 14 -> 15, of which waited for: 7 -> 6; matrix products, arithmetic and copies ran while one was open for 11% -> 15% of each run, Pallas kernels for 19% -> 19%
where the time goes in v17:
time: 171 us; the launch traced here: 170 us
  waiting for transfers between devices  62.8 us (37%)
  starting transfers between devices  43.2 us (25%)
  Pallas kernels  32.5 us (19%)
  local copies, waits for them, and re-layouts  14.7 us (9%)
  matrix products  12.9 us (8%)
  other arithmetic  4.08 us (2%)
    all_to_all x2, waiting for transfers between devices, shards(): lax.all_to_all(expert_out, 'ep', split_axis=0, concat_axis=0, tiled=True)  30.3 us
    ppermute x11, waiting for transfers between devices, xor_partner(): lax.ppermute(block, 'ep', [(low, gray_partner(low, mask)) for low in rang...  28.1 us
    pallas_call x2, Pallas kernels, expert_rows(): pl.pallas_call(ffn_kernel, out_shape=jax.ShapeDtypeStruct(token_block.sha...  26.9 us
    all_to_all x2, starting transfers between devices, shards(): lax.all_to_all(outgoing, 'ep', split_axis=0, concat_axis=0, tiled=True)  18.2 us
    ppermute x11, starting transfers between devices, xor_partner(): lax.ppermute(block, 'ep', [(low, gray_partner(low, mask)) for low in rang...  15.3 us
    all_to_all x2, starting transfers between devices, shards(): lax.all_to_all(expert_out, 'ep', split_axis=0, concat_axis=0, tiled=True)  9.72 us
    unnamed x21, local copies, waits for them, and re-layouts  8.39 us
    pallas_call x2, Pallas kernels, dispatch_rows(): pl.pallas_call(dispatch_kernel, out_shape=jax.ShapeDtypeStruct((experts,...  5.63 us
  transfers between devices with their start and end apart: 15, of which 6 were waited for; matrix products, arithmetic and copies ran while one was open for 15% of the time, Pallas kernels for 19%

profile of v17, /device:TPU:1, one launch (start us, length us, event | category | flops | bytes accessed | tf_op | source)
XLA Modules:
  0.0 170.4 jit_solution(7781635021387439661)
XLA Ops:
  3.1 2.8 %collective-permute-start.3 = (bf16[2,16,3584]{2,1,0:T(8,128)(2,1)}, bf16[2,16,3584]{2,1,0:T(8,128)(2,1)S(1)}, u32[]{:S(2)}, u32[]{:S(2)}) collective-permute-start(bf16[2,16,3584]{2,1,0:T(8,128)(2,1)} %param.7), channel_id=1, source_target_pairs={{0,6},{1,7},{2,4},{3,5},{4,2},{5,3},{6,0},{7,1},{8,14},{9,15},{10,... | collective-permute-start | bytes 688136 | tf_op jit(solution)/shard_map/ppermute | solution.py:133
  6.1 1.7 slice_bitcast_fusion.5
  9.8 2.8 %shard_map.75 = bf16[128,2,3584]{2,1,0:T(2,128)(2,1)} custom-call(bf16[256,16]{1,0:T(8,128)(2,1)} %convolution_convert_fusion.select_ref, bf16[16,3584]{1,0:T(8,128)(2,1)} %get-tuple-element.9.token_ref), custom_call_target="tpu_custom_call" | custom-call | tf_op jit(solution)/shard_map/pallas_call | solution.py:75
  12.6 10.0 %all-to-all-start.2 = ((bf16[128,2,3584]{2,1,0:T(2,128)(2,1)}), bf16[128,2,3584]{2,1,0:T(2,128)(2,1)S(1)}, u32[]{:S(2)}, u32[]{:S(2)}) async-start(bf16[128,2,3584]{2,1,0:T(2,128)(2,1)} %shard_map.75), calls=%async_computation.2 | async-start | bytes 3670016 | tf_op jit(solution)/shard_map/all_to_all | solution.py:165
  23.9 2.8 %shard_map.73 = bf16[128,2,3584]{2,1,0:T(2,128)(2,1)} custom-call(bf16[256,16]{1,0:T(8,128)(2,1)} %convolution_convert_fusion.1.select_ref, bf16[16,3584]{1,0:T(8,128)(2,1)} %get-tuple-element.8.token_ref), custom_call_target="tpu_custom_call" | custom-call | tf_op jit(solution)/shard_map/pallas_call | solution.py:75
  27.4 2.9 %collective-permute-start.5 = (bf16[2,16,3584]{2,1,0:T(8,128)(2,1)S(1)}, bf16[2,16,3584]{2,1,0:T(8,128)(2,1)S(1)}, u32[]{:S(2)}, u32[]{:S(2)}) collective-permute-start(bf16[2,16,3584]{2,1,0:T(8,128)(2,1)S(1)} %copy-done.3), channel_id=1, source_target_pairs={{0,4},{1,5},{2,6},{3,7},{4,0},{5,1},{6,2},{7,3},{8,12},{9,13},{10,... | collective-permute-start | bytes 688136 | tf_op jit(solution)/shard_map/ppermute | solution.py:133
  35.2 15.8 %collective-permute-done.5 = bf16[2,16,3584]{2,1,0:T(8,128)(2,1)S(1)} collective-permute-done((bf16[2,16,3584]{2,1,0:T(8,128)(2,1)S(1)}, bf16[2,16,3584]{2,1,0:T(8,128)(2,1)S(1)}, u32[]{:S(2)}, u32[]{:S(2)}) %collective-permute-start.5) | collective-permute-done | bytes 229408 | tf_op jit(solution)/shard_map/ppermute | solution.py:133
  53.0 8.2 %all-to-all-start = ((bf16[128,2,3584]{2,1,0:T(2,128)(2,1)}), bf16[128,2,3584]{2,1,0:T(2,128)(2,1)}, u32[]{:S(2)}, u32[]{:S(2)}) async-start(bf16[128,2,3584]{2,1,0:T(2,128)(2,1)} %shard_map.73), calls=%async_computation | async-start | bytes 3670016 | tf_op jit(solution)/shard_map/all_to_all | solution.py:165
  62.0 2.5 %fusion.8 = f32[256,128]{1,0:T(8,128)S(1)} fusion(bf16[256,3584]{1,0:T(8,128)(2,1)} %bitcast, bf16[3,3584,128]{2,1,0:T(8,128)(2,1)} %param.13), kind=kOutput, calls=%fused_computation.15 | convolution fusion | flops 234881024 | bytes 2883584 | tf_op jit(solution)/shard_map/dot_general | solution.py:141
  64.5 2.1 %multiply_convert_fusion = bf16[256,128]{1,0:T(8,128)(2,1)S(1)} fusion(f32[256,128]{1,0:T(8,128)S(1)} %fusion.8, bf16[256,3584]{1,0:T(8,128)(2,1)} %bitcast, bf16[3,3584,128]{2,1,0:T(8,128)(2,1)S(1)} %copy-done.4), kind=kOutput, calls=%fused_computation.35 | convolution fusion | flops 235077632 | bytes 2949120 | tf_op jit(solution)/shard_map/dot_general | solution.py:142
  67.3 1.5 slice.49
  70.8 13.4 %shard_map.76 = bf16[128,2,3584]{2,1,0:T(2,128)(2,1)} custom-call(bf16[128,2,3584]{2,1,0:T(2,128)(2,1)} %copy-done.1, bf16[1,3584,1024]{2,1,0:T(8,128)(2,1)} %gate_ref.3, bf16[1,3584,1024]{2,1,0:T(8,128)(2,1)} %up_ref.3, bf16[1,1024,3584]{2,1,0:T(8,128)(2,1)} %down_ref.3), custom_call_target="tpu_custom_call" | custom-call | flops 5637144576 | bytes 25690112 | tf_op jit(solution)/shard_map/pallas_call | solution.py:45
  84.2 4.4 %all-to-all-done.x_ref = bf16[128,2,3584]{2,1,0:T(2,128)(2,1)} async-done(((bf16[128,2,3584]{2,1,0:T(2,128)(2,1)}), bf16[128,2,3584]{2,1,0:T(2,128)(2,1)}, u32[]{:S(2)}, u32[]{:S(2)}) %all-to-all-start) | async-done | bytes 1835040 | tf_op jit(solution)/shard_map/all_to_all | solution.py:165
  88.7 4.4 %all-to-all-start.3 = ((bf16[128,2,3584]{2,1,0:T(2,128)(2,1)}), bf16[128,2,3584]{2,1,0:T(2,128)(2,1)S(1)}, u32[]{:S(2)}, u32[]{:S(2)}) async-start(bf16[128,2,3584]{2,1,0:T(2,128)(2,1)} %shard_map.76), calls=%async_computation.3 | async-start | bytes 3670016 | tf_op jit(solution)/shard_map/all_to_all | solution.py:167
  95.4 13.5 %shard_map.74 = bf16[128,2,3584]{2,1,0:T(2,128)(2,1)} custom-call(bf16[128,2,3584]{2,1,0:T(2,128)(2,1)} %all-to-all-done.x_ref, bf16[1,3584,1024]{2,1,0:T(8,128)(2,1)} %gate_ref.3, bf16[1,3584,1024]{2,1,0:T(8,128)(2,1)} %up_ref.3, bf16[1,1024,3584]{2,1,0:T(8,128)(2,1)} %down_ref.3), custom_call_target="tpu_custom_call" | custom-call | flops 5637144576 | bytes 25690112 | tf_op jit(solution)/shard_map/pallas_call | solution.py:45
  108.9 12.0 %all-to-all-done.3 = bf16[128,2,3584]{2,1,0:T(2,128)(2,1)S(1)} async-done(((bf16[128,2,3584]{2,1,0:T(2,128)(2,1)}), bf16[128,2,3584]{2,1,0:T(2,128)(2,1)S(1)}, u32[]{:S(2)}, u32[]{:S(2)}) %all-to-all-start.3) | async-done | bytes 1835040 | tf_op jit(solution)/shard_map/all_to_all | solution.py:167
  120.9 5.3 %all-to-all-start.1 = ((bf16[128,2,3584]{2,1,0:T(2,128)(2,1)}), bf16[128,2,3584]{2,1,0:T(2,128)(2,1)}, u32[]{:S(2)}, u32[]{:S(2)}) async-start(bf16[128,2,3584]{2,1,0:T(2,128)(2,1)} %shard_map.74), calls=%async_computation.1 | async-start | bytes 3670016 | tf_op jit(solution)/shard_map/all_to_all | solution.py:167
  126.2 2.3 %slice_add_fusion = f32[2,4,16,3584]{3,2,1,0:T(8,128)S(1)} fusion(f32[2,4,16,3584]{3,2,1,0:T(8,128)} %collective-permute-done.7, f32[2,8,16,3584]{3,2,1,0:T(8,128)} %copy-done), kind=kLoop, calls=%fused_computation.4 | loop fusion | flops 458752 | bytes 5505024 | tf_op jit(solution)/shard_map/add | solution.py:148
  130.9 3.0 %collective-permute-start.10 = (f32[2,16,3584]{2,1,0:T(8,128)}, f32[2,16,3584]{2,1,0:T(8,128)S(1)}, u32[]{:S(2)}, u32[]{:S(2)}) collective-permute-start(f32[2,16,3584]{2,1,0:T(8,128)} %get-tuple-element.6), channel_id=1, source_target_pairs={{0,4},{1,5},{2,6},{3,7},{4,0},{5,1},{6,2},{7,3},{8,12},{9,13},{10,... | collective-permute-start | bytes 1376264 | tf_op jit(solution)/shard_map/ppermute | solution.py:133
  135.6 18.3 %all-to-all-done.1 = bf16[128,2,3584]{2,1,0:T(2,128)(2,1)} async-done(((bf16[128,2,3584]{2,1,0:T(2,128)(2,1)}), bf16[128,2,3584]{2,1,0:T(2,128)(2,1)}, u32[]{:S(2)}, u32[]{:S(2)}) %all-to-all-start.1) | async-done | bytes 1835040 | tf_op jit(solution)/shard_map/all_to_all | solution.py:167
  153.9 2.5 %convolution_bitcast_fusion.1 = f32[1,16,3584]{2,1,0:T(8,128)S(1)} fusion(bf16[128,2,3584]{2,1,0:T(2,128)(2,1)} %all-to-all-done.1, f32[16,128,2]{0,2,1:T(2,128)} %bitcast.56), kind=kOutput, calls=%fused_computation.1 | convolution fusion | flops 176160768 | bytes 2080768 | tf_op jit(solution)/shard_map/tec,ecd->td/dot_general | solution.py:169
  156.4 3.0 %collective-permute-done.10 = f32[2,16,3584]{2,1,0:T(8,128)S(1)} collective-permute-done((f32[2,16,3584]{2,1,0:T(8,128)}, f32[2,16,3584]{2,1,0:T(8,128)S(1)}, u32[]{:S(2)}, u32[]{:S(2)}) %collective-permute-start.10) | collective-permute-done | bytes 458784 | tf_op jit(solution)/shard_map/ppermute | solution.py:133
  159.3 9.2 %collective-permute-done.9 = f32[2,16,3584]{2,1,0:T(8,128)S(1)} collective-permute-done((f32[2,16,3584]{2,1,0:T(8,128)}, f32[2,16,3584]{2,1,0:T(8,128)S(1)}, u32[]{:S(2)}, u32[]{:S(2)}) %collective-permute-start.9) | collective-permute-done | bytes 458784 | tf_op jit(solution)/shard_map/ppermute | solution.py:133
  168.6 1.8 %fusion.17 = bf16[2,16,3584]{2,1,0:T(8,128)(2,1)} fusion(f32[2,16,3584]{2,1,0:T(8,128)S(1)} %collective-permute-done.10, f32[2,16,3584]{2,1,0:T(8,128)S(1)} %collective-permute-done.9, f32[2,16,3584]{2,1,0:T(8,128)S(1)} %collective-permute-done.8, f32[2,4,16,3584]{3,2,1,0:T(8,128)} %copy-done.2, f32[1,16,3584]{2,1,0:T(8,128)S(1)} %convolution_bitcast_fusion, ...), kind=kLoop, calls=%fused_computation.28 | loop fusion | flops 688128 | bytes 2523136 | tf_op jit(solution)/shard_map/convert_element_type | solution.py:178
  (60 shorter events, 23.9 us)
Async XLA Ops:
  0.0 27.4 %collective-permute-start = (bf16[2,16,3584]{2,1,0:T(8,128)(2,1)}, bf16[2,16,3584]{2,1,0:T(8,128)(2,1)S(1)}, u32[]{:S(2)}, u32[]{:S(2)}) collective-permute-start(bf16[2,16,3584]{2,1,0:T(8,128)(2,1)} %param.7), channel_id=1, source_target_pairs={{0,1},{1,0},{2,3},{3,2},{4,5},{5,4},{6,7},{7,6},{8,9},{9,8},{10,11... | collective-permute-start | bytes 688136 | tf_op jit(solution)/shard_map/ppermute | solution.py:133
  1.4 29.6 %collective-permute-start.1 = (bf16[2,16,3584]{2,1,0:T(8,128)(2,1)}, bf16[2,16,3584]{2,1,0:T(8,128)(2,1)S(1)}, u32[]{:S(2)}, u32[]{:S(2)}) collective-permute-start(bf16[2,16,3584]{2,1,0:T(8,128)(2,1)} %param.7), channel_id=1, source_target_pairs={{0,2},{1,3},{2,0},{3,1},{4,6},{5,7},{6,4},{7,5},{8,10},{9,11},{10,... | collective-permute-start | bytes 688136 | tf_op jit(solution)/shard_map/ppermute | solution.py:133
  2.8 30.3 %collective-permute-start.2 = (bf16[2,16,3584]{2,1,0:T(8,128)(2,1)}, bf16[2,16,3584]{2,1,0:T(8,128)(2,1)S(1)}, u32[]{:S(2)}, u32[]{:S(2)}) collective-permute-start(bf16[2,16,3584]{2,1,0:T(8,128)(2,1)} %param.7), channel_id=1, source_target_pairs={{0,3},{1,2},{2,1},{3,0},{4,7},{5,6},{6,5},{7,4},{8,11},{9,10},{10,... | collective-permute-start | bytes 688136 | tf_op jit(solution)/shard_map/ppermute | solution.py:133
  3.1 30.7 %collective-permute-start.3 = (bf16[2,16,3584]{2,1,0:T(8,128)(2,1)}, bf16[2,16,3584]{2,1,0:T(8,128)(2,1)S(1)}, u32[]{:S(2)}, u32[]{:S(2)}) collective-permute-start(bf16[2,16,3584]{2,1,0:T(8,128)(2,1)} %param.7), channel_id=1, source_target_pairs={{0,6},{1,7},{2,4},{3,5},{4,2},{5,3},{6,0},{7,1},{8,14},{9,15},{10,... | collective-permute-start | bytes 688136 | tf_op jit(solution)/shard_map/ppermute | solution.py:133
  5.9 28.6 %collective-permute-start.4 = (bf16[2,16,3584]{2,1,0:T(8,128)(2,1)}, bf16[2,16,3584]{2,1,0:T(8,128)(2,1)S(1)}, u32[]{:S(2)}, u32[]{:S(2)}) collective-permute-start(bf16[2,16,3584]{2,1,0:T(8,128)(2,1)} %param.7), channel_id=1, source_target_pairs={{0,7},{1,6},{2,5},{3,4},{4,3},{5,2},{6,1},{7,0},{8,15},{9,14},{10,... | collective-permute-start | bytes 688136 | tf_op jit(solution)/shard_map/ppermute | solution.py:133
  12.6 39.2 %all-to-all-start.2 = ((bf16[128,2,3584]{2,1,0:T(2,128)(2,1)}), bf16[128,2,3584]{2,1,0:T(2,128)(2,1)S(1)}, u32[]{:S(2)}, u32[]{:S(2)}) async-start(bf16[128,2,3584]{2,1,0:T(2,128)(2,1)} %shard_map.75), calls=%async_computation.2 | async-start | bytes 3670016 | tf_op jit(solution)/shard_map/all_to_all | solution.py:165
  22.6 4.1 %copy-start.3 = (bf16[2,16,3584]{2,1,0:T(8,128)(2,1)S(1)}, bf16[2,16,3584]{2,1,0:T(8,128)(2,1)}, u32[]{:S(2)}) copy-start(bf16[2,16,3584]{2,1,0:T(8,128)(2,1)} %param.7) | copy-start | bytes 688132
  27.4 23.6 %collective-permute-start.5 = (bf16[2,16,3584]{2,1,0:T(8,128)(2,1)S(1)}, bf16[2,16,3584]{2,1,0:T(8,128)(2,1)S(1)}, u32[]{:S(2)}, u32[]{:S(2)}) collective-permute-start(bf16[2,16,3584]{2,1,0:T(8,128)(2,1)S(1)} %copy-done.3), channel_id=1, source_target_pairs={{0,4},{1,5},{2,6},{3,7},{4,0},{5,1},{6,2},{7,3},{8,12},{9,13},{10,... | collective-permute-start | bytes 688136 | tf_op jit(solution)/shard_map/ppermute | solution.py:133
  31.1 30.2 %collective-permute-start.6 = (bf16[2,16,3584]{2,1,0:T(8,128)(2,1)S(1)}, bf16[2,16,3584]{2,1,0:T(8,128)(2,1)S(1)}, u32[]{:S(2)}, u32[]{:S(2)}) collective-permute-start(bf16[2,16,3584]{2,1,0:T(8,128)(2,1)S(1)} %copy-done.3), channel_id=1, source_target_pairs={{0,5},{1,4},{2,7},{3,6},{4,1},{5,0},{6,3},{7,2},{8,13},{9,12},{10,... | collective-permute-start | bytes 688136 | tf_op jit(solution)/shard_map/ppermute | solution.py:133
  51.7 1.3 copy-start.1
  53.0 35.6 %all-to-all-start = ((bf16[128,2,3584]{2,1,0:T(2,128)(2,1)}), bf16[128,2,3584]{2,1,0:T(2,128)(2,1)}, u32[]{:S(2)}, u32[]{:S(2)}) async-start(bf16[128,2,3584]{2,1,0:T(2,128)(2,1)} %shard_map.73), calls=%async_computation | async-start | bytes 3670016 | tf_op jit(solution)/shard_map/all_to_all | solution.py:165
  61.2 3.3 %copy-start.4 = (bf16[3,3584,128]{2,1,0:T(8,128)(2,1)S(1)}, bf16[3,3584,128]{2,1,0:T(8,128)(2,1)}, u32[]{:S(2)}) copy-start(bf16[3,3584,128]{2,1,0:T(8,128)(2,1)} %param.13) | copy-start | bytes 8257540
  67.3 2.3 %copy-start = (f32[2,8,16,3584]{3,2,1,0:T(8,128)}, f32[2,8,16,3584]{3,2,1,0:T(8,128)S(1)}, u32[]{:S(2)}) copy-start(f32[2,8,16,3584]{3,2,1,0:T(8,128)S(1)} %fusion.4) | copy-start | bytes 11010052
  69.7 56.6 %collective-permute-start.7 = (f32[2,4,16,3584]{3,2,1,0:T(8,128)}, f32[2,4,16,3584]{3,2,1,0:T(8,128)}, u32[]{:S(2)}, u32[]{:S(2)}) collective-permute-start(f32[2,4,16,3584]{3,2,1,0:T(8,128)} %slice.49), channel_id=1, source_target_pairs={{0,1},{1,0},{2,3},{3,2},{4,5},{5,4},{6,7},{7,6},{8,9},{9,8},{10,11... | collective-permute-start | bytes 5505032 | tf_op jit(solution)/shard_map/ppermute | solution.py:133
  84.2 8.8 %copy-start.6 = (f32[2,16,8]{1,2,0:T(8,128)S(1)}, f32[2,16,8]{1,2,0:T(8,128)}, u32[]{:S(2)}) copy-start(f32[2,16,8]{1,2,0:T(8,128)} %param.9) | copy-start | bytes 3076
  88.7 32.2 %all-to-all-start.3 = ((bf16[128,2,3584]{2,1,0:T(2,128)(2,1)}), bf16[128,2,3584]{2,1,0:T(2,128)(2,1)S(1)}, u32[]{:S(2)}, u32[]{:S(2)}) async-start(bf16[128,2,3584]{2,1,0:T(2,128)(2,1)} %shard_map.76), calls=%async_computation.3 | async-start | bytes 3670016 | tf_op jit(solution)/shard_map/all_to_all | solution.py:167
  120.9 33.1 %all-to-all-start.1 = ((bf16[128,2,3584]{2,1,0:T(2,128)(2,1)}), bf16[128,2,3584]{2,1,0:T(2,128)(2,1)}, u32[]{:S(2)}, u32[]{:S(2)}) async-start(bf16[128,2,3584]{2,1,0:T(2,128)(2,1)} %shard_map.74), calls=%async_computation.1 | async-start | bytes 3670016 | tf_op jit(solution)/shard_map/all_to_all | solution.py:167
  128.5 1.3 copy-start.2
  129.8 5.0 %copy-start.5 = (f32[16,256]{0,1:T(8,128)S(1)}, f32[16,256]{0,1:T(8,128)}, u32[]{:S(2)}) copy-start(f32[16,256]{0,1:T(8,128)} %fusion.20) | copy-start | bytes 49156
  130.9 28.5 %collective-permute-start.10 = (f32[2,16,3584]{2,1,0:T(8,128)}, f32[2,16,3584]{2,1,0:T(8,128)S(1)}, u32[]{:S(2)}, u32[]{:S(2)}) collective-permute-start(f32[2,16,3584]{2,1,0:T(8,128)} %get-tuple-element.6), channel_id=1, source_target_pairs={{0,4},{1,5},{2,6},{3,7},{4,0},{5,1},{6,2},{7,3},{8,12},{9,13},{10,... | collective-permute-start | bytes 1376264 | tf_op jit(solution)/shard_map/ppermute | solution.py:133
  133.9 34.7 %collective-permute-start.9 = (f32[2,16,3584]{2,1,0:T(8,128)}, f32[2,16,3584]{2,1,0:T(8,128)S(1)}, u32[]{:S(2)}, u32[]{:S(2)}) collective-permute-start(f32[2,16,3584]{2,1,0:T(8,128)} %get-tuple-element.7), channel_id=1, source_target_pairs={{0,6},{1,7},{2,4},{3,5},{4,2},{5,3},{6,0},{7,1},{8,14},{9,15},{10,... | collective-permute-start | bytes 1376264 | tf_op jit(solution)/shard_map/ppermute | solution.py:133
  134.7 33.9 %collective-permute-start.8 = (f32[2,16,3584]{2,1,0:T(8,128)}, f32[2,16,3584]{2,1,0:T(8,128)S(1)}, u32[]{:S(2)}, u32[]{:S(2)}) collective-permute-start(f32[2,16,3584]{2,1,0:T(8,128)} %get-tuple-element.5), channel_id=1, source_target_pairs={{0,2},{1,3},{2,0},{3,1},{4,6},{5,7},{6,4},{7,5},{8,10},{9,11},{10,... | collective-permute-start | bytes 1376264 | tf_op jit(solution)/shard_map/ppermute | solution.py:133

commit v18 on v17

--- a/solution.py
+++ b/solution.py
@@ -133,7 +133,7 @@
     return lax.ppermute(block, "ep", [(low, gray_partner(low, mask)) for low in range(count)])
 
 
-def shared_expert(tokens, shared_weights, group=8):
+def shared_partials(tokens, shared_weights, group=8):
     step_count, row_count, model_width = tokens.shape
     pieces = [tokens] + [xor_partner(tokens, mask) for mask in range(1, group)]
     gathered = jnp.concatenate(pieces, axis=1)
@@ -145,7 +145,10 @@
         hidden, shared_weights[2], (((1,), (1,)), ((), ())), preferred_element_type=jnp.float32
     )
     partial_value = partial_value.reshape(step_count, group, row_count, model_width)
-    partial_value = partial_value[:, 0::2] + xor_partner(partial_value[:, 1::2], 1)
+    return partial_value[:, 0::2] + xor_partner(partial_value[:, 1::2], 1)
+
+
+def shared_finish(partial_value, group=8):
     total = partial_value[:, 0]
     for slot in range(1, group // 2):
         total = total + xor_partner(partial_value[:, slot], slot * 2)
@@ -158,11 +161,14 @@
     device_count = lax.axis_size("ep")
     experts = w_gate.shape[0] * device_count
     capacity = max(2, row_count * top_count * 2 // experts)
+    chip_sums = shared_partials(tokens, shared_weights)
     routed_steps = []
     for s in range(step_count):
         dispatch, combine = route_tables(expert_ids[s], combine_weights[s], experts, capacity)
         outgoing = dispatch_rows(dispatch, tokens[s], experts, capacity)
         received = lax.all_to_all(outgoing, "ep", split_axis=0, concat_axis=0, tiled=True)
+        if s == step_count - 1:
+            received, chip_sums = lax.optimization_barrier((received, chip_sums))
         expert_out = expert_rows(received, w_gate, w_up, w_down)
         returned = lax.all_to_all(expert_out, "ep", split_axis=0, concat_axis=0, tiled=True)
         routed_steps.append(
@@ -173,7 +179,7 @@
                 precision=lax.Precision.HIGHEST,
             )
         )
-    shared = shared_expert(tokens, shared_weights)
+    shared = shared_finish(chip_sums)
     routed = jnp.stack(routed_steps)
     return (shared + routed).astype(jnp.bfloat16)
 

time: 171 us -> 178 us (1.041)
  waiting for transfers between devices: 62.8 us -> 71 us
  local copies, waits for them, and re-layouts: 14.7 us -> 12.7 us
    ppermute x11, waiting for transfers between devices: 28.1 us -> 37.5 us  [xor_partner(): lax.ppermute(block, 'ep', [(low, gray_partner(low, mask)) for low in rang...]
    unnamed x21 -> x19, local copies, waits for them, and re-layouts: 8.39 us -> 3.5 us
    all_to_all x2, waiting for transfers between devices: 30.3 us -> 27.5 us  [shards(): lax.all_to_all(expert_out, 'ep', split_axis=0, concat_axis=0, tiled=True)]
    squeeze x1 -> x2, local copies, waits for them, and re-layouts: 1.12 us -> 3.89 us  [shared_finish(): total = total + xor_partner(partial_value[:, slot], slot * 2)]
  transfers between devices with their start and end apart: 15 -> 15, of which waited for: 6 -> 8; matrix products, arithmetic and copies ran while one was open for 15% -> 14% of each run, Pallas kernels for 19% -> 18%
where the time goes in v18:
time: 178 us; the launch traced here: 177 us
  waiting for transfers between devices  71 us (40%)
  starting transfers between devices  42.6 us (24%)
  Pallas kernels  32.7 us (18%)
  matrix products  12.9 us (7%)
  local copies, waits for them, and re-layouts  12.7 us (7%)
  other arithmetic  5.46 us (3%)
    ppermute x11, waiting for transfers between devices, xor_partner(): lax.ppermute(block, 'ep', [(low, gray_partner(low, mask)) for low in rang...  37.5 us
    all_to_all x2, waiting for transfers between devices, shards(): lax.all_to_all(expert_out, 'ep', split_axis=0, concat_axis=0, tiled=True)  27.5 us
    pallas_call x2, Pallas kernels, expert_rows(): pl.pallas_call(ffn_kernel, out_shape=jax.ShapeDtypeStruct(token_block.sha...  27 us
    all_to_all x2, starting transfers between devices, shards(): lax.all_to_all(outgoing, 'ep', split_axis=0, concat_axis=0, tiled=True)  17.3 us
    ppermute x11, starting transfers between devices, xor_partner(): lax.ppermute(block, 'ep', [(low, gray_partner(low, mask)) for low in rang...  15.6 us
    all_to_all x2, starting transfers between devices, shards(): lax.all_to_all(expert_out, 'ep', split_axis=0, concat_axis=0, tiled=True)  9.69 us
    all_to_all x2, waiting for transfers between devices, shards(): lax.all_to_all(outgoing, 'ep', split_axis=0, concat_axis=0, tiled=True)  5.98 us
    pallas_call x2, Pallas kernels, dispatch_rows(): pl.pallas_call(dispatch_kernel, out_shape=jax.ShapeDtypeStruct((experts,...  5.61 us
  transfers between devices with their start and end apart: 15, of which 8 were waited for; matrix products, arithmetic and copies ran while one was open for 14% of the time, Pallas kernels for 18%

profile of v18, /device:TPU:1, one launch (start us, length us, event | category | flops | bytes accessed | tf_op | source)
XLA Modules:
  0.0 177.4 jit_solution(15127963533164703385)
XLA Ops:
  3.1 2.8 %collective-permute-start.3 = (bf16[2,16,3584]{2,1,0:T(8,128)(2,1)}, bf16[2,16,3584]{2,1,0:T(8,128)(2,1)S(1)}, u32[]{:S(2)}, u32[]{:S(2)}) collective-permute-start(bf16[2,16,3584]{2,1,0:T(8,128)(2,1)} %param.7), channel_id=1, source_target_pairs={{0,6},{1,7},{2,4},{3,5},{4,2},{5,3},{6,0},{7,1},{8,14},{9,15},{10,... | collective-permute-start | bytes 688136 | tf_op jit(solution)/shard_map/ppermute | solution.py:133
  10.1 2.8 %shard_map.74 = bf16[128,2,3584]{2,1,0:T(2,128)(2,1)} custom-call(bf16[256,16]{1,0:T(8,128)(2,1)} %convolution_convert_fusion.select_ref, bf16[16,3584]{1,0:T(8,128)(2,1)} %get-tuple-element.11.token_ref), custom_call_target="tpu_custom_call" | custom-call | tf_op jit(solution)/shard_map/pallas_call | solution.py:75
  12.9 10.0 %all-to-all-start.1 = ((bf16[128,2,3584]{2,1,0:T(2,128)(2,1)}), bf16[128,2,3584]{2,1,0:T(2,128)(2,1)S(1)}, u32[]{:S(2)}, u32[]{:S(2)}) async-start(bf16[128,2,3584]{2,1,0:T(2,128)(2,1)} %shard_map.74), calls=%async_computation.1 | async-start | bytes 3670016 | tf_op jit(solution)/shard_map/all_to_all | solution.py:169
  24.0 2.8 %shard_map.73 = bf16[128,2,3584]{2,1,0:T(2,128)(2,1)} custom-call(bf16[256,16]{1,0:T(8,128)(2,1)} %copy.35.select_ref, bf16[16,3584]{1,0:T(8,128)(2,1)} %get-tuple-element.12.token_ref), custom_call_target="tpu_custom_call" | custom-call | tf_op jit(solution)/shard_map/pallas_call | solution.py:75
  26.8 3.0 %collective-permute-start.5 = (bf16[2,16,3584]{2,1,0:T(8,128)(2,1)S(1)}, bf16[2,16,3584]{2,1,0:T(8,128)(2,1)S(1)}, u32[]{:S(2)}, u32[]{:S(2)}) collective-permute-start(bf16[2,16,3584]{2,1,0:T(8,128)(2,1)S(1)} %copy-done.2), channel_id=1, source_target_pairs={{0,4},{1,5},{2,6},{3,7},{4,0},{5,1},{6,2},{7,3},{8,12},{9,13},{10,... | collective-permute-start | bytes 688136 | tf_op jit(solution)/shard_map/ppermute | solution.py:133
  31.3 20.1 %collective-permute-done.5 = bf16[2,16,3584]{2,1,0:T(8,128)(2,1)S(1)} collective-permute-done((bf16[2,16,3584]{2,1,0:T(8,128)(2,1)S(1)}, bf16[2,16,3584]{2,1,0:T(8,128)(2,1)S(1)}, u32[]{:S(2)}, u32[]{:S(2)}) %collective-permute-start.5) | collective-permute-done | bytes 229408 | tf_op jit(solution)/shard_map/ppermute | solution.py:133
  51.4 4.9 %collective-permute-done.6 = bf16[2,16,3584]{2,1,0:T(8,128)(2,1)S(1)} collective-permute-done((bf16[2,16,3584]{2,1,0:T(8,128)(2,1)S(1)}, bf16[2,16,3584]{2,1,0:T(8,128)(2,1)S(1)}, u32[]{:S(2)}, u32[]{:S(2)}) %collective-permute-start.6) | collective-permute-done | bytes 229408 | tf_op jit(solution)/shard_map/ppermute | solution.py:133
  60.7 7.3 %all-to-all-start = ((bf16[128,2,3584]{2,1,0:T(2,128)(2,1)}), bf16[128,2,3584]{2,1,0:T(2,128)(2,1)}, u32[]{:S(2)}, u32[]{:S(2)}) async-start(bf16[128,2,3584]{2,1,0:T(2,128)(2,1)} %shard_map.73), calls=%async_computation | async-start | bytes 3670016 | tf_op jit(solution)/shard_map/all_to_all | solution.py:169
  68.0 2.4 %multiply_convert_fusion = bf16[256,128]{1,0:T(8,128)(2,1)S(1)} fusion(f32[256,128]{1,0:T(8,128)S(1)} %fusion.8, bf16[256,3584]{1,0:T(8,128)(2,1)} %bitcast.54, bf16[3,3584,128]{2,1,0:T(8,128)(2,1)} %param.13), kind=kOutput, calls=%fused_computation.33 | convolution fusion | flops 235077632 | bytes 2949120 | tf_op jit(solution)/shard_map/dot_general | solution.py:142
  70.3 1.8 %fusion.4 = f32[2,8,16,3584]{3,2,1,0:T(8,128)S(1)} fusion(bf16[2,8,16,128]{3,2,1,0:T(8,128)(2,1)S(1)} %bitcast.52, bf16[3,3584,128]{2,1,0:T(8,128)(2,1)} %param.13), kind=kOutput, calls=%fused_computation.11 | convolution fusion | flops 234881024 | bytes 4653056 | tf_op jit(solution)/shard_map/dot_general | solution.py:144
  75.9 13.6 %shard_map.75 = bf16[128,2,3584]{2,1,0:T(2,128)(2,1)} custom-call(bf16[128,2,3584]{2,1,0:T(2,128)(2,1)} %copy-done.1, bf16[1,3584,1024]{2,1,0:T(8,128)(2,1)} %gate_ref.3, bf16[1,3584,1024]{2,1,0:T(8,128)(2,1)} %up_ref.3, bf16[1,1024,3584]{2,1,0:T(8,128)(2,1)} %down_ref.3), custom_call_target="tpu_custom_call" | custom-call | flops 5637144576 | bytes 25690112 | tf_op jit(solution)/shard_map/pallas_call | solution.py:45
  89.4 6.0 %all-to-all-done.x_ref = bf16[128,2,3584]{2,1,0:T(2,128)(2,1)} async-done(((bf16[128,2,3584]{2,1,0:T(2,128)(2,1)}), bf16[128,2,3584]{2,1,0:T(2,128)(2,1)}, u32[]{:S(2)}, u32[]{:S(2)}) %all-to-all-start) | async-done | bytes 1835040 | tf_op jit(solution)/shard_map/all_to_all | solution.py:169
  95.4 4.3 %all-to-all-start.2 = ((bf16[128,2,3584]{2,1,0:T(2,128)(2,1)}), bf16[128,2,3584]{2,1,0:T(2,128)(2,1)S(1)}, u32[]{:S(2)}, u32[]{:S(2)}) async-start(bf16[128,2,3584]{2,1,0:T(2,128)(2,1)} %shard_map.75), calls=%async_computation.2 | async-start | bytes 3670016 | tf_op jit(solution)/shard_map/all_to_all | solution.py:173
  101.9 3.5 %slice_add_fusion = f32[2,4,16,3584]{3,2,1,0:T(8,128)} fusion(f32[2,4,16,3584]{3,2,1,0:T(8,128)} %collective-permute-done.7, f32[2,8,16,3584]{3,2,1,0:T(8,128)} %copy-done), kind=kLoop, calls=%fused_computation.4 | loop fusion | flops 458752 | bytes 5505024 | tf_op jit(solution)/shard_map/add | solution.py:148
  105.4 13.5 %shard_map.76 = bf16[128,2,3584]{2,1,0:T(2,128)(2,1)} custom-call(bf16[128,2,3584]{2,1,0:T(2,128)(2,1)} %all-to-all-done.x_ref, bf16[1,3584,1024]{2,1,0:T(8,128)(2,1)} %gate_ref.3, bf16[1,3584,1024]{2,1,0:T(8,128)(2,1)} %up_ref.3, bf16[1,1024,3584]{2,1,0:T(8,128)(2,1)} %down_ref.3), custom_call_target="tpu_custom_call" | custom-call | flops 5637144576 | bytes 25690112 | tf_op jit(solution)/shard_map/pallas_call | solution.py:45
  118.9 8.7 %all-to-all-done.2 = bf16[128,2,3584]{2,1,0:T(2,128)(2,1)S(1)} async-done(((bf16[128,2,3584]{2,1,0:T(2,128)(2,1)}), bf16[128,2,3584]{2,1,0:T(2,128)(2,1)S(1)}, u32[]{:S(2)}, u32[]{:S(2)}) %all-to-all-start.2) | async-done | bytes 1835040 | tf_op jit(solution)/shard_map/all_to_all | solution.py:173
  127.6 5.3 %all-to-all-start.3 = ((bf16[128,2,3584]{2,1,0:T(2,128)(2,1)}), bf16[128,2,3584]{2,1,0:T(2,128)(2,1)}, u32[]{:S(2)}, u32[]{:S(2)}) async-start(bf16[128,2,3584]{2,1,0:T(2,128)(2,1)} %shard_map.76), calls=%async_computation.3 | async-start | bytes 3670016 | tf_op jit(solution)/shard_map/all_to_all | solution.py:173
  133.0 2.1 %slice_bitcast_fusion.1 = (f32[2,16,3584]{2,1,0:T(8,128)}, f32[2,16,3584]{2,1,0:T(8,128)S(1)}) fusion(f32[2,4,16,3584]{3,2,1,0:T(8,128)} %slice_add_fusion), kind=kLoop, calls=%fused_computation.21 | loop fusion | bytes 1835008 | tf_op jit(solution)/shard_map/squeeze | solution.py:154
  136.5 1.9 %collective-permute-start.9 = (f32[2,16,3584]{2,1,0:T(8,128)S(1)}, f32[2,16,3584]{2,1,0:T(8,128)S(1)}, u32[]{:S(2)}, u32[]{:S(2)}) collective-permute-start(f32[2,16,3584]{2,1,0:T(8,128)S(1)} %get-tuple-element.10), channel_id=1, source_target_pairs={{0,6},{1,7},{2,4},{3,5},{4,2},{5,3},{6,0},{7,1},{8,14},{9,15},{10,... | collective-permute-start | bytes 1376264 | tf_op jit(solution)/shard_map/ppermute | solution.py:133
  138.3 1.8 %slice_bitcast_fusion.3 = f32[2,16,3584]{2,1,0:T(8,128)} fusion(f32[2,4,16,3584]{3,2,1,0:T(8,128)} %slice_add_fusion), kind=kLoop, calls=%fused_computation.28 | loop fusion | bytes 917504 | tf_op jit(solution)/shard_map/squeeze | solution.py:154
  141.7 18.8 %all-to-all-done.3 = bf16[128,2,3584]{2,1,0:T(2,128)(2,1)} async-done(((bf16[128,2,3584]{2,1,0:T(2,128)(2,1)}), bf16[128,2,3584]{2,1,0:T(2,128)(2,1)}, u32[]{:S(2)}, u32[]{:S(2)}) %all-to-all-start.3) | async-done | bytes 1835040 | tf_op jit(solution)/shard_map/all_to_all | solution.py:173
  160.5 2.5 %convolution_bitcast_fusion = f32[1,16,3584]{2,1,0:T(8,128)S(1)} fusion(bf16[128,2,3584]{2,1,0:T(2,128)(2,1)} %all-to-all-done.3, f32[16,128,2]{0,2,1:T(2,128)} %bitcast.50), kind=kOutput, calls=%fused_computation | convolution fusion | flops 176160768 | bytes 2080768 | tf_op jit(solution)/shard_map/tec,ecd->td/dot_general | solution.py:175
  164.9 10.6 %collective-permute-done.10 = f32[2,16,3584]{2,1,0:T(8,128)} collective-permute-done((f32[2,16,3584]{2,1,0:T(8,128)}, f32[2,16,3584]{2,1,0:T(8,128)}, u32[]{:S(2)}, u32[]{:S(2)}) %collective-permute-start.10) | collective-permute-done | bytes 458784 | tf_op jit(solution)/shard_map/ppermute | solution.py:133
  175.5 2.0 %fusion.17 = bf16[2,16,3584]{2,1,0:T(8,128)(2,1)} fusion(f32[2,16,3584]{2,1,0:T(8,128)} %collective-permute-done.10, f32[2,16,3584]{2,1,0:T(8,128)S(1)} %collective-permute-done.9, f32[2,16,3584]{2,1,0:T(8,128)S(1)} %collective-permute-done.8, f32[1,16,3584]{2,1,0:T(8,128)S(1)} %convolution_bitcast_fusion, f32[1,16,3584]{2,1,0:T(8,128)S(1)} %convolution_bitcast_fusion.1, ...), kind=kLoop, calls=%fused_computation.27 | loop fusion | flops 688128 | bytes 2523136 | tf_op jit(solution)/shard_map/convert_element_type | solution.py:184
  (60 shorter events, 25.0 us)
Async XLA Ops:
  0.0 26.8 %collective-permute-start = (bf16[2,16,3584]{2,1,0:T(8,128)(2,1)}, bf16[2,16,3584]{2,1,0:T(8,128)(2,1)S(1)}, u32[]{:S(2)}, u32[]{:S(2)}) collective-permute-start(bf16[2,16,3584]{2,1,0:T(8,128)(2,1)} %param.7), channel_id=1, source_target_pairs={{0,1},{1,0},{2,3},{3,2},{4,5},{5,4},{6,7},{7,6},{8,9},{9,8},{10,11... | collective-permute-start | bytes 688136 | tf_op jit(solution)/shard_map/ppermute | solution.py:133
  1.4 28.4 %collective-permute-start.1 = (bf16[2,16,3584]{2,1,0:T(8,128)(2,1)}, bf16[2,16,3584]{2,1,0:T(8,128)(2,1)S(1)}, u32[]{:S(2)}, u32[]{:S(2)}) collective-permute-start(bf16[2,16,3584]{2,1,0:T(8,128)(2,1)} %param.7), channel_id=1, source_target_pairs={{0,2},{1,3},{2,0},{3,1},{4,6},{5,7},{6,4},{7,5},{8,10},{9,11},{10,... | collective-permute-start | bytes 688136 | tf_op jit(solution)/shard_map/ppermute | solution.py:133
  2.8 28.4 %collective-permute-start.2 = (bf16[2,16,3584]{2,1,0:T(8,128)(2,1)}, bf16[2,16,3584]{2,1,0:T(8,128)(2,1)S(1)}, u32[]{:S(2)}, u32[]{:S(2)}) collective-permute-start(bf16[2,16,3584]{2,1,0:T(8,128)(2,1)} %param.7), channel_id=1, source_target_pairs={{0,3},{1,2},{2,1},{3,0},{4,7},{5,6},{6,5},{7,4},{8,11},{9,10},{10,... | collective-permute-start | bytes 688136 | tf_op jit(solution)/shard_map/ppermute | solution.py:133
  3.1 28.2 %collective-permute-start.3 = (bf16[2,16,3584]{2,1,0:T(8,128)(2,1)}, bf16[2,16,3584]{2,1,0:T(8,128)(2,1)S(1)}, u32[]{:S(2)}, u32[]{:S(2)}) collective-permute-start(bf16[2,16,3584]{2,1,0:T(8,128)(2,1)} %param.7), channel_id=1, source_target_pairs={{0,6},{1,7},{2,4},{3,5},{4,2},{5,3},{6,0},{7,1},{8,14},{9,15},{10,... | collective-permute-start | bytes 688136 | tf_op jit(solution)/shard_map/ppermute | solution.py:133
  5.9 25.4 %collective-permute-start.4 = (bf16[2,16,3584]{2,1,0:T(8,128)(2,1)}, bf16[2,16,3584]{2,1,0:T(8,128)(2,1)S(1)}, u32[]{:S(2)}, u32[]{:S(2)}) collective-permute-start(bf16[2,16,3584]{2,1,0:T(8,128)(2,1)} %param.7), channel_id=1, source_target_pairs={{0,7},{1,6},{2,5},{3,4},{4,3},{5,2},{6,1},{7,0},{8,15},{9,14},{10,... | collective-permute-start | bytes 688136 | tf_op jit(solution)/shard_map/ppermute | solution.py:133
  12.9 46.5 %all-to-all-start.1 = ((bf16[128,2,3584]{2,1,0:T(2,128)(2,1)}), bf16[128,2,3584]{2,1,0:T(2,128)(2,1)S(1)}, u32[]{:S(2)}, u32[]{:S(2)}) async-start(bf16[128,2,3584]{2,1,0:T(2,128)(2,1)} %shard_map.74), calls=%async_computation.1 | async-start | bytes 3670016 | tf_op jit(solution)/shard_map/all_to_all | solution.py:169
  23.0 3.8 %copy-start.2 = (bf16[2,16,3584]{2,1,0:T(8,128)(2,1)S(1)}, bf16[2,16,3584]{2,1,0:T(8,128)(2,1)}, u32[]{:S(2)}) copy-start(bf16[2,16,3584]{2,1,0:T(8,128)(2,1)} %param.7) | copy-start | bytes 688132
  26.8 24.6 %collective-permute-start.5 = (bf16[2,16,3584]{2,1,0:T(8,128)(2,1)S(1)}, bf16[2,16,3584]{2,1,0:T(8,128)(2,1)S(1)}, u32[]{:S(2)}, u32[]{:S(2)}) collective-permute-start(bf16[2,16,3584]{2,1,0:T(8,128)(2,1)S(1)} %copy-done.2), channel_id=1, source_target_pairs={{0,4},{1,5},{2,6},{3,7},{4,0},{5,1},{6,2},{7,3},{8,12},{9,13},{10,... | collective-permute-start | bytes 688136 | tf_op jit(solution)/shard_map/ppermute | solution.py:133
  29.8 26.5 %collective-permute-start.6 = (bf16[2,16,3584]{2,1,0:T(8,128)(2,1)S(1)}, bf16[2,16,3584]{2,1,0:T(8,128)(2,1)S(1)}, u32[]{:S(2)}, u32[]{:S(2)}) collective-permute-start(bf16[2,16,3584]{2,1,0:T(8,128)(2,1)S(1)} %copy-done.2), channel_id=1, source_target_pairs={{0,5},{1,4},{2,7},{3,6},{4,1},{5,0},{6,3},{7,2},{8,13},{9,12},{10,... | collective-permute-start | bytes 688136 | tf_op jit(solution)/shard_map/ppermute | solution.py:133
  56.4 1.2 copy-start.4
  59.4 1.3 copy-start.1
  60.7 34.7 %all-to-all-start = ((bf16[128,2,3584]{2,1,0:T(2,128)(2,1)}), bf16[128,2,3584]{2,1,0:T(2,128)(2,1)}, u32[]{:S(2)}, u32[]{:S(2)}) async-start(bf16[128,2,3584]{2,1,0:T(2,128)(2,1)} %shard_map.73), calls=%async_computation | async-start | bytes 3670016 | tf_op jit(solution)/shard_map/all_to_all | solution.py:169
  72.2 2.4 %copy-start = (f32[2,8,16,3584]{3,2,1,0:T(8,128)}, f32[2,8,16,3584]{3,2,1,0:T(8,128)S(1)}, u32[]{:S(2)}) copy-start(f32[2,8,16,3584]{3,2,1,0:T(8,128)S(1)} %fusion.4) | copy-start | bytes 11010052
  72.2 3.5 %copy-start.5 = (f32[2,16,8]{1,2,0:T(8,128)S(1)}, f32[2,16,8]{1,2,0:T(8,128)}, u32[]{:S(2)}) copy-start(f32[2,16,8]{1,2,0:T(8,128)} %param.9) | copy-start | bytes 3076
  74.5 27.4 %collective-permute-start.7 = (f32[2,4,16,3584]{3,2,1,0:T(8,128)}, f32[2,4,16,3584]{3,2,1,0:T(8,128)}, u32[]{:S(2)}, u32[]{:S(2)}) collective-permute-start(f32[2,4,16,3584]{3,2,1,0:T(8,128)} %slice.51), channel_id=1, source_target_pairs={{0,1},{1,0},{2,3},{3,2},{4,5},{5,4},{6,7},{7,6},{8,9},{9,8},{10,11... | collective-permute-start | bytes 5505032 | tf_op jit(solution)/shard_map/ppermute | solution.py:133
  95.4 32.2 %all-to-all-start.2 = ((bf16[128,2,3584]{2,1,0:T(2,128)(2,1)}), bf16[128,2,3584]{2,1,0:T(2,128)(2,1)S(1)}, u32[]{:S(2)}, u32[]{:S(2)}) async-start(bf16[128,2,3584]{2,1,0:T(2,128)(2,1)} %shard_map.75), calls=%async_computation.2 | async-start | bytes 3670016 | tf_op jit(solution)/shard_map/all_to_all | solution.py:173
  127.6 32.9 %all-to-all-start.3 = ((bf16[128,2,3584]{2,1,0:T(2,128)(2,1)}), bf16[128,2,3584]{2,1,0:T(2,128)(2,1)}, u32[]{:S(2)}, u32[]{:S(2)}) async-start(bf16[128,2,3584]{2,1,0:T(2,128)(2,1)} %shard_map.76), calls=%async_computation.3 | async-start | bytes 3670016 | tf_op jit(solution)/shard_map/all_to_all | solution.py:173
  132.9 7.9 %copy-start.3 = (f32[16,256]{0,1:T(8,128)S(1)}, f32[16,256]{0,1:T(8,128)}, u32[]{:S(2)}) copy-start(f32[16,256]{0,1:T(8,128)} %fusion.20) | copy-start | bytes 49156
  135.0 28.6 %collective-permute-start.8 = (f32[2,16,3584]{2,1,0:T(8,128)}, f32[2,16,3584]{2,1,0:T(8,128)S(1)}, u32[]{:S(2)}, u32[]{:S(2)}) collective-permute-start(f32[2,16,3584]{2,1,0:T(8,128)} %get-tuple-element.9), channel_id=1, source_target_pairs={{0,2},{1,3},{2,0},{3,1},{4,6},{5,7},{6,4},{7,5},{8,10},{9,11},{10,... | collective-permute-start | bytes 1376264 | tf_op jit(solution)/shard_map/ppermute | solution.py:133
  136.5 28.5 %collective-permute-start.9 = (f32[2,16,3584]{2,1,0:T(8,128)S(1)}, f32[2,16,3584]{2,1,0:T(8,128)S(1)}, u32[]{:S(2)}, u32[]{:S(2)}) collective-permute-start(f32[2,16,3584]{2,1,0:T(8,128)S(1)} %get-tuple-element.10), channel_id=1, source_target_pairs={{0,6},{1,7},{2,4},{3,5},{4,2},{5,3},{6,0},{7,1},{8,14},{9,15},{10,... | collective-permute-start | bytes 1376264 | tf_op jit(solution)/shard_map/ppermute | solution.py:133
  140.1 35.3 %collective-permute-start.10 = (f32[2,16,3584]{2,1,0:T(8,128)}, f32[2,16,3584]{2,1,0:T(8,128)}, u32[]{:S(2)}, u32[]{:S(2)}) collective-permute-start(f32[2,16,3584]{2,1,0:T(8,128)} %slice_bitcast_fusion.3), channel_id=1, source_target_pairs={{0,4},{1,5},{2,6},{3,7},{4,0},{5,1},{6,2},{7,3},{8,12},{9,13},{10,... | collective-permute-start | bytes 1376264 | tf_op jit(solution)/shard_map/ppermute | solution.py:133
